TPU v7x, 128 devices: a whole 4x4x4 slice. The times are simulated.
128 devices in a mesh: row: 16 (over y, x), col: 8 (over z, core).
Axes of the slice: x: 4, y: 4, z: 4, core: 2. Of those that a mesh axis runs over, the one named last changes fastest.
Arguments:
- embeddings: bfloat16 [65536, 1024], P('row'), may hold values from -6 to 6
- vectors: bfloat16 [64, 65536], P(None, ('row', 'col')), may hold values from -6 to 6
- block_pairs: int32 [3968, 2], replicated, may hold values from 0 to 127, as said below
Outputs:
- new_basis: float32 [64, 65536], P(None, ('row', 'col'))
Inputs may be any that keep to these rules, and one draw needn't show every extreme that they name: `block_pairs`: no pair is listed twice, no pair has equal blocks, and every block occurs as a row block at least once.
All inputs are finite; a program needn't handle non-finite values.
Results may differ from a plain program's by a relative error of at most 0.0032.
Values may be sent and summed in bfloat16 or wider, within the bound.
No kernel may reach another device: no remote copies, remote signals or barrier semaphores. Data moves between devices by JAX's collectives and lax.ppermute only.
A program may use at most 128 MiB of HBM per device.

v0:
```python
import math

import jax
import jax.numpy as jnp
from jax import lax
from jax.sharding import PartitionSpec as P


def inverse_norms(blocks):
    return lax.rsqrt(jnp.mean(jnp.square(blocks.astype(jnp.float32)), axis=-1) + 1e-06)


def tile_terms(rows_x, cols_x, norm_rows, norm_cols, cols_v, feature_width):
    scores = jnp.dot(rows_x, cols_x.T, preferred_element_type=jnp.float32)
    affinity = jnp.exp(scores * norm_rows[:, None] * norm_cols[None, :] / math.sqrt(feature_width))
    rounded = affinity.astype(jnp.bfloat16)
    contrib = jnp.dot(cols_v, rounded.T, preferred_element_type=jnp.float32)
    return (contrib, jnp.sum(affinity, axis=1))


def tile_mask(block_pairs, near_column, col_count, row_count, here_row, here_col):
    near_ids = block_pairs[:, near_column]
    far_ids = block_pairs[:, 1 - near_column]
    member = (near_ids // col_count == here_row) & (far_ids % col_count == here_col)
    near_hot = ((near_ids % col_count)[:, None] == jnp.arange(col_count)[None, :]) & member[:, None]
    far_hot = (far_ids // col_count)[:, None] == jnp.arange(row_count)[None, :]
    return jnp.dot(
        near_hot.astype(jnp.float32).T,
        far_hot.astype(jnp.float32),
        preferred_element_type=jnp.float32,
    )


def add_block(running, contrib, row_totals, column_start, block_rows):
    sums_now, degree_now = running
    old_sums = lax.dynamic_slice_in_dim(sums_now, column_start, block_rows, 1)
    sums_now = lax.dynamic_update_slice_in_dim(sums_now, old_sums + contrib, column_start, 1)
    old_degree = lax.dynamic_slice_in_dim(degree_now, column_start, block_rows, 1)
    degree_now = lax.dynamic_update_slice_in_dim(
        degree_now, old_degree + row_totals[None, :], column_start, 1
    )
    return (sums_now, degree_now)


def per_device(embeddings, vectors, block_pairs):
    col_count = lax.axis_size("col")
    row_count = lax.axis_size("row")
    here_row = lax.axis_index("row")
    here_col = lax.axis_index("col")
    eig_count, block_rows = vectors.shape
    feature_width = embeddings.shape[1]
    near_blocks = embeddings.reshape(col_count, block_rows, feature_width)
    near_norms = inverse_norms(near_blocks)
    own_block = lax.dynamic_slice_in_dim(near_blocks, here_col, 1, 0)
    present = tile_mask(block_pairs, 0, col_count, row_count, here_row, here_col)
    start_sums = jnp.zeros((eig_count, col_count * block_rows), jnp.float32)
    start_degree = jnp.zeros((1, col_count * block_rows), jnp.float32)
    far_x = lax.all_gather(own_block, "row", axis=0, tiled=True)
    far_v = lax.all_gather(vectors[None], "row", axis=0, tiled=True)
    far_norms = inverse_norms(far_x)
    piece_blocks = far_x.shape[0]

    def visit(position, current):
        far_index = position // col_count
        near_index = position % col_count

        def compute(totals):
            contrib, row_totals = tile_terms(
                near_blocks[near_index],
                far_x[far_index],
                near_norms[near_index],
                far_norms[far_index],
                far_v[far_index],
                feature_width,
            )
            return add_block(totals, contrib, row_totals, near_index * block_rows, block_rows)

        return lax.cond(
            present[near_index, far_index] > 0.5, compute, lambda totals: totals, current
        )

    partial_sums, degree = lax.fori_loop(
        0, piece_blocks * col_count, visit, (start_sums, start_degree)
    )
    owned_sums, owned_degree = (
        lax.psum_scatter(partial_sums, "col", scatter_dimension=1, tiled=True),
        lax.psum_scatter(degree, "col", scatter_dimension=1, tiled=True),
    )
    smoothed = owned_sums / owned_degree
    total_rows = block_rows * col_count * row_count
    local_gram = jnp.dot(
        smoothed, smoothed.T, precision=lax.Precision.HIGHEST, preferred_element_type=jnp.float32
    )
    gram_matrix = lax.psum(local_gram, ("row", "col")) / total_rows
    factor = jnp.linalg.cholesky(gram_matrix)
    return lax.linalg.triangular_solve(factor, smoothed, left_side=True, lower=True)


def solution(mesh):
    return jax.shard_map(
        per_device,
        mesh=mesh,
        in_specs=(P("row", None), P(None, ("row", "col")), P()),
        out_specs=P(None, ("row", "col")),
        check_vma=False,
    )
```

profile of v0, /device:TPU:0, one launch (start us, length us, event | category | flops | bytes accessed | tf_op | source)
XLA Modules:
  0.0 733.1 jit_solution(13067909823361355176)
XLA Ops:
  9.7 5.1 multiply_reduce_fusion.1
  16.9 106.3 %all-gather.4.cloned.1.call-done = bf16[16,512,1024]{2,1,0:T(8,128)(2,1)} async-done(((bf16[1,512,1024]{2,1,0:T(8,128)(2,1)}), bf16[16,512,1024]{2,1,0:T(8,128)(2,1)}) %all-gather.4.cloned.1.call-update) | async-done | bytes 16777232 | tf_op jit(solution)/shard_map/all_gather | solution.py:58
  123.2 7.2 multiply_reduce_fusion
  130.4 37.3 %all-gather.6.cloned.1.call-done = bf16[1024,512]{1,0:T(8,128)(2,1)} async-done(((bf16[64,512]{1,0:T(8,128)(2,1)}), bf16[1024,512]{1,0:T(8,128)(2,1)}) %all-gather.6.cloned.1.call-update) | async-done | bytes 1048592 | tf_op jit(solution)/shard_map/all_gather | solution.py:59
  167.7 212.5 %while.17 = (s32[]{:T(128)}, f32[64,4096]{1,0:T(8,128)S(1)}, f32[1,4096]{1,0:T(1,128)S(1)}, f32[8,16]{1,0:T(8,128)S(1)}, bf16[16,64,512]{2,1,0:T(8,128)(2,1)}, /...) while((s32[]{:T(128)}, f32[64,4096]{1,0:T(8,128)S(1)}, ...), condition=%wide.region_6.7_spmd, body=%wide.region_2.6_spmd.sunk | while | flops 571768832 | bytes 3494516 | solution.py:82
  189.0 3.5 conditional.2
  257.8 3.5 conditional.2
  305.2 3.5 conditional.2
  305.3 2.4 fusion.27
  310.1 3.5 conditional.2
  314.9 3.5 conditional.2
  326.4 3.5 conditional.2
  331.2 3.5 conditional.2
  341.4 3.5 conditional.2
  347.6 3.5 conditional.2
  355.1 3.5 conditional.2
  369.2 3.5 conditional.2
  376.7 3.5 conditional.2
  376.8 2.4 fusion.27
  382.9 230.4 %reduce-scatter.7.cloned.1.call-done = f32[512,1]{1,0:T(8,128)} async-done(((f32[4096,1]{1,0:T(8,128)}), f32[512,1]{1,0:T(8,128)}) %reduce-scatter.7.cloned.1.call-update) | async-done | bytes 2064
  614.3 32.0 %reduce-scatter.5.cloned.1.call-done = f32[64,512]{1,0:T(8,128)} async-done(((f32[64,4096]{1,0:T(8,128)}), f32[64,512]{1,0:T(8,128)}) %reduce-scatter.5.cloned.1.call-update) | async-done | bytes 131088 | tf_op jit(solution)/shard_map/reduce_scatter | solution.py:86
  647.6 64.9 %psum.7 = f32[64,64]{0,1:T(8,128)S(1)} all-reduce(f32[64,64]{0,1:T(8,128)S(1)} %fusion.21), channel_id=1, replica_groups=mesh['row'=16,'col'=8] {'row','col'}, use_global_device_ids=true, to_apply=%region_9.10 | all-reduce | flops 4096 | bytes 32768 | tf_op jit(solution)/shard_map/psum | solution.py:94
  712.6 5.8 cholesky.16
  719.8 4.9 custom-call.6
  (319 shorter events, 134.9 us)
Async XLA Ops:
  6.5 116.7 %all-gather.4.cloned.1.call-start = ((), (), s32[]{:S(2)}) async-start(), calls=%async_computation.2 | async-start | bytes 17825792 | tf_op jit(solution)/shard_map/all_gather | solution.py:58
  8.9 158.8 %all-gather.6.cloned.1.call-start = ((), (), s32[]{:S(2)}) async-start(), calls=%async_computation.4 | async-start | bytes 1114112 | tf_op jit(solution)/shard_map/all_gather | solution.py:59
  9.6 603.6 %reduce-scatter.7.cloned.1.call-start = ((), (), s32[]{:S(2)}) async-start(), calls=%async_computation.5 | async-start | bytes 2359296
  380.3 2.1 copy-start
  382.3 264.1 %reduce-scatter.5.cloned.1.call-start = ((), (), s32[]{:S(2)}) async-start(), calls=%async_computation.3 | async-start | bytes 1179648 | tf_op jit(solution)/shard_map/reduce_scatter | solution.py:86
Sparse Core Ops, SparseCore 0:
  9.5 113.6 all-gather.3
  125.3 42.2 all-gather.5
  382.4 230.8 reduce-scatter.6
  615.5 30.8 reduce-scatter.4
where the time goes:
time: 728 us; the launch traced here: 733 us
  waiting for transfers between devices  407 us (56%)
  local copies, waits for them, and re-layouts  89 us (12%)
  loops' own time  87.5 us (12%)
  blocking collectives  64.9 us (9%)
  matrix products  44.6 us (6%)
  other arithmetic  26.5 us (4%)
  between operations  13.2 us (2%)
    unnamed x5, waiting for transfers between devices  232 us
    all_gather x1, waiting for transfers between devices, per_device(): far_x = lax.all_gather(own_block, 'row', axis=0, tiled=True)  106 us
    another operation x1, loops' own time, per_device(): lax.fori_loop(0, piece_blocks * col_count, visit, (start_sums, start_degr...  85.8 us
    dynamic_slice x128, local copies, waits for them, and re-layouts, visit(): present[near_index, far_index] > 0.5  83.3 us
    psum x1, blocking collectives, per_device(): gram_matrix = lax.psum(local_gram, ('row', 'col')) / total_rows  64.9 us
    all_gather x1, waiting for transfers between devices, per_device(): far_v = lax.all_gather(vectors[None], 'row', axis=0, tiled=True)  37.3 us
    reduce_scatter x1, waiting for transfers between devices, per_device(): lax.psum_scatter(partial_sums, 'col', scatter_dimension=1, tiled=True)  32 us
    dot_general x12, matrix products, tile_terms(): scores = jnp.dot(rows_x, cols_x.T, preferred_element_type=jnp.float32)  28.7 us
  transfers between devices with their start and end apart: 4, of which 4 were waited for; matrix products, arithmetic and copies ran while one was open for 2% of the time, Pallas kernels for 0%

commit v1 on v0

v1 whole, which is shorter than its diff:
```python
import functools
import math

import jax
import jax.numpy as jnp
from jax import lax
from jax.experimental import pallas as pl
from jax.experimental.pallas import tpu as pltpu
from jax.sharding import PartitionSpec as P

BLOCK = 512
WIDTH = 1024
EIGS = 64
NBLOCKS = 128
SIDE = 4
COLS = 8
CORES = 2
VROWS = BLOCK + EIGS // 2
PAYLOAD = VROWS + 16
ACC = EIGS + 8
SCALE = math.log2(math.e) / math.sqrt(WIDTH)
NT = (((1,), (1,)), ((), ()))


def shift(dy, dx, keep=None):
    pairs = []
    for y in range(SIDE):
        for x in range(SIDE):
            to_y, to_x = (y + dy) % SIDE, (x + dx) % SIDE
            if keep is None or keep(to_y, to_x):
                pairs.append((y * SIDE + x, to_y * SIDE + to_x))
    return pairs


def left_half(y, x):
    return x < SIDE // 2


def top_half(y, x):
    return y < SIDE // 2


STAGES = {
    "own": ((0, 0), None),
    "a": ((0, 1), None),
    "b": ((1, 0), None),
    "c": ((-1, -1), None),
    "d": ((-1, 1), None),
    "e": ((-1, -2), None),
    "g": ((0, 2), left_half),
    "h": ((2, 0), top_half),
    "f": ((2, 1), None),
    "k": ((2, 2), top_half),
}


def row_norm(x):
    return lax.rsqrt(jnp.sum(x * x, axis=1, keepdims=True) * (1.0 / WIDTH) + 1e-06)


def payload_kernel(index_ref, x_ref, v_ref, out_ref):
    x = x_ref[0]
    out_ref[0:BLOCK, :] = x
    half = EIGS // 2
    out_ref[BLOCK:VROWS, 0:BLOCK] = v_ref[0:half, :]
    out_ref[BLOCK:VROWS, BLOCK : 2 * BLOCK] = v_ref[half:EIGS, :]
    norms = jnp.broadcast_to(row_norm(x.astype(jnp.float32)) * SCALE, (BLOCK, 128))
    rows = norms.T[0:16, :]
    high = rows.astype(jnp.bfloat16)
    low = (rows - high.astype(jnp.float32)).astype(jnp.bfloat16)
    out_ref[VROWS:PAYLOAD, 0:BLOCK] = high
    out_ref[VROWS:PAYLOAD, BLOCK : 2 * BLOCK] = low


def make_payload(here_col, blocks, vectors):
    return pl.pallas_call(
        payload_kernel,
        out_shape=jax.ShapeDtypeStruct((PAYLOAD, WIDTH), jnp.bfloat16),
        grid_spec=pltpu.PrefetchScalarGridSpec(
            num_scalar_prefetch=1,
            grid=(1,),
            in_specs=[
                pl.BlockSpec((1, BLOCK, WIDTH), lambda g, index: (index[0], 0, 0)),
                pl.BlockSpec((EIGS, BLOCK), lambda g, index: (0, 0)),
            ],
            out_specs=pl.BlockSpec((PAYLOAD, WIDTH), lambda g, index: (0, 0)),
        ),
        name="payload",
    )(here_col, blocks, vectors)


def norms_kernel(x_ref, out_ref):
    out_ref[0] = jnp.broadcast_to(row_norm(x_ref[0].astype(jnp.float32)), (BLOCK, 128))


def local_norms(blocks):
    return pl.pallas_call(
        norms_kernel,
        out_shape=jax.ShapeDtypeStruct((COLS, BLOCK, 128), jnp.float32),
        grid=(COLS,),
        in_specs=[pl.BlockSpec((1, BLOCK, WIDTH), lambda g: (g, 0, 0))],
        out_specs=pl.BlockSpec((1, BLOCK, 128), lambda g: (g, 0, 0)),
        name="norms",
    )(blocks)


def cells_kernel(order_ref, flags_ref, x_ref, far_ref, v_ref, norm_ref, old_ref, new_ref, far_sums_ref, p_ref):
    step = pl.program_id(0)
    flag = flags_ref[step]
    ones = jnp.ones((16, BLOCK), jnp.bfloat16)

    @pl.when(step == 0)
    def _():
        far_sums_ref[...] = jnp.zeros_like(far_sums_ref)

    new_ref[...] = old_ref[...]

    @pl.when(flag > 0)
    def _():
        near = norm_ref[0]
        near = jnp.concatenate([near, near], axis=1)
        for at in range(0, BLOCK, 256):
            scores = lax.dot_general(
                x_ref[0], far_ref[at : at + 256, :], NT, preferred_element_type=jnp.float32
            )
            far = far_ref[VROWS : VROWS + 1, at : at + 256].astype(jnp.float32)
            far = far + far_ref[VROWS : VROWS + 1, BLOCK + at : BLOCK + at + 256].astype(jnp.float32)
            p_ref[:, at : at + 256] = jnp.exp2(scores * near * far).astype(jnp.bfloat16)

    @pl.when(flag % 2 == 1)
    def _():
        far_v = jnp.concatenate(
            [far_ref[BLOCK:VROWS, 0:BLOCK], far_ref[BLOCK:VROWS, BLOCK : 2 * BLOCK], ones], axis=0
        )
        part = lax.dot_general(far_v, p_ref[...], NT, preferred_element_type=jnp.float32)
        new_ref[0] += part[0:ACC, :]

    @pl.when(flag >= 2)
    def _():
        near_v = jnp.concatenate([v_ref[0], ones], axis=0)
        part = jnp.dot(near_v, p_ref[...], preferred_element_type=jnp.float32)
        far_sums_ref[...] += part[0:ACC, :]


def cells(order, flags, blocks, far, near_v, norms, sums):
    near = lambda g, order, flags: (order[g], 0, 0)
    whole = lambda g, order, flags: (0, 0)
    return pl.pallas_call(
        cells_kernel,
        out_shape=(
            jax.ShapeDtypeStruct((COLS, ACC, BLOCK), jnp.float32),
            jax.ShapeDtypeStruct((ACC, BLOCK), jnp.float32),
        ),
        grid_spec=pltpu.PrefetchScalarGridSpec(
            num_scalar_prefetch=2,
            grid=(COLS,),
            in_specs=[
                pl.BlockSpec((1, BLOCK, WIDTH), near),
                pl.BlockSpec((PAYLOAD, WIDTH), whole),
                pl.BlockSpec((1, EIGS, BLOCK), lambda g, order, flags: (g, 0, 0)),
                pl.BlockSpec((1, BLOCK, 128), near),
                pl.BlockSpec((1, ACC, BLOCK), near),
            ],
            out_specs=(
                pl.BlockSpec((1, ACC, BLOCK), near),
                pl.BlockSpec((ACC, BLOCK), whole),
            ),
            scratch_shapes=[pltpu.VMEM((BLOCK, BLOCK), jnp.bfloat16)],
        ),
        input_output_aliases={6: 0},
        compiler_params=pltpu.CompilerParams(vmem_limit_bytes=32 << 20),
        cost_estimate=pl.CostEstimate(
            flops=4 * 2 * BLOCK * BLOCK * WIDTH, bytes_accessed=12 << 20, transcendentals=4 * BLOCK * BLOCK
        ),
        name="cells",
    )(order, flags, blocks, far, near_v, norms, sums)


def solve_kernel(gram_ref, smoothed_ref, out_ref):
    rows = lax.broadcasted_iota(jnp.int32, (EIGS, 2 * EIGS), 0)
    lanes = lax.broadcasted_iota(jnp.int32, (EIGS, 2 * EIGS), 1)
    eye = jnp.where(rows + EIGS == lanes, 1.0, 0.0)[:, EIGS:]
    work = jnp.concatenate([gram_ref[...], eye], axis=1)
    pivots = jnp.ones((EIGS, 1), jnp.float32)
    below = rows[:, 0:1]
    for j in range(EIGS):
        row = work[j : j + 1, :]
        pivot = work[j : j + 1, j : j + 1]
        column = work[:, j : j + 1]
        pivots = jnp.where(below == j, pivot, pivots)
        factor = jnp.where(below > j, column / pivot, 0.0)
        work = work - factor * row
    inverse = work[:, EIGS:] * lax.rsqrt(pivots)
    out_ref[...] = jnp.dot(
        inverse, smoothed_ref[...], precision=lax.Precision.HIGHEST, preferred_element_type=jnp.float32
    )


def solve(gram, smoothed):
    return pl.pallas_call(
        solve_kernel,
        out_shape=jax.ShapeDtypeStruct(smoothed.shape, jnp.float32),
        in_specs=[pl.BlockSpec(memory_space=pltpu.VMEM)] * 2,
        out_specs=pl.BlockSpec(memory_space=pltpu.VMEM),
        name="solve",
    )(gram, smoothed)


def per_device(embeddings, vectors, block_pairs):
    here_row = lax.axis_index("row")
    here_col = lax.axis_index("col")
    here_y, here_x = here_row // SIDE, here_row % SIDE
    blocks = embeddings.reshape(COLS, BLOCK, WIDTH)

    def move(array, dy, dx, keep=None):
        return lax.ppermute(array, "row", shift(dy, dx, keep))

    def turn(array, by):
        return lax.ppermute(array, "col", [(i, (i + by * CORES) % COLS) for i in range(COLS)])

    def swap(array):
        return lax.ppermute(array, "col", [(i, i ^ 1) for i in range(COLS)])

    far = {"own": make_payload(here_col[None], blocks, vectors)}
    far["a"] = move(far["own"], 0, 1)
    far["b"] = move(far["own"], 1, 0)
    far["c"] = move(far["own"], -1, -1)
    far["d"] = move(far["a"], -1, 0)
    far["e"] = move(far["c"], 0, -1)
    far["g"] = move(far["a"], 0, 1, left_half)
    far["h"] = move(far["b"], 1, 0)
    far["f"] = move(far["h"], 0, 1)
    far["k"] = move(far["e"], -1, 0, top_half)

    pair_v = jnp.stack([vectors, swap(vectors)])
    near_v = jnp.concatenate([pair_v] + [turn(pair_v, k) for k in range(1, SIDE)], axis=0)
    order = jnp.stack([(here_col - CORES * k) % COLS ^ core for k in range(SIDE) for core in range(CORES)])
    norms = local_norms(blocks)

    far_ids, works = [], []
    ahead = (order - here_col) % COLS
    for name, ((dy, dx), keep) in STAGES.items():
        from_row = (here_y - dy) % SIDE * SIDE + (here_x - dx) % SIDE
        far_ids.append(from_row * COLS + here_col)
        if name == "own":
            half = COLS // 2
            works.append((ahead > 0) & ((ahead < half) | ((ahead == half) & (here_col < half))))
        else:
            works.append(jnp.broadcast_to(True if keep is None else keep(here_y, here_x), (COLS,)))
    far_ids = jnp.stack(far_ids)[:, None]
    near_ids = (here_row * COLS + order)[None, :]
    wanted = jnp.stack([near_ids * NBLOCKS + far_ids, far_ids * NBLOCKS + near_ids])
    listed = block_pairs[:, 0] * NBLOCKS + block_pairs[:, 1]
    found = jnp.any(wanted[..., None] == listed, axis=-1)
    flags = jnp.where(jnp.stack(works), found[0] + 2 * found[1], 0).astype(jnp.int32)

    sums = jnp.zeros((COLS, ACC, BLOCK), jnp.float32)
    owned = None
    for at, (name, ((dy, dx), keep)) in enumerate(STAGES.items()):
        sums, far_sums = cells(order, flags[at], blocks, far[name], near_v, norms, sums)
        if name == "own":
            owned = far_sums
        else:
            back = [(to, source) for source, to in shift(dy, dx, keep)]
            owned = owned + lax.ppermute(far_sums, "row", back)
    owned = owned + jnp.sum(lax.all_to_all(sums, "col", 0, 0), axis=0)

    smoothed = owned[0:EIGS] / owned[EIGS : EIGS + 1]
    gram = jnp.dot(
        smoothed, smoothed.T, precision=lax.Precision.HIGHEST, preferred_element_type=jnp.float32
    ) / (BLOCK * NBLOCKS)
    gram = gram + swap(gram)
    gram = gram + (turn(gram, 1) + turn(gram, 2) + turn(gram, 3))
    gram = gram + (move(gram, 0, 1) + move(gram, 0, 2) + move(gram, 0, 3))
    gram = gram + (move(gram, 1, 0) + move(gram, 2, 0) + move(gram, 3, 0))
    return solve(gram, smoothed)


def solution(mesh):
    return jax.shard_map(
        per_device,
        mesh=mesh,
        in_specs=(P("row", None), P(None, ("row", "col")), P()),
        out_specs=P(None, ("row", "col")),
        check_vma=False,
    )
```

time: 728 us -> 226 us (0.31); the launches traced: 733 us -> 224 us
  waiting for transfers between devices: 407 us -> 39.3 us
  starting transfers between devices: 0.12 us -> 91.3 us
  loops' own time: 87.5 us -> 0 us
  Pallas kernels: 0 us -> 83.5 us
  local copies, waits for them, and re-layouts: 89 us -> 6.19 us
  blocking collectives: 64.9 us -> 0 us
  matrix products: 44.6 us -> 0.26 us
  other arithmetic: 26.5 us -> 2.6 us
  between operations: 13.2 us -> 0.28 us
    unnamed x5 -> x0, waiting for transfers between devices: 232 us -> none
    all_gather x2 -> x0, waiting for transfers between devices: 144 us -> none  [the longest x1 106 us: per_device(): far_x = lax.all_gather(own_block, 'row', axis=0, tiled=True)]
    another operation x129 -> x0, loops' own time: 87.5 us -> none  [the longest x1 85.8 us: per_device(): lax.fori_loop(0, piece_blocks * col_count, visit, (start_sums, start_degr...]
    ppermute x0 -> x32, starting transfers between devices: none -> 87.4 us  [the longest x9 44.5 us: per_device(): owned = owned + lax.ppermute(far_sums, 'row', back)]
    dynamic_slice x141 -> x0, local copies, waits for them, and re-layouts: 85.8 us -> none  [the longest x128 83.3 us: visit(): present[near_index, far_index] > 0.5]
    pallas_call x0 -> x13, Pallas kernels: none -> 83.5 us  [the longest x10 65.3 us: cells(): pl.pallas_call(cells_kernel, out_shape=(jax.ShapeDtypeStruct((COLS, ACC,...]
    psum x1 -> x0, blocking collectives: 64.9 us -> none  [per_device(): gram_matrix = lax.psum(local_gram, ('row', 'col')) / total_rows]
    dot_general x25 -> x0, matrix products: 41.5 us -> none  [the longest x12 28.7 us: tile_terms(): scores = jnp.dot(rows_x, cols_x.T, preferred_element_type=jnp.float32)]
  transfers between devices with their start and end apart: 4 -> 33, of which waited for: 4 -> 12; matrix products, arithmetic and copies ran while one was open for 2% -> 1% of each run, Pallas kernels for 0% -> 31%
where the time goes in v1:
time: 226 us; the launch traced here: 224 us
  starting transfers between devices  91.3 us (40%)
  Pallas kernels  83.5 us (37%)
  waiting for transfers between devices  39.3 us (17%)
  local copies, waits for them, and re-layouts  6.19 us (3%)
  other arithmetic  2.6 us (1%)
    pallas_call x10, Pallas kernels, cells(): pl.pallas_call(cells_kernel, out_shape=(jax.ShapeDtypeStruct((COLS, ACC,...  65.3 us
    ppermute x9, starting transfers between devices, per_device(): owned = owned + lax.ppermute(far_sums, 'row', back)  44.5 us
    ppermute x15, starting transfers between devices, move(): return lax.ppermute(array, 'row', shift(dy, dx, keep))  29 us
    ppermute x15, waiting for transfers between devices, move(): return lax.ppermute(array, 'row', shift(dy, dx, keep))  27.8 us
    ppermute x6, starting transfers between devices, turn(): lax.ppermute(array, 'col', [(i, (i + by * CORES) % COLS) for i in range(C...  13.8 us
    pallas_call x1, Pallas kernels, local_norms(): pl.pallas_call(norms_kernel, out_shape=jax.ShapeDtypeStruct((COLS, BLOCK,...  8.01 us
    pallas_call x1, Pallas kernels, solve(): pl.pallas_call(solve_kernel, out_shape=jax.ShapeDtypeStruct(smoothed.shap...  7.58 us
    ppermute x9, waiting for transfers between devices, per_device(): owned = owned + lax.ppermute(far_sums, 'row', back)  7.46 us
  transfers between devices with their start and end apart: 33, of which 12 were waited for; matrix products, arithmetic and copies ran while one was open for 1% of the time, Pallas kernels for 31%

profile of v1, /device:TPU:0, one launch (start us, length us, event | category | flops | bytes accessed | tf_op | source)
XLA Modules:
  0.0 223.6 jit_solution(955951878917301012)
XLA Ops:
  5.8 2.8 %collective-permute-start.8 = (bf16[560,1024]{1,0:T(8,128)(2,1)}, bf16[560,1024]{1,0:T(8,128)(2,1)}, u32[]{:S(2)}, u32[]{:S(2)}) collective-permute-start(bf16[560,1024]{1,0:T(8,128)(2,1)} %payload.1.far_ref), channel_id=1, source_target_pairs={{0,120},{8,96},{16,104},{24,112},{32,24},{40,0},{48,8},{56,16},{64... | collective-permute-start | bytes 3440648 | tf_op jit(solution)/shard_map/ppermute | solution.py:216
  9.9 23.3 %collective-permute-done.6.far_ref = bf16[560,1024]{1,0:T(8,128)(2,1)} collective-permute-done((bf16[560,1024]{1,0:T(8,128)(2,1)}, bf16[560,1024]{1,0:T(8,128)(2,1)}, u32[]{:S(2)}, u32[]{:S(2)}) %collective-permute-start.6) | collective-permute-done | bytes 1146912 | tf_op jit(solution)/shard_map/ppermute | solution.py:216
  33.8 8.0 %norms.1.norm_ref = f32[8,512,128]{2,1,0:T(8,128)} custom-call(bf16[8,512,1024]{2,1,0:T(8,128)(2,1)} %bitcast.38), custom_call_target="tpu_custom_call" | custom-call | tf_op jit(solution)/shard_map/norms/pallas_call | solution.py:97
  43.9 3.6 %collective-permute-start.2 = (bf16[2,64,512]{2,1,0:T(8,128)(2,1)S(1)}, bf16[2,64,512]{2,1,0:T(8,128)(2,1)S(1)}, u32[]{:S(2)}, u32[]{:S(2)}) collective-permute-start(bf16[2,64,512]{2,1,0:T(8,128)(2,1)S(1)} %pad_maximum_fusion), channel_id=1, source_target_pairs={{0,4},{1,5},{2,6},{3,7},{4,0},{5,1},{6,2},{7,3},{8,12},{9,13},{10,... | collective-permute-start | bytes 393224 | tf_op jit(solution)/shard_map/ppermute | solution.py:219
  52.0 3.0 %collective-permute-start.10 = (bf16[560,1024]{1,0:T(8,128)(2,1)S(1)}, bf16[560,1024]{1,0:T(8,128)(2,1)S(1)}, u32[]{:S(2)}, u32[]{:S(2)}) collective-permute-start(bf16[560,1024]{1,0:T(8,128)(2,1)S(1)} %collective-permute-done.4.far_ref), channel_id=1, source_target_pairs={{0,96},{8,104},{16,112},{24,120},{32,0},{40,8},{48,16},{56,24},{64... | collective-permute-start | bytes 3440648 | tf_op jit(solution)/shard_map/ppermute | solution.py:216
  55.1 3.4 %collective-permute-start.14 = (bf16[560,1024]{1,0:T(8,128)(2,1)S(1)}, bf16[560,1024]{1,0:T(8,128)(2,1)S(1)}, u32[]{:S(2)}, u32[]{:S(2)}) collective-permute-start(bf16[560,1024]{1,0:T(8,128)(2,1)S(1)} %collective-permute-done.4.far_ref), channel_id=1, source_target_pairs={{0,8},{24,0},{32,40},{56,32},{64,72},{88,64},{96,104},{120,96},{1,... | collective-permute-start | bytes 3440648 | tf_op jit(solution)/shard_map/ppermute | solution.py:216
  59.6 3.4 %copy-done = bf16[4096,1024]{1,0:T(8,128)(2,1)S(1)} copy-done((bf16[4096,1024]{1,0:T(8,128)(2,1)S(1)}, bf16[4096,1024]{1,0:T(8,128)(2,1)}, u32[]{:S(2)}) %copy-start) | copy-done | bytes 8388632
  63.0 6.4 %cells.10 = (f32[8,72,512]{2,1,0:T(8,128)}, f32[72,512]{1,0:T(8,128)S(1)}) custom-call(s32[8]{0:T(128)S(1)} %stack.107.order_ref, s32[8]{0:T(128)S(1)} %get-tuple-element.45.flags_ref, bf16[8,512,1024]{2,1,0:T(8,128)(2,1)S(1)} %bitcast.39, bf16[560,1024]{1,0:T(8,128)(2,1)S(1)} %copy-done.2, ...), custom_call_target="tpu_custom_call", output_to_operand_aliasing={{0}: (6, {})} | custom-call | flops 2147483648 | bytes 12582912 | tf_op jit(solution)/shard_map/cells/pallas_call | solution.py:148
  69.4 5.9 %cells.11 = (f32[8,72,512]{2,1,0:T(8,128)}, f32[72,512]{1,0:T(8,128)S(1)}) custom-call(s32[8]{0:T(128)S(1)} %stack.107.order_ref, s32[8]{0:T(128)S(1)} %get-tuple-element.54.flags_ref, bf16[8,512,1024]{2,1,0:T(8,128)(2,1)S(1)} %bitcast.40, bf16[560,1024]{1,0:T(8,128)(2,1)S(1)} %collective-permute-done.4.far_ref, ...), custom_call_target="tpu_custom_call", output_to_operand_aliasing={{0}: (6, {})} | custom-call | flops 2147483648 | bytes 12582912 | tf_op jit(solution)/shard_map/cells/pallas_call | solution.py:148
  75.3 9.8 %cells.12 = (f32[8,72,512]{2,1,0:T(8,128)}, f32[72,512]{1,0:T(8,128)S(1)}) custom-call(s32[8]{0:T(128)S(1)} %stack.107.order_ref, s32[8]{0:T(128)S(1)} %get-tuple-element.53.flags_ref, bf16[8,512,1024]{2,1,0:T(8,128)(2,1)S(1)} %bitcast.41, bf16[560,1024]{1,0:T(8,128)(2,1)} %collective-permute-done.6.far_ref, ...), custom_call_target="tpu_custom_call", output_to_operand_aliasing={{0}: (6, {})} | custom-call | flops 2147483648 | bytes 12582912 | tf_op jit(solution)/shard_map/cells/pallas_call | solution.py:148
  87.3 6.3 %cells.13 = (f32[8,72,512]{2,1,0:T(8,128)}, f32[72,512]{1,0:T(8,128)S(1)}) custom-call(s32[8]{0:T(128)S(1)} %stack.107.order_ref, s32[8]{0:T(128)S(1)} %get-tuple-element.52.flags_ref, bf16[8,512,1024]{2,1,0:T(8,128)(2,1)S(1)} %bitcast.42, bf16[560,1024]{1,0:T(8,128)(2,1)} %collective-permute-done.8.far_ref, ...), custom_call_target="tpu_custom_call", output_to_operand_aliasing={{0}: (6, {})} | custom-call | flops 2147483648 | bytes 12582912 | tf_op jit(solution)/shard_map/cells/pallas_call | solution.py:148
  93.6 5.9 %cells.14 = (f32[8,72,512]{2,1,0:T(8,128)}, f32[72,512]{1,0:T(8,128)S(1)}) custom-call(s32[8]{0:T(128)S(1)} %stack.107.order_ref, s32[8]{0:T(128)S(1)} %get-tuple-element.51.flags_ref, bf16[8,512,1024]{2,1,0:T(8,128)(2,1)S(1)} %bitcast.43, bf16[560,1024]{1,0:T(8,128)(2,1)S(1)} %collective-permute-done.10.far_ref, ...), custom_call_target="tpu_custom_call", output_to_operand_aliasing={{0}: (6, {})} | custom-call | flops 2147483648 | bytes 12582912 | tf_op jit(solution)/shard_map/cells/pallas_call | solution.py:148
  99.5 5.9 %cells.15 = (f32[8,72,512]{2,1,0:T(8,128)}, f32[72,512]{1,0:T(8,128)S(1)}) custom-call(s32[8]{0:T(128)S(1)} %stack.107.order_ref, s32[8]{0:T(128)S(1)} %get-tuple-element.50.flags_ref, bf16[8,512,1024]{2,1,0:T(8,128)(2,1)S(1)} %bitcast.44, bf16[560,1024]{1,0:T(8,128)(2,1)S(1)} %collective-permute-done.12.far_ref, ...), custom_call_target="tpu_custom_call", output_to_operand_aliasing={{0}: (6, {})} | custom-call | flops 2147483648 | bytes 12582912 | tf_op jit(solution)/shard_map/cells/pallas_call | solution.py:148
  105.3 5.9 %cells.16 = (f32[8,72,512]{2,1,0:T(8,128)}, f32[72,512]{1,0:T(8,128)S(1)}) custom-call(s32[8]{0:T(128)S(1)} %stack.107.order_ref, s32[8]{0:T(128)S(1)} %get-tuple-element.49.flags_ref, bf16[8,512,1024]{2,1,0:T(8,128)(2,1)S(1)} %bitcast.45, bf16[560,1024]{1,0:T(8,128)(2,1)S(1)} %collective-permute-done.14.far_ref, ...), custom_call_target="tpu_custom_call", output_to_operand_aliasing={{0}: (6, {})} | custom-call | flops 2147483648 | bytes 12582912 | tf_op jit(solution)/shard_map/cells/pallas_call | solution.py:148
  111.2 7.6 %cells.17 = (f32[8,72,512]{2,1,0:T(8,128)}, f32[72,512]{1,0:T(8,128)S(1)}) custom-call(s32[8]{0:T(128)S(1)} %stack.107.order_ref, s32[8]{0:T(128)S(1)} %get-tuple-element.48.flags_ref, bf16[8,512,1024]{2,1,0:T(8,128)(2,1)S(1)} %bitcast.46, bf16[560,1024]{1,0:T(8,128)(2,1)} %collective-permute-done.16.far_ref, ...), custom_call_target="tpu_custom_call", output_to_operand_aliasing={{0}: (6, {})} | custom-call | flops 2147483648 | bytes 12582912 | tf_op jit(solution)/shard_map/cells/pallas_call | solution.py:148
  118.8 5.9 %cells.18 = (f32[8,72,512]{2,1,0:T(8,128)}, f32[72,512]{1,0:T(8,128)S(1)}) custom-call(s32[8]{0:T(128)S(1)} %stack.107.order_ref, s32[8]{0:T(128)S(1)} %get-tuple-element.47.flags_ref, bf16[8,512,1024]{2,1,0:T(8,128)(2,1)S(1)} %bitcast.47, bf16[560,1024]{1,0:T(8,128)(2,1)S(1)} %collective-permute-done.18.far_ref, ...), custom_call_target="tpu_custom_call", output_to_operand_aliasing={{0}: (6, {})} | custom-call | flops 2147483648 | bytes 12582912 | tf_op jit(solution)/shard_map/cells/pallas_call | solution.py:148
  124.6 5.9 %cells.19 = (f32[8,72,512]{2,1,0:T(8,128)}, f32[72,512]{1,0:T(8,128)S(1)}) custom-call(s32[8]{0:T(128)S(1)} %stack.107.order_ref, s32[8]{0:T(128)S(1)} %get-tuple-element.46.flags_ref, bf16[8,512,1024]{2,1,0:T(8,128)(2,1)S(1)} %bitcast.48, bf16[560,1024]{1,0:T(8,128)(2,1)S(1)} %collective-permute-done.20.far_ref, ...), custom_call_target="tpu_custom_call", output_to_operand_aliasing={{0}: (6, {})} | custom-call | flops 2147483648 | bytes 12582912 | tf_op jit(solution)/shard_map/cells/pallas_call | solution.py:148
  130.5 3.9 %all-to-all-start = ((f32[8,72,512]{2,1,0:T(8,128)}), f32[8,72,512]{2,1,0:T(8,128)S(1)}, u32[]{:S(2)}, u32[]{:S(2)}) async-start(f32[8,72,512]{2,1,0:T(8,128)} %get-tuple-element.44), calls=%async_computation | async-start | bytes 2359296 | tf_op jit(solution)/shard_map/all_to_all | solution.py:266
  134.4 26.7 %collective-permute-start.9 = (f32[72,512]{1,0:T(8,128)S(1)}, f32[72,512]{1,0:T(8,128)S(1)}, u32[]{:S(2)}, u32[]{:S(2)}) collective-permute-start(f32[72,512]{1,0:T(8,128)S(1)} %copy-done.6), channel_id=1, source_target_pairs={{120,0},{96,8},{104,16},{112,24},{24,32},{0,40},{8,48},{16,56},{56... | collective-permute-start | bytes 442376 | tf_op jit(solution)/shard_map/ppermute | solution.py:265
  162.6 5.9 %collective-permute-start.17 = (f32[72,512]{1,0:T(8,128)S(1)}, f32[72,512]{1,0:T(8,128)S(1)}, u32[]{:S(2)}, u32[]{:S(2)}) collective-permute-start(f32[72,512]{1,0:T(8,128)S(1)} %get-tuple-element.39), channel_id=1, source_target_pairs={{0,64},{8,72},{16,80},{24,88},{32,96},{40,104},{48,112},{56,120},{... | collective-permute-start | bytes 442376 | tf_op jit(solution)/shard_map/ppermute | solution.py:265
  172.9 4.9 %collective-permute-start.21 = (f32[72,512]{1,0:T(8,128)S(1)}, f32[72,512]{1,0:T(8,128)S(1)}, u32[]{:S(2)}, u32[]{:S(2)}) collective-permute-start(f32[72,512]{1,0:T(8,128)S(1)} %get-tuple-element.43), channel_id=1, source_target_pairs={{16,64},{24,72},{0,80},{8,88},{48,96},{56,104},{32,112},{40,120},{... | collective-permute-start | bytes 442376 | tf_op jit(solution)/shard_map/ppermute | solution.py:265
  183.7 2.9 %collective-permute-done.19 = f32[72,512]{1,0:T(8,128)S(1)} collective-permute-done((f32[72,512]{1,0:T(8,128)S(1)}, f32[72,512]{1,0:T(8,128)S(1)}, u32[]{:S(2)}, u32[]{:S(2)}) %collective-permute-start.19) | collective-permute-done | bytes 147488 | tf_op jit(solution)/shard_map/ppermute | solution.py:265
  207.2 4.2 %collective-permute-start.30 = (f32[64,64]{1,0:T(8,128)S(1)}, f32[64,64]{1,0:T(8,128)S(1)}, u32[]{:S(2)}, u32[]{:S(2)}) collective-permute-start(f32[64,64]{1,0:T(8,128)S(1)} %add_add_fusion.2), channel_id=1, source_target_pairs={{0,64},{8,72},{16,80},{24,88},{32,96},{40,104},{48,112},{56,120},{... | collective-permute-start | bytes 49160 | tf_op jit(solution)/shard_map/ppermute | solution.py:216
  216.0 7.6 %solve.1 = f32[64,512]{1,0:T(8,128)} custom-call(f32[64,64]{1,0:T(8,128)} %add_add_fusion.1.gram_ref, f32[64,512]{1,0:T(8,128)} %copy-done.7), custom_call_target="tpu_custom_call" | custom-call | tf_op jit(solution)/shard_map/solve/pallas_call | solution.py:200
  (111 shorter events, 54.4 us)
Async XLA Ops:
  0.0 41.9 %collective-permute-start = (bf16[64,512]{1,0:T(8,128)(2,1)}, bf16[64,512]{1,0:T(8,128)(2,1)S(1)}, u32[]{:S(2)}, u32[]{:S(2)}) collective-permute-start(bf16[64,512]{1,0:T(8,128)(2,1)} %v_ref.1), channel_id=1, source_target_pairs={{0,1},{1,0},{2,3},{3,2},{4,5},{5,4},{6,7},{7,6},{8,9},{9,8},{10,11... | collective-permute-start | bytes 196616 | tf_op jit(solution)/shard_map/ppermute | solution.py:222
  2.6 49.4 %collective-permute-start.4 = (bf16[560,1024]{1,0:T(8,128)(2,1)}, bf16[560,1024]{1,0:T(8,128)(2,1)S(1)}, u32[]{:S(2)}, u32[]{:S(2)}) collective-permute-start(bf16[560,1024]{1,0:T(8,128)(2,1)} %payload.1.far_ref), channel_id=1, source_target_pairs={{0,8},{8,16},{16,24},{24,0},{32,40},{40,48},{48,56},{56,32},{64,72... | collective-permute-start | bytes 3440648 | tf_op jit(solution)/shard_map/ppermute | solution.py:216
  4.2 29.0 %collective-permute-start.6 = (bf16[560,1024]{1,0:T(8,128)(2,1)}, bf16[560,1024]{1,0:T(8,128)(2,1)}, u32[]{:S(2)}, u32[]{:S(2)}) collective-permute-start(bf16[560,1024]{1,0:T(8,128)(2,1)} %payload.1.far_ref), channel_id=1, source_target_pairs={{0,32},{8,40},{16,48},{24,56},{32,64},{40,72},{48,80},{56,88},{64,... | collective-permute-start | bytes 3440648 | tf_op jit(solution)/shard_map/ppermute | solution.py:216
  5.8 41.6 %collective-permute-start.8 = (bf16[560,1024]{1,0:T(8,128)(2,1)}, bf16[560,1024]{1,0:T(8,128)(2,1)}, u32[]{:S(2)}, u32[]{:S(2)}) collective-permute-start(bf16[560,1024]{1,0:T(8,128)(2,1)} %payload.1.far_ref), channel_id=1, source_target_pairs={{0,120},{8,96},{16,104},{24,112},{32,24},{40,0},{48,8},{56,16},{64... | collective-permute-start | bytes 3440648 | tf_op jit(solution)/shard_map/ppermute | solution.py:216
  33.2 42.1 %collective-permute-start.16 = (bf16[560,1024]{1,0:T(8,128)(2,1)}, bf16[560,1024]{1,0:T(8,128)(2,1)}, u32[]{:S(2)}, u32[]{:S(2)}) collective-permute-start(bf16[560,1024]{1,0:T(8,128)(2,1)} %collective-permute-done.6.far_ref), channel_id=1, source_target_pairs={{0,32},{8,40},{16,48},{24,56},{32,64},{40,72},{48,80},{56,88},{64,... | collective-permute-start | bytes 3440648 | tf_op jit(solution)/shard_map/ppermute | solution.py:216
  41.9 7.7 %collective-permute-start.1 = (bf16[2,64,512]{2,1,0:T(8,128)(2,1)S(1)}, bf16[2,64,512]{2,1,0:T(8,128)(2,1)S(1)}, u32[]{:S(2)}, u32[]{:S(2)}) collective-permute-start(bf16[2,64,512]{2,1,0:T(8,128)(2,1)S(1)} %pad_maximum_fusion), channel_id=1, source_target_pairs={{0,2},{1,3},{2,4},{3,5},{4,6},{5,7},{6,0},{7,1},{8,10},{9,11},{10,... | collective-permute-start | bytes 393224 | tf_op jit(solution)/shard_map/ppermute | solution.py:219
  43.9 11.1 %collective-permute-start.2 = (bf16[2,64,512]{2,1,0:T(8,128)(2,1)S(1)}, bf16[2,64,512]{2,1,0:T(8,128)(2,1)S(1)}, u32[]{:S(2)}, u32[]{:S(2)}) collective-permute-start(bf16[2,64,512]{2,1,0:T(8,128)(2,1)S(1)} %pad_maximum_fusion), channel_id=1, source_target_pairs={{0,4},{1,5},{2,6},{3,7},{4,0},{5,1},{6,2},{7,3},{8,12},{9,13},{10,... | collective-permute-start | bytes 393224 | tf_op jit(solution)/shard_map/ppermute | solution.py:219
  47.4 38.3 %collective-permute-start.12 = (bf16[560,1024]{1,0:T(8,128)(2,1)}, bf16[560,1024]{1,0:T(8,128)(2,1)S(1)}, u32[]{:S(2)}, u32[]{:S(2)}) collective-permute-start(bf16[560,1024]{1,0:T(8,128)(2,1)} %collective-permute-done.8.far_ref), channel_id=1, source_target_pairs={{0,24},{8,0},{16,8},{24,16},{32,56},{40,32},{48,40},{56,48},{64,88... | collective-permute-start | bytes 3440648 | tf_op jit(solution)/shard_map/ppermute | solution.py:216
  52.0 41.6 %collective-permute-start.10 = (bf16[560,1024]{1,0:T(8,128)(2,1)S(1)}, bf16[560,1024]{1,0:T(8,128)(2,1)S(1)}, u32[]{:S(2)}, u32[]{:S(2)}) collective-permute-start(bf16[560,1024]{1,0:T(8,128)(2,1)S(1)} %collective-permute-done.4.far_ref), channel_id=1, source_target_pairs={{0,96},{8,104},{16,112},{24,120},{32,0},{40,8},{48,16},{56,24},{64... | collective-permute-start | bytes 3440648 | tf_op jit(solution)/shard_map/ppermute | solution.py:216
  55.1 50.3 %collective-permute-start.14 = (bf16[560,1024]{1,0:T(8,128)(2,1)S(1)}, bf16[560,1024]{1,0:T(8,128)(2,1)S(1)}, u32[]{:S(2)}, u32[]{:S(2)}) collective-permute-start(bf16[560,1024]{1,0:T(8,128)(2,1)S(1)} %collective-permute-done.4.far_ref), channel_id=1, source_target_pairs={{0,8},{24,0},{32,40},{56,32},{64,72},{88,64},{96,104},{120,96},{1,... | collective-permute-start | bytes 3440648 | tf_op jit(solution)/shard_map/ppermute | solution.py:216
  75.3 43.5 %collective-permute-start.18 = (bf16[560,1024]{1,0:T(8,128)(2,1)}, bf16[560,1024]{1,0:T(8,128)(2,1)S(1)}, u32[]{:S(2)}, u32[]{:S(2)}) collective-permute-start(bf16[560,1024]{1,0:T(8,128)(2,1)} %collective-permute-done.16.far_ref), channel_id=1, source_target_pairs={{0,8},{8,16},{16,24},{24,0},{32,40},{40,48},{48,56},{56,32},{64,72... | collective-permute-start | bytes 3440648 | tf_op jit(solution)/shard_map/ppermute | solution.py:216
  85.8 38.8 %collective-permute-start.20 = (bf16[560,1024]{1,0:T(8,128)(2,1)S(1)}, bf16[560,1024]{1,0:T(8,128)(2,1)S(1)}, u32[]{:S(2)}, u32[]{:S(2)}) collective-permute-start(bf16[560,1024]{1,0:T(8,128)(2,1)S(1)} %collective-permute-done.12.far_ref), channel_id=1, source_target_pairs={{32,0},{40,8},{48,16},{56,24},{64,32},{72,40},{80,48},{88,56},{33,... | collective-permute-start | bytes 3440648 | tf_op jit(solution)/shard_map/ppermute | solution.py:216
  130.5 48.5 %all-to-all-start = ((f32[8,72,512]{2,1,0:T(8,128)}), f32[8,72,512]{2,1,0:T(8,128)S(1)}, u32[]{:S(2)}, u32[]{:S(2)}) async-start(f32[8,72,512]{2,1,0:T(8,128)} %get-tuple-element.44), calls=%async_computation | async-start | bytes 2359296 | tf_op jit(solution)/shard_map/all_to_all | solution.py:266
  134.4 36.1 %collective-permute-start.9 = (f32[72,512]{1,0:T(8,128)S(1)}, f32[72,512]{1,0:T(8,128)S(1)}, u32[]{:S(2)}, u32[]{:S(2)}) collective-permute-start(f32[72,512]{1,0:T(8,128)S(1)} %copy-done.6), channel_id=1, source_target_pairs={{120,0},{96,8},{104,16},{112,24},{24,32},{0,40},{8,48},{16,56},{56... | collective-permute-start | bytes 442376 | tf_op jit(solution)/shard_map/ppermute | solution.py:265
  161.2 9.3 %collective-permute-start.7 = (f32[72,512]{1,0:T(8,128)S(1)}, f32[72,512]{1,0:T(8,128)S(1)}, u32[]{:S(2)}, u32[]{:S(2)}) collective-permute-start(f32[72,512]{1,0:T(8,128)S(1)} %copy-done.4), channel_id=1, source_target_pairs={{32,0},{40,8},{48,16},{56,24},{64,32},{72,40},{80,48},{88,56},{96,... | collective-permute-start | bytes 442376 | tf_op jit(solution)/shard_map/ppermute | solution.py:265
  162.6 10.3 %collective-permute-start.5 = (f32[72,512]{1,0:T(8,128)S(1)}, f32[72,512]{1,0:T(8,128)S(1)}, u32[]{:S(2)}, u32[]{:S(2)}) collective-permute-start(f32[72,512]{1,0:T(8,128)S(1)} %get-tuple-element.27), channel_id=1, source_target_pairs={{8,0},{16,8},{24,16},{0,24},{40,32},{48,40},{56,48},{32,56},{72,64... | collective-permute-start | bytes 442376 | tf_op jit(solution)/shard_map/ppermute | solution.py:265
  162.6 15.2 %collective-permute-start.17 = (f32[72,512]{1,0:T(8,128)S(1)}, f32[72,512]{1,0:T(8,128)S(1)}, u32[]{:S(2)}, u32[]{:S(2)}) collective-permute-start(f32[72,512]{1,0:T(8,128)S(1)} %get-tuple-element.39), channel_id=1, source_target_pairs={{0,64},{8,72},{16,80},{24,88},{32,96},{40,104},{48,112},{56,120},{... | collective-permute-start | bytes 442376 | tf_op jit(solution)/shard_map/ppermute | solution.py:265
  168.5 10.5 %collective-permute-start.15 = (f32[72,512]{1,0:T(8,128)S(1)}, f32[72,512]{1,0:T(8,128)}, u32[]{:S(2)}, u32[]{:S(2)}) collective-permute-start(f32[72,512]{1,0:T(8,128)S(1)} %get-tuple-element.37), channel_id=1, source_target_pairs={{0,16},{8,24},{32,48},{40,56},{64,80},{72,88},{96,112},{104,120},{... | collective-permute-start | bytes 442376 | tf_op jit(solution)/shard_map/ppermute | solution.py:265
  170.5 10.7 %collective-permute-start.13 = (f32[72,512]{1,0:T(8,128)S(1)}, f32[72,512]{1,0:T(8,128)S(1)}, u32[]{:S(2)}, u32[]{:S(2)}) collective-permute-start(f32[72,512]{1,0:T(8,128)S(1)} %get-tuple-element.35), channel_id=1, source_target_pairs={{112,0},{120,8},{96,16},{104,24},{16,32},{24,40},{0,48},{8,56},{48... | collective-permute-start | bytes 442376 | tf_op jit(solution)/shard_map/ppermute | solution.py:265
  170.5 13.1 %collective-permute-start.11 = (f32[72,512]{1,0:T(8,128)S(1)}, f32[72,512]{1,0:T(8,128)}, u32[]{:S(2)}, u32[]{:S(2)}) collective-permute-start(f32[72,512]{1,0:T(8,128)S(1)} %get-tuple-element.33), channel_id=1, source_target_pairs={{104,0},{112,8},{120,16},{96,24},{8,32},{16,40},{24,48},{0,56},{40... | collective-permute-start | bytes 442376 | tf_op jit(solution)/shard_map/ppermute | solution.py:265
  172.9 10.8 %collective-permute-start.21 = (f32[72,512]{1,0:T(8,128)S(1)}, f32[72,512]{1,0:T(8,128)S(1)}, u32[]{:S(2)}, u32[]{:S(2)}) collective-permute-start(f32[72,512]{1,0:T(8,128)S(1)} %get-tuple-element.43), channel_id=1, source_target_pairs={{16,64},{24,72},{0,80},{8,88},{48,96},{56,104},{32,112},{40,120},{... | collective-permute-start | bytes 442376 | tf_op jit(solution)/shard_map/ppermute | solution.py:265
  177.8 8.7 %collective-permute-start.19 = (f32[72,512]{1,0:T(8,128)S(1)}, f32[72,512]{1,0:T(8,128)S(1)}, u32[]{:S(2)}, u32[]{:S(2)}) collective-permute-start(f32[72,512]{1,0:T(8,128)S(1)} %get-tuple-element.41), channel_id=1, source_target_pairs={{72,0},{80,8},{88,16},{64,24},{104,32},{112,40},{120,48},{96,56},{... | collective-permute-start | bytes 442376 | tf_op jit(solution)/shard_map/ppermute | solution.py:265
  197.5 7.2 %collective-permute-start.26 = (f32[64,64]{1,0:T(8,128)S(1)}, f32[64,64]{1,0:T(8,128)S(1)}, u32[]{:S(2)}, u32[]{:S(2)}) collective-permute-start(f32[64,64]{1,0:T(8,128)S(1)} %add_add_fusion.3), channel_id=1, source_target_pairs={{0,8},{8,16},{16,24},{24,0},{32,40},{40,48},{48,56},{56,32},{64,72... | collective-permute-start | bytes 49160 | tf_op jit(solution)/shard_map/ppermute | solution.py:216
  207.2 6.5 %collective-permute-start.30 = (f32[64,64]{1,0:T(8,128)S(1)}, f32[64,64]{1,0:T(8,128)S(1)}, u32[]{:S(2)}, u32[]{:S(2)}) collective-permute-start(f32[64,64]{1,0:T(8,128)S(1)} %add_add_fusion.2), channel_id=1, source_target_pairs={{0,64},{8,72},{16,80},{24,88},{32,96},{40,104},{48,112},{56,120},{... | collective-permute-start | bytes 49160 | tf_op jit(solution)/shard_map/ppermute | solution.py:216
  (19 other events, 176.4 us)

commit v2 on v1

--- a/solution.py
+++ b/solution.py
@@ -18,7 +18,8 @@
 VROWS = BLOCK + EIGS // 2
 PAYLOAD = VROWS + 16
 ACC = EIGS + 8
-SCALE = math.log2(math.e) / math.sqrt(WIDTH)
+SCALE = math.sqrt(math.log2(math.e) / math.sqrt(WIDTH))
+COST = 8
 NT = (((1,), (1,)), ((), ()))
 
 
@@ -89,91 +90,117 @@
     )(here_col, blocks, vectors)
 
 
-def norms_kernel(x_ref, out_ref):
-    out_ref[0] = jnp.broadcast_to(row_norm(x_ref[0].astype(jnp.float32)), (BLOCK, 128))
-
-
-def local_norms(blocks):
-    return pl.pallas_call(
-        norms_kernel,
-        out_shape=jax.ShapeDtypeStruct((COLS, BLOCK, 128), jnp.float32),
-        grid=(COLS,),
-        in_specs=[pl.BlockSpec((1, BLOCK, WIDTH), lambda g: (g, 0, 0))],
-        out_specs=pl.BlockSpec((1, BLOCK, 128), lambda g: (g, 0, 0)),
-        name="norms",
-    )(blocks)
-
-
-def cells_kernel(order_ref, flags_ref, x_ref, far_ref, v_ref, norm_ref, old_ref, new_ref, far_sums_ref, p_ref):
+def side_vectors(side):
+    half = EIGS // 2
+    ones = jnp.ones((16, BLOCK), jnp.bfloat16)
+    return jnp.concatenate([side[0:half, 0:BLOCK], side[0:half, BLOCK : 2 * BLOCK], ones], axis=0)
+
+
+def side_norms(side):
+    row = side[EIGS // 2 : EIGS // 2 + 1, :].astype(jnp.float32)
+    return row[:, 0:BLOCK] + row[:, BLOCK : 2 * BLOCK]
+
+
+def cells_kernel(count, first, order_ref, flags_ref, x_ref, side_ref, *refs):
+    far_refs, refs = refs[:count], refs[count:]
+    if first:
+        new_ref, norm_ref, refs = refs[0], refs[1], refs[2:]
+    else:
+        norm_ref, old_ref, new_ref, refs = refs[0], refs[1], refs[2], refs[3:]
+    far_sums_refs, token_ref, p_ref = refs[:count], refs[count], refs[count + 1]
     step = pl.program_id(0)
-    flag = flags_ref[step]
-    ones = jnp.ones((16, BLOCK), jnp.bfloat16)
 
     @pl.when(step == 0)
     def _():
-        far_sums_ref[...] = jnp.zeros_like(far_sums_ref)
-
-    new_ref[...] = old_ref[...]
-
-    @pl.when(flag > 0)
-    def _():
+        for far_sums_ref in far_sums_refs:
+            far_sums_ref[...] = jnp.zeros_like(far_sums_ref)
+        token_ref[...] = jnp.zeros_like(token_ref)
+
+    if first:
+        new_ref[...] = jnp.zeros_like(new_ref)
+        norm_ref[0] = jnp.broadcast_to(side_norms(side_ref[0, 0]), (128, BLOCK)).T
+    else:
+        new_ref[...] = old_ref[...]
+
+    def score(far_ref):
         near = norm_ref[0]
         near = jnp.concatenate([near, near], axis=1)
+        far = side_norms(far_ref[BLOCK:PAYLOAD, :])
         for at in range(0, BLOCK, 256):
             scores = lax.dot_general(
                 x_ref[0], far_ref[at : at + 256, :], NT, preferred_element_type=jnp.float32
             )
-            far = far_ref[VROWS : VROWS + 1, at : at + 256].astype(jnp.float32)
-            far = far + far_ref[VROWS : VROWS + 1, BLOCK + at : BLOCK + at + 256].astype(jnp.float32)
-            p_ref[:, at : at + 256] = jnp.exp2(scores * near * far).astype(jnp.bfloat16)
-
-    @pl.when(flag % 2 == 1)
-    def _():
-        far_v = jnp.concatenate(
-            [far_ref[BLOCK:VROWS, 0:BLOCK], far_ref[BLOCK:VROWS, BLOCK : 2 * BLOCK], ones], axis=0
-        )
-        part = lax.dot_general(far_v, p_ref[...], NT, preferred_element_type=jnp.float32)
+            p_ref[:, at : at + 256] = jnp.exp2(scores * near * far[:, at : at + 256]).astype(jnp.bfloat16)
+
+    def forward(far_ref):
+        vectors = side_vectors(far_ref[BLOCK:PAYLOAD, :])
+        part = lax.dot_general(vectors, p_ref[...], NT, preferred_element_type=jnp.float32)
         new_ref[0] += part[0:ACC, :]
 
-    @pl.when(flag >= 2)
-    def _():
-        near_v = jnp.concatenate([v_ref[0], ones], axis=0)
-        part = jnp.dot(near_v, p_ref[...], preferred_element_type=jnp.float32)
+    def backward(far_sums_ref):
+        vectors = side_vectors(side_ref[0, 0])
+        part = jnp.dot(vectors, p_ref[...], preferred_element_type=jnp.float32)
         far_sums_ref[...] += part[0:ACC, :]
 
-
-def cells(order, flags, blocks, far, near_v, norms, sums):
+    for at in range(count):
+        flag = flags_ref[at * COLS + step]
+        pl.when(flag > 0)(functools.partial(score, far_refs[at]))
+        pl.when(flag % 2 == 1)(functools.partial(forward, far_refs[at]))
+        pl.when(flag >= 2)(functools.partial(backward, far_sums_refs[at]))
+
+
+def tie_kernel(*refs):
+    pass
+
+
+def tie(arrays, token):
+    return pl.pallas_call(
+        tie_kernel,
+        out_shape=[jax.ShapeDtypeStruct(array.shape, array.dtype) for array in arrays],
+        in_specs=[pl.BlockSpec(memory_space=pl.ANY)] * (len(arrays) + 1),
+        out_specs=[pl.BlockSpec(memory_space=pl.ANY)] * len(arrays),
+        input_output_aliases={at: at for at in range(len(arrays))},
+        name="tie",
+    )(*arrays, token)
+
+
+def cells(order, flags, blocks, sides, fars, norms=None, sums=None):
+    count, first = len(fars), sums is None
     near = lambda g, order, flags: (order[g], 0, 0)
+    step = lambda g, order, flags: (g, 0, 0)
     whole = lambda g, order, flags: (0, 0)
-    return pl.pallas_call(
-        cells_kernel,
-        out_shape=(
-            jax.ShapeDtypeStruct((COLS, ACC, BLOCK), jnp.float32),
-            jax.ShapeDtypeStruct((ACC, BLOCK), jnp.float32),
-        ),
+    norm_spec, norm_shape = pl.BlockSpec((1, BLOCK, 128), step), (COLS, BLOCK, 128)
+    sums_spec, sums_shape = pl.BlockSpec((1, ACC, BLOCK), step), (COLS, ACC, BLOCK)
+    far_sums = [(pl.BlockSpec((ACC, BLOCK), whole), (ACC, BLOCK))] * count
+    outs = [(sums_spec, sums_shape)] + ([(norm_spec, norm_shape)] if first else []) + far_sums
+    outs += [(pl.BlockSpec((8, 128), whole), (8, 128))]
+    result = pl.pallas_call(
+        functools.partial(cells_kernel, count, first),
+        out_shape=[jax.ShapeDtypeStruct(shape, jnp.float32) for _, shape in outs],
         grid_spec=pltpu.PrefetchScalarGridSpec(
             num_scalar_prefetch=2,
             grid=(COLS,),
             in_specs=[
                 pl.BlockSpec((1, BLOCK, WIDTH), near),
-                pl.BlockSpec((PAYLOAD, WIDTH), whole),
-                pl.BlockSpec((1, EIGS, BLOCK), lambda g, order, flags: (g, 0, 0)),
-                pl.BlockSpec((1, BLOCK, 128), near),
-                pl.BlockSpec((1, ACC, BLOCK), near),
-            ],
-            out_specs=(
-                pl.BlockSpec((1, ACC, BLOCK), near),
-                pl.BlockSpec((ACC, BLOCK), whole),
-            ),
+                pl.BlockSpec((1, 1, PAYLOAD - BLOCK, WIDTH), lambda g, order, flags: (g % SIDE, g // SIDE, 0, 0)),
+            ]
+            + [pl.BlockSpec((PAYLOAD, WIDTH), whole)] * count
+            + ([] if first else [norm_spec, sums_spec]),
+            out_specs=[spec for spec, _ in outs],
             scratch_shapes=[pltpu.VMEM((BLOCK, BLOCK), jnp.bfloat16)],
         ),
-        input_output_aliases={6: 0},
-        compiler_params=pltpu.CompilerParams(vmem_limit_bytes=32 << 20),
+        input_output_aliases={} if first else {5 + count: 0},
+        compiler_params=pltpu.CompilerParams(vmem_limit_bytes=56 << 20),
         cost_estimate=pl.CostEstimate(
-            flops=4 * 2 * BLOCK * BLOCK * WIDTH, bytes_accessed=12 << 20, transcendentals=4 * BLOCK * BLOCK
+            flops=count * COST * BLOCK * BLOCK * WIDTH,
+            bytes_accessed=(12 + count) << 20,
+            transcendentals=count * 4 * BLOCK * BLOCK,
         ),
         name="cells",
-    )(order, flags, blocks, far, near_v, norms, sums)
+    )(order, flags, blocks, sides, *fars, *([] if first else [norms, sums]))
+    if first:
+        return result[0], result[1], result[2:-1], result[-1]
+    return result[0], norms, result[1:-1], result[-1]
 
 
 def solve_kernel(gram_ref, smoothed_ref, out_ref):
@@ -225,17 +252,10 @@
     far["a"] = move(far["own"], 0, 1)
     far["b"] = move(far["own"], 1, 0)
     far["c"] = move(far["own"], -1, -1)
-    far["d"] = move(far["a"], -1, 0)
-    far["e"] = move(far["c"], 0, -1)
-    far["g"] = move(far["a"], 0, 1, left_half)
-    far["h"] = move(far["b"], 1, 0)
-    far["f"] = move(far["h"], 0, 1)
-    far["k"] = move(far["e"], -1, 0, top_half)
-
-    pair_v = jnp.stack([vectors, swap(vectors)])
-    near_v = jnp.concatenate([pair_v] + [turn(pair_v, k) for k in range(1, SIDE)], axis=0)
-    order = jnp.stack([(here_col - CORES * k) % COLS ^ core for k in range(SIDE) for core in range(CORES)])
-    norms = local_norms(blocks)
+    side = far["own"][BLOCK:PAYLOAD]
+    pair = jnp.stack([side, swap(side)])
+    sides = jnp.stack([pair] + [turn(pair, k) for k in range(1, SIDE)])
+    order = jnp.stack([(here_col - CORES * k) % COLS ^ core for core in range(CORES) for k in range(SIDE)])
 
     far_ids, works = [], []
     ahead = (order - here_col) % COLS
@@ -254,16 +274,47 @@
     found = jnp.any(wanted[..., None] == listed, axis=-1)
     flags = jnp.where(jnp.stack(works), found[0] + 2 * found[1], 0).astype(jnp.int32)
 
-    sums = jnp.zeros((COLS, ACC, BLOCK), jnp.float32)
-    owned = None
-    for at, (name, ((dy, dx), keep)) in enumerate(STAGES.items()):
-        sums, far_sums = cells(order, flags[at], blocks, far[name], near_v, norms, sums)
-        if name == "own":
-            owned = far_sums
-        else:
-            back = [(to, source) for source, to in shift(dy, dx, keep)]
-            owned = owned + lax.ppermute(far_sums, "row", back)
-    owned = owned + jnp.sum(lax.all_to_all(sums, "col", 0, 0), axis=0)
+    starts = {name: at for at, name in enumerate(STAGES)}
+
+    def work(group, norms=None, sums=None):
+        at = starts[group[0]]
+        return cells(
+            order, flags[at : at + len(group)].reshape(-1), blocks, sides, [far[name] for name in group], norms, sums
+        )
+
+    def give_back(group, parts):
+        moved = []
+        for name, part in zip(group, parts):
+            (dy, dx), keep = STAGES[name]
+            moved.append(lax.ppermute(part, "row", [(to, source) for source, to in shift(dy, dx, keep)]))
+        return moved
+
+    sums, norms, returned, token = work(("own",))
+    far["a"], far["b"], far["c"] = tie([far["a"], far["b"], far["c"]], token)
+    far["d"] = move(far["a"], -1, 0)
+    far["e"] = move(far["c"], 0, -1)
+    far["g"] = move(far["a"], 0, 1, left_half)
+    far["h"] = move(far["b"], 1, 0)
+
+    group = ("a", "b", "c")
+    sums, norms, parts, token = work(group, norms, sums)
+    far["h"], far["e"] = tie([far["h"], far["e"]], token)
+    early = sum(give_back(group, parts)) + returned[0]
+    far["f"] = move(far["h"], 0, 1)
+    far["k"] = move(far["e"], -1, 0, top_half)
+
+    group = ("d", "e", "g", "h")
+    sums, norms, parts, token = work(group, norms, sums)
+    returned = give_back(group, parts)
+
+    far["f"], far["k"] = tie([far["f"], far["k"]], early[0:8, 0:128])
+    group = ("f", "k")
+    sums, norms, parts, token = work(group, norms, sums)
+    returned = [early] + returned + give_back(group, parts)
+
+    kept = sums[:SIDE] + swap(sums[SIDE:])
+    returned += [kept[0]] + [turn(kept[k], SIDE - k) for k in range(1, SIDE)]
+    owned = sum(returned)
 
     smoothed = owned[0:EIGS] / owned[EIGS : EIGS + 1]
     gram = jnp.dot(

time: 226 us -> 196 us (0.87); the launches traced: 224 us -> 197 us
  Pallas kernels: 83.5 us -> 51.6 us
  starting transfers between devices: 91.3 us -> 78.9 us
  waiting for transfers between devices: 39.3 us -> 46.8 us
  other arithmetic: 2.6 us -> 7.98 us
  local copies, waits for them, and re-layouts: 6.19 us -> 11.3 us
    pallas_call x11 -> x7, Pallas kernels: 73.3 us -> 41.4 us  [the longest x4 41.4 us: cells(): pl.pallas_call(functools.partial(cells_kernel, count, first), out_shape=[...]
    ppermute x6 -> x9, waiting for transfers between devices: 2.85 us -> 21 us  [turn(): lax.ppermute(array, 'col', [(i, (i + by * CORES) % COLS) for i in range(C...]
    ppermute x15, waiting for transfers between devices: 27.8 us -> 16.2 us  [move(): return lax.ppermute(array, 'row', shift(dy, dx, keep))]
    ppermute x9, starting transfers between devices: 44.5 us -> 35.4 us  [give_back(): lax.ppermute(part, 'row', [(to, source) for source, to in shift(dy, dx, k...]
    all_to_all x1 -> x0, starting transfers between devices: 3.91 us -> none  [per_device(): owned = owned + jnp.sum(lax.all_to_all(sums, 'col', 0, 0), axis=0)]
    another operation x1 -> x2, other arithmetic: 0.01 us -> 3.67 us  [per_device(): sides = jnp.stack([pair] + [turn(pair, k) for k in range(1, SIDE)])]
    slice x1 -> x9, local copies, waits for them, and re-layouts: 0.32 us -> 2.94 us  [the longest x1 1.2 us: per_device(): kept = sums[:SIDE] + swap(sums[SIDE:])]
    ppermute x6 -> x9, starting transfers between devices: 13.8 us -> 15.5 us  [turn(): lax.ppermute(array, 'col', [(i, (i + by * CORES) % COLS) for i in range(C...]
  transfers between devices with their start and end apart: 33 -> 36, of which waited for: 12 -> 21; matrix products, arithmetic and copies ran while one was open for 1% -> 7% of each run, Pallas kernels for 31% -> 16%
where the time goes in v2:
time: 196 us; the launch traced here: 197 us
  starting transfers between devices  78.9 us (40%)
  Pallas kernels  51.6 us (26%)
  waiting for transfers between devices  46.8 us (24%)
  local copies, waits for them, and re-layouts  11.3 us (6%)
  other arithmetic  7.98 us (4%)
    pallas_call x4, Pallas kernels, cells(): pl.pallas_call(functools.partial(cells_kernel, count, first), out_shape=[...  41.4 us
    ppermute x9, starting transfers between devices, give_back(): lax.ppermute(part, 'row', [(to, source) for source, to in shift(dy, dx, k...  35.4 us
    ppermute x15, starting transfers between devices, move(): return lax.ppermute(array, 'row', shift(dy, dx, keep))  27.8 us
    ppermute x9, waiting for transfers between devices, turn(): lax.ppermute(array, 'col', [(i, (i + by * CORES) % COLS) for i in range(C...  21 us
    ppermute x15, waiting for transfers between devices, move(): return lax.ppermute(array, 'row', shift(dy, dx, keep))  16.2 us
    ppermute x9, starting transfers between devices, turn(): lax.ppermute(array, 'col', [(i, (i + by * CORES) % COLS) for i in range(C...  15.5 us
    ppermute x9, waiting for transfers between devices, give_back(): lax.ppermute(part, 'row', [(to, source) for source, to in shift(dy, dx, k...  8.41 us
    pallas_call x1, Pallas kernels, solve(): pl.pallas_call(solve_kernel, out_shape=jax.ShapeDtypeStruct(smoothed.shap...  7.57 us
  transfers between devices with their start and end apart: 36, of which 21 were waited for; matrix products, arithmetic and copies ran while one was open for 7% of the time, Pallas kernels for 16%

profile of v2, /device:TPU:0, one launch (start us, length us, event | category | flops | bytes accessed | tf_op | source)
XLA Modules:
  0.0 197.1 jit_solution(7934059822988022434)
XLA Ops:
  5.7 2.8 %collective-permute-start.6 = (bf16[560,1024]{1,0:T(8,128)(2,1)}, bf16[560,1024]{1,0:T(8,128)(2,1)S(1)}, u32[]{:S(2)}, u32[]{:S(2)}) collective-permute-start(bf16[560,1024]{1,0:T(8,128)(2,1)} %payload.1.refs_0_), channel_id=1, source_target_pairs={{0,120},{8,96},{16,104},{24,112},{32,24},{40,0},{48,8},{56,16},{64... | collective-permute-start | bytes 3440648 | tf_op jit(solution)/shard_map/ppermute | solution.py:243
  18.3 3.6 %collective-permute-start.2 = (bf16[2,48,1024]{2,1,0:T(8,128)(2,1)}, bf16[2,48,1024]{2,1,0:T(8,128)(2,1)S(1)}, u32[]{:S(2)}, u32[]{:S(2)}) collective-permute-start(bf16[2,48,1024]{2,1,0:T(8,128)(2,1)} %get-tuple-element.61), channel_id=1, source_target_pairs={{0,4},{1,5},{2,6},{3,7},{4,0},{5,1},{6,2},{7,3},{8,12},{9,13},{10,... | collective-permute-start | bytes 589832 | tf_op jit(solution)/shard_map/ppermute | solution.py:246
  21.9 4.2 %collective-permute-done.1 = bf16[2,48,1024]{2,1,0:T(8,128)(2,1)} collective-permute-done((bf16[2,48,1024]{2,1,0:T(8,128)(2,1)}, bf16[2,48,1024]{2,1,0:T(8,128)(2,1)}, u32[]{:S(2)}, u32[]{:S(2)}) %collective-permute-start.1) | collective-permute-done | bytes 196640 | tf_op jit(solution)/shard_map/ppermute | solution.py:246
  35.2 9.8 %cells.4 = (f32[8,72,512]{2,1,0:T(8,128)}, f32[8,512,128]{2,1,0:T(8,128)}, f32[72,512]{1,0:T(8,128)}, f32[8,128]{1,0:T(8,128)}) custom-call(s32[8]{0:T(128)} %stack.122.order_ref, s32[8]{0:T(128)} %slice_reduce_fusion.flags_ref, bf16[8,512,1024]{2,1,0:T(8,128)(2,1)} %bitcast.58, bf16[4,2,48,1024]{3,2,1,0:T(8,128)(2,1)} %pad_maximum_fusion.side_ref, ...), custom_call_target="tpu_custom_call" | custom-call | flops 2147483648 | bytes 13631488 | tf_op jit(solution)/shard_map/cells/pallas_call | solution.py:177
  48.7 3.0 %collective-permute-start.10 = (bf16[560,1024]{1,0:T(8,128)(2,1)}, bf16[560,1024]{1,0:T(8,128)(2,1)}, u32[]{:S(2)}, u32[]{:S(2)}) collective-permute-start(bf16[560,1024]{1,0:T(8,128)(2,1)} %get-tuple-element.30.refs_0_), channel_id=1, source_target_pairs={{0,96},{8,104},{16,112},{24,120},{32,0},{40,8},{48,16},{56,24},{64... | collective-permute-start | bytes 3440648 | tf_op jit(solution)/shard_map/ppermute | solution.py:243
  54.7 11.2 %cells.5 = (f32[8,72,512]{2,1,0:T(8,128)}, f32[72,512]{1,0:T(8,128)}, f32[72,512]{1,0:T(8,128)}, f32[72,512]{1,0:T(8,128)}, f32[8,128]{1,0:T(8,128)}) custom-call(s32[8]{0:T(128)} %stack.122.order_ref, s32[24]{0:T(128)} %reshape.482.flags_ref, bf16[8,512,1024]{2,1,0:T(8,128)(2,1)} %bitcast.59, ...), custom_call_target="tpu_custom_call", output_to_operand_aliasing={{0}: (8, {})} | custom-call | flops 6442450944 | bytes 15728640 | tf_op jit(solution)/shard_map/cells/pallas_call | solution.py:177
  66.0 5.1 %collective-permute-start.7 = (f32[72,512]{1,0:T(8,128)}, f32[72,512]{1,0:T(8,128)S(1)}, u32[]{:S(2)}, u32[]{:S(2)}) collective-permute-start(f32[72,512]{1,0:T(8,128)} %get-tuple-element.35), channel_id=1, source_target_pairs={{8,0},{16,8},{24,16},{0,24},{40,32},{48,40},{56,48},{32,56},{72,64... | collective-permute-start | bytes 442376 | tf_op jit(solution)/shard_map/ppermute | solution.py:289
  73.3 10.7 %collective-permute-start.8 = (f32[72,512]{1,0:T(8,128)}, f32[72,512]{1,0:T(8,128)S(1)}, u32[]{:S(2)}, u32[]{:S(2)}) collective-permute-start(f32[72,512]{1,0:T(8,128)} %get-tuple-element.36), channel_id=1, source_target_pairs={{32,0},{40,8},{48,16},{56,24},{64,32},{72,40},{80,48},{88,56},{96,... | collective-permute-start | bytes 442376 | tf_op jit(solution)/shard_map/ppermute | solution.py:289
  89.9 4.4 %collective-permute-done.9 = f32[72,512]{1,0:T(8,128)S(1)} collective-permute-done((f32[72,512]{1,0:T(8,128)}, f32[72,512]{1,0:T(8,128)S(1)}, u32[]{:S(2)}, u32[]{:S(2)}) %collective-permute-start.9) | collective-permute-done | bytes 147488 | tf_op jit(solution)/shard_map/ppermute | solution.py:289
  94.9 11.2 %cells.6 = (f32[8,72,512]{2,1,0:T(8,128)}, f32[72,512]{1,0:T(8,128)}, f32[72,512]{1,0:T(8,128)}, f32[72,512]{1,0:T(8,128)}, f32[72,512]{1,0:T(8,128)}, /*index=5*/f32[8,128]{1,0:T(8,128)}) custom-call(s32[8]{0:T(128)} %stack.122.order_ref, s32[32]{0:T(128)} %reshape.485.flags_ref, bf16[8,512,1024]{2,1,0:T(8,128)(2,1)} %bitcast.60, ...), custom_call_target="tpu_custom_call", output_to_operand_aliasing={{0}: (9, {})} | custom-call | flops 8589934592 | bytes 16777216 | tf_op jit(solution)/shard_map/cells/pallas_call | solution.py:177
  106.1 6.3 %collective-permute-done.18.refs_0_ = bf16[560,1024]{1,0:T(8,128)(2,1)S(1)} collective-permute-done((bf16[560,1024]{1,0:T(8,128)(2,1)}, bf16[560,1024]{1,0:T(8,128)(2,1)S(1)}, u32[]{:S(2)}, u32[]{:S(2)}) %collective-permute-start.18) | collective-permute-done | bytes 1146912 | tf_op jit(solution)/shard_map/ppermute | solution.py:243
  115.4 9.1 %cells.7 = (f32[8,72,512]{2,1,0:T(8,128)}, f32[72,512]{1,0:T(8,128)}, f32[72,512]{1,0:T(8,128)}, f32[8,128]{1,0:T(8,128)}) custom-call(s32[8]{0:T(128)} %stack.122.order_ref, s32[16]{0:T(128)} %reshape.486.flags_ref, bf16[8,512,1024]{2,1,0:T(8,128)(2,1)} %bitcast.61, ...), custom_call_target="tpu_custom_call", output_to_operand_aliasing={{0}: (7, {})} | custom-call | flops 4294967296 | bytes 14680064 | tf_op jit(solution)/shard_map/cells/pallas_call | solution.py:177
  125.9 8.8 %collective-permute-start.14 = (f32[72,512]{1,0:T(8,128)S(1)}, f32[72,512]{1,0:T(8,128)S(1)}, u32[]{:S(2)}, u32[]{:S(2)}) collective-permute-start(f32[72,512]{1,0:T(8,128)S(1)} %copy-done.15), channel_id=1, source_target_pairs={{104,0},{112,8},{120,16},{96,24},{8,32},{16,40},{24,48},{0,56},{40... | collective-permute-start | bytes 442376 | tf_op jit(solution)/shard_map/ppermute | solution.py:289
  134.7 3.3 %collective-permute-start.16 = (f32[72,512]{1,0:T(8,128)S(1)}, f32[72,512]{1,0:T(8,128)S(1)}, u32[]{:S(2)}, u32[]{:S(2)}) collective-permute-start(f32[72,512]{1,0:T(8,128)S(1)} %copy-done.12), channel_id=1, source_target_pairs={{0,16},{8,24},{32,48},{40,56},{64,80},{72,88},{96,112},{104,120},{... | collective-permute-start | bytes 442376 | tf_op jit(solution)/shard_map/ppermute | solution.py:289
  138.0 4.9 %collective-permute-start.17 = (f32[72,512]{1,0:T(8,128)S(1)}, f32[72,512]{1,0:T(8,128)S(1)}, u32[]{:S(2)}, u32[]{:S(2)}) collective-permute-start(f32[72,512]{1,0:T(8,128)S(1)} %copy-done.11), channel_id=1, source_target_pairs={{0,64},{8,72},{16,80},{24,88},{32,96},{40,104},{48,112},{56,120},{... | collective-permute-start | bytes 442376 | tf_op jit(solution)/shard_map/ppermute | solution.py:289
  145.1 2.7 %collective-permute-start.21 = (f32[72,512]{1,0:T(8,128)S(1)}, f32[72,512]{1,0:T(8,128)S(1)}, u32[]{:S(2)}, u32[]{:S(2)}) collective-permute-start(f32[72,512]{1,0:T(8,128)S(1)} %copy-done.13), channel_id=1, source_target_pairs={{16,64},{24,72},{0,80},{8,88},{48,96},{56,104},{32,112},{40,120},{... | collective-permute-start | bytes 442376 | tf_op jit(solution)/shard_map/ppermute | solution.py:289
  147.7 2.8 %collective-permute-start.23 = (f32[72,512]{1,0:T(8,128)S(1)}, f32[72,512]{1,0:T(8,128)S(1)}, u32[]{:S(2)}, u32[]{:S(2)}) collective-permute-start(f32[72,512]{1,0:T(8,128)S(1)} %get-tuple-element.57), channel_id=1, source_target_pairs={{0,6},{1,7},{2,0},{3,1},{4,2},{5,3},{6,4},{7,5},{8,14},{9,15},{10,... | collective-permute-start | bytes 442376 | tf_op jit(solution)/shard_map/ppermute | solution.py:246
  152.3 4.3 %collective-permute-done.23 = f32[72,512]{1,0:T(8,128)S(1)} collective-permute-done((f32[72,512]{1,0:T(8,128)S(1)}, f32[72,512]{1,0:T(8,128)S(1)}, u32[]{:S(2)}, u32[]{:S(2)}) %collective-permute-start.23) | collective-permute-done | bytes 147488 | tf_op jit(solution)/shard_map/ppermute | solution.py:246
  157.2 3.8 %collective-permute-done.25 = f32[72,512]{1,0:T(8,128)S(1)} collective-permute-done((f32[72,512]{1,0:T(8,128)S(1)}, f32[72,512]{1,0:T(8,128)S(1)}, u32[]{:S(2)}, u32[]{:S(2)}) %collective-permute-start.25) | collective-permute-done | bytes 147488 | tf_op jit(solution)/shard_map/ppermute | solution.py:246
  162.8 3.2 %collective-permute-start.28 = (f32[64,64]{1,0:T(8,128)S(1)}, f32[64,64]{1,0:T(8,128)S(1)}, u32[]{:S(2)}, u32[]{:S(2)}) collective-permute-start(f32[64,64]{1,0:T(8,128)S(1)} %add.344), channel_id=1, source_target_pairs={{0,4},{1,5},{2,6},{3,7},{4,0},{5,1},{6,2},{7,3},{8,12},{9,13},{10,... | collective-permute-start | bytes 49160 | tf_op jit(solution)/shard_map/ppermute | solution.py:246
  169.9 7.2 %collective-permute-start.30 = (f32[64,64]{1,0:T(8,128)S(1)}, f32[64,64]{1,0:T(8,128)S(1)}, u32[]{:S(2)}, u32[]{:S(2)}) collective-permute-start(f32[64,64]{1,0:T(8,128)S(1)} %add_add_fusion.3), channel_id=1, source_target_pairs={{0,8},{8,16},{16,24},{24,0},{32,40},{40,48},{48,56},{56,32},{64,72... | collective-permute-start | bytes 49160 | tf_op jit(solution)/shard_map/ppermute | solution.py:243
  177.1 2.8 %collective-permute-start.32 = (f32[64,64]{1,0:T(8,128)S(1)}, f32[64,64]{1,0:T(8,128)S(1)}, u32[]{:S(2)}, u32[]{:S(2)}) collective-permute-start(f32[64,64]{1,0:T(8,128)S(1)} %add_add_fusion.3), channel_id=1, source_target_pairs={{0,24},{8,0},{16,8},{24,16},{32,56},{40,32},{48,40},{56,48},{64,88... | collective-permute-start | bytes 49160 | tf_op jit(solution)/shard_map/ppermute | solution.py:243
  179.9 2.6 %collective-permute-done.31 = f32[64,64]{1,0:T(8,128)S(1)} collective-permute-done((f32[64,64]{1,0:T(8,128)S(1)}, f32[64,64]{1,0:T(8,128)S(1)}, u32[]{:S(2)}, u32[]{:S(2)}) %collective-permute-start.31) | collective-permute-done | bytes 16416 | tf_op jit(solution)/shard_map/ppermute | solution.py:243
  189.6 7.6 %solve.1 = f32[64,512]{1,0:T(8,128)} custom-call(f32[64,64]{1,0:T(8,128)} %add_add_fusion.1.gram_ref, f32[64,512]{1,0:T(8,128)} %copy-done), custom_call_target="tpu_custom_call" | custom-call | tf_op jit(solution)/shard_map/solve/pallas_call | solution.py:227
  (134 shorter events, 61.5 us)
Async XLA Ops:
  2.6 42.4 %collective-permute-start.4 = (bf16[560,1024]{1,0:T(8,128)(2,1)}, bf16[560,1024]{1,0:T(8,128)(2,1)S(1)}, u32[]{:S(2)}, u32[]{:S(2)}) collective-permute-start(bf16[560,1024]{1,0:T(8,128)(2,1)} %payload.1.refs_0_), channel_id=1, source_target_pairs={{0,8},{8,16},{16,24},{24,0},{32,40},{40,48},{48,56},{56,32},{64,72... | collective-permute-start | bytes 3440648 | tf_op jit(solution)/shard_map/ppermute | solution.py:243
  4.2 40.9 %collective-permute-start.5 = (bf16[560,1024]{1,0:T(8,128)(2,1)}, bf16[560,1024]{1,0:T(8,128)(2,1)S(1)}, u32[]{:S(2)}, u32[]{:S(2)}) collective-permute-start(bf16[560,1024]{1,0:T(8,128)(2,1)} %payload.1.refs_0_), channel_id=1, source_target_pairs={{0,32},{8,40},{16,48},{24,56},{32,64},{40,72},{48,80},{56,88},{64,... | collective-permute-start | bytes 3440648 | tf_op jit(solution)/shard_map/ppermute | solution.py:243
  5.7 39.3 %collective-permute-start.6 = (bf16[560,1024]{1,0:T(8,128)(2,1)}, bf16[560,1024]{1,0:T(8,128)(2,1)S(1)}, u32[]{:S(2)}, u32[]{:S(2)}) collective-permute-start(bf16[560,1024]{1,0:T(8,128)(2,1)} %payload.1.refs_0_), channel_id=1, source_target_pairs={{0,120},{8,96},{16,104},{24,112},{32,24},{40,0},{48,8},{56,16},{64... | collective-permute-start | bytes 3440648 | tf_op jit(solution)/shard_map/ppermute | solution.py:243
  16.0 10.0 %collective-permute-start.1 = (bf16[2,48,1024]{2,1,0:T(8,128)(2,1)}, bf16[2,48,1024]{2,1,0:T(8,128)(2,1)}, u32[]{:S(2)}, u32[]{:S(2)}) collective-permute-start(bf16[2,48,1024]{2,1,0:T(8,128)(2,1)} %get-tuple-element.61), channel_id=1, source_target_pairs={{0,2},{1,3},{2,4},{3,5},{4,6},{5,7},{6,0},{7,1},{8,10},{9,11},{10,... | collective-permute-start | bytes 589832 | tf_op jit(solution)/shard_map/ppermute | solution.py:246
  18.3 13.1 %collective-permute-start.2 = (bf16[2,48,1024]{2,1,0:T(8,128)(2,1)}, bf16[2,48,1024]{2,1,0:T(8,128)(2,1)S(1)}, u32[]{:S(2)}, u32[]{:S(2)}) collective-permute-start(bf16[2,48,1024]{2,1,0:T(8,128)(2,1)} %get-tuple-element.61), channel_id=1, source_target_pairs={{0,4},{1,5},{2,6},{3,7},{4,0},{5,1},{6,2},{7,3},{8,12},{9,13},{10,... | collective-permute-start | bytes 589832 | tf_op jit(solution)/shard_map/ppermute | solution.py:246
  46.8 26.5 %collective-permute-start.11 = (bf16[560,1024]{1,0:T(8,128)(2,1)}, bf16[560,1024]{1,0:T(8,128)(2,1)S(1)}, u32[]{:S(2)}, u32[]{:S(2)}) collective-permute-start(bf16[560,1024]{1,0:T(8,128)(2,1)} %get-tuple-element.31.refs_1_), channel_id=1, source_target_pairs={{0,32},{8,40},{16,48},{24,56},{32,64},{40,72},{48,80},{56,88},{64,... | collective-permute-start | bytes 3440648 | tf_op jit(solution)/shard_map/ppermute | solution.py:243
  47.2 36.8 %collective-permute-start.12 = (bf16[560,1024]{1,0:T(8,128)(2,1)}, bf16[560,1024]{1,0:T(8,128)(2,1)S(1)}, u32[]{:S(2)}, u32[]{:S(2)}) collective-permute-start(bf16[560,1024]{1,0:T(8,128)(2,1)} %get-tuple-element.32.refs_2_), channel_id=1, source_target_pairs={{0,24},{8,0},{16,8},{24,16},{32,56},{40,32},{48,40},{56,48},{64,88... | collective-permute-start | bytes 3440648 | tf_op jit(solution)/shard_map/ppermute | solution.py:243
  48.7 46.2 %collective-permute-start.10 = (bf16[560,1024]{1,0:T(8,128)(2,1)}, bf16[560,1024]{1,0:T(8,128)(2,1)}, u32[]{:S(2)}, u32[]{:S(2)}) collective-permute-start(bf16[560,1024]{1,0:T(8,128)(2,1)} %get-tuple-element.30.refs_0_), channel_id=1, source_target_pairs={{0,96},{8,104},{16,112},{24,120},{32,0},{40,8},{48,16},{56,24},{64... | collective-permute-start | bytes 3440648 | tf_op jit(solution)/shard_map/ppermute | solution.py:243
  51.7 43.2 %collective-permute-start.13 = (bf16[560,1024]{1,0:T(8,128)(2,1)}, bf16[560,1024]{1,0:T(8,128)(2,1)}, u32[]{:S(2)}, u32[]{:S(2)}) collective-permute-start(bf16[560,1024]{1,0:T(8,128)(2,1)} %get-tuple-element.30.refs_0_), channel_id=1, source_target_pairs={{0,8},{24,0},{32,40},{56,32},{64,72},{88,64},{96,104},{120,96},{1,... | collective-permute-start | bytes 3440648 | tf_op jit(solution)/shard_map/ppermute | solution.py:243
  66.0 19.1 %collective-permute-start.7 = (f32[72,512]{1,0:T(8,128)}, f32[72,512]{1,0:T(8,128)S(1)}, u32[]{:S(2)}, u32[]{:S(2)}) collective-permute-start(f32[72,512]{1,0:T(8,128)} %get-tuple-element.35), channel_id=1, source_target_pairs={{8,0},{16,8},{24,16},{0,24},{40,32},{48,40},{56,48},{32,56},{72,64... | collective-permute-start | bytes 442376 | tf_op jit(solution)/shard_map/ppermute | solution.py:289
  73.3 13.7 %collective-permute-start.8 = (f32[72,512]{1,0:T(8,128)}, f32[72,512]{1,0:T(8,128)S(1)}, u32[]{:S(2)}, u32[]{:S(2)}) collective-permute-start(f32[72,512]{1,0:T(8,128)} %get-tuple-element.36), channel_id=1, source_target_pairs={{32,0},{40,8},{48,16},{56,24},{64,32},{72,40},{80,48},{88,56},{96,... | collective-permute-start | bytes 442376 | tf_op jit(solution)/shard_map/ppermute | solution.py:289
  83.9 10.3 %collective-permute-start.9 = (f32[72,512]{1,0:T(8,128)}, f32[72,512]{1,0:T(8,128)S(1)}, u32[]{:S(2)}, u32[]{:S(2)}) collective-permute-start(f32[72,512]{1,0:T(8,128)} %get-tuple-element.37), channel_id=1, source_target_pairs={{120,0},{96,8},{104,16},{112,24},{24,32},{0,40},{8,48},{16,56},{56... | collective-permute-start | bytes 442376 | tf_op jit(solution)/shard_map/ppermute | solution.py:289
  85.0 27.4 %collective-permute-start.18 = (bf16[560,1024]{1,0:T(8,128)(2,1)}, bf16[560,1024]{1,0:T(8,128)(2,1)S(1)}, u32[]{:S(2)}, u32[]{:S(2)}) collective-permute-start(bf16[560,1024]{1,0:T(8,128)(2,1)} %get-tuple-element.41.refs_3_), channel_id=1, source_target_pairs={{0,8},{8,16},{16,24},{24,0},{32,40},{40,48},{48,56},{56,32},{64,72... | collective-permute-start | bytes 3440648 | tf_op jit(solution)/shard_map/ppermute | solution.py:243
  86.9 27.5 %collective-permute-start.19 = (bf16[560,1024]{1,0:T(8,128)(2,1)}, bf16[560,1024]{1,0:T(8,128)(2,1)S(1)}, u32[]{:S(2)}, u32[]{:S(2)}) collective-permute-start(bf16[560,1024]{1,0:T(8,128)(2,1)} %get-tuple-element.40.refs_1_), channel_id=1, source_target_pairs={{32,0},{40,8},{48,16},{56,24},{64,32},{72,40},{80,48},{88,56},{33,... | collective-permute-start | bytes 3440648 | tf_op jit(solution)/shard_map/ppermute | solution.py:243
  125.8 17.1 %collective-permute-start.22 = (f32[4,72,512]{2,1,0:T(8,128)S(1)}, f32[4,72,512]{2,1,0:T(8,128)S(1)}, u32[]{:S(2)}, u32[]{:S(2)}) collective-permute-start(f32[4,72,512]{2,1,0:T(8,128)S(1)} %slice.65), channel_id=1, source_target_pairs={{0,1},{1,0},{2,3},{3,2},{4,5},{5,4},{6,7},{7,6},{8,9},{9,8},{10,11... | collective-permute-start | bytes 1769480 | tf_op jit(solution)/shard_map/ppermute | solution.py:249
  125.9 19.1 %collective-permute-start.14 = (f32[72,512]{1,0:T(8,128)S(1)}, f32[72,512]{1,0:T(8,128)S(1)}, u32[]{:S(2)}, u32[]{:S(2)}) collective-permute-start(f32[72,512]{1,0:T(8,128)S(1)} %copy-done.15), channel_id=1, source_target_pairs={{104,0},{112,8},{120,16},{96,24},{8,32},{16,40},{24,48},{0,56},{40... | collective-permute-start | bytes 442376 | tf_op jit(solution)/shard_map/ppermute | solution.py:289
  134.7 13.1 %collective-permute-start.15 = (f32[72,512]{1,0:T(8,128)S(1)}, f32[72,512]{1,0:T(8,128)S(1)}, u32[]{:S(2)}, u32[]{:S(2)}) collective-permute-start(f32[72,512]{1,0:T(8,128)S(1)} %copy-done.14), channel_id=1, source_target_pairs={{112,0},{120,8},{96,16},{104,24},{16,32},{24,40},{0,48},{8,56},{48... | collective-permute-start | bytes 442376 | tf_op jit(solution)/shard_map/ppermute | solution.py:289
  134.7 15.9 %collective-permute-start.16 = (f32[72,512]{1,0:T(8,128)S(1)}, f32[72,512]{1,0:T(8,128)S(1)}, u32[]{:S(2)}, u32[]{:S(2)}) collective-permute-start(f32[72,512]{1,0:T(8,128)S(1)} %copy-done.12), channel_id=1, source_target_pairs={{0,16},{8,24},{32,48},{40,56},{64,80},{72,88},{96,112},{104,120},{... | collective-permute-start | bytes 442376 | tf_op jit(solution)/shard_map/ppermute | solution.py:289
  138.0 14.3 %collective-permute-start.17 = (f32[72,512]{1,0:T(8,128)S(1)}, f32[72,512]{1,0:T(8,128)S(1)}, u32[]{:S(2)}, u32[]{:S(2)}) collective-permute-start(f32[72,512]{1,0:T(8,128)S(1)} %copy-done.11), channel_id=1, source_target_pairs={{0,64},{8,72},{16,80},{24,88},{32,96},{40,104},{48,112},{56,120},{... | collective-permute-start | bytes 442376 | tf_op jit(solution)/shard_map/ppermute | solution.py:289
  142.9 9.4 %collective-permute-start.20 = (f32[72,512]{1,0:T(8,128)}, f32[72,512]{1,0:T(8,128)S(1)}, u32[]{:S(2)}, u32[]{:S(2)}) collective-permute-start(f32[72,512]{1,0:T(8,128)} %get-tuple-element.50), channel_id=1, source_target_pairs={{72,0},{80,8},{88,16},{64,24},{104,32},{112,40},{120,48},{96,56},{... | collective-permute-start | bytes 442376 | tf_op jit(solution)/shard_map/ppermute | solution.py:289
  145.1 7.2 %collective-permute-start.21 = (f32[72,512]{1,0:T(8,128)S(1)}, f32[72,512]{1,0:T(8,128)S(1)}, u32[]{:S(2)}, u32[]{:S(2)}) collective-permute-start(f32[72,512]{1,0:T(8,128)S(1)} %copy-done.13), channel_id=1, source_target_pairs={{16,64},{24,72},{0,80},{8,88},{48,96},{56,104},{32,112},{40,120},{... | collective-permute-start | bytes 442376 | tf_op jit(solution)/shard_map/ppermute | solution.py:289
  147.7 8.9 %collective-permute-start.23 = (f32[72,512]{1,0:T(8,128)S(1)}, f32[72,512]{1,0:T(8,128)S(1)}, u32[]{:S(2)}, u32[]{:S(2)}) collective-permute-start(f32[72,512]{1,0:T(8,128)S(1)} %get-tuple-element.57), channel_id=1, source_target_pairs={{0,6},{1,7},{2,0},{3,1},{4,2},{5,3},{6,4},{7,5},{8,14},{9,15},{10,... | collective-permute-start | bytes 442376 | tf_op jit(solution)/shard_map/ppermute | solution.py:246
  152.3 8.8 %collective-permute-start.25 = (f32[72,512]{1,0:T(8,128)S(1)}, f32[72,512]{1,0:T(8,128)S(1)}, u32[]{:S(2)}, u32[]{:S(2)}) collective-permute-start(f32[72,512]{1,0:T(8,128)S(1)} %get-tuple-element.58), channel_id=1, source_target_pairs={{0,2},{1,3},{2,4},{3,5},{4,6},{5,7},{6,0},{7,1},{8,10},{9,11},{10,... | collective-permute-start | bytes 442376 | tf_op jit(solution)/shard_map/ppermute | solution.py:246
  169.9 10.0 %collective-permute-start.30 = (f32[64,64]{1,0:T(8,128)S(1)}, f32[64,64]{1,0:T(8,128)S(1)}, u32[]{:S(2)}, u32[]{:S(2)}) collective-permute-start(f32[64,64]{1,0:T(8,128)S(1)} %add_add_fusion.3), channel_id=1, source_target_pairs={{0,8},{8,16},{16,24},{24,0},{32,40},{40,48},{48,56},{56,32},{64,72... | collective-permute-start | bytes 49160 | tf_op jit(solution)/shard_map/ppermute | solution.py:243
  (28 other events, 209.8 us)

commit v3 on v2

--- a/solution.py
+++ b/solution.py
@@ -101,106 +101,139 @@
     return row[:, 0:BLOCK] + row[:, BLOCK : 2 * BLOCK]
 
 
-def cells_kernel(count, first, order_ref, flags_ref, x_ref, side_ref, *refs):
-    far_refs, refs = refs[:count], refs[count:]
-    if first:
-        new_ref, norm_ref, refs = refs[0], refs[1], refs[2:]
-    else:
-        norm_ref, old_ref, new_ref, refs = refs[0], refs[1], refs[2], refs[3:]
-    far_sums_refs, token_ref, p_ref = refs[:count], refs[count], refs[count + 1]
+def double(columns):
+    return jnp.concatenate([columns, columns], axis=1)
+
+
+def own_kernel(order_ref, flags_ref, x_ref, far_ref, new_ref, norm_ref, token_ref, p_ref):
     step = pl.program_id(0)
-
-    @pl.when(step == 0)
+    new_ref[...] = jnp.zeros_like(new_ref)
+    token_ref[...] = jnp.zeros_like(token_ref)
+    norm_ref[0] = jnp.broadcast_to(row_norm(x_ref[0].astype(jnp.float32)) * SCALE, (BLOCK, 128))
+
+    @pl.when(flags_ref[step] > 0)
     def _():
-        for far_sums_ref in far_sums_refs:
-            far_sums_ref[...] = jnp.zeros_like(far_sums_ref)
-        token_ref[...] = jnp.zeros_like(token_ref)
-
-    if first:
-        new_ref[...] = jnp.zeros_like(new_ref)
-        norm_ref[0] = jnp.broadcast_to(side_norms(side_ref[0, 0]), (128, BLOCK)).T
-    else:
-        new_ref[...] = old_ref[...]
-
-    def score(far_ref):
-        near = norm_ref[0]
-        near = jnp.concatenate([near, near], axis=1)
-        far = side_norms(far_ref[BLOCK:PAYLOAD, :])
+        side = far_ref[BLOCK:PAYLOAD, :]
+        near, far = double(norm_ref[0]), side_norms(side)
         for at in range(0, BLOCK, 256):
             scores = lax.dot_general(
                 x_ref[0], far_ref[at : at + 256, :], NT, preferred_element_type=jnp.float32
             )
             p_ref[:, at : at + 256] = jnp.exp2(scores * near * far[:, at : at + 256]).astype(jnp.bfloat16)
-
-    def forward(far_ref):
-        vectors = side_vectors(far_ref[BLOCK:PAYLOAD, :])
-        part = lax.dot_general(vectors, p_ref[...], NT, preferred_element_type=jnp.float32)
+        part = lax.dot_general(side_vectors(side), p_ref[...], NT, preferred_element_type=jnp.float32)
+        new_ref[0] = part[0:ACC, :]
+
+
+def cells_kernel(count, order_ref, flags_ref, x_ref, side_ref, *refs):
+    far_refs, refs = refs[:count], refs[count:]
+    norm_ref, old_ref, new_ref, refs = refs[0], refs[1], refs[2], refs[3:]
+    far_sums_refs, token_ref, p_ref, column_ref = refs[:count], refs[count], refs[count + 1], refs[count + 2]
+    step = pl.program_id(0)
+
+    @pl.when(step == 0)
+    def _():
+        token_ref[...] = jnp.zeros_like(token_ref)
+        for at in range(count):
+            far_sums_refs[at][...] = jnp.zeros_like(far_sums_refs[at])
+            column_ref[at] = jnp.broadcast_to(side_norms(far_refs[at][BLOCK:PAYLOAD, :]), (128, BLOCK)).T
+
+    new_ref[...] = old_ref[...]
+
+    def forward_only(at):
+        far_ref = far_refs[at]
+        near, far = side_norms(side_ref[0, 0]), double(column_ref[at])
+        for to in range(0, BLOCK, 256):
+            scores = lax.dot_general(
+                far_ref[0:BLOCK, :], x_ref[0, to : to + 256, :], NT, preferred_element_type=jnp.float32
+            )
+            p_ref[:, to : to + 256] = jnp.exp2(scores * near[:, to : to + 256] * far).astype(jnp.bfloat16)
+        part = jnp.dot(side_vectors(far_ref[BLOCK:PAYLOAD, :]), p_ref[...], preferred_element_type=jnp.float32)
         new_ref[0] += part[0:ACC, :]
 
-    def backward(far_sums_ref):
-        vectors = side_vectors(side_ref[0, 0])
-        part = jnp.dot(vectors, p_ref[...], preferred_element_type=jnp.float32)
-        far_sums_ref[...] += part[0:ACC, :]
+    def backward(at, both):
+        far_ref = far_refs[at]
+        side = far_ref[BLOCK:PAYLOAD, :]
+        near, far = double(norm_ref[0]), side_norms(side)
+        for to in range(0, BLOCK, 256):
+            scores = lax.dot_general(
+                x_ref[0], far_ref[to : to + 256, :], NT, preferred_element_type=jnp.float32
+            )
+            p_ref[:, to : to + 256] = jnp.exp2(scores * near * far[:, to : to + 256]).astype(jnp.bfloat16)
+        part = jnp.dot(side_vectors(side_ref[0, 0]), p_ref[...], preferred_element_type=jnp.float32)
+        far_sums_refs[at][...] += part[0:ACC, :]
+        if both:
+            part = lax.dot_general(side_vectors(side), p_ref[...], NT, preferred_element_type=jnp.float32)
+            new_ref[0] += part[0:ACC, :]
 
     for at in range(count):
         flag = flags_ref[at * COLS + step]
-        pl.when(flag > 0)(functools.partial(score, far_refs[at]))
-        pl.when(flag % 2 == 1)(functools.partial(forward, far_refs[at]))
-        pl.when(flag >= 2)(functools.partial(backward, far_sums_refs[at]))
-
-
-def tie_kernel(*refs):
-    pass
-
-
-def tie(arrays, token):
+        pl.when(flag == 1)(functools.partial(forward_only, at))
+        pl.when(flag == 2)(functools.partial(backward, at, False))
+        pl.when(flag == 3)(functools.partial(backward, at, True))
+
+
+NEAR = lambda g, order, flags: (order[g], 0, 0)
+STEP = lambda g, order, flags: (g, 0, 0)
+WHOLE = lambda g, order, flags: (0, 0)
+X_SPEC = pl.BlockSpec((1, BLOCK, WIDTH), NEAR)
+FAR_SPEC = pl.BlockSpec((PAYLOAD, WIDTH), WHOLE)
+NORM = (pl.BlockSpec((1, BLOCK, 128), STEP), (COLS, BLOCK, 128))
+SUMS = (pl.BlockSpec((1, ACC, BLOCK), STEP), (COLS, ACC, BLOCK))
+PART = (pl.BlockSpec((ACC, BLOCK), WHOLE), (ACC, BLOCK))
+TOKEN = (pl.BlockSpec((8, 128), WHOLE), (8, 128))
+
+
+def cells_call(kernel, count, ins, outs, scratch, aliases, name, args):
     return pl.pallas_call(
-        tie_kernel,
-        out_shape=[jax.ShapeDtypeStruct(array.shape, array.dtype) for array in arrays],
-        in_specs=[pl.BlockSpec(memory_space=pl.ANY)] * (len(arrays) + 1),
-        out_specs=[pl.BlockSpec(memory_space=pl.ANY)] * len(arrays),
-        input_output_aliases={at: at for at in range(len(arrays))},
-        name="tie",
-    )(*arrays, token)
-
-
-def cells(order, flags, blocks, sides, fars, norms=None, sums=None):
-    count, first = len(fars), sums is None
-    near = lambda g, order, flags: (order[g], 0, 0)
-    step = lambda g, order, flags: (g, 0, 0)
-    whole = lambda g, order, flags: (0, 0)
-    norm_spec, norm_shape = pl.BlockSpec((1, BLOCK, 128), step), (COLS, BLOCK, 128)
-    sums_spec, sums_shape = pl.BlockSpec((1, ACC, BLOCK), step), (COLS, ACC, BLOCK)
-    far_sums = [(pl.BlockSpec((ACC, BLOCK), whole), (ACC, BLOCK))] * count
-    outs = [(sums_spec, sums_shape)] + ([(norm_spec, norm_shape)] if first else []) + far_sums
-    outs += [(pl.BlockSpec((8, 128), whole), (8, 128))]
-    result = pl.pallas_call(
-        functools.partial(cells_kernel, count, first),
+        kernel,
         out_shape=[jax.ShapeDtypeStruct(shape, jnp.float32) for _, shape in outs],
         grid_spec=pltpu.PrefetchScalarGridSpec(
-            num_scalar_prefetch=2,
-            grid=(COLS,),
-            in_specs=[
-                pl.BlockSpec((1, BLOCK, WIDTH), near),
-                pl.BlockSpec((1, 1, PAYLOAD - BLOCK, WIDTH), lambda g, order, flags: (g % SIDE, g // SIDE, 0, 0)),
-            ]
-            + [pl.BlockSpec((PAYLOAD, WIDTH), whole)] * count
-            + ([] if first else [norm_spec, sums_spec]),
-            out_specs=[spec for spec, _ in outs],
-            scratch_shapes=[pltpu.VMEM((BLOCK, BLOCK), jnp.bfloat16)],
+            num_scalar_prefetch=2, grid=(COLS,), in_specs=ins, out_specs=[spec for spec, _ in outs], scratch_shapes=scratch
         ),
-        input_output_aliases={} if first else {5 + count: 0},
+        input_output_aliases=aliases,
         compiler_params=pltpu.CompilerParams(vmem_limit_bytes=56 << 20),
         cost_estimate=pl.CostEstimate(
             flops=count * COST * BLOCK * BLOCK * WIDTH,
             bytes_accessed=(12 + count) << 20,
             transcendentals=count * 4 * BLOCK * BLOCK,
         ),
-        name="cells",
-    )(order, flags, blocks, sides, *fars, *([] if first else [norms, sums]))
-    if first:
-        return result[0], result[1], result[2:-1], result[-1]
-    return result[0], norms, result[1:-1], result[-1]
+        name=name,
+    )(*args)
+
+
+SCORES = pltpu.VMEM((BLOCK, BLOCK), jnp.bfloat16)
+
+
+def own_cells(order, flags, blocks, far):
+    ins, outs = [X_SPEC, FAR_SPEC], [SUMS, NORM, TOKEN]
+    return cells_call(own_kernel, 1, ins, outs, [SCORES], {}, "cells_own", (order, flags, blocks, far))
+
+
+def cells(order, flags, blocks, sides, fars, norms, sums):
+    count = len(fars)
+    side = pl.BlockSpec((1, 1, PAYLOAD - BLOCK, WIDTH), lambda g, order, flags: (g % SIDE, g // SIDE, 0, 0))
+    ins = [X_SPEC, side] + [FAR_SPEC] * count + [NORM[0], SUMS[0]]
+    outs = [SUMS] + [PART] * count + [TOKEN]
+    scratch = [SCORES, pltpu.VMEM((count, BLOCK, 128), jnp.float32)]
+    args = (order, flags, blocks, sides, *fars, norms, sums)
+    kernel = functools.partial(cells_kernel, count)
+    result = cells_call(kernel, count, ins, outs, scratch, {5 + count: 0}, "cells", args)
+    return result[0], result[1:-1], result[-1]
+
+
+def tie_kernel(*refs):
+    pass
+
+
+def tie(arrays, *tokens):
+    return pl.pallas_call(
+        tie_kernel,
+        out_shape=[jax.ShapeDtypeStruct(array.shape, array.dtype) for array in arrays],
+        in_specs=[pl.BlockSpec(memory_space=pl.ANY)] * (len(arrays) + len(tokens)),
+        out_specs=[pl.BlockSpec(memory_space=pl.ANY)] * len(arrays),
+        input_output_aliases={at: at for at in range(len(arrays))},
+        name="tie",
+    )(*arrays, *tokens)
 
 
 def solve_kernel(gram_ref, smoothed_ref, out_ref):
@@ -258,25 +291,21 @@
     order = jnp.stack([(here_col - CORES * k) % COLS ^ core for core in range(CORES) for k in range(SIDE)])
 
     far_ids, works = [], []
-    ahead = (order - here_col) % COLS
     for name, ((dy, dx), keep) in STAGES.items():
         from_row = (here_y - dy) % SIDE * SIDE + (here_x - dx) % SIDE
         far_ids.append(from_row * COLS + here_col)
-        if name == "own":
-            half = COLS // 2
-            works.append((ahead > 0) & ((ahead < half) | ((ahead == half) & (here_col < half))))
-        else:
-            works.append(jnp.broadcast_to(True if keep is None else keep(here_y, here_x), (COLS,)))
+        works.append(jnp.broadcast_to(True if keep is None else keep(here_y, here_x), (COLS,)))
     far_ids = jnp.stack(far_ids)[:, None]
     near_ids = (here_row * COLS + order)[None, :]
     wanted = jnp.stack([near_ids * NBLOCKS + far_ids, far_ids * NBLOCKS + near_ids])
     listed = block_pairs[:, 0] * NBLOCKS + block_pairs[:, 1]
     found = jnp.any(wanted[..., None] == listed, axis=-1)
-    flags = jnp.where(jnp.stack(works), found[0] + 2 * found[1], 0).astype(jnp.int32)
+    both_ways = (jnp.arange(len(STAGES)) > 0)[:, None]
+    flags = jnp.where(jnp.stack(works), found[0] + 2 * (found[1] & both_ways), 0).astype(jnp.int32)
 
     starts = {name: at for at, name in enumerate(STAGES)}
 
-    def work(group, norms=None, sums=None):
+    def work(group, sums):
         at = starts[group[0]]
         return cells(
             order, flags[at : at + len(group)].reshape(-1), blocks, sides, [far[name] for name in group], norms, sums
@@ -289,27 +318,27 @@
             moved.append(lax.ppermute(part, "row", [(to, source) for source, to in shift(dy, dx, keep)]))
         return moved
 
-    sums, norms, returned, token = work(("own",))
-    far["a"], far["b"], far["c"] = tie([far["a"], far["b"], far["c"]], token)
+    sums, norms, token = own_cells(order, flags[0], blocks, far["own"])
+    far["a"], far["b"], far["c"] = tie([far["a"], far["b"], far["c"]], token, sides)
     far["d"] = move(far["a"], -1, 0)
     far["e"] = move(far["c"], 0, -1)
     far["g"] = move(far["a"], 0, 1, left_half)
     far["h"] = move(far["b"], 1, 0)
 
     group = ("a", "b", "c")
-    sums, norms, parts, token = work(group, norms, sums)
+    sums, parts, token = work(group, sums)
     far["h"], far["e"] = tie([far["h"], far["e"]], token)
-    early = sum(give_back(group, parts)) + returned[0]
+    early = sum(give_back(group, parts))
     far["f"] = move(far["h"], 0, 1)
     far["k"] = move(far["e"], -1, 0, top_half)
 
     group = ("d", "e", "g", "h")
-    sums, norms, parts, token = work(group, norms, sums)
+    sums, parts, token = work(group, sums)
     returned = give_back(group, parts)
 
     far["f"], far["k"] = tie([far["f"], far["k"]], early[0:8, 0:128])
     group = ("f", "k")
-    sums, norms, parts, token = work(group, norms, sums)
+    sums, parts, token = work(group, sums)
     returned = [early] + returned + give_back(group, parts)
 
     kept = sums[:SIDE] + swap(sums[SIDE:])

time: 196 us -> 195 us (level); the launches traced: 197 us -> 194 us
  local copies, waits for them, and re-layouts: 11.3 us -> 16.4 us
  waiting for transfers between devices: 46.8 us -> 42.7 us
  starting transfers between devices: 78.9 us -> 75.2 us
    ppermute x9, waiting for transfers between devices: 21 us -> 13.5 us  [turn(): lax.ppermute(array, 'col', [(i, (i + by * CORES) % COLS) for i in range(C...]
    ppermute x9, starting transfers between devices: 15.5 us -> 11.2 us  [turn(): lax.ppermute(array, 'col', [(i, (i + by * CORES) % COLS) for i in range(C...]
    ppermute x9, waiting for transfers between devices: 8.41 us -> 12.5 us  [give_back(): lax.ppermute(part, 'row', [(to, source) for source, to in shift(dy, dx, k...]
    ppermute x9, starting transfers between devices: 35.4 us -> 38.2 us  [give_back(): lax.ppermute(part, 'row', [(to, source) for source, to in shift(dy, dx, k...]
    ppermute x15, starting transfers between devices: 27.8 us -> 25.7 us  [move(): return lax.ppermute(array, 'row', shift(dy, dx, keep))]
    unnamed x32 -> x31, local copies, waits for them, and re-layouts: 3.9 us -> 5.32 us
  transfers between devices with their start and end apart: 36 -> 36, of which waited for: 21 -> 20; matrix products, arithmetic and copies ran while one was open for 7% -> 8% of each run, Pallas kernels for 16% -> 17%
where the time goes in v3:
time: 195 us; the launch traced here: 194 us
  starting transfers between devices  75.2 us (39%)
  Pallas kernels  52.4 us (27%)
  waiting for transfers between devices  42.7 us (22%)
  local copies, waits for them, and re-layouts  16.4 us (8%)
  other arithmetic  6.79 us (3%)
    pallas_call x4, Pallas kernels, cells_call(): pl.pallas_call(kernel, out_shape=[jax.ShapeDtypeStruct(shape, jnp.float32...  42.2 us
    ppermute x9, starting transfers between devices, give_back(): lax.ppermute(part, 'row', [(to, source) for source, to in shift(dy, dx, k...  38.2 us
    ppermute x15, starting transfers between devices, move(): return lax.ppermute(array, 'row', shift(dy, dx, keep))  25.7 us
    ppermute x15, waiting for transfers between devices, move(): return lax.ppermute(array, 'row', shift(dy, dx, keep))  15.5 us
    ppermute x9, waiting for transfers between devices, turn(): lax.ppermute(array, 'col', [(i, (i + by * CORES) % COLS) for i in range(C...  13.5 us
    ppermute x9, waiting for transfers between devices, give_back(): lax.ppermute(part, 'row', [(to, source) for source, to in shift(dy, dx, k...  12.5 us
    ppermute x9, starting transfers between devices, turn(): lax.ppermute(array, 'col', [(i, (i + by * CORES) % COLS) for i in range(C...  11.2 us
    pallas_call x1, Pallas kernels, solve(): pl.pallas_call(solve_kernel, out_shape=jax.ShapeDtypeStruct(smoothed.shap...  7.57 us
  transfers between devices with their start and end apart: 36, of which 20 were waited for; matrix products, arithmetic and copies ran while one was open for 8% of the time, Pallas kernels for 17%

profile of v3, /device:TPU:0, one launch (start us, length us, event | category | flops | bytes accessed | tf_op | source)
XLA Modules:
  0.0 194.1 jit_solution(5129342494918363917)
XLA Ops:
  0.0 2.6 %payload.1.far_ref = bf16[560,1024]{1,0:T(8,128)(2,1)} custom-call(s32[1]{0:T(128)} %bitcast.21.index_ref, bf16[8,512,1024]{2,1,0:T(8,128)(2,1)} %bitcast.55, bf16[64,512]{1,0:T(8,128)(2,1)} %v_ref.1), custom_call_target="tpu_custom_call" | custom-call | tf_op jit(solution)/shard_map/payload/pallas_call | solution.py:77
  5.7 2.8 %collective-permute-start.6 = (bf16[560,1024]{1,0:T(8,128)(2,1)}, bf16[560,1024]{1,0:T(8,128)(2,1)S(1)}, u32[]{:S(2)}, u32[]{:S(2)}) collective-permute-start(bf16[560,1024]{1,0:T(8,128)(2,1)} %payload.1.far_ref), channel_id=1, source_target_pairs={{0,120},{8,96},{16,104},{24,112},{32,24},{40,0},{48,8},{56,16},{64... | collective-permute-start | bytes 3440648 | tf_op jit(solution)/shard_map/ppermute | solution.py:276
  22.5 3.6 %collective-permute-start.2 = (bf16[2,48,1024]{2,1,0:T(8,128)(2,1)S(1)}, bf16[2,48,1024]{2,1,0:T(8,128)(2,1)S(1)}, u32[]{:S(2)}, u32[]{:S(2)}) collective-permute-start(bf16[2,48,1024]{2,1,0:T(8,128)(2,1)S(1)} %get-tuple-element.59), channel_id=1, source_target_pairs={{0,4},{1,5},{2,6},{3,7},{4,0},{5,1},{6,2},{7,3},{8,12},{9,13},{10,... | collective-permute-start | bytes 589832 | tf_op jit(solution)/shard_map/ppermute | solution.py:279
  26.1 3.5 %collective-permute-done.1 = bf16[2,48,1024]{2,1,0:T(8,128)(2,1)S(1)} collective-permute-done((bf16[2,48,1024]{2,1,0:T(8,128)(2,1)S(1)}, bf16[2,48,1024]{2,1,0:T(8,128)(2,1)S(1)}, u32[]{:S(2)}, u32[]{:S(2)}) %collective-permute-start.1) | collective-permute-done | bytes 196640 | tf_op jit(solution)/shard_map/ppermute | solution.py:279
  31.7 9.2 %cells_own.1 = (f32[8,72,512]{2,1,0:T(8,128)}, f32[8,512,128]{2,1,0:T(8,128)}, f32[8,128]{1,0:T(8,128)}) custom-call(s32[8]{0:T(128)} %stack.103.order_ref, s32[8]{0:T(128)} %slice_reduce_fusion.flags_ref, bf16[8,512,1024]{2,1,0:T(8,128)(2,1)} %bitcast.56, bf16[560,1024]{1,0:T(8,128)(2,1)} %payload.1.far_ref), custom_call_target="tpu_custom_call" | custom-call | flops 2147483648 | bytes 13631488 | tf_op jit(solution)/shard_map/cells_own/pallas_call | solution.py:187
  45.7 4.0 %collective-permute-start.10 = (bf16[560,1024]{1,0:T(8,128)(2,1)}, bf16[560,1024]{1,0:T(8,128)(2,1)}, u32[]{:S(2)}, u32[]{:S(2)}) collective-permute-start(bf16[560,1024]{1,0:T(8,128)(2,1)} %get-tuple-element.29.refs_0_), channel_id=1, source_target_pairs={{0,96},{8,104},{16,112},{24,120},{32,0},{40,8},{48,16},{56,24},{64... | collective-permute-start | bytes 3440648 | tf_op jit(solution)/shard_map/ppermute | solution.py:276
  52.5 12.1 %cells.3 = (f32[8,72,512]{2,1,0:T(8,128)}, f32[72,512]{1,0:T(8,128)}, f32[72,512]{1,0:T(8,128)}, f32[72,512]{1,0:T(8,128)}, f32[8,128]{1,0:T(8,128)}) custom-call(s32[8]{0:T(128)} %stack.103.order_ref, s32[24]{0:T(128)} %reshape.314.flags_ref, bf16[8,512,1024]{2,1,0:T(8,128)(2,1)} %bitcast.57, ...), custom_call_target="tpu_custom_call", output_to_operand_aliasing={{0}: (8, {})} | custom-call | flops 6442450944 | bytes 15728640 | tf_op jit(solution)/shard_map/cells/pallas_call | solution.py:187
  64.6 4.9 %collective-permute-start.7 = (f32[72,512]{1,0:T(8,128)}, f32[72,512]{1,0:T(8,128)S(1)}, u32[]{:S(2)}, u32[]{:S(2)}) collective-permute-start(f32[72,512]{1,0:T(8,128)} %get-tuple-element.34), channel_id=1, source_target_pairs={{8,0},{16,8},{24,16},{0,24},{40,32},{48,40},{56,48},{32,56},{72,64... | collective-permute-start | bytes 442376 | tf_op jit(solution)/shard_map/ppermute | solution.py:318
  69.5 3.4 %collective-permute-done.11.refs_0_ = bf16[560,1024]{1,0:T(8,128)(2,1)S(1)} collective-permute-done((bf16[560,1024]{1,0:T(8,128)(2,1)}, bf16[560,1024]{1,0:T(8,128)(2,1)S(1)}, u32[]{:S(2)}, u32[]{:S(2)}) %collective-permute-start.11) | collective-permute-done | bytes 1146912 | tf_op jit(solution)/shard_map/ppermute | solution.py:276
  72.9 9.8 %collective-permute-start.8 = (f32[72,512]{1,0:T(8,128)}, f32[72,512]{1,0:T(8,128)S(1)}, u32[]{:S(2)}, u32[]{:S(2)}) collective-permute-start(f32[72,512]{1,0:T(8,128)} %get-tuple-element.35), channel_id=1, source_target_pairs={{32,0},{40,8},{48,16},{56,24},{64,32},{72,40},{80,48},{88,56},{96,... | collective-permute-start | bytes 442376 | tf_op jit(solution)/shard_map/ppermute | solution.py:318
  88.8 4.3 %collective-permute-done.9 = f32[72,512]{1,0:T(8,128)S(1)} collective-permute-done((f32[72,512]{1,0:T(8,128)}, f32[72,512]{1,0:T(8,128)S(1)}, u32[]{:S(2)}, u32[]{:S(2)}) %collective-permute-start.9) | collective-permute-done | bytes 147488 | tf_op jit(solution)/shard_map/ppermute | solution.py:318
  93.7 11.3 %cells.4 = (f32[8,72,512]{2,1,0:T(8,128)}, f32[72,512]{1,0:T(8,128)}, f32[72,512]{1,0:T(8,128)}, f32[72,512]{1,0:T(8,128)}, f32[72,512]{1,0:T(8,128)}, /*index=5*/f32[8,128]{1,0:T(8,128)}) custom-call(s32[8]{0:T(128)} %stack.103.order_ref, s32[32]{0:T(128)} %reshape.316.flags_ref, bf16[8,512,1024]{2,1,0:T(8,128)(2,1)} %bitcast.58, ...), custom_call_target="tpu_custom_call", output_to_operand_aliasing={{0}: (9, {})} | custom-call | flops 8589934592 | bytes 16777216 | tf_op jit(solution)/shard_map/cells/pallas_call | solution.py:187
  105.0 4.3 %collective-permute-done.18.refs_0_ = bf16[560,1024]{1,0:T(8,128)(2,1)S(1)} collective-permute-done((bf16[560,1024]{1,0:T(8,128)(2,1)}, bf16[560,1024]{1,0:T(8,128)(2,1)S(1)}, u32[]{:S(2)}, u32[]{:S(2)}) %collective-permute-start.18) | collective-permute-done | bytes 1146912 | tf_op jit(solution)/shard_map/ppermute | solution.py:276
  111.3 9.6 %cells.5 = (f32[8,72,512]{2,1,0:T(8,128)}, f32[72,512]{1,0:T(8,128)}, f32[72,512]{1,0:T(8,128)}, f32[8,128]{1,0:T(8,128)}) custom-call(s32[8]{0:T(128)} %stack.103.order_ref, s32[16]{0:T(128)} %reshape.317.flags_ref, bf16[8,512,1024]{2,1,0:T(8,128)(2,1)} %bitcast.59, ...), custom_call_target="tpu_custom_call", output_to_operand_aliasing={{0}: (7, {})} | custom-call | flops 4294967296 | bytes 14680064 | tf_op jit(solution)/shard_map/cells/pallas_call | solution.py:187
  122.1 8.8 %collective-permute-start.14 = (f32[72,512]{1,0:T(8,128)S(1)}, f32[72,512]{1,0:T(8,128)S(1)}, u32[]{:S(2)}, u32[]{:S(2)}) collective-permute-start(f32[72,512]{1,0:T(8,128)S(1)} %copy-done.14), channel_id=1, source_target_pairs={{104,0},{112,8},{120,16},{96,24},{8,32},{16,40},{24,48},{0,56},{40... | collective-permute-start | bytes 442376 | tf_op jit(solution)/shard_map/ppermute | solution.py:318
  131.0 9.8 %collective-permute-start.16 = (f32[72,512]{1,0:T(8,128)S(1)}, f32[72,512]{1,0:T(8,128)S(1)}, u32[]{:S(2)}, u32[]{:S(2)}) collective-permute-start(f32[72,512]{1,0:T(8,128)S(1)} %copy-done.11), channel_id=1, source_target_pairs={{0,16},{8,24},{32,48},{40,56},{64,80},{72,88},{96,112},{104,120},{... | collective-permute-start | bytes 442376 | tf_op jit(solution)/shard_map/ppermute | solution.py:318
  143.0 3.5 %collective-permute-start.21 = (f32[72,512]{1,0:T(8,128)S(1)}, f32[72,512]{1,0:T(8,128)S(1)}, u32[]{:S(2)}, u32[]{:S(2)}) collective-permute-start(f32[72,512]{1,0:T(8,128)S(1)} %copy-done.12), channel_id=1, source_target_pairs={{16,64},{24,72},{0,80},{8,88},{48,96},{56,104},{32,112},{40,120},{... | collective-permute-start | bytes 442376 | tf_op jit(solution)/shard_map/ppermute | solution.py:318
  146.8 6.3 %collective-permute-done.17 = f32[72,512]{1,0:T(8,128)S(1)} collective-permute-done((f32[72,512]{1,0:T(8,128)S(1)}, f32[72,512]{1,0:T(8,128)S(1)}, u32[]{:S(2)}, u32[]{:S(2)}) %collective-permute-start.17) | collective-permute-done | bytes 147488 | tf_op jit(solution)/shard_map/ppermute | solution.py:318
  154.8 5.2 %collective-permute-done.25 = f32[72,512]{1,0:T(8,128)S(1)} collective-permute-done((f32[72,512]{1,0:T(8,128)S(1)}, f32[72,512]{1,0:T(8,128)S(1)}, u32[]{:S(2)}, u32[]{:S(2)}) %collective-permute-start.25) | collective-permute-done | bytes 147488 | tf_op jit(solution)/shard_map/ppermute | solution.py:279
  162.8 2.2 %collective-permute-start.29 = (f32[64,64]{1,0:T(8,128)S(1)}, f32[64,64]{1,0:T(8,128)S(1)}, u32[]{:S(2)}, u32[]{:S(2)}) collective-permute-start(f32[64,64]{1,0:T(8,128)S(1)} %add.322), channel_id=1, source_target_pairs={{0,6},{1,7},{2,0},{3,1},{4,2},{5,3},{6,4},{7,5},{8,14},{9,15},{10,... | collective-permute-start | bytes 49160 | tf_op jit(solution)/shard_map/ppermute | solution.py:279
  168.3 2.7 %collective-permute-start.31 = (f32[64,64]{1,0:T(8,128)S(1)}, f32[64,64]{1,0:T(8,128)S(1)}, u32[]{:S(2)}, u32[]{:S(2)}) collective-permute-start(f32[64,64]{1,0:T(8,128)S(1)} %add_add_fusion.3), channel_id=1, source_target_pairs={{0,16},{8,24},{16,0},{24,8},{32,48},{40,56},{48,32},{56,40},{64,80... | collective-permute-start | bytes 49160 | tf_op jit(solution)/shard_map/ppermute | solution.py:276
  175.0 3.9 %collective-permute-start.33 = (f32[64,64]{1,0:T(8,128)S(1)}, f32[64,64]{1,0:T(8,128)S(1)}, u32[]{:S(2)}, u32[]{:S(2)}) collective-permute-start(f32[64,64]{1,0:T(8,128)S(1)} %add_add_fusion.2), channel_id=1, source_target_pairs={{0,32},{8,40},{16,48},{24,56},{32,64},{40,72},{48,80},{56,88},{64,... | collective-permute-start | bytes 49160 | tf_op jit(solution)/shard_map/ppermute | solution.py:276
  178.9 3.1 %collective-permute-start.34 = (f32[64,64]{1,0:T(8,128)S(1)}, f32[64,64]{1,0:T(8,128)S(1)}, u32[]{:S(2)}, u32[]{:S(2)}) collective-permute-start(f32[64,64]{1,0:T(8,128)S(1)} %add_add_fusion.2), channel_id=1, source_target_pairs={{0,64},{8,72},{16,80},{24,88},{32,96},{40,104},{48,112},{56,120},{... | collective-permute-start | bytes 49160 | tf_op jit(solution)/shard_map/ppermute | solution.py:276
  186.5 7.6 %solve.1 = f32[64,512]{1,0:T(8,128)} custom-call(f32[64,64]{1,0:T(8,128)} %add_add_fusion.1.gram_ref, f32[64,512]{1,0:T(8,128)} %copy-done), custom_call_target="tpu_custom_call" | custom-call | tf_op jit(solution)/shard_map/solve/pallas_call | solution.py:260
  (132 shorter events, 55.3 us)
Async XLA Ops:
  2.6 39.4 %collective-permute-start.4 = (bf16[560,1024]{1,0:T(8,128)(2,1)}, bf16[560,1024]{1,0:T(8,128)(2,1)S(1)}, u32[]{:S(2)}, u32[]{:S(2)}) collective-permute-start(bf16[560,1024]{1,0:T(8,128)(2,1)} %payload.1.far_ref), channel_id=1, source_target_pairs={{0,8},{8,16},{16,24},{24,0},{32,40},{40,48},{48,56},{56,32},{64,72... | collective-permute-start | bytes 3440648 | tf_op jit(solution)/shard_map/ppermute | solution.py:276
  4.2 37.8 %collective-permute-start.5 = (bf16[560,1024]{1,0:T(8,128)(2,1)}, bf16[560,1024]{1,0:T(8,128)(2,1)S(1)}, u32[]{:S(2)}, u32[]{:S(2)}) collective-permute-start(bf16[560,1024]{1,0:T(8,128)(2,1)} %payload.1.far_ref), channel_id=1, source_target_pairs={{0,32},{8,40},{16,48},{24,56},{32,64},{40,72},{48,80},{56,88},{64,... | collective-permute-start | bytes 3440648 | tf_op jit(solution)/shard_map/ppermute | solution.py:276
  5.7 36.2 %collective-permute-start.6 = (bf16[560,1024]{1,0:T(8,128)(2,1)}, bf16[560,1024]{1,0:T(8,128)(2,1)S(1)}, u32[]{:S(2)}, u32[]{:S(2)}) collective-permute-start(bf16[560,1024]{1,0:T(8,128)(2,1)} %payload.1.far_ref), channel_id=1, source_target_pairs={{0,120},{8,96},{16,104},{24,112},{32,24},{40,0},{48,8},{56,16},{64... | collective-permute-start | bytes 3440648 | tf_op jit(solution)/shard_map/ppermute | solution.py:276
  10.1 8.8 %collective-permute-start = (bf16[48,1024]{1,0:T(8,128)(2,1)}, bf16[48,1024]{1,0:T(8,128)(2,1)}, u32[]{:S(2)}, u32[]{:S(2)}) collective-permute-start(bf16[48,1024]{1,0:T(8,128)(2,1)} %get-tuple-element.54), channel_id=1, source_target_pairs={{0,1},{1,0},{2,3},{3,2},{4,5},{5,4},{6,7},{7,6},{8,9},{9,8},{10,11... | collective-permute-start | bytes 294920 | tf_op jit(solution)/shard_map/ppermute | solution.py:282
  19.8 9.8 %collective-permute-start.1 = (bf16[2,48,1024]{2,1,0:T(8,128)(2,1)S(1)}, bf16[2,48,1024]{2,1,0:T(8,128)(2,1)S(1)}, u32[]{:S(2)}, u32[]{:S(2)}) collective-permute-start(bf16[2,48,1024]{2,1,0:T(8,128)(2,1)S(1)} %get-tuple-element.59), channel_id=1, source_target_pairs={{0,2},{1,3},{2,4},{3,5},{4,6},{5,7},{6,0},{7,1},{8,10},{9,11},{10,... | collective-permute-start | bytes 589832 | tf_op jit(solution)/shard_map/ppermute | solution.py:279
  22.5 18.4 %collective-permute-start.2 = (bf16[2,48,1024]{2,1,0:T(8,128)(2,1)S(1)}, bf16[2,48,1024]{2,1,0:T(8,128)(2,1)S(1)}, u32[]{:S(2)}, u32[]{:S(2)}) collective-permute-start(bf16[2,48,1024]{2,1,0:T(8,128)(2,1)S(1)} %get-tuple-element.59), channel_id=1, source_target_pairs={{0,4},{1,5},{2,6},{3,7},{4,0},{5,1},{6,2},{7,3},{8,12},{9,13},{10,... | collective-permute-start | bytes 589832 | tf_op jit(solution)/shard_map/ppermute | solution.py:279
  29.6 11.4 %collective-permute-start.3 = (bf16[2,48,1024]{2,1,0:T(8,128)(2,1)S(1)}, bf16[2,48,1024]{2,1,0:T(8,128)(2,1)S(1)}, u32[]{:S(2)}, u32[]{:S(2)}) collective-permute-start(bf16[2,48,1024]{2,1,0:T(8,128)(2,1)S(1)} %get-tuple-element.59), channel_id=1, source_target_pairs={{0,6},{1,7},{2,0},{3,1},{4,2},{5,3},{6,4},{7,5},{8,14},{9,15},{10,... | collective-permute-start | bytes 589832 | tf_op jit(solution)/shard_map/ppermute | solution.py:279
  43.7 29.2 %collective-permute-start.11 = (bf16[560,1024]{1,0:T(8,128)(2,1)}, bf16[560,1024]{1,0:T(8,128)(2,1)S(1)}, u32[]{:S(2)}, u32[]{:S(2)}) collective-permute-start(bf16[560,1024]{1,0:T(8,128)(2,1)} %get-tuple-element.30.refs_1_), channel_id=1, source_target_pairs={{0,32},{8,40},{16,48},{24,56},{32,64},{40,72},{48,80},{56,88},{64,... | collective-permute-start | bytes 3440648 | tf_op jit(solution)/shard_map/ppermute | solution.py:276
  44.1 38.6 %collective-permute-start.12 = (bf16[560,1024]{1,0:T(8,128)(2,1)}, bf16[560,1024]{1,0:T(8,128)(2,1)S(1)}, u32[]{:S(2)}, u32[]{:S(2)}) collective-permute-start(bf16[560,1024]{1,0:T(8,128)(2,1)} %get-tuple-element.31.refs_2_), channel_id=1, source_target_pairs={{0,24},{8,0},{16,8},{24,16},{32,56},{40,32},{48,40},{56,48},{64,88... | collective-permute-start | bytes 3440648 | tf_op jit(solution)/shard_map/ppermute | solution.py:276
  45.7 48.0 %collective-permute-start.10 = (bf16[560,1024]{1,0:T(8,128)(2,1)}, bf16[560,1024]{1,0:T(8,128)(2,1)}, u32[]{:S(2)}, u32[]{:S(2)}) collective-permute-start(bf16[560,1024]{1,0:T(8,128)(2,1)} %get-tuple-element.29.refs_0_), channel_id=1, source_target_pairs={{0,96},{8,104},{16,112},{24,120},{32,0},{40,8},{48,16},{56,24},{64... | collective-permute-start | bytes 3440648 | tf_op jit(solution)/shard_map/ppermute | solution.py:276
  49.6 44.0 %collective-permute-start.13 = (bf16[560,1024]{1,0:T(8,128)(2,1)}, bf16[560,1024]{1,0:T(8,128)(2,1)}, u32[]{:S(2)}, u32[]{:S(2)}) collective-permute-start(bf16[560,1024]{1,0:T(8,128)(2,1)} %get-tuple-element.29.refs_0_), channel_id=1, source_target_pairs={{0,8},{24,0},{32,40},{56,32},{64,72},{88,64},{96,104},{120,96},{1,... | collective-permute-start | bytes 3440648 | tf_op jit(solution)/shard_map/ppermute | solution.py:276
  64.6 19.2 %collective-permute-start.7 = (f32[72,512]{1,0:T(8,128)}, f32[72,512]{1,0:T(8,128)S(1)}, u32[]{:S(2)}, u32[]{:S(2)}) collective-permute-start(f32[72,512]{1,0:T(8,128)} %get-tuple-element.34), channel_id=1, source_target_pairs={{8,0},{16,8},{24,16},{0,24},{40,32},{48,40},{56,48},{32,56},{72,64... | collective-permute-start | bytes 442376 | tf_op jit(solution)/shard_map/ppermute | solution.py:318
  72.9 12.8 %collective-permute-start.8 = (f32[72,512]{1,0:T(8,128)}, f32[72,512]{1,0:T(8,128)S(1)}, u32[]{:S(2)}, u32[]{:S(2)}) collective-permute-start(f32[72,512]{1,0:T(8,128)} %get-tuple-element.35), channel_id=1, source_target_pairs={{32,0},{40,8},{48,16},{56,24},{64,32},{72,40},{80,48},{88,56},{96,... | collective-permute-start | bytes 442376 | tf_op jit(solution)/shard_map/ppermute | solution.py:318
  82.7 10.3 %collective-permute-start.9 = (f32[72,512]{1,0:T(8,128)}, f32[72,512]{1,0:T(8,128)S(1)}, u32[]{:S(2)}, u32[]{:S(2)}) collective-permute-start(f32[72,512]{1,0:T(8,128)} %get-tuple-element.36), channel_id=1, source_target_pairs={{120,0},{96,8},{104,16},{112,24},{24,32},{0,40},{8,48},{16,56},{56... | collective-permute-start | bytes 442376 | tf_op jit(solution)/shard_map/ppermute | solution.py:318
  83.8 25.4 %collective-permute-start.18 = (bf16[560,1024]{1,0:T(8,128)(2,1)}, bf16[560,1024]{1,0:T(8,128)(2,1)S(1)}, u32[]{:S(2)}, u32[]{:S(2)}) collective-permute-start(bf16[560,1024]{1,0:T(8,128)(2,1)} %get-tuple-element.39.refs_3_), channel_id=1, source_target_pairs={{0,8},{8,16},{16,24},{24,0},{32,40},{40,48},{48,56},{56,32},{64,72... | collective-permute-start | bytes 3440648 | tf_op jit(solution)/shard_map/ppermute | solution.py:276
  85.7 23.9 %collective-permute-start.19 = (bf16[560,1024]{1,0:T(8,128)(2,1)}, bf16[560,1024]{1,0:T(8,128)(2,1)S(1)}, u32[]{:S(2)}, u32[]{:S(2)}) collective-permute-start(bf16[560,1024]{1,0:T(8,128)(2,1)} %get-tuple-element.38.refs_1_), channel_id=1, source_target_pairs={{32,0},{40,8},{48,16},{56,24},{64,32},{72,40},{80,48},{88,56},{33,... | collective-permute-start | bytes 3440648 | tf_op jit(solution)/shard_map/ppermute | solution.py:276
  122.0 20.1 %collective-permute-start.22 = (f32[4,72,512]{2,1,0:T(8,128)S(1)}, f32[4,72,512]{2,1,0:T(8,128)S(1)}, u32[]{:S(2)}, u32[]{:S(2)}) collective-permute-start(f32[4,72,512]{2,1,0:T(8,128)S(1)} %slice.65), channel_id=1, source_target_pairs={{0,1},{1,0},{2,3},{3,2},{4,5},{5,4},{6,7},{7,6},{8,9},{9,8},{10,11... | collective-permute-start | bytes 1769480 | tf_op jit(solution)/shard_map/ppermute | solution.py:282
  122.1 20.2 %collective-permute-start.14 = (f32[72,512]{1,0:T(8,128)S(1)}, f32[72,512]{1,0:T(8,128)S(1)}, u32[]{:S(2)}, u32[]{:S(2)}) collective-permute-start(f32[72,512]{1,0:T(8,128)S(1)} %copy-done.14), channel_id=1, source_target_pairs={{104,0},{112,8},{120,16},{96,24},{8,32},{16,40},{24,48},{0,56},{40... | collective-permute-start | bytes 442376 | tf_op jit(solution)/shard_map/ppermute | solution.py:318
  131.0 15.6 %collective-permute-start.15 = (f32[72,512]{1,0:T(8,128)S(1)}, f32[72,512]{1,0:T(8,128)S(1)}, u32[]{:S(2)}, u32[]{:S(2)}) collective-permute-start(f32[72,512]{1,0:T(8,128)S(1)} %copy-done.13), channel_id=1, source_target_pairs={{112,0},{120,8},{96,16},{104,24},{16,32},{24,40},{0,48},{8,56},{48... | collective-permute-start | bytes 442376 | tf_op jit(solution)/shard_map/ppermute | solution.py:318
  131.0 15.7 %collective-permute-start.16 = (f32[72,512]{1,0:T(8,128)S(1)}, f32[72,512]{1,0:T(8,128)S(1)}, u32[]{:S(2)}, u32[]{:S(2)}) collective-permute-start(f32[72,512]{1,0:T(8,128)S(1)} %copy-done.11), channel_id=1, source_target_pairs={{0,16},{8,24},{32,48},{40,56},{64,80},{72,88},{96,112},{104,120},{... | collective-permute-start | bytes 442376 | tf_op jit(solution)/shard_map/ppermute | solution.py:318
  140.8 12.3 %collective-permute-start.17 = (f32[72,512]{1,0:T(8,128)S(1)}, f32[72,512]{1,0:T(8,128)S(1)}, u32[]{:S(2)}, u32[]{:S(2)}) collective-permute-start(f32[72,512]{1,0:T(8,128)S(1)} %copy-done.10), channel_id=1, source_target_pairs={{0,64},{8,72},{16,80},{24,88},{32,96},{40,104},{48,112},{56,120},{... | collective-permute-start | bytes 442376 | tf_op jit(solution)/shard_map/ppermute | solution.py:318
  142.1 11.0 %collective-permute-start.20 = (f32[72,512]{1,0:T(8,128)}, f32[72,512]{1,0:T(8,128)S(1)}, u32[]{:S(2)}, u32[]{:S(2)}) collective-permute-start(f32[72,512]{1,0:T(8,128)} %get-tuple-element.48), channel_id=1, source_target_pairs={{72,0},{80,8},{88,16},{64,24},{104,32},{112,40},{120,48},{96,56},{... | collective-permute-start | bytes 442376 | tf_op jit(solution)/shard_map/ppermute | solution.py:318
  143.0 10.1 %collective-permute-start.21 = (f32[72,512]{1,0:T(8,128)S(1)}, f32[72,512]{1,0:T(8,128)S(1)}, u32[]{:S(2)}, u32[]{:S(2)}) collective-permute-start(f32[72,512]{1,0:T(8,128)S(1)} %copy-done.12), channel_id=1, source_target_pairs={{16,64},{24,72},{0,80},{8,88},{48,96},{56,104},{32,112},{40,120},{... | collective-permute-start | bytes 442376 | tf_op jit(solution)/shard_map/ppermute | solution.py:318
  146.7 8.2 %collective-permute-start.24 = (f32[72,512]{1,0:T(8,128)S(1)}, f32[72,512]{1,0:T(8,128)S(1)}, u32[]{:S(2)}, u32[]{:S(2)}) collective-permute-start(f32[72,512]{1,0:T(8,128)S(1)} %get-tuple-element.57), channel_id=1, source_target_pairs={{0,4},{1,5},{2,6},{3,7},{4,0},{5,1},{6,2},{7,3},{8,12},{9,13},{10,... | collective-permute-start | bytes 442376 | tf_op jit(solution)/shard_map/ppermute | solution.py:279
  (27 other events, 208.5 us)

commit v4 on v3

--- a/solution.py
+++ b/solution.py
@@ -18,6 +18,7 @@
 VROWS = BLOCK + EIGS // 2
 PAYLOAD = VROWS + 16
 ACC = EIGS + 8
+SENT = EIGS + 16
 SCALE = math.sqrt(math.log2(math.e) / math.sqrt(WIDTH))
 COST = 8
 NT = (((1,), (1,)), ((), ()))
@@ -33,12 +34,22 @@
     return pairs
 
 
-def left_half(y, x):
-    return x < SIDE // 2
-
-
 def top_half(y, x):
     return y < SIDE // 2
+
+
+def turn_step(y, x):
+    half = SIDE // 2
+    return (0, half) if (y < half) == (x < half) else (half, 0)
+
+
+def cycle():
+    pairs = []
+    for y in range(SIDE):
+        for x in range(SIDE):
+            dy, dx = turn_step(y, x)
+            pairs.append(((y - dy) % SIDE * SIDE + (x - dx) % SIDE, y * SIDE + x))
+    return pairs
 
 
 STAGES = {
@@ -48,11 +59,15 @@
     "c": ((-1, -1), None),
     "d": ((-1, 1), None),
     "e": ((-1, -2), None),
-    "g": ((0, 2), left_half),
-    "h": ((2, 0), top_half),
-    "f": ((2, 1), None),
+    "m": (None, None),
+    "f": ((-2, -1), None),
     "k": ((2, 2), top_half),
 }
+
+
+def pairs_of(name):
+    moved, keep = STAGES[name]
+    return cycle() if moved is None else shift(*moved, keep)
 
 
 def row_norm(x):
@@ -127,14 +142,14 @@
 def cells_kernel(count, order_ref, flags_ref, x_ref, side_ref, *refs):
     far_refs, refs = refs[:count], refs[count:]
     norm_ref, old_ref, new_ref, refs = refs[0], refs[1], refs[2], refs[3:]
-    far_sums_refs, token_ref, p_ref, column_ref = refs[:count], refs[count], refs[count + 1], refs[count + 2]
+    sent_refs, token_ref, (p_ref, column_ref, far_sums_ref) = refs[:count], refs[count], refs[count + 1 :]
     step = pl.program_id(0)
 
     @pl.when(step == 0)
     def _():
         token_ref[...] = jnp.zeros_like(token_ref)
+        far_sums_ref[...] = jnp.zeros_like(far_sums_ref)
         for at in range(count):
-            far_sums_refs[at][...] = jnp.zeros_like(far_sums_refs[at])
             column_ref[at] = jnp.broadcast_to(side_norms(far_refs[at][BLOCK:PAYLOAD, :]), (128, BLOCK)).T
 
     new_ref[...] = old_ref[...]
@@ -160,7 +175,7 @@
             )
             p_ref[:, to : to + 256] = jnp.exp2(scores * near * far[:, to : to + 256]).astype(jnp.bfloat16)
         part = jnp.dot(side_vectors(side_ref[0, 0]), p_ref[...], preferred_element_type=jnp.float32)
-        far_sums_refs[at][...] += part[0:ACC, :]
+        far_sums_ref[at] += part[0:ACC, :]
         if both:
             part = lax.dot_general(side_vectors(side), p_ref[...], NT, preferred_element_type=jnp.float32)
             new_ref[0] += part[0:ACC, :]
@@ -171,24 +186,32 @@
         pl.when(flag == 2)(functools.partial(backward, at, False))
         pl.when(flag == 3)(functools.partial(backward, at, True))
 
+    @pl.when(step == COLS - 1)
+    def _():
+        for at in range(count):
+            degrees = far_sums_ref[at, EIGS:ACC, :]
+            high = degrees.astype(jnp.bfloat16).astype(jnp.float32)
+            sent = jnp.concatenate([far_sums_ref[at, 0:EIGS, :], high, degrees - high], axis=0)
+            sent_refs[at][...] = sent.astype(jnp.bfloat16)
+
 
 NEAR = lambda g, order, flags: (order[g], 0, 0)
 STEP = lambda g, order, flags: (g, 0, 0)
 WHOLE = lambda g, order, flags: (0, 0)
 X_SPEC = pl.BlockSpec((1, BLOCK, WIDTH), NEAR)
 FAR_SPEC = pl.BlockSpec((PAYLOAD, WIDTH), WHOLE)
-NORM = (pl.BlockSpec((1, BLOCK, 128), STEP), (COLS, BLOCK, 128))
-SUMS = (pl.BlockSpec((1, ACC, BLOCK), STEP), (COLS, ACC, BLOCK))
-PART = (pl.BlockSpec((ACC, BLOCK), WHOLE), (ACC, BLOCK))
-TOKEN = (pl.BlockSpec((8, 128), WHOLE), (8, 128))
+NORM = (pl.BlockSpec((1, BLOCK, 128), STEP), (COLS, BLOCK, 128), jnp.float32)
+SUMS = (pl.BlockSpec((1, ACC, BLOCK), STEP), (COLS, ACC, BLOCK), jnp.float32)
+PART = (pl.BlockSpec((SENT, BLOCK), WHOLE), (SENT, BLOCK), jnp.bfloat16)
+TOKEN = (pl.BlockSpec((8, 128), WHOLE), (8, 128), jnp.float32)
 
 
 def cells_call(kernel, count, ins, outs, scratch, aliases, name, args):
     return pl.pallas_call(
         kernel,
-        out_shape=[jax.ShapeDtypeStruct(shape, jnp.float32) for _, shape in outs],
+        out_shape=[jax.ShapeDtypeStruct(shape, dtype) for _, shape, dtype in outs],
         grid_spec=pltpu.PrefetchScalarGridSpec(
-            num_scalar_prefetch=2, grid=(COLS,), in_specs=ins, out_specs=[spec for spec, _ in outs], scratch_shapes=scratch
+            num_scalar_prefetch=2, grid=(COLS,), in_specs=ins, out_specs=[spec for spec, _, _ in outs], scratch_shapes=scratch
         ),
         input_output_aliases=aliases,
         compiler_params=pltpu.CompilerParams(vmem_limit_bytes=56 << 20),
@@ -214,7 +237,7 @@
     side = pl.BlockSpec((1, 1, PAYLOAD - BLOCK, WIDTH), lambda g, order, flags: (g % SIDE, g // SIDE, 0, 0))
     ins = [X_SPEC, side] + [FAR_SPEC] * count + [NORM[0], SUMS[0]]
     outs = [SUMS] + [PART] * count + [TOKEN]
-    scratch = [SCORES, pltpu.VMEM((count, BLOCK, 128), jnp.float32)]
+    scratch = [SCORES] + [pltpu.VMEM((count, *shape), jnp.float32) for shape in ((BLOCK, 128), (ACC, BLOCK))]
     args = (order, flags, blocks, sides, *fars, norms, sums)
     kernel = functools.partial(cells_kernel, count)
     result = cells_call(kernel, count, ins, outs, scratch, {5 + count: 0}, "cells", args)
@@ -229,8 +252,8 @@
     return pl.pallas_call(
         tie_kernel,
         out_shape=[jax.ShapeDtypeStruct(array.shape, array.dtype) for array in arrays],
-        in_specs=[pl.BlockSpec(memory_space=pl.ANY)] * (len(arrays) + len(tokens)),
-        out_specs=[pl.BlockSpec(memory_space=pl.ANY)] * len(arrays),
+        in_specs=[pl.BlockSpec(memory_space=pltpu.HBM)] * (len(arrays) + len(tokens)),
+        out_specs=[pl.BlockSpec(memory_space=pltpu.HBM)] * len(arrays),
         input_output_aliases={at: at for at in range(len(arrays))},
         name="tie",
     )(*arrays, *tokens)
@@ -243,13 +266,18 @@
     work = jnp.concatenate([gram_ref[...], eye], axis=1)
     pivots = jnp.ones((EIGS, 1), jnp.float32)
     below = rows[:, 0:1]
-    for j in range(EIGS):
-        row = work[j : j + 1, :]
-        pivot = work[j : j + 1, j : j + 1]
-        column = work[:, j : j + 1]
-        pivots = jnp.where(below == j, pivot, pivots)
-        factor = jnp.where(below > j, column / pivot, 0.0)
-        work = work - factor * row
+    for j in range(0, EIGS, 2):
+        row1, row2 = work[j : j + 1, :], work[j + 1 : j + 2, :]
+        first, cross = work[j : j + 1, j : j + 1], work[j : j + 1, j + 1 : j + 2]
+        second = work[j + 1 : j + 2, j + 1 : j + 2]
+        column1, column2 = work[:, j : j + 1], work[:, j + 1 : j + 2]
+        scale = 1.0 / (first * second - cross * cross)
+        ratio = cross / first
+        pivots = jnp.where(below == j, first, jnp.where(below == j + 1, second - cross * ratio, pivots))
+        factor1 = jnp.where(below > j + 1, (column1 * second - column2 * cross) * scale, 0.0)
+        factor1 = jnp.where(below == j + 1, ratio, factor1)
+        factor2 = jnp.where(below > j + 1, (column2 * first - column1 * cross) * scale, 0.0)
+        work = work - (factor1 * row1 + factor2 * row2)
     inverse = work[:, EIGS:] * lax.rsqrt(pivots)
     out_ref[...] = jnp.dot(
         inverse, smoothed_ref[...], precision=lax.Precision.HIGHEST, preferred_element_type=jnp.float32
@@ -285,13 +313,12 @@
     far["a"] = move(far["own"], 0, 1)
     far["b"] = move(far["own"], 1, 0)
     far["c"] = move(far["own"], -1, -1)
-    side = far["own"][BLOCK:PAYLOAD]
-    pair = jnp.stack([side, swap(side)])
-    sides = jnp.stack([pair] + [turn(pair, k) for k in range(1, SIDE)])
     order = jnp.stack([(here_col - CORES * k) % COLS ^ core for core in range(CORES) for k in range(SIDE)])
 
     far_ids, works = [], []
-    for name, ((dy, dx), keep) in STAGES.items():
+    diagonal = (here_y < SIDE // 2) == (here_x < SIDE // 2)
+    for moved, keep in STAGES.values():
+        dy, dx = moved or (jnp.where(diagonal, 0, SIDE // 2), jnp.where(diagonal, SIDE // 2, 0))
         from_row = (here_y - dy) % SIDE * SIDE + (here_x - dx) % SIDE
         far_ids.append(from_row * COLS + here_col)
         works.append(jnp.broadcast_to(True if keep is None else keep(here_y, here_x), (COLS,)))
@@ -312,34 +339,29 @@
         )
 
     def give_back(group, parts):
-        moved = []
+        returned = []
         for name, part in zip(group, parts):
-            (dy, dx), keep = STAGES[name]
-            moved.append(lax.ppermute(part, "row", [(to, source) for source, to in shift(dy, dx, keep)]))
-        return moved
-
+            part = lax.ppermute(part, "row", [(to, source) for source, to in pairs_of(name)]).astype(jnp.float32)
+            degrees = part[EIGS:ACC] + part[ACC:SENT]
+            returned.append(jnp.concatenate([part[0:EIGS], degrees], axis=0))
+        return returned
+
+    side = far["own"][BLOCK:PAYLOAD]
+    pair = jnp.stack([side, swap(side)])
     sums, norms, token = own_cells(order, flags[0], blocks, far["own"])
-    far["a"], far["b"], far["c"] = tie([far["a"], far["b"], far["c"]], token, sides)
+    (pair,) = tie([pair], token)
+    sides = jnp.stack([pair] + [turn(pair, k) for k in range(1, SIDE)])
+    far["a"], far["b"], far["c"] = tie([far["a"], far["b"], far["c"]], sides)
     far["d"] = move(far["a"], -1, 0)
     far["e"] = move(far["c"], 0, -1)
-    far["g"] = move(far["a"], 0, 1, left_half)
-    far["h"] = move(far["b"], 1, 0)
-
-    group = ("a", "b", "c")
-    sums, parts, token = work(group, sums)
-    far["h"], far["e"] = tie([far["h"], far["e"]], token)
-    early = sum(give_back(group, parts))
-    far["f"] = move(far["h"], 0, 1)
+    far["m"] = lax.ppermute(far["own"], "row", cycle())
+    far["f"] = move(far["c"], -1, 0)
     far["k"] = move(far["e"], -1, 0, top_half)
 
-    group = ("d", "e", "g", "h")
-    sums, parts, token = work(group, sums)
-    returned = give_back(group, parts)
-
-    far["f"], far["k"] = tie([far["f"], far["k"]], early[0:8, 0:128])
-    group = ("f", "k")
-    sums, parts, token = work(group, sums)
-    returned = [early] + returned + give_back(group, parts)
+    returned = []
+    for group in (("a", "b", "c"), ("d", "e", "m"), ("f", "k")):
+        sums, parts, token = work(group, sums)
+        returned += give_back(group, parts)
 
     kept = sums[:SIDE] + swap(sums[SIDE:])
     returned += [kept[0]] + [turn(kept[k], SIDE - k) for k in range(1, SIDE)]

time: 195 us -> 231 us (1.18)
  waiting for transfers between devices: 42.7 us -> 94.9 us
  local copies, waits for them, and re-layouts: 16.4 us -> 8.05 us
  starting transfers between devices: 75.2 us -> 68 us
  other arithmetic: 6.79 us -> 4.36 us
    ppermute x9, waiting for transfers between devices: 12.5 us -> 42.5 us  [the longest x8 42.5 us: give_back(): lax.ppermute(part, 'row', [(to, source) for source, to in pairs_of(name)])]
    ppermute x9, waiting for transfers between devices: 13.5 us -> 28.7 us  [turn(): lax.ppermute(array, 'col', [(i, (i + by * CORES) % COLS) for i in range(C...]
    ppermute x9, starting transfers between devices: 38.2 us -> 27.1 us  [the longest x8 24.7 us: give_back(): lax.ppermute(part, 'row', [(to, source) for source, to in pairs_of(name)])]
    ppermute x15 -> x13, waiting for transfers between devices: 15.5 us -> 22.5 us  [move(): return lax.ppermute(array, 'row', shift(dy, dx, keep))]
    ppermute x15 -> x13, starting transfers between devices: 25.7 us -> 30.2 us  [move(): return lax.ppermute(array, 'row', shift(dy, dx, keep))]
    unnamed x31 -> x25, local copies, waits for them, and re-layouts: 5.32 us -> 2.61 us
  transfers between devices with their start and end apart: 36 -> 34, of which waited for: 20 -> 19; matrix products, arithmetic and copies ran while one was open for 8% -> 3% of each run, Pallas kernels for 17% -> 14%
where the time goes in v4:
time: 231 us; the launch traced here: 229 us
  waiting for transfers between devices  94.9 us (41%)
  starting transfers between devices  68 us (29%)
  Pallas kernels  52.6 us (23%)
  local copies, waits for them, and re-layouts  8.05 us (3%)
  other arithmetic  4.36 us (2%)
    ppermute x8, waiting for transfers between devices, give_back(): lax.ppermute(part, 'row', [(to, source) for source, to in pairs_of(name)])  42.5 us
    pallas_call x4, Pallas kernels, cells_call(): pl.pallas_call(kernel, out_shape=[jax.ShapeDtypeStruct(shape, dtype) for...  40.1 us
    ppermute x13, starting transfers between devices, move(): return lax.ppermute(array, 'row', shift(dy, dx, keep))  30.2 us
    ppermute x9, waiting for transfers between devices, turn(): lax.ppermute(array, 'col', [(i, (i + by * CORES) % COLS) for i in range(C...  28.7 us
    ppermute x8, starting transfers between devices, give_back(): lax.ppermute(part, 'row', [(to, source) for source, to in pairs_of(name)])  24.7 us
    ppermute x13, waiting for transfers between devices, move(): return lax.ppermute(array, 'row', shift(dy, dx, keep))  22.5 us
    ppermute x9, starting transfers between devices, turn(): lax.ppermute(array, 'col', [(i, (i + by * CORES) % COLS) for i in range(C...  10.4 us
    pallas_call x1, Pallas kernels, solve(): pl.pallas_call(solve_kernel, out_shape=jax.ShapeDtypeStruct(smoothed.shap...  9.84 us
  transfers between devices with their start and end apart: 34, of which 19 were waited for; matrix products, arithmetic and copies ran while one was open for 3% of the time, Pallas kernels for 14%

profile of v4, /device:TPU:0, one launch (start us, length us, event | category | flops | bytes accessed | tf_op | source)
XLA Modules:
  0.0 229.1 jit_solution(5824181047175494211)
XLA Ops:
  2.6 5.3 %collective-permute-start.6 = (bf16[560,1024]{1,0:T(8,128)(2,1)}, bf16[560,1024]{1,0:T(8,128)(2,1)S(1)}, u32[]{:S(2)}, u32[]{:S(2)}) collective-permute-start(bf16[560,1024]{1,0:T(8,128)(2,1)} %payload.1.far_ref), channel_id=1, source_target_pairs={{0,120},{8,96},{16,104},{24,112},{32,24},{40,0},{48,8},{56,16},{64... | collective-permute-start | bytes 3440648 | tf_op jit(solution)/shard_map/ppermute | solution.py:304
  11.2 9.2 %cells_own.1 = (f32[8,72,512]{2,1,0:T(8,128)}, f32[8,512,128]{2,1,0:T(8,128)}, f32[8,128]{1,0:T(8,128)}) custom-call(s32[8]{0:T(128)} %copy-done.7, s32[8]{0:T(128)} %slice_reduce_fusion.flags_ref, bf16[8,512,1024]{2,1,0:T(8,128)(2,1)} %bitcast.54, bf16[560,1024]{1,0:T(8,128)(2,1)} %payload.1.far_ref), custom_call_target="tpu_custom_call" | custom-call | flops 2147483648 | bytes 13631488 | tf_op jit(solution)/shard_map/cells_own/pallas_call | solution.py:210
  21.2 5.1 %collective-permute-start.3 = (bf16[2,48,1024]{2,1,0:T(8,128)(2,1)}, bf16[2,48,1024]{2,1,0:T(8,128)(2,1)S(1)}, u32[]{:S(2)}, u32[]{:S(2)}) collective-permute-start(bf16[2,48,1024]{2,1,0:T(8,128)(2,1)} %tie.2), channel_id=1, source_target_pairs={{0,6},{1,7},{2,0},{3,1},{4,2},{5,3},{6,4},{7,5},{8,14},{9,15},{10,... | collective-permute-start | bytes 589832 | tf_op jit(solution)/shard_map/ppermute | solution.py:307
  26.3 8.8 %collective-permute-done.3 = bf16[2,48,1024]{2,1,0:T(8,128)(2,1)S(1)} collective-permute-done((bf16[2,48,1024]{2,1,0:T(8,128)(2,1)}, bf16[2,48,1024]{2,1,0:T(8,128)(2,1)S(1)}, u32[]{:S(2)}, u32[]{:S(2)}) %collective-permute-start.3) | collective-permute-done | bytes 196640 | tf_op jit(solution)/shard_map/ppermute | solution.py:307
  35.1 8.1 %collective-permute-done.1 = bf16[2,48,1024]{2,1,0:T(8,128)(2,1)S(1)} collective-permute-done((bf16[2,48,1024]{2,1,0:T(8,128)(2,1)}, bf16[2,48,1024]{2,1,0:T(8,128)(2,1)S(1)}, u32[]{:S(2)}, u32[]{:S(2)}) %collective-permute-start.1) | collective-permute-done | bytes 196640 | tf_op jit(solution)/shard_map/ppermute | solution.py:307
  46.5 3.1 %collective-permute-start.11 = (bf16[560,1024]{1,0:T(8,128)(2,1)}, bf16[560,1024]{1,0:T(8,128)(2,1)}, u32[]{:S(2)}, u32[]{:S(2)}) collective-permute-start(bf16[560,1024]{1,0:T(8,128)(2,1)} %get-tuple-element.25.refs_2_), channel_id=1, source_target_pairs={{0,24},{8,0},{16,8},{24,16},{32,56},{40,32},{48,40},{56,48},{64,88... | collective-permute-start | bytes 3440648 | tf_op jit(solution)/shard_map/ppermute | solution.py:304
  52.0 3.0 %collective-permute-start.10 = (bf16[560,1024]{1,0:T(8,128)(2,1)}, bf16[560,1024]{1,0:T(8,128)(2,1)}, u32[]{:S(2)}, u32[]{:S(2)}) collective-permute-start(bf16[560,1024]{1,0:T(8,128)(2,1)} %get-tuple-element.23.refs_0_), channel_id=1, source_target_pairs={{0,96},{8,104},{16,112},{24,120},{32,0},{40,8},{48,16},{56,24},{64... | collective-permute-start | bytes 3440648 | tf_op jit(solution)/shard_map/ppermute | solution.py:304
  55.7 12.2 %cells.3 = (f32[8,72,512]{2,1,0:T(8,128)}, bf16[80,512]{1,0:T(8,128)(2,1)}, bf16[80,512]{1,0:T(8,128)(2,1)}, bf16[80,512]{1,0:T(8,128)(2,1)}, f32[8,128]{1,0:T(8,128)}) custom-call(s32[8]{0:T(128)} %copy-done.7, s32[24]{0:T(128)} %reshape.306.flags_ref, bf16[8,512,1024]{2,1,0:T(8,128)(2,1)} %bitcast.55, ...), custom_call_target="tpu_custom_call", output_to_operand_aliasing={{0}: (8, {})} | custom-call | flops 6442450944 | bytes 15728640 | tf_op jit(solution)/shard_map/cells/pallas_call | solution.py:210
  68.0 6.4 %collective-permute-start.8 = (bf16[80,512]{1,0:T(8,128)(2,1)}, bf16[80,512]{1,0:T(8,128)(2,1)S(1)}, u32[]{:S(2)}, u32[]{:S(2)}) collective-permute-start(bf16[80,512]{1,0:T(8,128)(2,1)} %get-tuple-element.29), channel_id=1, source_target_pairs={{32,0},{40,8},{48,16},{56,24},{64,32},{72,40},{80,48},{88,56},{96,... | collective-permute-start | bytes 245768 | tf_op jit(solution)/shard_map/ppermute | solution.py:344
  75.8 3.0 %collective-permute-done.9 = bf16[80,512]{1,0:T(8,128)(2,1)S(1)} collective-permute-done((bf16[80,512]{1,0:T(8,128)(2,1)}, bf16[80,512]{1,0:T(8,128)(2,1)S(1)}, u32[]{:S(2)}, u32[]{:S(2)}) %collective-permute-start.9) | collective-permute-done | bytes 81952 | tf_op jit(solution)/shard_map/ppermute | solution.py:344
  81.1 27.0 %collective-permute-done.8 = bf16[80,512]{1,0:T(8,128)(2,1)S(1)} collective-permute-done((bf16[80,512]{1,0:T(8,128)(2,1)}, bf16[80,512]{1,0:T(8,128)(2,1)S(1)}, u32[]{:S(2)}, u32[]{:S(2)}) %collective-permute-start.8) | collective-permute-done | bytes 81952 | tf_op jit(solution)/shard_map/ppermute | solution.py:344
  109.7 3.1 %collective-permute-done.7 = bf16[80,512]{1,0:T(8,128)(2,1)S(1)} collective-permute-done((bf16[80,512]{1,0:T(8,128)(2,1)}, bf16[80,512]{1,0:T(8,128)(2,1)S(1)}, u32[]{:S(2)}, u32[]{:S(2)}) %collective-permute-start.7) | collective-permute-done | bytes 81952 | tf_op jit(solution)/shard_map/ppermute | solution.py:344
  112.8 9.6 %cells.4 = (f32[8,72,512]{2,1,0:T(8,128)}, bf16[80,512]{1,0:T(8,128)(2,1)}, bf16[80,512]{1,0:T(8,128)(2,1)}, bf16[80,512]{1,0:T(8,128)(2,1)}, f32[8,128]{1,0:T(8,128)}) custom-call(s32[8]{0:T(128)} %copy-done.7, s32[24]{0:T(128)} %reshape.308.flags_ref, bf16[8,512,1024]{2,1,0:T(8,128)(2,1)} %bitcast.56, ...), custom_call_target="tpu_custom_call", output_to_operand_aliasing={{0}: (8, {})} | custom-call | flops 6442450944 | bytes 15728640 | tf_op jit(solution)/shard_map/cells/pallas_call | solution.py:210
  122.4 10.2 %collective-permute-start.13 = (bf16[80,512]{1,0:T(8,128)(2,1)}, bf16[80,512]{1,0:T(8,128)(2,1)S(1)}, u32[]{:S(2)}, u32[]{:S(2)}) collective-permute-start(bf16[80,512]{1,0:T(8,128)(2,1)} %get-tuple-element.32), channel_id=1, source_target_pairs={{104,0},{112,8},{120,16},{96,24},{8,32},{16,40},{24,48},{0,56},{40... | collective-permute-start | bytes 245768 | tf_op jit(solution)/shard_map/ppermute | solution.py:344
  135.3 3.7 %collective-permute-start.15 = (bf16[80,512]{1,0:T(8,128)(2,1)}, bf16[80,512]{1,0:T(8,128)(2,1)S(1)}, u32[]{:S(2)}, u32[]{:S(2)}) collective-permute-start(bf16[80,512]{1,0:T(8,128)(2,1)} %get-tuple-element.34), channel_id=1, source_target_pairs={{0,16},{8,24},{16,80},{24,88},{32,48},{40,56},{48,112},{56,120},{6... | collective-permute-start | bytes 245768 | tf_op jit(solution)/shard_map/ppermute | solution.py:344
  141.9 12.8 %collective-permute-done.17.refs_1_ = bf16[560,1024]{1,0:T(8,128)(2,1)S(1)} collective-permute-done((bf16[560,1024]{1,0:T(8,128)(2,1)}, bf16[560,1024]{1,0:T(8,128)(2,1)S(1)}, u32[]{:S(2)}, u32[]{:S(2)}) %collective-permute-start.17) | collective-permute-done | bytes 1146912 | tf_op jit(solution)/shard_map/ppermute | solution.py:304
  155.7 9.1 %cells.5 = (f32[8,72,512]{2,1,0:T(8,128)}, bf16[80,512]{1,0:T(8,128)(2,1)}, bf16[80,512]{1,0:T(8,128)(2,1)}, f32[8,128]{1,0:T(8,128)}) custom-call(s32[8]{0:T(128)} %copy-done.7, s32[16]{0:T(128)} %reshape.309.flags_ref, bf16[8,512,1024]{2,1,0:T(8,128)(2,1)} %bitcast.57, ...), custom_call_target="tpu_custom_call", output_to_operand_aliasing={{0}: (7, {})} | custom-call | flops 4294967296 | bytes 14680064 | tf_op jit(solution)/shard_map/cells/pallas_call | solution.py:210
  170.6 4.0 %collective-permute-done.18 = bf16[80,512]{1,0:T(8,128)(2,1)S(1)} collective-permute-done((bf16[80,512]{1,0:T(8,128)(2,1)S(1)}, bf16[80,512]{1,0:T(8,128)(2,1)S(1)}, u32[]{:S(2)}, u32[]{:S(2)}) %collective-permute-start.18) | collective-permute-done | bytes 81952 | tf_op jit(solution)/shard_map/ppermute | solution.py:344
  180.3 5.2 %collective-permute-done.23 = f32[72,512]{1,0:T(8,128)S(1)} collective-permute-done((f32[72,512]{1,0:T(8,128)S(1)}, f32[72,512]{1,0:T(8,128)S(1)}, u32[]{:S(2)}, u32[]{:S(2)}) %collective-permute-start.23) | collective-permute-done | bytes 147488 | tf_op jit(solution)/shard_map/ppermute | solution.py:307
  193.9 4.3 %collective-permute-start.29 = (f32[64,64]{1,0:T(8,128)S(1)}, f32[64,64]{1,0:T(8,128)S(1)}, u32[]{:S(2)}, u32[]{:S(2)}) collective-permute-start(f32[64,64]{1,0:T(8,128)S(1)} %add_add_fusion.2), channel_id=1, source_target_pairs={{0,16},{8,24},{16,0},{24,8},{32,48},{40,56},{48,32},{56,40},{64,80... | collective-permute-start | bytes 49160 | tf_op jit(solution)/shard_map/ppermute | solution.py:304
  200.1 3.2 %collective-permute-done.28 = f32[64,64]{1,0:T(8,128)S(1)} collective-permute-done((f32[64,64]{1,0:T(8,128)S(1)}, f32[64,64]{1,0:T(8,128)S(1)}, u32[]{:S(2)}, u32[]{:S(2)}) %collective-permute-start.28) | collective-permute-done | bytes 16416 | tf_op jit(solution)/shard_map/ppermute | solution.py:304
  203.4 9.8 %collective-permute-start.33 = (f32[64,64]{1,0:T(8,128)S(1)}, f32[64,64]{1,0:T(8,128)S(1)}, u32[]{:S(2)}, u32[]{:S(2)}) collective-permute-start(f32[64,64]{1,0:T(8,128)S(1)} %add_add_fusion.1), channel_id=1, source_target_pairs={{0,96},{8,104},{16,112},{24,120},{32,0},{40,8},{48,16},{56,24},{64... | collective-permute-start | bytes 49160 | tf_op jit(solution)/shard_map/ppermute | solution.py:304
  214.8 3.9 %collective-permute-done.32 = f32[64,64]{1,0:T(8,128)S(1)} collective-permute-done((f32[64,64]{1,0:T(8,128)S(1)}, f32[64,64]{1,0:T(8,128)S(1)}, u32[]{:S(2)}, u32[]{:S(2)}) %collective-permute-start.32) | collective-permute-done | bytes 16416 | tf_op jit(solution)/shard_map/ppermute | solution.py:304
  219.3 9.8 %solve.1 = f32[64,512]{1,0:T(8,128)} custom-call(f32[64,64]{1,0:T(8,128)} %add_add_fusion.gram_ref, f32[64,512]{1,0:T(8,128)} %copy-done.1), custom_call_target="tpu_custom_call" | custom-call | tf_op jit(solution)/shard_map/solve/pallas_call | solution.py:288
  (138 shorter events, 48.4 us)
Async XLA Ops:
  2.6 42.5 %collective-permute-start.6 = (bf16[560,1024]{1,0:T(8,128)(2,1)}, bf16[560,1024]{1,0:T(8,128)(2,1)S(1)}, u32[]{:S(2)}, u32[]{:S(2)}) collective-permute-start(bf16[560,1024]{1,0:T(8,128)(2,1)} %payload.1.far_ref), channel_id=1, source_target_pairs={{0,120},{8,96},{16,104},{24,112},{32,24},{40,0},{48,8},{56,16},{64... | collective-permute-start | bytes 3440648 | tf_op jit(solution)/shard_map/ppermute | solution.py:304
  7.9 37.2 %collective-permute-start.5 = (bf16[560,1024]{1,0:T(8,128)(2,1)}, bf16[560,1024]{1,0:T(8,128)(2,1)S(1)}, u32[]{:S(2)}, u32[]{:S(2)}) collective-permute-start(bf16[560,1024]{1,0:T(8,128)(2,1)} %payload.1.far_ref), channel_id=1, source_target_pairs={{0,32},{8,40},{16,48},{24,56},{32,64},{40,72},{48,80},{56,88},{64,... | collective-permute-start | bytes 3440648 | tf_op jit(solution)/shard_map/ppermute | solution.py:304
  7.9 37.2 %collective-permute-start.4 = (bf16[560,1024]{1,0:T(8,128)(2,1)}, bf16[560,1024]{1,0:T(8,128)(2,1)}, u32[]{:S(2)}, u32[]{:S(2)}) collective-permute-start(bf16[560,1024]{1,0:T(8,128)(2,1)} %payload.1.far_ref), channel_id=1, source_target_pairs={{0,8},{8,16},{16,24},{24,0},{32,40},{40,48},{48,56},{56,32},{64,72... | collective-permute-start | bytes 3440648 | tf_op jit(solution)/shard_map/ppermute | solution.py:304
  8.9 11.6 %collective-permute-start = (bf16[48,1024]{1,0:T(8,128)(2,1)S(1)}, bf16[48,1024]{1,0:T(8,128)(2,1)S(1)}, u32[]{:S(2)}, u32[]{:S(2)}) collective-permute-start(bf16[48,1024]{1,0:T(8,128)(2,1)S(1)} %get-tuple-element.42), channel_id=1, source_target_pairs={{0,1},{1,0},{2,3},{3,2},{4,5},{5,4},{6,7},{7,6},{8,9},{9,8},{10,11... | collective-permute-start | bytes 294920 | tf_op jit(solution)/shard_map/ppermute | solution.py:310
  21.2 13.9 %collective-permute-start.3 = (bf16[2,48,1024]{2,1,0:T(8,128)(2,1)}, bf16[2,48,1024]{2,1,0:T(8,128)(2,1)S(1)}, u32[]{:S(2)}, u32[]{:S(2)}) collective-permute-start(bf16[2,48,1024]{2,1,0:T(8,128)(2,1)} %tie.2), channel_id=1, source_target_pairs={{0,6},{1,7},{2,0},{3,1},{4,2},{5,3},{6,4},{7,5},{8,14},{9,15},{10,... | collective-permute-start | bytes 589832 | tf_op jit(solution)/shard_map/ppermute | solution.py:307
  26.3 8.8 %collective-permute-start.2 = (bf16[2,48,1024]{2,1,0:T(8,128)(2,1)}, bf16[2,48,1024]{2,1,0:T(8,128)(2,1)S(1)}, u32[]{:S(2)}, u32[]{:S(2)}) collective-permute-start(bf16[2,48,1024]{2,1,0:T(8,128)(2,1)} %tie.2), channel_id=1, source_target_pairs={{0,4},{1,5},{2,6},{3,7},{4,0},{5,1},{6,2},{7,3},{8,12},{9,13},{10,... | collective-permute-start | bytes 589832 | tf_op jit(solution)/shard_map/ppermute | solution.py:307
  35.1 8.1 %collective-permute-start.1 = (bf16[2,48,1024]{2,1,0:T(8,128)(2,1)}, bf16[2,48,1024]{2,1,0:T(8,128)(2,1)S(1)}, u32[]{:S(2)}, u32[]{:S(2)}) collective-permute-start(bf16[2,48,1024]{2,1,0:T(8,128)(2,1)} %tie.2), channel_id=1, source_target_pairs={{0,2},{1,3},{2,4},{3,5},{4,6},{5,7},{6,0},{7,1},{8,10},{9,11},{10,... | collective-permute-start | bytes 589832 | tf_op jit(solution)/shard_map/ppermute | solution.py:307
  46.5 61.6 %collective-permute-start.11 = (bf16[560,1024]{1,0:T(8,128)(2,1)}, bf16[560,1024]{1,0:T(8,128)(2,1)}, u32[]{:S(2)}, u32[]{:S(2)}) collective-permute-start(bf16[560,1024]{1,0:T(8,128)(2,1)} %get-tuple-element.25.refs_2_), channel_id=1, source_target_pairs={{0,24},{8,0},{16,8},{24,16},{32,56},{40,32},{48,40},{56,48},{64,88... | collective-permute-start | bytes 3440648 | tf_op jit(solution)/shard_map/ppermute | solution.py:304
  49.6 63.2 %collective-permute-start.12 = (bf16[560,1024]{1,0:T(8,128)(2,1)S(1)}, bf16[560,1024]{1,0:T(8,128)(2,1)}, u32[]{:S(2)}, u32[]{:S(2)}) collective-permute-start(bf16[560,1024]{1,0:T(8,128)(2,1)S(1)} %copy-done), channel_id=1, source_target_pairs={{16,0},{24,8},{80,16},{88,24},{48,32},{56,40},{112,48},{120,56},{0... | collective-permute-start | bytes 3440648 | tf_op jit(solution)/shard_map/ppermute | solution.py:357
  52.0 60.8 %collective-permute-start.10 = (bf16[560,1024]{1,0:T(8,128)(2,1)}, bf16[560,1024]{1,0:T(8,128)(2,1)}, u32[]{:S(2)}, u32[]{:S(2)}) collective-permute-start(bf16[560,1024]{1,0:T(8,128)(2,1)} %get-tuple-element.23.refs_0_), channel_id=1, source_target_pairs={{0,96},{8,104},{16,112},{24,120},{32,0},{40,8},{48,16},{56,24},{64... | collective-permute-start | bytes 3440648 | tf_op jit(solution)/shard_map/ppermute | solution.py:304
  67.9 11.0 %collective-permute-start.9 = (bf16[80,512]{1,0:T(8,128)(2,1)}, bf16[80,512]{1,0:T(8,128)(2,1)S(1)}, u32[]{:S(2)}, u32[]{:S(2)}) collective-permute-start(bf16[80,512]{1,0:T(8,128)(2,1)} %get-tuple-element.30), channel_id=1, source_target_pairs={{120,0},{96,8},{104,16},{112,24},{24,32},{0,40},{8,48},{16,56},{56... | collective-permute-start | bytes 245768 | tf_op jit(solution)/shard_map/ppermute | solution.py:344
  68.0 40.1 %collective-permute-start.8 = (bf16[80,512]{1,0:T(8,128)(2,1)}, bf16[80,512]{1,0:T(8,128)(2,1)S(1)}, u32[]{:S(2)}, u32[]{:S(2)}) collective-permute-start(bf16[80,512]{1,0:T(8,128)(2,1)} %get-tuple-element.29), channel_id=1, source_target_pairs={{32,0},{40,8},{48,16},{56,24},{64,32},{72,40},{80,48},{88,56},{96,... | collective-permute-start | bytes 245768 | tf_op jit(solution)/shard_map/ppermute | solution.py:344
  78.9 63.0 %collective-permute-start.16 = (bf16[560,1024]{1,0:T(8,128)(2,1)S(1)}, bf16[560,1024]{1,0:T(8,128)(2,1)S(1)}, u32[]{:S(2)}, u32[]{:S(2)}) collective-permute-start(bf16[560,1024]{1,0:T(8,128)(2,1)S(1)} %copy-done.4), channel_id=1, source_target_pairs={{0,96},{8,104},{16,112},{24,120},{32,0},{40,8},{48,16},{56,24},{64... | collective-permute-start | bytes 3440648 | tf_op jit(solution)/shard_map/ppermute | solution.py:304
  108.2 46.5 %collective-permute-start.17 = (bf16[560,1024]{1,0:T(8,128)(2,1)}, bf16[560,1024]{1,0:T(8,128)(2,1)S(1)}, u32[]{:S(2)}, u32[]{:S(2)}) collective-permute-start(bf16[560,1024]{1,0:T(8,128)(2,1)} %collective-permute-done.11.refs_1_), channel_id=1, source_target_pairs={{32,0},{40,8},{48,16},{56,24},{64,32},{72,40},{80,48},{88,56},{33,... | collective-permute-start | bytes 3440648 | tf_op jit(solution)/shard_map/ppermute | solution.py:304
  122.4 19.4 %collective-permute-start.13 = (bf16[80,512]{1,0:T(8,128)(2,1)}, bf16[80,512]{1,0:T(8,128)(2,1)S(1)}, u32[]{:S(2)}, u32[]{:S(2)}) collective-permute-start(bf16[80,512]{1,0:T(8,128)(2,1)} %get-tuple-element.32), channel_id=1, source_target_pairs={{104,0},{112,8},{120,16},{96,24},{8,32},{16,40},{24,48},{0,56},{40... | collective-permute-start | bytes 245768 | tf_op jit(solution)/shard_map/ppermute | solution.py:344
  132.6 9.2 %collective-permute-start.14 = (bf16[80,512]{1,0:T(8,128)(2,1)}, bf16[80,512]{1,0:T(8,128)(2,1)S(1)}, u32[]{:S(2)}, u32[]{:S(2)}) collective-permute-start(bf16[80,512]{1,0:T(8,128)(2,1)} %get-tuple-element.33), channel_id=1, source_target_pairs={{112,0},{120,8},{96,16},{104,24},{16,32},{24,40},{0,48},{8,56},{48... | collective-permute-start | bytes 245768 | tf_op jit(solution)/shard_map/ppermute | solution.py:344
  135.3 6.5 %collective-permute-start.15 = (bf16[80,512]{1,0:T(8,128)(2,1)}, bf16[80,512]{1,0:T(8,128)(2,1)S(1)}, u32[]{:S(2)}, u32[]{:S(2)}) collective-permute-start(bf16[80,512]{1,0:T(8,128)(2,1)} %get-tuple-element.34), channel_id=1, source_target_pairs={{0,16},{8,24},{16,80},{24,88},{32,48},{40,56},{48,112},{56,120},{6... | collective-permute-start | bytes 245768 | tf_op jit(solution)/shard_map/ppermute | solution.py:344
  166.0 8.6 %collective-permute-start.20 = (f32[4,72,512]{2,1,0:T(8,128)S(1)}, f32[4,72,512]{2,1,0:T(8,128)S(1)}, u32[]{:S(2)}, u32[]{:S(2)}) collective-permute-start(f32[4,72,512]{2,1,0:T(8,128)S(1)} %slice.157), channel_id=1, source_target_pairs={{0,1},{1,0},{2,3},{3,2},{4,5},{5,4},{6,7},{7,6},{8,9},{9,8},{10,11... | collective-permute-start | bytes 1769480 | tf_op jit(solution)/shard_map/ppermute | solution.py:310
  166.1 8.4 %collective-permute-start.18 = (bf16[80,512]{1,0:T(8,128)(2,1)S(1)}, bf16[80,512]{1,0:T(8,128)(2,1)S(1)}, u32[]{:S(2)}, u32[]{:S(2)}) collective-permute-start(bf16[80,512]{1,0:T(8,128)(2,1)S(1)} %copy-done.10), channel_id=1, source_target_pairs={{88,0},{64,8},{72,16},{80,24},{120,32},{96,40},{104,48},{112,56},{... | collective-permute-start | bytes 245768 | tf_op jit(solution)/shard_map/ppermute | solution.py:344
  176.3 9.2 %collective-permute-start.23 = (f32[72,512]{1,0:T(8,128)S(1)}, f32[72,512]{1,0:T(8,128)S(1)}, u32[]{:S(2)}, u32[]{:S(2)}) collective-permute-start(f32[72,512]{1,0:T(8,128)S(1)} %get-tuple-element.44), channel_id=1, source_target_pairs={{0,2},{1,3},{2,4},{3,5},{4,6},{5,7},{6,0},{7,1},{8,10},{9,11},{10,... | collective-permute-start | bytes 442376 | tf_op jit(solution)/shard_map/ppermute | solution.py:307
  176.9 8.6 %collective-permute-start.22 = (f32[72,512]{1,0:T(8,128)S(1)}, f32[72,512]{1,0:T(8,128)S(1)}, u32[]{:S(2)}, u32[]{:S(2)}) collective-permute-start(f32[72,512]{1,0:T(8,128)S(1)} %get-tuple-element.45), channel_id=1, source_target_pairs={{0,4},{1,5},{2,6},{3,7},{4,0},{5,1},{6,2},{7,3},{8,12},{9,13},{10,... | collective-permute-start | bytes 442376 | tf_op jit(solution)/shard_map/ppermute | solution.py:307
  188.2 5.6 %collective-permute-start.25 = (f32[64,64]{1,0:T(8,128)S(1)}, f32[64,64]{1,0:T(8,128)S(1)}, u32[]{:S(2)}, u32[]{:S(2)}) collective-permute-start(f32[64,64]{1,0:T(8,128)S(1)} %add.350), channel_id=1, source_target_pairs={{0,2},{1,3},{2,4},{3,5},{4,6},{5,7},{6,0},{7,1},{8,10},{9,11},{10,... | collective-permute-start | bytes 49160 | tf_op jit(solution)/shard_map/ppermute | solution.py:307
  193.9 6.2 %collective-permute-start.29 = (f32[64,64]{1,0:T(8,128)S(1)}, f32[64,64]{1,0:T(8,128)S(1)}, u32[]{:S(2)}, u32[]{:S(2)}) collective-permute-start(f32[64,64]{1,0:T(8,128)S(1)} %add_add_fusion.2), channel_id=1, source_target_pairs={{0,16},{8,24},{16,0},{24,8},{32,48},{40,56},{48,32},{56,40},{64,80... | collective-permute-start | bytes 49160 | tf_op jit(solution)/shard_map/ppermute | solution.py:304
  203.4 11.4 %collective-permute-start.33 = (f32[64,64]{1,0:T(8,128)S(1)}, f32[64,64]{1,0:T(8,128)S(1)}, u32[]{:S(2)}, u32[]{:S(2)}) collective-permute-start(f32[64,64]{1,0:T(8,128)S(1)} %add_add_fusion.1), channel_id=1, source_target_pairs={{0,96},{8,104},{16,112},{24,120},{32,0},{40,8},{48,16},{56,24},{64... | collective-permute-start | bytes 49160 | tf_op jit(solution)/shard_map/ppermute | solution.py:304
  (22 other events, 145.5 us)

commit v5 on v4

--- a/solution.py
+++ b/solution.py
@@ -34,22 +34,12 @@
     return pairs
 
 
+def left_half(y, x):
+    return x < SIDE // 2
+
+
 def top_half(y, x):
     return y < SIDE // 2
-
-
-def turn_step(y, x):
-    half = SIDE // 2
-    return (0, half) if (y < half) == (x < half) else (half, 0)
-
-
-def cycle():
-    pairs = []
-    for y in range(SIDE):
-        for x in range(SIDE):
-            dy, dx = turn_step(y, x)
-            pairs.append(((y - dy) % SIDE * SIDE + (x - dx) % SIDE, y * SIDE + x))
-    return pairs
 
 
 STAGES = {
@@ -59,15 +49,11 @@
     "c": ((-1, -1), None),
     "d": ((-1, 1), None),
     "e": ((-1, -2), None),
-    "m": (None, None),
-    "f": ((-2, -1), None),
+    "g": ((0, 2), left_half),
+    "h": ((2, 0), top_half),
+    "f": ((2, 1), None),
     "k": ((2, 2), top_half),
 }
-
-
-def pairs_of(name):
-    moved, keep = STAGES[name]
-    return cycle() if moved is None else shift(*moved, keep)
 
 
 def row_norm(x):
@@ -120,11 +106,13 @@
     return jnp.concatenate([columns, columns], axis=1)
 
 
-def own_kernel(order_ref, flags_ref, x_ref, far_ref, new_ref, norm_ref, token_ref, p_ref):
+def own_kernel(order_ref, flags_ref, x_ref, far_ref, new_ref, norm_ref, row_ref, token_ref, p_ref):
     step = pl.program_id(0)
     new_ref[...] = jnp.zeros_like(new_ref)
     token_ref[...] = jnp.zeros_like(token_ref)
-    norm_ref[0] = jnp.broadcast_to(row_norm(x_ref[0].astype(jnp.float32)) * SCALE, (BLOCK, 128))
+    norms = jnp.broadcast_to(row_norm(x_ref[0].astype(jnp.float32)) * SCALE, (BLOCK, 128))
+    norm_ref[0] = norms
+    row_ref[0] = norms.T[0:8, :]
 
     @pl.when(flags_ref[step] > 0)
     def _():
@@ -139,9 +127,9 @@
         new_ref[0] = part[0:ACC, :]
 
 
-def cells_kernel(count, order_ref, flags_ref, x_ref, side_ref, *refs):
+def cells_kernel(count, order_ref, flags_ref, x_ref, near_v_ref, *refs):
     far_refs, refs = refs[:count], refs[count:]
-    norm_ref, old_ref, new_ref, refs = refs[0], refs[1], refs[2], refs[3:]
+    norm_ref, row_ref, old_ref, new_ref, refs = refs[0], refs[1], refs[2], refs[3], refs[4:]
     sent_refs, token_ref, (p_ref, column_ref, far_sums_ref) = refs[:count], refs[count], refs[count + 1 :]
     step = pl.program_id(0)
 
@@ -156,7 +144,7 @@
 
     def forward_only(at):
         far_ref = far_refs[at]
-        near, far = side_norms(side_ref[0, 0]), double(column_ref[at])
+        near, far = row_ref[0, 0:1, :], double(column_ref[at])
         for to in range(0, BLOCK, 256):
             scores = lax.dot_general(
                 far_ref[0:BLOCK, :], x_ref[0, to : to + 256, :], NT, preferred_element_type=jnp.float32
@@ -174,7 +162,8 @@
                 x_ref[0], far_ref[to : to + 256, :], NT, preferred_element_type=jnp.float32
             )
             p_ref[:, to : to + 256] = jnp.exp2(scores * near * far[:, to : to + 256]).astype(jnp.bfloat16)
-        part = jnp.dot(side_vectors(side_ref[0, 0]), p_ref[...], preferred_element_type=jnp.float32)
+        vectors = jnp.concatenate([near_v_ref[0], jnp.ones((16, BLOCK), jnp.bfloat16)], axis=0)
+        part = jnp.dot(vectors, p_ref[...], preferred_element_type=jnp.float32)
         far_sums_ref[at] += part[0:ACC, :]
         if both:
             part = lax.dot_general(side_vectors(side), p_ref[...], NT, preferred_element_type=jnp.float32)
@@ -201,6 +190,7 @@
 X_SPEC = pl.BlockSpec((1, BLOCK, WIDTH), NEAR)
 FAR_SPEC = pl.BlockSpec((PAYLOAD, WIDTH), WHOLE)
 NORM = (pl.BlockSpec((1, BLOCK, 128), STEP), (COLS, BLOCK, 128), jnp.float32)
+ROW = (pl.BlockSpec((1, 8, BLOCK), STEP), (COLS, 8, BLOCK), jnp.float32)
 SUMS = (pl.BlockSpec((1, ACC, BLOCK), STEP), (COLS, ACC, BLOCK), jnp.float32)
 PART = (pl.BlockSpec((SENT, BLOCK), WHOLE), (SENT, BLOCK), jnp.bfloat16)
 TOKEN = (pl.BlockSpec((8, 128), WHOLE), (8, 128), jnp.float32)
@@ -228,19 +218,18 @@
 
 
 def own_cells(order, flags, blocks, far):
-    ins, outs = [X_SPEC, FAR_SPEC], [SUMS, NORM, TOKEN]
+    ins, outs = [X_SPEC, FAR_SPEC], [SUMS, NORM, ROW, TOKEN]
     return cells_call(own_kernel, 1, ins, outs, [SCORES], {}, "cells_own", (order, flags, blocks, far))
 
 
-def cells(order, flags, blocks, sides, fars, norms, sums):
+def cells(order, flags, blocks, near_v, fars, norms, rows, sums):
     count = len(fars)
-    side = pl.BlockSpec((1, 1, PAYLOAD - BLOCK, WIDTH), lambda g, order, flags: (g % SIDE, g // SIDE, 0, 0))
-    ins = [X_SPEC, side] + [FAR_SPEC] * count + [NORM[0], SUMS[0]]
+    ins = [X_SPEC, pl.BlockSpec((1, EIGS, BLOCK), NEAR)] + [FAR_SPEC] * count + [NORM[0], ROW[0], SUMS[0]]
     outs = [SUMS] + [PART] * count + [TOKEN]
     scratch = [SCORES] + [pltpu.VMEM((count, *shape), jnp.float32) for shape in ((BLOCK, 128), (ACC, BLOCK))]
-    args = (order, flags, blocks, sides, *fars, norms, sums)
+    args = (order, flags, blocks, near_v, *fars, norms, rows, sums)
     kernel = functools.partial(cells_kernel, count)
-    result = cells_call(kernel, count, ins, outs, scratch, {5 + count: 0}, "cells", args)
+    result = cells_call(kernel, count, ins, outs, scratch, {6 + count: 0}, "cells", args)
     return result[0], result[1:-1], result[-1]
 
 
@@ -264,21 +253,20 @@
     lanes = lax.broadcasted_iota(jnp.int32, (EIGS, 2 * EIGS), 1)
     eye = jnp.where(rows + EIGS == lanes, 1.0, 0.0)[:, EIGS:]
     work = jnp.concatenate([gram_ref[...], eye], axis=1)
-    pivots = jnp.ones((EIGS, 1), jnp.float32)
-    below = rows[:, 0:1]
-    for j in range(0, EIGS, 2):
-        row1, row2 = work[j : j + 1, :], work[j + 1 : j + 2, :]
-        first, cross = work[j : j + 1, j : j + 1], work[j : j + 1, j + 1 : j + 2]
-        second = work[j + 1 : j + 2, j + 1 : j + 2]
-        column1, column2 = work[:, j : j + 1], work[:, j + 1 : j + 2]
-        scale = 1.0 / (first * second - cross * cross)
-        ratio = cross / first
-        pivots = jnp.where(below == j, first, jnp.where(below == j + 1, second - cross * ratio, pivots))
-        factor1 = jnp.where(below > j + 1, (column1 * second - column2 * cross) * scale, 0.0)
-        factor1 = jnp.where(below == j + 1, ratio, factor1)
-        factor2 = jnp.where(below > j + 1, (column2 * first - column1 * cross) * scale, 0.0)
-        work = work - (factor1 * row1 + factor2 * row2)
-    inverse = work[:, EIGS:] * lax.rsqrt(pivots)
+    below = rows[0:8, :]
+    tiles, done = [work[at : at + 8, :] for at in range(0, EIGS, 8)], []
+    while tiles:
+        for j in range(8):
+            at = len(done) * 8 + j
+            columns = [jnp.broadcast_to(tile[:, at : at + 1], tile.shape) for tile in tiles]
+            pivot = columns[0][j : j + 1, :]
+            row = tiles[0][j : j + 1, :]
+            scaled = row / pivot
+            columns[0] = jnp.where(below > j, columns[0], 0.0)
+            tiles = [tile - column * scaled for tile, column in zip(tiles, columns)]
+            tiles[0] = jnp.where(below == j, row * lax.rsqrt(pivot), tiles[0])
+        done.append(tiles.pop(0))
+    inverse = jnp.concatenate(done, axis=0)[:, EIGS:]
     out_ref[...] = jnp.dot(
         inverse, smoothed_ref[...], precision=lax.Precision.HIGHEST, preferred_element_type=jnp.float32
     )
@@ -316,9 +304,7 @@
     order = jnp.stack([(here_col - CORES * k) % COLS ^ core for core in range(CORES) for k in range(SIDE)])
 
     far_ids, works = [], []
-    diagonal = (here_y < SIDE // 2) == (here_x < SIDE // 2)
-    for moved, keep in STAGES.values():
-        dy, dx = moved or (jnp.where(diagonal, 0, SIDE // 2), jnp.where(diagonal, SIDE // 2, 0))
+    for (dy, dx), keep in STAGES.values():
         from_row = (here_y - dy) % SIDE * SIDE + (here_x - dx) % SIDE
         far_ids.append(from_row * COLS + here_col)
         works.append(jnp.broadcast_to(True if keep is None else keep(here_y, here_x), (COLS,)))
@@ -335,39 +321,54 @@
     def work(group, sums):
         at = starts[group[0]]
         return cells(
-            order, flags[at : at + len(group)].reshape(-1), blocks, sides, [far[name] for name in group], norms, sums
+            order,
+            flags[at : at + len(group)].reshape(-1),
+            blocks,
+            near_v,
+            [far[name] for name in group],
+            norms,
+            rows,
+            sums,
         )
 
     def give_back(group, parts):
         returned = []
         for name, part in zip(group, parts):
-            part = lax.ppermute(part, "row", [(to, source) for source, to in pairs_of(name)]).astype(jnp.float32)
-            degrees = part[EIGS:ACC] + part[ACC:SENT]
-            returned.append(jnp.concatenate([part[0:EIGS], degrees], axis=0))
+            back = [(to, source) for source, to in shift(*STAGES[name][0], STAGES[name][1])]
+            returned.append(lax.ppermute(part, "row", back))
         return returned
 
-    side = far["own"][BLOCK:PAYLOAD]
-    pair = jnp.stack([side, swap(side)])
-    sums, norms, token = own_cells(order, flags[0], blocks, far["own"])
-    (pair,) = tie([pair], token)
-    sides = jnp.stack([pair] + [turn(pair, k) for k in range(1, SIDE)])
-    far["a"], far["b"], far["c"] = tie([far["a"], far["b"], far["c"]], sides)
+    near_v = lax.all_gather(vectors, "col")
+    sums, norms, rows, token = own_cells(order, flags[0], blocks, far["own"])
+
+    far["a"], far["b"], far["c"] = tie([far["a"], far["b"], far["c"]], token, near_v)
     far["d"] = move(far["a"], -1, 0)
     far["e"] = move(far["c"], 0, -1)
-    far["m"] = lax.ppermute(far["own"], "row", cycle())
-    far["f"] = move(far["c"], -1, 0)
+    far["g"] = move(far["a"], 0, 1, left_half)
+    far["h"] = move(far["b"], 1, 0)
+    group1, group2, group3 = ("a", "b", "c"), ("d", "e", "g", "h"), ("f", "k")
+    sums, parts, token = work(group1, sums)
+
+    far["h"], far["e"], *parts = tie([far["h"], far["e"], *parts], token, far["d"], far["g"])
+    far["f"] = move(far["h"], 0, 1)
     far["k"] = move(far["e"], -1, 0, top_half)
-
-    returned = []
-    for group in (("a", "b", "c"), ("d", "e", "m"), ("f", "k")):
-        sums, parts, token = work(group, sums)
-        returned += give_back(group, parts)
+    returned1 = give_back(group1, parts)
+    sums, parts, token = work(group2, sums)
+
+    far["f"], far["k"], *parts = tie([far["f"], far["k"], *parts], *returned1)
+    returned2 = give_back(group2, parts)
+    sums, parts, token = work(group3, sums)
+
+    sums, *parts = tie([sums, *parts], *returned2)
+    returned = returned1 + returned2 + give_back(group3, parts)
 
     kept = sums[:SIDE] + swap(sums[SIDE:])
-    returned += [kept[0]] + [turn(kept[k], SIDE - k) for k in range(1, SIDE)]
-    owned = sum(returned)
-
-    smoothed = owned[0:EIGS] / owned[EIGS : EIGS + 1]
+    summed = kept[0] + (turn(kept[1], 3) + turn(kept[2], 2) + turn(kept[3], 1))
+    totals, degrees = summed[0:EIGS], summed[EIGS : EIGS + 1]
+    for part in returned:
+        part = part.astype(jnp.float32)
+        totals, degrees = totals + part[0:EIGS], degrees + (part[EIGS : EIGS + 1] + part[ACC : ACC + 1])
+    smoothed = totals / degrees
     gram = jnp.dot(
         smoothed, smoothed.T, precision=lax.Precision.HIGHEST, preferred_element_type=jnp.float32
     ) / (BLOCK * NBLOCKS)

time: 231 us -> 193 us (0.84)
  waiting for transfers between devices: 94.9 us -> 43.2 us
  blocking collectives: 0 us -> 16.4 us
  other arithmetic: 4.36 us -> 1.73 us
    ppermute x9, waiting for transfers between devices: 42.5 us -> 13.7 us  [give_back(): returned.append(lax.ppermute(part, 'row', back))]
    ppermute x9 -> x6, waiting for transfers between devices: 28.7 us -> 5.13 us  [turn(): lax.ppermute(array, 'col', [(i, (i + by * CORES) % COLS) for i in range(C...]
    all_gather x0 -> x1, blocking collectives: none -> 16.4 us  [per_device(): near_v = lax.all_gather(vectors, 'col')]
    ppermute x13 -> x15, starting transfers between devices: 30.2 us -> 34.6 us  [move(): return lax.ppermute(array, 'row', shift(dy, dx, keep))]
    ppermute x9 -> x6, starting transfers between devices: 10.4 us -> 7.57 us  [turn(): lax.ppermute(array, 'col', [(i, (i + by * CORES) % COLS) for i in range(C...]
    another operation x2 -> x0, other arithmetic: 2.63 us -> none  [the longest x1 1.92 us: per_device(): sides = jnp.stack([pair] + [turn(pair, k) for k in range(1, SIDE)])]
    pallas_call x1, Pallas kernels: 9.84 us -> 7.22 us  [solve(): pl.pallas_call(solve_kernel, out_shape=jax.ShapeDtypeStruct(smoothed.shap...]
    pallas_call x4, Pallas kernels: 40.1 us -> 42.7 us  [cells_call(): pl.pallas_call(kernel, out_shape=[jax.ShapeDtypeStruct(shape, dtype) for...]
  transfers between devices with their start and end apart: 34 -> 32, of which waited for: 19 -> 16; matrix products, arithmetic and copies ran while one was open for 3% -> 2% of each run, Pallas kernels for 14% -> 22%
where the time goes in v5:
time: 193 us
  starting transfers between devices  68.4 us (35%)
  Pallas kernels  52.6 us (27%)
  waiting for transfers between devices  43.2 us (22%)
  blocking collectives  16.4 us (8%)
  local copies, waits for them, and re-layouts  9.43 us (5%)
    pallas_call x4, Pallas kernels, cells_call(): pl.pallas_call(kernel, out_shape=[jax.ShapeDtypeStruct(shape, dtype) for...  42.7 us
    ppermute x15, starting transfers between devices, move(): return lax.ppermute(array, 'row', shift(dy, dx, keep))  34.6 us
    ppermute x9, starting transfers between devices, give_back(): returned.append(lax.ppermute(part, 'row', back))  26.1 us
    ppermute x15, waiting for transfers between devices, move(): return lax.ppermute(array, 'row', shift(dy, dx, keep))  21.1 us
    all_gather x1, blocking collectives, per_device(): near_v = lax.all_gather(vectors, 'col')  16.4 us
    ppermute x9, waiting for transfers between devices, give_back(): returned.append(lax.ppermute(part, 'row', back))  13.7 us
    ppermute x6, starting transfers between devices, turn(): lax.ppermute(array, 'col', [(i, (i + by * CORES) % COLS) for i in range(C...  7.57 us
    pallas_call x1, Pallas kernels, solve(): pl.pallas_call(solve_kernel, out_shape=jax.ShapeDtypeStruct(smoothed.shap...  7.22 us
  transfers between devices with their start and end apart: 32, of which 16 were waited for; matrix products, arithmetic and copies ran while one was open for 2% of the time, Pallas kernels for 22%

profile of v5, /device:TPU:0, one launch (start us, length us, event | category | flops | bytes accessed | tf_op | source)
XLA Modules:
  0.0 192.6 jit_solution(1438777409463536396)
XLA Ops:
  0.0 2.6 %payload.1.far_ref = bf16[560,1024]{1,0:T(8,128)(2,1)} custom-call(s32[1]{0:T(128)} %bitcast.22.index_ref, bf16[8,512,1024]{2,1,0:T(8,128)(2,1)} %bitcast.42, bf16[64,512]{1,0:T(8,128)(2,1)} %v_ref.1), custom_call_target="tpu_custom_call" | custom-call | tf_op jit(solution)/shard_map/payload/pallas_call | solution.py:78
  2.6 5.3 %collective-permute-start.2 = (bf16[560,1024]{1,0:T(8,128)(2,1)}, bf16[560,1024]{1,0:T(8,128)(2,1)S(1)}, u32[]{:S(2)}, u32[]{:S(2)}) collective-permute-start(bf16[560,1024]{1,0:T(8,128)(2,1)} %payload.1.far_ref), channel_id=1, source_target_pairs={{0,120},{8,96},{16,104},{24,112},{32,24},{40,0},{48,8},{56,16},{64... | collective-permute-start | bytes 3440648 | tf_op jit(solution)/shard_map/ppermute | solution.py:292
  9.8 9.6 %cells_own.1 = (f32[8,72,512]{2,1,0:T(8,128)}, f32[8,512,128]{2,1,0:T(8,128)}, f32[8,8,512]{2,1,0:T(8,128)}, f32[8,128]{1,0:T(8,128)}) custom-call(s32[8]{0:T(128)} %copy-done.28, s32[8]{0:T(128)} %slice_reduce_fusion.flags_ref, bf16[8,512,1024]{2,1,0:T(8,128)(2,1)} %bitcast.43, bf16[560,1024]{1,0:T(8,128)(2,1)} %payload.1.far_ref), custom_call_target="tpu_custom_call" | custom-call | flops 2147483648 | bytes 13631488 | tf_op jit(solution)/shard_map/cells_own/pallas_call | solution.py:200
  19.4 16.4 %all-gather = bf16[512,512]{1,0:T(8,128)(2,1)} all-gather(bf16[64,512]{1,0:T(8,128)(2,1)S(1)} %copy-done.24), channel_id=2, replica_groups=mesh['row'=16,'col'=8] {'col'}, dimensions={0}, use_global_device_ids=true | all-gather | bytes 589824 | tf_op jit(solution)/shard_map/all_gather | solution.py:341
  38.2 3.2 %collective-permute-start.4 = (bf16[560,1024]{1,0:T(8,128)(2,1)}, bf16[560,1024]{1,0:T(8,128)(2,1)}, u32[]{:S(2)}, u32[]{:S(2)}) collective-permute-start(bf16[560,1024]{1,0:T(8,128)(2,1)} %get-tuple-element.41.refs_2_), channel_id=1, source_target_pairs={{0,24},{8,0},{16,8},{24,16},{32,56},{40,32},{48,40},{56,48},{64,88... | collective-permute-start | bytes 3440648 | tf_op jit(solution)/shard_map/ppermute | solution.py:292
  43.4 5.3 %collective-permute-start.5 = (bf16[560,1024]{1,0:T(8,128)(2,1)}, bf16[560,1024]{1,0:T(8,128)(2,1)S(1)}, u32[]{:S(2)}, u32[]{:S(2)}) collective-permute-start(bf16[560,1024]{1,0:T(8,128)(2,1)} %get-tuple-element.42.refs_0_), channel_id=1, source_target_pairs={{0,96},{8,104},{16,112},{24,120},{32,0},{40,8},{48,16},{56,24},{64... | collective-permute-start | bytes 3440648 | tf_op jit(solution)/shard_map/ppermute | solution.py:292
  49.5 12.4 %cells.3 = (f32[8,72,512]{2,1,0:T(8,128)}, bf16[80,512]{1,0:T(8,128)(2,1)}, bf16[80,512]{1,0:T(8,128)(2,1)}, bf16[80,512]{1,0:T(8,128)(2,1)}, f32[8,128]{1,0:T(8,128)}) custom-call(s32[8]{0:T(128)} %copy-done.28, s32[24]{0:T(128)} %reshape.316.flags_ref, bf16[8,512,1024]{2,1,0:T(8,128)(2,1)} %bitcast.44, ...), custom_call_target="tpu_custom_call", output_to_operand_aliasing={{0}: (9, {})} | custom-call | flops 6442450944 | bytes 15728640 | tf_op jit(solution)/shard_map/cells/pallas_call | solution.py:200
  61.9 6.5 %collective-permute-done.3.refs_0_ = bf16[560,1024]{1,0:T(8,128)(2,1)S(1)} collective-permute-done((bf16[560,1024]{1,0:T(8,128)(2,1)}, bf16[560,1024]{1,0:T(8,128)(2,1)S(1)}, u32[]{:S(2)}, u32[]{:S(2)}) %collective-permute-start.3) | collective-permute-done | bytes 1146912 | tf_op jit(solution)/shard_map/ppermute | solution.py:292
  68.4 3.3 %collective-permute-done.6.refs_7_.refs_2_ = bf16[560,1024]{1,0:T(8,128)(2,1)S(1)} collective-permute-done((bf16[560,1024]{1,0:T(8,128)(2,1)}, bf16[560,1024]{1,0:T(8,128)(2,1)S(1)}, u32[]{:S(2)}, u32[]{:S(2)}) %collective-permute-start.6) | collective-permute-done | bytes 1146912 | tf_op jit(solution)/shard_map/ppermute | solution.py:292
  77.8 3.2 %collective-permute-start.9 = (bf16[80,512]{1,0:T(8,128)(2,1)}, bf16[80,512]{1,0:T(8,128)(2,1)S(1)}, u32[]{:S(2)}, u32[]{:S(2)}) collective-permute-start(bf16[80,512]{1,0:T(8,128)(2,1)} %get-tuple-element.57), channel_id=1, source_target_pairs={{8,0},{16,8},{24,16},{0,24},{40,32},{48,40},{56,48},{32,56},{72,64... | collective-permute-start | bytes 245768 | tf_op jit(solution)/shard_map/ppermute | solution.py:338
  81.0 3.3 %collective-permute-start.10 = (bf16[80,512]{1,0:T(8,128)(2,1)}, bf16[80,512]{1,0:T(8,128)(2,1)S(1)}, u32[]{:S(2)}, u32[]{:S(2)}) collective-permute-start(bf16[80,512]{1,0:T(8,128)(2,1)} %get-tuple-element.58), channel_id=1, source_target_pairs={{32,0},{40,8},{48,16},{56,24},{64,32},{72,40},{80,48},{88,56},{96,... | collective-permute-start | bytes 245768 | tf_op jit(solution)/shard_map/ppermute | solution.py:338
  84.3 11.4 %cells.4 = (f32[8,72,512]{2,1,0:T(8,128)}, bf16[80,512]{1,0:T(8,128)(2,1)}, bf16[80,512]{1,0:T(8,128)(2,1)}, bf16[80,512]{1,0:T(8,128)(2,1)}, bf16[80,512]{1,0:T(8,128)(2,1)}, /*index=5*/f32[8,128]{1,0:T(8,128)}) custom-call(s32[8]{0:T(128)} %copy-done.28, s32[32]{0:T(128)} %reshape.317.flags_ref, ...), custom_call_target="tpu_custom_call", output_to_operand_aliasing={{0}: (10, {})} | custom-call | flops 8589934592 | bytes 16777216 | tf_op jit(solution)/shard_map/cells/pallas_call | solution.py:200
  95.8 9.8 %collective-permute-done.10.refs_7_ = bf16[80,512]{1,0:T(8,128)(2,1)S(1)} collective-permute-done((bf16[80,512]{1,0:T(8,128)(2,1)}, bf16[80,512]{1,0:T(8,128)(2,1)S(1)}, u32[]{:S(2)}, u32[]{:S(2)}) %collective-permute-start.10) | collective-permute-done | bytes 81952 | tf_op jit(solution)/shard_map/ppermute | solution.py:338
  105.5 2.2 %collective-permute-done.11.refs_8_ = bf16[80,512]{1,0:T(8,128)(2,1)S(1)} collective-permute-done((bf16[80,512]{1,0:T(8,128)(2,1)}, bf16[80,512]{1,0:T(8,128)(2,1)S(1)}, u32[]{:S(2)}, u32[]{:S(2)}) %collective-permute-start.11) | collective-permute-done | bytes 81952 | tf_op jit(solution)/shard_map/ppermute | solution.py:338
  109.2 2.1 %collective-permute-start.12 = (bf16[80,512]{1,0:T(8,128)(2,1)}, bf16[80,512]{1,0:T(8,128)(2,1)S(1)}, u32[]{:S(2)}, u32[]{:S(2)}) collective-permute-start(bf16[80,512]{1,0:T(8,128)(2,1)} %get-tuple-element.66), channel_id=1, source_target_pairs={{104,0},{112,8},{120,16},{96,24},{8,32},{16,40},{24,48},{0,56},{40... | collective-permute-start | bytes 245768 | tf_op jit(solution)/shard_map/ppermute | solution.py:338
  111.3 3.0 %collective-permute-start.13 = (bf16[80,512]{1,0:T(8,128)(2,1)}, bf16[80,512]{1,0:T(8,128)(2,1)S(1)}, u32[]{:S(2)}, u32[]{:S(2)}) collective-permute-start(bf16[80,512]{1,0:T(8,128)(2,1)} %get-tuple-element.67), channel_id=1, source_target_pairs={{112,0},{120,8},{96,16},{104,24},{16,32},{24,40},{0,48},{8,56},{48... | collective-permute-start | bytes 245768 | tf_op jit(solution)/shard_map/ppermute | solution.py:338
  115.8 5.7 %collective-permute-start.15 = (bf16[80,512]{1,0:T(8,128)(2,1)}, bf16[80,512]{1,0:T(8,128)(2,1)S(1)}, u32[]{:S(2)}, u32[]{:S(2)}) collective-permute-start(bf16[80,512]{1,0:T(8,128)(2,1)} %get-tuple-element.69), channel_id=1, source_target_pairs={{0,64},{8,72},{16,80},{24,88},{32,96},{40,104},{48,112},{56,120},{... | collective-permute-start | bytes 245768 | tf_op jit(solution)/shard_map/ppermute | solution.py:338
  121.5 9.3 %cells.5 = (f32[8,72,512]{2,1,0:T(8,128)}, bf16[80,512]{1,0:T(8,128)(2,1)}, bf16[80,512]{1,0:T(8,128)(2,1)}, f32[8,128]{1,0:T(8,128)}) custom-call(s32[8]{0:T(128)} %copy-done.28, s32[16]{0:T(128)} %reshape.314.flags_ref, bf16[8,512,1024]{2,1,0:T(8,128)(2,1)} %bitcast.46, bf16[8,64,512]{2,1,0:T(8,128)(2,1)} %bitcast.50, ...), custom_call_target="tpu_custom_call", output_to_operand_aliasing={{0}: (8, {})} | custom-call | flops 4294967296 | bytes 14680064 | tf_op jit(solution)/shard_map/cells/pallas_call | solution.py:200
  139.8 7.2 %collective-permute-start.21 = (bf16[80,512]{1,0:T(8,128)(2,1)S(1)}, bf16[80,512]{1,0:T(8,128)(2,1)S(1)}, u32[]{:S(2)}, u32[]{:S(2)}) collective-permute-start(bf16[80,512]{1,0:T(8,128)(2,1)S(1)} %copy-done.26), channel_id=1, source_target_pairs={{16,64},{24,72},{0,80},{8,88},{48,96},{56,104},{32,112},{40,120},{... | collective-permute-start | bytes 245768 | tf_op jit(solution)/shard_map/ppermute | solution.py:338
  154.8 3.1 %collective-permute-done.24 = f32[64,64]{1,0:T(8,128)S(1)} collective-permute-done((f32[64,64]{1,0:T(8,128)S(1)}, f32[64,64]{1,0:T(8,128)S(1)}, u32[]{:S(2)}, u32[]{:S(2)}) %collective-permute-start.24) | collective-permute-done | bytes 16416 | tf_op jit(solution)/shard_map/ppermute | solution.py:295
  162.8 3.4 %collective-permute-done.27 = f32[64,64]{1,0:T(8,128)S(1)} collective-permute-done((f32[64,64]{1,0:T(8,128)S(1)}, f32[64,64]{1,0:T(8,128)S(1)}, u32[]{:S(2)}, u32[]{:S(2)}) %collective-permute-start.27) | collective-permute-done | bytes 16416 | tf_op jit(solution)/shard_map/ppermute | solution.py:292
  166.2 13.1 %collective-permute-start.31 = (f32[64,64]{1,0:T(8,128)S(1)}, f32[64,64]{1,0:T(8,128)S(1)}, u32[]{:S(2)}, u32[]{:S(2)}) collective-permute-start(f32[64,64]{1,0:T(8,128)S(1)} %add_add_fusion.1), channel_id=1, source_target_pairs={{0,96},{8,104},{16,112},{24,120},{32,0},{40,8},{48,16},{56,24},{64... | collective-permute-start | bytes 49160 | tf_op jit(solution)/shard_map/ppermute | solution.py:292
  180.8 3.9 %collective-permute-done.30 = f32[64,64]{1,0:T(8,128)S(1)} collective-permute-done((f32[64,64]{1,0:T(8,128)S(1)}, f32[64,64]{1,0:T(8,128)S(1)}, u32[]{:S(2)}, u32[]{:S(2)}) %collective-permute-start.30) | collective-permute-done | bytes 16416 | tf_op jit(solution)/shard_map/ppermute | solution.py:292
  185.4 7.2 %solve.1 = f32[64,512]{1,0:T(8,128)} custom-call(f32[64,64]{1,0:T(8,128)} %add_add_fusion.gram_ref, f32[64,512]{1,0:T(8,128)} %copy-done.1), custom_call_target="tpu_custom_call" | custom-call | tf_op jit(solution)/shard_map/solve/pallas_call | solution.py:276
  (158 shorter events, 39.5 us)
Async XLA Ops:
  2.6 33.2 %collective-permute-start.2 = (bf16[560,1024]{1,0:T(8,128)(2,1)}, bf16[560,1024]{1,0:T(8,128)(2,1)S(1)}, u32[]{:S(2)}, u32[]{:S(2)}) collective-permute-start(bf16[560,1024]{1,0:T(8,128)(2,1)} %payload.1.far_ref), channel_id=1, source_target_pairs={{0,120},{8,96},{16,104},{24,112},{32,24},{40,0},{48,8},{56,16},{64... | collective-permute-start | bytes 3440648 | tf_op jit(solution)/shard_map/ppermute | solution.py:292
  7.9 28.1 %collective-permute-start.1 = (bf16[560,1024]{1,0:T(8,128)(2,1)}, bf16[560,1024]{1,0:T(8,128)(2,1)S(1)}, u32[]{:S(2)}, u32[]{:S(2)}) collective-permute-start(bf16[560,1024]{1,0:T(8,128)(2,1)} %payload.1.far_ref), channel_id=1, source_target_pairs={{0,32},{8,40},{16,48},{24,56},{32,64},{40,72},{48,80},{56,88},{64,... | collective-permute-start | bytes 3440648 | tf_op jit(solution)/shard_map/ppermute | solution.py:292
  7.9 28.1 %collective-permute-start = (bf16[560,1024]{1,0:T(8,128)(2,1)}, bf16[560,1024]{1,0:T(8,128)(2,1)S(1)}, u32[]{:S(2)}, u32[]{:S(2)}) collective-permute-start(bf16[560,1024]{1,0:T(8,128)(2,1)} %payload.1.far_ref), channel_id=1, source_target_pairs={{0,8},{8,16},{16,24},{24,0},{32,40},{40,48},{48,56},{56,32},{64,72... | collective-permute-start | bytes 3440648 | tf_op jit(solution)/shard_map/ppermute | solution.py:292
  37.6 30.8 %collective-permute-start.3 = (bf16[560,1024]{1,0:T(8,128)(2,1)}, bf16[560,1024]{1,0:T(8,128)(2,1)S(1)}, u32[]{:S(2)}, u32[]{:S(2)}) collective-permute-start(bf16[560,1024]{1,0:T(8,128)(2,1)} %get-tuple-element.40.refs_1_), channel_id=1, source_target_pairs={{0,32},{8,40},{16,48},{24,56},{32,64},{40,72},{48,80},{56,88},{64,... | collective-permute-start | bytes 3440648 | tf_op jit(solution)/shard_map/ppermute | solution.py:292
  38.2 30.2 %collective-permute-start.4 = (bf16[560,1024]{1,0:T(8,128)(2,1)}, bf16[560,1024]{1,0:T(8,128)(2,1)}, u32[]{:S(2)}, u32[]{:S(2)}) collective-permute-start(bf16[560,1024]{1,0:T(8,128)(2,1)} %get-tuple-element.41.refs_2_), channel_id=1, source_target_pairs={{0,24},{8,0},{16,8},{24,16},{32,56},{40,32},{48,40},{56,48},{64,88... | collective-permute-start | bytes 3440648 | tf_op jit(solution)/shard_map/ppermute | solution.py:292
  41.4 30.3 %collective-permute-start.6 = (bf16[560,1024]{1,0:T(8,128)(2,1)}, bf16[560,1024]{1,0:T(8,128)(2,1)S(1)}, u32[]{:S(2)}, u32[]{:S(2)}) collective-permute-start(bf16[560,1024]{1,0:T(8,128)(2,1)} %get-tuple-element.42.refs_0_), channel_id=1, source_target_pairs={{0,8},{24,0},{32,40},{56,32},{64,72},{88,64},{96,104},{120,96},{1,... | collective-permute-start | bytes 3440648 | tf_op jit(solution)/shard_map/ppermute | solution.py:292
  43.4 30.4 %collective-permute-start.5 = (bf16[560,1024]{1,0:T(8,128)(2,1)}, bf16[560,1024]{1,0:T(8,128)(2,1)S(1)}, u32[]{:S(2)}, u32[]{:S(2)}) collective-permute-start(bf16[560,1024]{1,0:T(8,128)(2,1)} %get-tuple-element.42.refs_0_), channel_id=1, source_target_pairs={{0,96},{8,104},{16,112},{24,120},{32,0},{40,8},{48,16},{56,24},{64... | collective-permute-start | bytes 3440648 | tf_op jit(solution)/shard_map/ppermute | solution.py:292
  74.8 32.9 %collective-permute-start.7 = (bf16[560,1024]{1,0:T(8,128)(2,1)}, bf16[560,1024]{1,0:T(8,128)(2,1)S(1)}, u32[]{:S(2)}, u32[]{:S(2)}) collective-permute-start(bf16[560,1024]{1,0:T(8,128)(2,1)} %get-tuple-element.50.refs_3_), channel_id=1, source_target_pairs={{0,8},{8,16},{16,24},{24,0},{32,40},{40,48},{48,56},{56,32},{64,72... | collective-permute-start | bytes 3440648 | tf_op jit(solution)/shard_map/ppermute | solution.py:292
  74.8 32.9 %collective-permute-start.8 = (bf16[560,1024]{1,0:T(8,128)(2,1)}, bf16[560,1024]{1,0:T(8,128)(2,1)S(1)}, u32[]{:S(2)}, u32[]{:S(2)}) collective-permute-start(bf16[560,1024]{1,0:T(8,128)(2,1)} %get-tuple-element.51.refs_1_), channel_id=1, source_target_pairs={{32,0},{40,8},{48,16},{56,24},{64,32},{72,40},{80,48},{88,56},{33,... | collective-permute-start | bytes 3440648 | tf_op jit(solution)/shard_map/ppermute | solution.py:292
  77.8 18.0 %collective-permute-start.9 = (bf16[80,512]{1,0:T(8,128)(2,1)}, bf16[80,512]{1,0:T(8,128)(2,1)S(1)}, u32[]{:S(2)}, u32[]{:S(2)}) collective-permute-start(bf16[80,512]{1,0:T(8,128)(2,1)} %get-tuple-element.57), channel_id=1, source_target_pairs={{8,0},{16,8},{24,16},{0,24},{40,32},{48,40},{56,48},{32,56},{72,64... | collective-permute-start | bytes 245768 | tf_op jit(solution)/shard_map/ppermute | solution.py:338
  81.0 24.5 %collective-permute-start.10 = (bf16[80,512]{1,0:T(8,128)(2,1)}, bf16[80,512]{1,0:T(8,128)(2,1)S(1)}, u32[]{:S(2)}, u32[]{:S(2)}) collective-permute-start(bf16[80,512]{1,0:T(8,128)(2,1)} %get-tuple-element.58), channel_id=1, source_target_pairs={{32,0},{40,8},{48,16},{56,24},{64,32},{72,40},{80,48},{88,56},{96,... | collective-permute-start | bytes 245768 | tf_op jit(solution)/shard_map/ppermute | solution.py:338
  84.3 23.3 %collective-permute-start.11 = (bf16[80,512]{1,0:T(8,128)(2,1)}, bf16[80,512]{1,0:T(8,128)(2,1)S(1)}, u32[]{:S(2)}, u32[]{:S(2)}) collective-permute-start(bf16[80,512]{1,0:T(8,128)(2,1)} %get-tuple-element.59), channel_id=1, source_target_pairs={{120,0},{96,8},{104,16},{112,24},{24,32},{0,40},{8,48},{16,56},{56... | collective-permute-start | bytes 245768 | tf_op jit(solution)/shard_map/ppermute | solution.py:338
  109.2 21.6 %collective-permute-start.12 = (bf16[80,512]{1,0:T(8,128)(2,1)}, bf16[80,512]{1,0:T(8,128)(2,1)S(1)}, u32[]{:S(2)}, u32[]{:S(2)}) collective-permute-start(bf16[80,512]{1,0:T(8,128)(2,1)} %get-tuple-element.66), channel_id=1, source_target_pairs={{104,0},{112,8},{120,16},{96,24},{8,32},{16,40},{24,48},{0,56},{40... | collective-permute-start | bytes 245768 | tf_op jit(solution)/shard_map/ppermute | solution.py:338
  111.3 19.6 %collective-permute-start.13 = (bf16[80,512]{1,0:T(8,128)(2,1)}, bf16[80,512]{1,0:T(8,128)(2,1)S(1)}, u32[]{:S(2)}, u32[]{:S(2)}) collective-permute-start(bf16[80,512]{1,0:T(8,128)(2,1)} %get-tuple-element.67), channel_id=1, source_target_pairs={{112,0},{120,8},{96,16},{104,24},{16,32},{24,40},{0,48},{8,56},{48... | collective-permute-start | bytes 245768 | tf_op jit(solution)/shard_map/ppermute | solution.py:338
  114.3 16.5 %collective-permute-start.14 = (bf16[80,512]{1,0:T(8,128)(2,1)}, bf16[80,512]{1,0:T(8,128)(2,1)S(1)}, u32[]{:S(2)}, u32[]{:S(2)}) collective-permute-start(bf16[80,512]{1,0:T(8,128)(2,1)} %get-tuple-element.68), channel_id=1, source_target_pairs={{0,16},{8,24},{32,48},{40,56},{64,80},{72,88},{96,112},{104,120},{... | collective-permute-start | bytes 245768 | tf_op jit(solution)/shard_map/ppermute | solution.py:338
  115.8 15.1 %collective-permute-start.15 = (bf16[80,512]{1,0:T(8,128)(2,1)}, bf16[80,512]{1,0:T(8,128)(2,1)S(1)}, u32[]{:S(2)}, u32[]{:S(2)}) collective-permute-start(bf16[80,512]{1,0:T(8,128)(2,1)} %get-tuple-element.69), channel_id=1, source_target_pairs={{0,64},{8,72},{16,80},{24,88},{32,96},{40,104},{48,112},{56,120},{... | collective-permute-start | bytes 245768 | tf_op jit(solution)/shard_map/ppermute | solution.py:338
  135.0 14.0 %collective-permute-start.18 = (f32[72,512]{1,0:T(8,128)S(1)}, f32[72,512]{1,0:T(8,128)S(1)}, u32[]{:S(2)}, u32[]{:S(2)}) collective-permute-start(f32[72,512]{1,0:T(8,128)S(1)} %get-tuple-element.75), channel_id=1, source_target_pairs={{0,4},{1,5},{2,6},{3,7},{4,0},{5,1},{6,2},{7,3},{8,12},{9,13},{10,... | collective-permute-start | bytes 442376 | tf_op jit(solution)/shard_map/ppermute | solution.py:295
  136.6 12.5 %collective-permute-start.19 = (f32[72,512]{1,0:T(8,128)S(1)}, f32[72,512]{1,0:T(8,128)S(1)}, u32[]{:S(2)}, u32[]{:S(2)}) collective-permute-start(f32[72,512]{1,0:T(8,128)S(1)} %get-tuple-element.76), channel_id=1, source_target_pairs={{0,2},{1,3},{2,4},{3,5},{4,6},{5,7},{6,0},{7,1},{8,10},{9,11},{10,... | collective-permute-start | bytes 442376 | tf_op jit(solution)/shard_map/ppermute | solution.py:295
  138.5 10.6 %collective-permute-start.17 = (f32[72,512]{1,0:T(8,128)S(1)}, f32[72,512]{1,0:T(8,128)S(1)}, u32[]{:S(2)}, u32[]{:S(2)}) collective-permute-start(f32[72,512]{1,0:T(8,128)S(1)} %get-tuple-element.77), channel_id=1, source_target_pairs={{0,6},{1,7},{2,0},{3,1},{4,2},{5,3},{6,4},{7,5},{8,14},{9,15},{10,... | collective-permute-start | bytes 442376 | tf_op jit(solution)/shard_map/ppermute | solution.py:295
  139.8 7.4 %collective-permute-start.20 = (bf16[80,512]{1,0:T(8,128)(2,1)S(1)}, bf16[80,512]{1,0:T(8,128)(2,1)S(1)}, u32[]{:S(2)}, u32[]{:S(2)}) collective-permute-start(bf16[80,512]{1,0:T(8,128)(2,1)S(1)} %copy-done.25), channel_id=1, source_target_pairs={{72,0},{80,8},{88,16},{64,24},{104,32},{112,40},{120,48},{96,56},{... | collective-permute-start | bytes 245768 | tf_op jit(solution)/shard_map/ppermute | solution.py:338
  139.8 9.2 %collective-permute-start.21 = (bf16[80,512]{1,0:T(8,128)(2,1)S(1)}, bf16[80,512]{1,0:T(8,128)(2,1)S(1)}, u32[]{:S(2)}, u32[]{:S(2)}) collective-permute-start(bf16[80,512]{1,0:T(8,128)(2,1)S(1)} %copy-done.26), channel_id=1, source_target_pairs={{16,64},{24,72},{0,80},{8,88},{48,96},{56,104},{32,112},{40,120},{... | collective-permute-start | bytes 245768 | tf_op jit(solution)/shard_map/ppermute | solution.py:338
  152.2 5.7 %collective-permute-start.24 = (f32[64,64]{1,0:T(8,128)S(1)}, f32[64,64]{1,0:T(8,128)S(1)}, u32[]{:S(2)}, u32[]{:S(2)}) collective-permute-start(f32[64,64]{1,0:T(8,128)S(1)} %add.394), channel_id=1, source_target_pairs={{0,4},{1,5},{2,6},{3,7},{4,0},{5,1},{6,2},{7,3},{8,12},{9,13},{10,... | collective-permute-start | bytes 49160 | tf_op jit(solution)/shard_map/ppermute | solution.py:295
  160.7 5.5 %collective-permute-start.27 = (f32[64,64]{1,0:T(8,128)S(1)}, f32[64,64]{1,0:T(8,128)S(1)}, u32[]{:S(2)}, u32[]{:S(2)}) collective-permute-start(f32[64,64]{1,0:T(8,128)S(1)} %add_add_fusion.2), channel_id=1, source_target_pairs={{0,16},{8,24},{16,0},{24,8},{32,48},{40,56},{48,32},{56,40},{64,80... | collective-permute-start | bytes 49160 | tf_op jit(solution)/shard_map/ppermute | solution.py:292
  166.2 14.7 %collective-permute-start.31 = (f32[64,64]{1,0:T(8,128)S(1)}, f32[64,64]{1,0:T(8,128)S(1)}, u32[]{:S(2)}, u32[]{:S(2)}) collective-permute-start(f32[64,64]{1,0:T(8,128)S(1)} %add_add_fusion.1), channel_id=1, source_target_pairs={{0,96},{8,104},{16,112},{24,120},{32,0},{40,8},{48,16},{56,24},{64... | collective-permute-start | bytes 49160 | tf_op jit(solution)/shard_map/ppermute | solution.py:292
  (37 other events, 229.4 us)

commit v6 on v5

--- a/solution.py
+++ b/solution.py
@@ -49,9 +49,9 @@
     "c": ((-1, -1), None),
     "d": ((-1, 1), None),
     "e": ((-1, -2), None),
-    "g": ((0, 2), left_half),
     "h": ((2, 0), top_half),
     "f": ((2, 1), None),
+    "g": ((0, 2), left_half),
     "k": ((2, 2), top_half),
 }
 
@@ -256,15 +256,26 @@
     below = rows[0:8, :]
     tiles, done = [work[at : at + 8, :] for at in range(0, EIGS, 8)], []
     while tiles:
-        for j in range(8):
+        for j in range(0, 8, 2):
             at = len(done) * 8 + j
-            columns = [jnp.broadcast_to(tile[:, at : at + 1], tile.shape) for tile in tiles]
-            pivot = columns[0][j : j + 1, :]
-            row = tiles[0][j : j + 1, :]
-            scaled = row / pivot
-            columns[0] = jnp.where(below > j, columns[0], 0.0)
-            tiles = [tile - column * scaled for tile, column in zip(tiles, columns)]
-            tiles[0] = jnp.where(below == j, row * lax.rsqrt(pivot), tiles[0])
+            columns1 = [jnp.broadcast_to(tile[:, at : at + 1], tile.shape) for tile in tiles]
+            columns2 = [jnp.broadcast_to(tile[:, at + 1 : at + 2], tile.shape) for tile in tiles]
+            first, cross = columns1[0][j : j + 1, :], columns1[0][j + 1 : j + 2, :]
+            second = columns2[0][j + 1 : j + 2, :]
+            row1, row2 = tiles[0][j : j + 1, :], tiles[0][j + 1 : j + 2, :]
+            scale = 1.0 / (first * second - cross * cross)
+            scaled1 = (second * row1 - cross * row2) * scale
+            scaled2 = (first * row2 - cross * row1) * scale
+            ratio = cross / first
+            columns1[0] = jnp.where(below > j + 1, columns1[0], 0.0)
+            columns2[0] = jnp.where(below > j + 1, columns2[0], 0.0)
+            tiles = [
+                tile - (column1 * scaled1 + column2 * scaled2)
+                for tile, column1, column2 in zip(tiles, columns1, columns2)
+            ]
+            tiles[0] = jnp.where(below == j, row1 * lax.rsqrt(first), tiles[0])
+            last = (row2 - ratio * row1) * lax.rsqrt(second - ratio * cross)
+            tiles[0] = jnp.where(below == j + 1, last, tiles[0])
         done.append(tiles.pop(0))
     inverse = jnp.concatenate(done, axis=0)[:, EIGS:]
     out_ref[...] = jnp.dot(
@@ -346,7 +357,7 @@
     far["e"] = move(far["c"], 0, -1)
     far["g"] = move(far["a"], 0, 1, left_half)
     far["h"] = move(far["b"], 1, 0)
-    group1, group2, group3 = ("a", "b", "c"), ("d", "e", "g", "h"), ("f", "k")
+    group1, group2, group3 = ("a", "b", "c"), ("d", "e", "h"), ("f", "g", "k")
     sums, parts, token = work(group1, sums)
 
     far["h"], far["e"], *parts = tie([far["h"], far["e"], *parts], token, far["d"], far["g"])
@@ -374,8 +385,8 @@
     ) / (BLOCK * NBLOCKS)
     gram = gram + swap(gram)
     gram = gram + (turn(gram, 1) + turn(gram, 2) + turn(gram, 3))
-    gram = gram + (move(gram, 0, 1) + move(gram, 0, 2) + move(gram, 0, 3))
-    gram = gram + (move(gram, 1, 0) + move(gram, 2, 0) + move(gram, 3, 0))
+    everyone = jnp.broadcast_to(gram, (SIDE * SIDE, EIGS, EIGS))
+    gram = jnp.sum(lax.all_to_all(everyone, "row", 0, 0), axis=0)
     return solve(gram, smoothed)
 
 

time: 193 us -> 188 us (0.974)
  blocking collectives: 16.4 us -> 41.5 us
  starting transfers between devices: 68.4 us -> 48.4 us
  waiting for transfers between devices: 43.2 us -> 33.5 us
  Pallas kernels: 52.6 us -> 49.4 us
    all_to_all x0 -> x1, blocking collectives: none -> 25 us  [per_device(): gram = jnp.sum(lax.all_to_all(everyone, 'row', 0, 0), axis=0)]
    ppermute x15 -> x9, starting transfers between devices: 34.6 us -> 17.4 us  [move(): return lax.ppermute(array, 'row', shift(dy, dx, keep))]
    ppermute x15 -> x9, waiting for transfers between devices: 21.1 us -> 12.9 us  [move(): return lax.ppermute(array, 'row', shift(dy, dx, keep))]
    ppermute x9, starting transfers between devices: 26.1 us -> 22.7 us  [give_back(): returned.append(lax.ppermute(part, 'row', back))]
    pallas_call x1, Pallas kernels: 7.22 us -> 4.98 us  [solve(): pl.pallas_call(solve_kernel, out_shape=jax.ShapeDtypeStruct(smoothed.shap...]
    ppermute x2, waiting for transfers between devices: 3.18 us -> 1.2 us  [swap(): return lax.ppermute(array, 'col', [(i, i ^ 1) for i in range(COLS)])]
    unnamed x59 -> x57, local copies, waits for them, and re-layouts: 4.85 us -> 5.42 us
  transfers between devices with their start and end apart: 32 -> 26, of which waited for: 16 -> 12; matrix products, arithmetic and copies ran while one was open for 2% -> 2% of each run, Pallas kernels for 22% -> 22%
where the time goes in v6:
time: 188 us; the launch traced here: 187 us
  Pallas kernels  49.4 us (26%)
  starting transfers between devices  48.4 us (26%)
  blocking collectives  41.5 us (22%)
  waiting for transfers between devices  33.5 us (18%)
  local copies, waits for them, and re-layouts  10.6 us (6%)
  other arithmetic  3.03 us (2%)
    pallas_call x4, Pallas kernels, cells_call(): pl.pallas_call(kernel, out_shape=[jax.ShapeDtypeStruct(shape, dtype) for...  41.8 us
    all_to_all x1, blocking collectives, per_device(): gram = jnp.sum(lax.all_to_all(everyone, 'row', 0, 0), axis=0)  25 us
    ppermute x9, starting transfers between devices, give_back(): returned.append(lax.ppermute(part, 'row', back))  22.7 us
    ppermute x9, starting transfers between devices, move(): return lax.ppermute(array, 'row', shift(dy, dx, keep))  17.4 us
    all_gather x1, blocking collectives, per_device(): near_v = lax.all_gather(vectors, 'col')  16.5 us
    ppermute x9, waiting for transfers between devices, give_back(): returned.append(lax.ppermute(part, 'row', back))  14.3 us
    ppermute x9, waiting for transfers between devices, move(): return lax.ppermute(array, 'row', shift(dy, dx, keep))  12.9 us
    ppermute x6, starting transfers between devices, turn(): lax.ppermute(array, 'col', [(i, (i + by * CORES) % COLS) for i in range(C...  8.09 us
  transfers between devices with their start and end apart: 26, of which 12 were waited for; matrix products, arithmetic and copies ran while one was open for 2% of the time, Pallas kernels for 22%

profile of v6, /device:TPU:0, one launch (start us, length us, event | category | flops | bytes accessed | tf_op | source)
XLA Modules:
  0.0 187.2 jit_solution(13187237408954043467)
XLA Ops:
  0.0 2.6 %payload.1.far_ref = bf16[560,1024]{1,0:T(8,128)(2,1)} custom-call(s32[1]{0:T(128)} %bitcast.22.index_ref, bf16[8,512,1024]{2,1,0:T(8,128)(2,1)} %bitcast.42, bf16[64,512]{1,0:T(8,128)(2,1)} %v_ref.1), custom_call_target="tpu_custom_call" | custom-call | tf_op jit(solution)/shard_map/payload/pallas_call | solution.py:78
  2.6 5.3 %collective-permute-start.2 = (bf16[560,1024]{1,0:T(8,128)(2,1)}, bf16[560,1024]{1,0:T(8,128)(2,1)S(1)}, u32[]{:S(2)}, u32[]{:S(2)}) collective-permute-start(bf16[560,1024]{1,0:T(8,128)(2,1)} %payload.1.far_ref), channel_id=1, source_target_pairs={{0,120},{8,96},{16,104},{24,112},{32,24},{40,0},{48,8},{56,16},{64... | collective-permute-start | bytes 3440648 | tf_op jit(solution)/shard_map/ppermute | solution.py:303
  9.9 9.5 %cells_own.1 = (f32[8,72,512]{2,1,0:T(8,128)}, f32[8,512,128]{2,1,0:T(8,128)}, f32[8,8,512]{2,1,0:T(8,128)}, f32[8,128]{1,0:T(8,128)}) custom-call(s32[8]{0:T(128)} %copy-done.26, s32[8]{0:T(128)} %slice_reduce_fusion.flags_ref, bf16[8,512,1024]{2,1,0:T(8,128)(2,1)} %bitcast.43, bf16[560,1024]{1,0:T(8,128)(2,1)} %payload.1.far_ref), custom_call_target="tpu_custom_call" | custom-call | flops 2147483648 | bytes 13631488 | tf_op jit(solution)/shard_map/cells_own/pallas_call | solution.py:200
  19.4 16.5 %all-gather = bf16[512,512]{1,0:T(8,128)(2,1)} all-gather(bf16[64,512]{1,0:T(8,128)(2,1)S(1)} %copy-done.22), channel_id=2, replica_groups=mesh['row'=16,'col'=8] {'col'}, dimensions={0}, use_global_device_ids=true | all-gather | bytes 589824 | tf_op jit(solution)/shard_map/all_gather | solution.py:352
  38.2 3.2 %collective-permute-start.4 = (bf16[560,1024]{1,0:T(8,128)(2,1)}, bf16[560,1024]{1,0:T(8,128)(2,1)}, u32[]{:S(2)}, u32[]{:S(2)}) collective-permute-start(bf16[560,1024]{1,0:T(8,128)(2,1)} %get-tuple-element.41.refs_2_), channel_id=1, source_target_pairs={{0,24},{8,0},{16,8},{24,16},{32,56},{40,32},{48,40},{56,48},{64,88... | collective-permute-start | bytes 3440648 | tf_op jit(solution)/shard_map/ppermute | solution.py:303
  41.5 1.9 %collective-permute-start.6 = (bf16[560,1024]{1,0:T(8,128)(2,1)}, bf16[560,1024]{1,0:T(8,128)(2,1)S(1)}, u32[]{:S(2)}, u32[]{:S(2)}) collective-permute-start(bf16[560,1024]{1,0:T(8,128)(2,1)} %get-tuple-element.42.refs_0_), channel_id=1, source_target_pairs={{0,8},{24,0},{32,40},{56,32},{64,72},{88,64},{96,104},{120,96},{1,... | collective-permute-start | bytes 3440648 | tf_op jit(solution)/shard_map/ppermute | solution.py:303
  43.4 5.0 %collective-permute-start.5 = (bf16[560,1024]{1,0:T(8,128)(2,1)}, bf16[560,1024]{1,0:T(8,128)(2,1)S(1)}, u32[]{:S(2)}, u32[]{:S(2)}) collective-permute-start(bf16[560,1024]{1,0:T(8,128)(2,1)} %get-tuple-element.42.refs_0_), channel_id=1, source_target_pairs={{0,96},{8,104},{16,112},{24,120},{32,0},{40,8},{48,16},{56,24},{64... | collective-permute-start | bytes 3440648 | tf_op jit(solution)/shard_map/ppermute | solution.py:303
  49.2 11.5 %cells.3 = (f32[8,72,512]{2,1,0:T(8,128)}, bf16[80,512]{1,0:T(8,128)(2,1)}, bf16[80,512]{1,0:T(8,128)(2,1)}, bf16[80,512]{1,0:T(8,128)(2,1)}, f32[8,128]{1,0:T(8,128)}) custom-call(s32[8]{0:T(128)} %copy-done.26, s32[24]{0:T(128)} %reshape.316.flags_ref, bf16[8,512,1024]{2,1,0:T(8,128)(2,1)} %bitcast.44, ...), custom_call_target="tpu_custom_call", output_to_operand_aliasing={{0}: (9, {})} | custom-call | flops 6442450944 | bytes 15728640 | tf_op jit(solution)/shard_map/cells/pallas_call | solution.py:200
  60.7 7.7 %collective-permute-done.3.refs_0_ = bf16[560,1024]{1,0:T(8,128)(2,1)S(1)} collective-permute-done((bf16[560,1024]{1,0:T(8,128)(2,1)}, bf16[560,1024]{1,0:T(8,128)(2,1)S(1)}, u32[]{:S(2)}, u32[]{:S(2)}) %collective-permute-start.3) | collective-permute-done | bytes 1146912 | tf_op jit(solution)/shard_map/ppermute | solution.py:303
  68.4 3.4 %collective-permute-done.6.refs_7_.refs_1_ = bf16[560,1024]{1,0:T(8,128)(2,1)S(1)} collective-permute-done((bf16[560,1024]{1,0:T(8,128)(2,1)}, bf16[560,1024]{1,0:T(8,128)(2,1)S(1)}, u32[]{:S(2)}, u32[]{:S(2)}) %collective-permute-start.6) | collective-permute-done | bytes 1146912 | tf_op jit(solution)/shard_map/ppermute | solution.py:303
  77.5 3.2 %collective-permute-start.9 = (bf16[80,512]{1,0:T(8,128)(2,1)}, bf16[80,512]{1,0:T(8,128)(2,1)S(1)}, u32[]{:S(2)}, u32[]{:S(2)}) collective-permute-start(bf16[80,512]{1,0:T(8,128)(2,1)} %get-tuple-element.56), channel_id=1, source_target_pairs={{8,0},{16,8},{24,16},{0,24},{40,32},{48,40},{56,48},{32,56},{72,64... | collective-permute-start | bytes 245768 | tf_op jit(solution)/shard_map/ppermute | solution.py:349
  80.7 3.3 %collective-permute-start.10 = (bf16[80,512]{1,0:T(8,128)(2,1)}, bf16[80,512]{1,0:T(8,128)(2,1)S(1)}, u32[]{:S(2)}, u32[]{:S(2)}) collective-permute-start(bf16[80,512]{1,0:T(8,128)(2,1)} %get-tuple-element.57), channel_id=1, source_target_pairs={{32,0},{40,8},{48,16},{56,24},{64,32},{72,40},{80,48},{88,56},{96,... | collective-permute-start | bytes 245768 | tf_op jit(solution)/shard_map/ppermute | solution.py:349
  84.0 10.9 %cells.4 = (f32[8,72,512]{2,1,0:T(8,128)}, bf16[80,512]{1,0:T(8,128)(2,1)}, bf16[80,512]{1,0:T(8,128)(2,1)}, bf16[80,512]{1,0:T(8,128)(2,1)}, f32[8,128]{1,0:T(8,128)}) custom-call(s32[8]{0:T(128)} %copy-done.26, s32[24]{0:T(128)} %reshape.317.flags_ref, bf16[8,512,1024]{2,1,0:T(8,128)(2,1)} %bitcast.45, ...), custom_call_target="tpu_custom_call", output_to_operand_aliasing={{0}: (9, {})} | custom-call | flops 6442450944 | bytes 15728640 | tf_op jit(solution)/shard_map/cells/pallas_call | solution.py:200
  95.0 9.8 %collective-permute-done.10.refs_6_ = bf16[80,512]{1,0:T(8,128)(2,1)S(1)} collective-permute-done((bf16[80,512]{1,0:T(8,128)(2,1)}, bf16[80,512]{1,0:T(8,128)(2,1)S(1)}, u32[]{:S(2)}, u32[]{:S(2)}) %collective-permute-start.10) | collective-permute-done | bytes 81952 | tf_op jit(solution)/shard_map/ppermute | solution.py:349
  104.8 2.6 %collective-permute-done.11.refs_7_ = bf16[80,512]{1,0:T(8,128)(2,1)S(1)} collective-permute-done((bf16[80,512]{1,0:T(8,128)(2,1)}, bf16[80,512]{1,0:T(8,128)(2,1)S(1)}, u32[]{:S(2)}, u32[]{:S(2)}) %collective-permute-start.11) | collective-permute-done | bytes 81952 | tf_op jit(solution)/shard_map/ppermute | solution.py:349
  108.9 2.1 %collective-permute-start.12 = (bf16[80,512]{1,0:T(8,128)(2,1)}, bf16[80,512]{1,0:T(8,128)(2,1)S(1)}, u32[]{:S(2)}, u32[]{:S(2)}) collective-permute-start(bf16[80,512]{1,0:T(8,128)(2,1)} %get-tuple-element.66), channel_id=1, source_target_pairs={{104,0},{112,8},{120,16},{96,24},{8,32},{16,40},{24,48},{0,56},{40... | collective-permute-start | bytes 245768 | tf_op jit(solution)/shard_map/ppermute | solution.py:349
  111.4 4.4 %collective-permute-start.14 = (bf16[80,512]{1,0:T(8,128)(2,1)}, bf16[80,512]{1,0:T(8,128)(2,1)S(1)}, u32[]{:S(2)}, u32[]{:S(2)}) collective-permute-start(bf16[80,512]{1,0:T(8,128)(2,1)} %get-tuple-element.68), channel_id=1, source_target_pairs={{0,64},{8,72},{16,80},{24,88},{32,96},{40,104},{48,112},{56,120},{... | collective-permute-start | bytes 245768 | tf_op jit(solution)/shard_map/ppermute | solution.py:349
  115.7 9.8 %cells.5 = (f32[8,72,512]{2,1,0:T(8,128)}, bf16[80,512]{1,0:T(8,128)(2,1)}, bf16[80,512]{1,0:T(8,128)(2,1)}, bf16[80,512]{1,0:T(8,128)(2,1)}, f32[8,128]{1,0:T(8,128)}) custom-call(s32[8]{0:T(128)} %copy-done.26, s32[24]{0:T(128)} %reshape.314.flags_ref, bf16[8,512,1024]{2,1,0:T(8,128)(2,1)} %bitcast.46, ...), custom_call_target="tpu_custom_call", output_to_operand_aliasing={{0}: (9, {})} | custom-call | flops 6442450944 | bytes 15728640 | tf_op jit(solution)/shard_map/cells/pallas_call | solution.py:200
  127.6 2.4 %collective-permute-start.19 = (bf16[80,512]{1,0:T(8,128)(2,1)}, bf16[80,512]{1,0:T(8,128)(2,1)S(1)}, u32[]{:S(2)}, u32[]{:S(2)}) collective-permute-start(bf16[80,512]{1,0:T(8,128)(2,1)} %get-tuple-element.70), channel_id=1, source_target_pairs={{72,0},{80,8},{88,16},{64,24},{104,32},{112,40},{120,48},{96,56},{... | collective-permute-start | bytes 245768 | tf_op jit(solution)/shard_map/ppermute | solution.py:349
  131.8 2.8 %collective-permute-start.18 = (f32[72,512]{1,0:T(8,128)S(1)}, f32[72,512]{1,0:T(8,128)S(1)}, u32[]{:S(2)}, u32[]{:S(2)}) collective-permute-start(f32[72,512]{1,0:T(8,128)S(1)} %get-tuple-element.76), channel_id=1, source_target_pairs={{0,2},{1,3},{2,4},{3,5},{4,6},{5,7},{6,0},{7,1},{8,10},{9,11},{10,... | collective-permute-start | bytes 442376 | tf_op jit(solution)/shard_map/ppermute | solution.py:306
  135.0 5.1 %collective-permute-start.20 = (bf16[80,512]{1,0:T(8,128)(2,1)S(1)}, bf16[80,512]{1,0:T(8,128)(2,1)S(1)}, u32[]{:S(2)}, u32[]{:S(2)}) collective-permute-start(bf16[80,512]{1,0:T(8,128)(2,1)S(1)} %copy-done.23), channel_id=1, source_target_pairs={{0,16},{8,24},{32,48},{40,56},{64,80},{72,88},{96,112},{104,120},{... | collective-permute-start | bytes 245768 | tf_op jit(solution)/shard_map/ppermute | solution.py:349
  150.0 3.2 %collective-permute-done.24 = f32[64,64]{1,0:T(8,128)S(1)} collective-permute-done((f32[64,64]{1,0:T(8,128)S(1)}, f32[64,64]{1,0:T(8,128)S(1)}, u32[]{:S(2)}, u32[]{:S(2)}) %collective-permute-start.24) | collective-permute-done | bytes 16416 | tf_op jit(solution)/shard_map/ppermute | solution.py:306
  154.6 25.0 %all_to_all.5 = f32[16,1,4096]{2,1,0:T(1,128)S(1)} all-to-all(f32[16,1,4096]{2,1,0:T(1,128)S(1)} %reshape.322), channel_id=1, replica_groups=mesh['row'=16,'col'=8] {'row'}, dimensions={0} | all-to-all | bytes 524288 | tf_op jit(solution)/shard_map/all_to_all | solution.py:389
  182.2 5.0 %solve.1 = f32[64,512]{1,0:T(8,128)} custom-call(f32[64,64]{1,0:T(8,128)} %reduce_sum.9.gram_ref, f32[64,512]{1,0:T(8,128)} %copy-done.1), custom_call_target="tpu_custom_call" | custom-call | tf_op jit(solution)/shard_map/solve/pallas_call | solution.py:287
  (145 shorter events, 30.4 us)
Async XLA Ops:
  2.6 33.3 %collective-permute-start.2 = (bf16[560,1024]{1,0:T(8,128)(2,1)}, bf16[560,1024]{1,0:T(8,128)(2,1)S(1)}, u32[]{:S(2)}, u32[]{:S(2)}) collective-permute-start(bf16[560,1024]{1,0:T(8,128)(2,1)} %payload.1.far_ref), channel_id=1, source_target_pairs={{0,120},{8,96},{16,104},{24,112},{32,24},{40,0},{48,8},{56,16},{64... | collective-permute-start | bytes 3440648 | tf_op jit(solution)/shard_map/ppermute | solution.py:303
  7.9 28.1 %collective-permute-start.1 = (bf16[560,1024]{1,0:T(8,128)(2,1)}, bf16[560,1024]{1,0:T(8,128)(2,1)S(1)}, u32[]{:S(2)}, u32[]{:S(2)}) collective-permute-start(bf16[560,1024]{1,0:T(8,128)(2,1)} %payload.1.far_ref), channel_id=1, source_target_pairs={{0,32},{8,40},{16,48},{24,56},{32,64},{40,72},{48,80},{56,88},{64,... | collective-permute-start | bytes 3440648 | tf_op jit(solution)/shard_map/ppermute | solution.py:303
  7.9 28.1 %collective-permute-start = (bf16[560,1024]{1,0:T(8,128)(2,1)}, bf16[560,1024]{1,0:T(8,128)(2,1)S(1)}, u32[]{:S(2)}, u32[]{:S(2)}) collective-permute-start(bf16[560,1024]{1,0:T(8,128)(2,1)} %payload.1.far_ref), channel_id=1, source_target_pairs={{0,8},{8,16},{16,24},{24,0},{32,40},{40,48},{48,56},{56,32},{64,72... | collective-permute-start | bytes 3440648 | tf_op jit(solution)/shard_map/ppermute | solution.py:303
  37.7 30.7 %collective-permute-start.3 = (bf16[560,1024]{1,0:T(8,128)(2,1)}, bf16[560,1024]{1,0:T(8,128)(2,1)S(1)}, u32[]{:S(2)}, u32[]{:S(2)}) collective-permute-start(bf16[560,1024]{1,0:T(8,128)(2,1)} %get-tuple-element.40.refs_1_), channel_id=1, source_target_pairs={{0,32},{8,40},{16,48},{24,56},{32,64},{40,72},{48,80},{56,88},{64,... | collective-permute-start | bytes 3440648 | tf_op jit(solution)/shard_map/ppermute | solution.py:303
  38.2 30.1 %collective-permute-start.4 = (bf16[560,1024]{1,0:T(8,128)(2,1)}, bf16[560,1024]{1,0:T(8,128)(2,1)}, u32[]{:S(2)}, u32[]{:S(2)}) collective-permute-start(bf16[560,1024]{1,0:T(8,128)(2,1)} %get-tuple-element.41.refs_2_), channel_id=1, source_target_pairs={{0,24},{8,0},{16,8},{24,16},{32,56},{40,32},{48,40},{56,48},{64,88... | collective-permute-start | bytes 3440648 | tf_op jit(solution)/shard_map/ppermute | solution.py:303
  41.5 30.3 %collective-permute-start.6 = (bf16[560,1024]{1,0:T(8,128)(2,1)}, bf16[560,1024]{1,0:T(8,128)(2,1)S(1)}, u32[]{:S(2)}, u32[]{:S(2)}) collective-permute-start(bf16[560,1024]{1,0:T(8,128)(2,1)} %get-tuple-element.42.refs_0_), channel_id=1, source_target_pairs={{0,8},{24,0},{32,40},{56,32},{64,72},{88,64},{96,104},{120,96},{1,... | collective-permute-start | bytes 3440648 | tf_op jit(solution)/shard_map/ppermute | solution.py:303
  43.4 30.0 %collective-permute-start.5 = (bf16[560,1024]{1,0:T(8,128)(2,1)}, bf16[560,1024]{1,0:T(8,128)(2,1)S(1)}, u32[]{:S(2)}, u32[]{:S(2)}) collective-permute-start(bf16[560,1024]{1,0:T(8,128)(2,1)} %get-tuple-element.42.refs_0_), channel_id=1, source_target_pairs={{0,96},{8,104},{16,112},{24,120},{32,0},{40,8},{48,16},{56,24},{64... | collective-permute-start | bytes 3440648 | tf_op jit(solution)/shard_map/ppermute | solution.py:303
  74.5 32.9 %collective-permute-start.7 = (bf16[560,1024]{1,0:T(8,128)(2,1)}, bf16[560,1024]{1,0:T(8,128)(2,1)S(1)}, u32[]{:S(2)}, u32[]{:S(2)}) collective-permute-start(bf16[560,1024]{1,0:T(8,128)(2,1)} %get-tuple-element.50.refs_2_), channel_id=1, source_target_pairs={{0,8},{8,16},{16,24},{24,0},{32,40},{40,48},{48,56},{56,32},{64,72... | collective-permute-start | bytes 3440648 | tf_op jit(solution)/shard_map/ppermute | solution.py:303
  74.5 32.9 %collective-permute-start.8 = (bf16[560,1024]{1,0:T(8,128)(2,1)}, bf16[560,1024]{1,0:T(8,128)(2,1)S(1)}, u32[]{:S(2)}, u32[]{:S(2)}) collective-permute-start(bf16[560,1024]{1,0:T(8,128)(2,1)} %get-tuple-element.51.refs_1_), channel_id=1, source_target_pairs={{32,0},{40,8},{48,16},{56,24},{64,32},{72,40},{80,48},{88,56},{33,... | collective-permute-start | bytes 3440648 | tf_op jit(solution)/shard_map/ppermute | solution.py:303
  77.5 17.5 %collective-permute-start.9 = (bf16[80,512]{1,0:T(8,128)(2,1)}, bf16[80,512]{1,0:T(8,128)(2,1)S(1)}, u32[]{:S(2)}, u32[]{:S(2)}) collective-permute-start(bf16[80,512]{1,0:T(8,128)(2,1)} %get-tuple-element.56), channel_id=1, source_target_pairs={{8,0},{16,8},{24,16},{0,24},{40,32},{48,40},{56,48},{32,56},{72,64... | collective-permute-start | bytes 245768 | tf_op jit(solution)/shard_map/ppermute | solution.py:349
  80.7 24.1 %collective-permute-start.10 = (bf16[80,512]{1,0:T(8,128)(2,1)}, bf16[80,512]{1,0:T(8,128)(2,1)S(1)}, u32[]{:S(2)}, u32[]{:S(2)}) collective-permute-start(bf16[80,512]{1,0:T(8,128)(2,1)} %get-tuple-element.57), channel_id=1, source_target_pairs={{32,0},{40,8},{48,16},{56,24},{64,32},{72,40},{80,48},{88,56},{96,... | collective-permute-start | bytes 245768 | tf_op jit(solution)/shard_map/ppermute | solution.py:349
  84.0 23.4 %collective-permute-start.11 = (bf16[80,512]{1,0:T(8,128)(2,1)}, bf16[80,512]{1,0:T(8,128)(2,1)S(1)}, u32[]{:S(2)}, u32[]{:S(2)}) collective-permute-start(bf16[80,512]{1,0:T(8,128)(2,1)} %get-tuple-element.58), channel_id=1, source_target_pairs={{120,0},{96,8},{104,16},{112,24},{24,32},{0,40},{8,48},{16,56},{56... | collective-permute-start | bytes 245768 | tf_op jit(solution)/shard_map/ppermute | solution.py:349
  108.9 16.7 %collective-permute-start.12 = (bf16[80,512]{1,0:T(8,128)(2,1)}, bf16[80,512]{1,0:T(8,128)(2,1)S(1)}, u32[]{:S(2)}, u32[]{:S(2)}) collective-permute-start(bf16[80,512]{1,0:T(8,128)(2,1)} %get-tuple-element.66), channel_id=1, source_target_pairs={{104,0},{112,8},{120,16},{96,24},{8,32},{16,40},{24,48},{0,56},{40... | collective-permute-start | bytes 245768 | tf_op jit(solution)/shard_map/ppermute | solution.py:349
  111.0 14.6 %collective-permute-start.13 = (bf16[80,512]{1,0:T(8,128)(2,1)}, bf16[80,512]{1,0:T(8,128)(2,1)S(1)}, u32[]{:S(2)}, u32[]{:S(2)}) collective-permute-start(bf16[80,512]{1,0:T(8,128)(2,1)} %get-tuple-element.67), channel_id=1, source_target_pairs={{112,0},{120,8},{96,16},{104,24},{16,32},{24,40},{0,48},{8,56},{48... | collective-permute-start | bytes 245768 | tf_op jit(solution)/shard_map/ppermute | solution.py:349
  111.4 14.3 %collective-permute-start.14 = (bf16[80,512]{1,0:T(8,128)(2,1)}, bf16[80,512]{1,0:T(8,128)(2,1)S(1)}, u32[]{:S(2)}, u32[]{:S(2)}) collective-permute-start(bf16[80,512]{1,0:T(8,128)(2,1)} %get-tuple-element.68), channel_id=1, source_target_pairs={{0,64},{8,72},{16,80},{24,88},{32,96},{40,104},{48,112},{56,120},{... | collective-permute-start | bytes 245768 | tf_op jit(solution)/shard_map/ppermute | solution.py:349
  127.6 12.5 %collective-permute-start.19 = (bf16[80,512]{1,0:T(8,128)(2,1)}, bf16[80,512]{1,0:T(8,128)(2,1)S(1)}, u32[]{:S(2)}, u32[]{:S(2)}) collective-permute-start(bf16[80,512]{1,0:T(8,128)(2,1)} %get-tuple-element.70), channel_id=1, source_target_pairs={{72,0},{80,8},{88,16},{64,24},{104,32},{112,40},{120,48},{96,56},{... | collective-permute-start | bytes 245768 | tf_op jit(solution)/shard_map/ppermute | solution.py:349
  130.2 13.7 %collective-permute-start.17 = (f32[72,512]{1,0:T(8,128)S(1)}, f32[72,512]{1,0:T(8,128)S(1)}, u32[]{:S(2)}, u32[]{:S(2)}) collective-permute-start(f32[72,512]{1,0:T(8,128)S(1)} %get-tuple-element.75), channel_id=1, source_target_pairs={{0,4},{1,5},{2,6},{3,7},{4,0},{5,1},{6,2},{7,3},{8,12},{9,13},{10,... | collective-permute-start | bytes 442376 | tf_op jit(solution)/shard_map/ppermute | solution.py:306
  131.8 12.2 %collective-permute-start.18 = (f32[72,512]{1,0:T(8,128)S(1)}, f32[72,512]{1,0:T(8,128)S(1)}, u32[]{:S(2)}, u32[]{:S(2)}) collective-permute-start(f32[72,512]{1,0:T(8,128)S(1)} %get-tuple-element.76), channel_id=1, source_target_pairs={{0,2},{1,3},{2,4},{3,5},{4,6},{5,7},{6,0},{7,1},{8,10},{9,11},{10,... | collective-permute-start | bytes 442376 | tf_op jit(solution)/shard_map/ppermute | solution.py:306
  134.6 9.4 %collective-permute-start.16 = (f32[72,512]{1,0:T(8,128)S(1)}, f32[72,512]{1,0:T(8,128)S(1)}, u32[]{:S(2)}, u32[]{:S(2)}) collective-permute-start(f32[72,512]{1,0:T(8,128)S(1)} %get-tuple-element.77), channel_id=1, source_target_pairs={{0,6},{1,7},{2,0},{3,1},{4,2},{5,3},{6,4},{7,5},{8,14},{9,15},{10,... | collective-permute-start | bytes 442376 | tf_op jit(solution)/shard_map/ppermute | solution.py:306
  135.0 7.7 %collective-permute-start.20 = (bf16[80,512]{1,0:T(8,128)(2,1)S(1)}, bf16[80,512]{1,0:T(8,128)(2,1)S(1)}, u32[]{:S(2)}, u32[]{:S(2)}) collective-permute-start(bf16[80,512]{1,0:T(8,128)(2,1)S(1)} %copy-done.23), channel_id=1, source_target_pairs={{0,16},{8,24},{32,48},{40,56},{64,80},{72,88},{96,112},{104,120},{... | collective-permute-start | bytes 245768 | tf_op jit(solution)/shard_map/ppermute | solution.py:349
  140.2 3.8 %collective-permute-start.21 = (bf16[80,512]{1,0:T(8,128)(2,1)S(1)}, bf16[80,512]{1,0:T(8,128)(2,1)S(1)}, u32[]{:S(2)}, u32[]{:S(2)}) collective-permute-start(bf16[80,512]{1,0:T(8,128)(2,1)S(1)} %copy-done.24), channel_id=1, source_target_pairs={{16,64},{24,72},{0,80},{8,88},{48,96},{56,104},{32,112},{40,120},{... | collective-permute-start | bytes 245768 | tf_op jit(solution)/shard_map/ppermute | solution.py:349
  145.8 4.2 %collective-permute-start.25 = (f32[64,64]{1,0:T(8,128)S(1)}, f32[64,64]{1,0:T(8,128)S(1)}, u32[]{:S(2)}, u32[]{:S(2)}) collective-permute-start(f32[64,64]{1,0:T(8,128)S(1)} %add.376), channel_id=1, source_target_pairs={{0,6},{1,7},{2,0},{3,1},{4,2},{5,3},{6,4},{7,5},{8,14},{9,15},{10,... | collective-permute-start | bytes 49160 | tf_op jit(solution)/shard_map/ppermute | solution.py:306
  147.6 5.5 %collective-permute-start.24 = (f32[64,64]{1,0:T(8,128)S(1)}, f32[64,64]{1,0:T(8,128)S(1)}, u32[]{:S(2)}, u32[]{:S(2)}) collective-permute-start(f32[64,64]{1,0:T(8,128)S(1)} %add.376), channel_id=1, source_target_pairs={{0,4},{1,5},{2,6},{3,7},{4,0},{5,1},{6,2},{7,3},{8,12},{9,13},{10,... | collective-permute-start | bytes 49160 | tf_op jit(solution)/shard_map/ppermute | solution.py:306
  149.1 5.1 %collective-permute-start.23 = (f32[64,64]{1,0:T(8,128)S(1)}, f32[64,64]{1,0:T(8,128)S(1)}, u32[]{:S(2)}, u32[]{:S(2)}) collective-permute-start(f32[64,64]{1,0:T(8,128)S(1)} %add.376), channel_id=1, source_target_pairs={{0,2},{1,3},{2,4},{3,5},{4,6},{5,7},{6,0},{7,1},{8,10},{9,11},{10,... | collective-permute-start | bytes 49160 | tf_op jit(solution)/shard_map/ppermute | solution.py:306
  (29 other events, 192.9 us)

commit v7 on v6

--- a/solution.py
+++ b/solution.py
@@ -106,7 +106,7 @@
     return jnp.concatenate([columns, columns], axis=1)
 
 
-def own_kernel(order_ref, flags_ref, x_ref, far_ref, new_ref, norm_ref, row_ref, token_ref, p_ref):
+def own_kernel(flags_ref, x_ref, far_ref, new_ref, norm_ref, row_ref, token_ref, p_ref):
     step = pl.program_id(0)
     new_ref[...] = jnp.zeros_like(new_ref)
     token_ref[...] = jnp.zeros_like(token_ref)
@@ -127,109 +127,160 @@
         new_ref[0] = part[0:ACC, :]
 
 
-def cells_kernel(count, order_ref, flags_ref, x_ref, near_v_ref, *refs):
-    far_refs, refs = refs[:count], refs[count:]
-    norm_ref, row_ref, old_ref, new_ref, refs = refs[0], refs[1], refs[2], refs[3], refs[4:]
-    sent_refs, token_ref, (p_ref, column_ref, far_sums_ref) = refs[:count], refs[count], refs[count + 1 :]
-    step = pl.program_id(0)
-
-    @pl.when(step == 0)
-    def _():
-        token_ref[...] = jnp.zeros_like(token_ref)
-        far_sums_ref[...] = jnp.zeros_like(far_sums_ref)
-        for at in range(count):
-            column_ref[at] = jnp.broadcast_to(side_norms(far_refs[at][BLOCK:PAYLOAD, :]), (128, BLOCK)).T
-
-    new_ref[...] = old_ref[...]
-
-    def forward_only(at):
-        far_ref = far_refs[at]
-        near, far = row_ref[0, 0:1, :], double(column_ref[at])
+def cells_kernel(count, flags_ref, x_hbm, v_hbm, *refs):
+    far_hbms, (norm_hbm, row_hbm, old_hbm, new_hbm), refs = refs[:count], refs[count : count + 4], refs[count + 4 :]
+    sent_refs, token_ref, refs = refs[:count], refs[count], refs[count + 1 :]
+    x_ref, v_ref, far_ref, norm_ref, row_ref, old_ref, sums_ref, p_ref, column_ref, far_sums_ref = refs[:10]
+    near_sem, far_sem, sem = refs[10:]
+
+    def near_copies(near):
+        pairs = ((x_hbm, x_ref), (norm_hbm, norm_ref), (v_hbm, v_ref))
+        return [
+            pltpu.make_async_copy(source.at[near], to.at[near], near_sem.at[at, near])
+            for at, (source, to) in enumerate(pairs)
+        ]
+
+    far_copies = [pltpu.make_async_copy(far_hbms[at], far_ref.at[at], far_sem.at[at]) for at in range(count)]
+    row_copy = pltpu.make_async_copy(row_hbm, row_ref, sem.at[0])
+    old_copy = pltpu.make_async_copy(old_hbm, old_ref, sem.at[1])
+    for copy in (far_copies[0], *near_copies(0), row_copy, *far_copies[1:], *near_copies(1), old_copy):
+        copy.start()
+
+    token_ref[...] = jnp.zeros_like(token_ref)
+    far_sums_ref[...] = jnp.zeros_like(far_sums_ref)
+    sums_ref[...] = jnp.zeros_like(sums_ref)
+
+    def forward_only(at, near):
+        rows, far = row_ref[near, 0:1, :], double(column_ref[at])
         for to in range(0, BLOCK, 256):
             scores = lax.dot_general(
-                far_ref[0:BLOCK, :], x_ref[0, to : to + 256, :], NT, preferred_element_type=jnp.float32
+                far_ref[at, 0:BLOCK, :], x_ref[near, to : to + 256, :], NT, preferred_element_type=jnp.float32
             )
-            p_ref[:, to : to + 256] = jnp.exp2(scores * near[:, to : to + 256] * far).astype(jnp.bfloat16)
-        part = jnp.dot(side_vectors(far_ref[BLOCK:PAYLOAD, :]), p_ref[...], preferred_element_type=jnp.float32)
-        new_ref[0] += part[0:ACC, :]
-
-    def backward(at, both):
-        far_ref = far_refs[at]
-        side = far_ref[BLOCK:PAYLOAD, :]
-        near, far = double(norm_ref[0]), side_norms(side)
+            p_ref[:, to : to + 256] = jnp.exp2(scores * rows[:, to : to + 256] * far).astype(jnp.bfloat16)
+        part = jnp.dot(side_vectors(far_ref[at, BLOCK:PAYLOAD, :]), p_ref[...], preferred_element_type=jnp.float32)
+        sums_ref[near] += part[0:ACC, :]
+
+    def backward(at, near, both):
+        side = far_ref[at, BLOCK:PAYLOAD, :]
+        columns, far = double(norm_ref[near]), side_norms(side)
         for to in range(0, BLOCK, 256):
             scores = lax.dot_general(
-                x_ref[0], far_ref[to : to + 256, :], NT, preferred_element_type=jnp.float32
+                x_ref[near], far_ref[at, to : to + 256, :], NT, preferred_element_type=jnp.float32
             )
-            p_ref[:, to : to + 256] = jnp.exp2(scores * near * far[:, to : to + 256]).astype(jnp.bfloat16)
-        vectors = jnp.concatenate([near_v_ref[0], jnp.ones((16, BLOCK), jnp.bfloat16)], axis=0)
+            p_ref[:, to : to + 256] = jnp.exp2(scores * columns * far[:, to : to + 256]).astype(jnp.bfloat16)
+        vectors = jnp.concatenate([v_ref[near], jnp.ones((16, BLOCK), jnp.bfloat16)], axis=0)
         part = jnp.dot(vectors, p_ref[...], preferred_element_type=jnp.float32)
         far_sums_ref[at] += part[0:ACC, :]
         if both:
             part = lax.dot_general(side_vectors(side), p_ref[...], NT, preferred_element_type=jnp.float32)
-            new_ref[0] += part[0:ACC, :]
-
+            sums_ref[near] += part[0:ACC, :]
+
+    @pl.loop(0, COLS)
+    def _(near):
+        @pl.when(near + 2 < COLS)
+        def _():
+            for copy in near_copies(near + 2):
+                copy.start()
+
+        for copy in near_copies(near):
+            copy.wait()
+        for at in range(count):
+
+            @pl.when(near == 0)
+            def _():
+                if at == 0:
+                    row_copy.wait()
+                far_copies[at].wait()
+                column_ref[at] = jnp.broadcast_to(side_norms(far_ref[at, BLOCK:PAYLOAD, :]), (128, BLOCK)).T
+
+            flag = flags_ref[at * COLS + near]
+            pl.when(flag == 1)(functools.partial(forward_only, at, near))
+            pl.when(flag == 2)(functools.partial(backward, at, near, False))
+            pl.when(flag == 3)(functools.partial(backward, at, near, True))
+
+    old_copy.wait()
+    sums_ref[...] += old_ref[...]
+    out_copy = pltpu.make_async_copy(sums_ref, new_hbm, sem.at[0])
+    out_copy.start()
     for at in range(count):
-        flag = flags_ref[at * COLS + step]
-        pl.when(flag == 1)(functools.partial(forward_only, at))
-        pl.when(flag == 2)(functools.partial(backward, at, False))
-        pl.when(flag == 3)(functools.partial(backward, at, True))
-
-    @pl.when(step == COLS - 1)
-    def _():
-        for at in range(count):
-            degrees = far_sums_ref[at, EIGS:ACC, :]
-            high = degrees.astype(jnp.bfloat16).astype(jnp.float32)
-            sent = jnp.concatenate([far_sums_ref[at, 0:EIGS, :], high, degrees - high], axis=0)
-            sent_refs[at][...] = sent.astype(jnp.bfloat16)
-
-
-NEAR = lambda g, order, flags: (order[g], 0, 0)
-STEP = lambda g, order, flags: (g, 0, 0)
-WHOLE = lambda g, order, flags: (0, 0)
-X_SPEC = pl.BlockSpec((1, BLOCK, WIDTH), NEAR)
-FAR_SPEC = pl.BlockSpec((PAYLOAD, WIDTH), WHOLE)
-NORM = (pl.BlockSpec((1, BLOCK, 128), STEP), (COLS, BLOCK, 128), jnp.float32)
-ROW = (pl.BlockSpec((1, 8, BLOCK), STEP), (COLS, 8, BLOCK), jnp.float32)
-SUMS = (pl.BlockSpec((1, ACC, BLOCK), STEP), (COLS, ACC, BLOCK), jnp.float32)
-PART = (pl.BlockSpec((SENT, BLOCK), WHOLE), (SENT, BLOCK), jnp.bfloat16)
-TOKEN = (pl.BlockSpec((8, 128), WHOLE), (8, 128), jnp.float32)
-
-
-def cells_call(kernel, count, ins, outs, scratch, aliases, name, args):
+        degrees = far_sums_ref[at, EIGS:ACC, :]
+        high = degrees.astype(jnp.bfloat16).astype(jnp.float32)
+        sent = jnp.concatenate([far_sums_ref[at, 0:EIGS, :], high, degrees - high], axis=0)
+        sent_refs[at][...] = sent.astype(jnp.bfloat16)
+    out_copy.wait()
+
+
+SUMS = jax.ShapeDtypeStruct((COLS, ACC, BLOCK), jnp.float32)
+NORM = jax.ShapeDtypeStruct((COLS, BLOCK, 128), jnp.float32)
+ROW = jax.ShapeDtypeStruct((COLS, 8, BLOCK), jnp.float32)
+TOKEN = jax.ShapeDtypeStruct((8, 128), jnp.float32)
+SENT_SHAPE = jax.ShapeDtypeStruct((SENT, BLOCK), jnp.bfloat16)
+
+
+def block_of(shape):
+    return pl.BlockSpec((1, *shape[1:]), lambda g, flags: (g, 0, 0))
+
+
+def whole(shape):
+    return pl.BlockSpec(shape, lambda g, flags: (0, 0))
+
+
+def own_cells(flags, blocks, far):
     return pl.pallas_call(
-        kernel,
-        out_shape=[jax.ShapeDtypeStruct(shape, dtype) for _, shape, dtype in outs],
+        own_kernel,
+        out_shape=[SUMS, NORM, ROW, TOKEN],
         grid_spec=pltpu.PrefetchScalarGridSpec(
-            num_scalar_prefetch=2, grid=(COLS,), in_specs=ins, out_specs=[spec for spec, _, _ in outs], scratch_shapes=scratch
+            num_scalar_prefetch=1,
+            grid=(COLS,),
+            in_specs=[block_of(blocks.shape), whole(far.shape)],
+            out_specs=[block_of(SUMS.shape), block_of(NORM.shape), block_of(ROW.shape), whole(TOKEN.shape)],
+            scratch_shapes=[pltpu.VMEM((BLOCK, BLOCK), jnp.bfloat16)],
         ),
-        input_output_aliases=aliases,
         compiler_params=pltpu.CompilerParams(vmem_limit_bytes=56 << 20),
-        cost_estimate=pl.CostEstimate(
-            flops=count * COST * BLOCK * BLOCK * WIDTH,
-            bytes_accessed=(12 + count) << 20,
-            transcendentals=count * 4 * BLOCK * BLOCK,
+        cost_estimate=estimate(1),
+        name="cells_own",
+    )(flags, blocks, far)
+
+
+def estimate(count):
+    return pl.CostEstimate(
+        flops=count * COST * BLOCK * BLOCK * WIDTH,
+        bytes_accessed=(12 + count) << 20,
+        transcendentals=count * 4 * BLOCK * BLOCK,
+    )
+
+
+def cells(flags, blocks, near_v, fars, norms, rows, sums):
+    count = len(fars)
+    buffers = [
+        ((COLS, BLOCK, WIDTH), jnp.bfloat16),
+        ((COLS, EIGS, BLOCK), jnp.bfloat16),
+        ((count, PAYLOAD, WIDTH), jnp.bfloat16),
+        ((COLS, BLOCK, 128), jnp.float32),
+        ((COLS, 8, BLOCK), jnp.float32),
+        ((COLS, ACC, BLOCK), jnp.float32),
+        ((COLS, ACC, BLOCK), jnp.float32),
+        ((BLOCK, BLOCK), jnp.bfloat16),
+        ((count, BLOCK, 128), jnp.float32),
+        ((count, ACC, BLOCK), jnp.float32),
+    ]
+    in_place = pl.BlockSpec(memory_space=pltpu.HBM)
+    result = pl.pallas_call(
+        functools.partial(cells_kernel, count),
+        out_shape=[SUMS] + [SENT_SHAPE] * count + [TOKEN],
+        grid_spec=pltpu.PrefetchScalarGridSpec(
+            num_scalar_prefetch=1,
+            grid=(1,),
+            in_specs=[in_place] * (5 + count),
+            out_specs=[in_place] + [whole(SENT_SHAPE.shape)] * count + [whole(TOKEN.shape)],
+            scratch_shapes=[pltpu.VMEM(*buffer) for buffer in buffers]
+            + [pltpu.SemaphoreType.DMA(size) for size in ((3, COLS), (count,), (2,))],
         ),
-        name=name,
-    )(*args)
-
-
-SCORES = pltpu.VMEM((BLOCK, BLOCK), jnp.bfloat16)
-
-
-def own_cells(order, flags, blocks, far):
-    ins, outs = [X_SPEC, FAR_SPEC], [SUMS, NORM, ROW, TOKEN]
-    return cells_call(own_kernel, 1, ins, outs, [SCORES], {}, "cells_own", (order, flags, blocks, far))
-
-
-def cells(order, flags, blocks, near_v, fars, norms, rows, sums):
-    count = len(fars)
-    ins = [X_SPEC, pl.BlockSpec((1, EIGS, BLOCK), NEAR)] + [FAR_SPEC] * count + [NORM[0], ROW[0], SUMS[0]]
-    outs = [SUMS] + [PART] * count + [TOKEN]
-    scratch = [SCORES] + [pltpu.VMEM((count, *shape), jnp.float32) for shape in ((BLOCK, 128), (ACC, BLOCK))]
-    args = (order, flags, blocks, near_v, *fars, norms, rows, sums)
-    kernel = functools.partial(cells_kernel, count)
-    result = cells_call(kernel, count, ins, outs, scratch, {6 + count: 0}, "cells", args)
+        input_output_aliases={5 + count: 0},
+        compiler_params=pltpu.CompilerParams(vmem_limit_bytes=56 << 20),
+        cost_estimate=estimate(count),
+        name="cells",
+    )(flags, blocks, near_v, *fars, norms, rows, sums)
     return result[0], result[1:-1], result[-1]
 
 
@@ -312,15 +363,13 @@
     far["a"] = move(far["own"], 0, 1)
     far["b"] = move(far["own"], 1, 0)
     far["c"] = move(far["own"], -1, -1)
-    order = jnp.stack([(here_col - CORES * k) % COLS ^ core for core in range(CORES) for k in range(SIDE)])
-
     far_ids, works = [], []
     for (dy, dx), keep in STAGES.values():
         from_row = (here_y - dy) % SIDE * SIDE + (here_x - dx) % SIDE
         far_ids.append(from_row * COLS + here_col)
         works.append(jnp.broadcast_to(True if keep is None else keep(here_y, here_x), (COLS,)))
     far_ids = jnp.stack(far_ids)[:, None]
-    near_ids = (here_row * COLS + order)[None, :]
+    near_ids = (here_row * COLS + jnp.arange(COLS, dtype=jnp.int32))[None, :]
     wanted = jnp.stack([near_ids * NBLOCKS + far_ids, far_ids * NBLOCKS + near_ids])
     listed = block_pairs[:, 0] * NBLOCKS + block_pairs[:, 1]
     found = jnp.any(wanted[..., None] == listed, axis=-1)
@@ -332,7 +381,6 @@
     def work(group, sums):
         at = starts[group[0]]
         return cells(
-            order,
             flags[at : at + len(group)].reshape(-1),
             blocks,
             near_v,
@@ -350,7 +398,7 @@
         return returned
 
     near_v = lax.all_gather(vectors, "col")
-    sums, norms, rows, token = own_cells(order, flags[0], blocks, far["own"])
+    sums, norms, rows, token = own_cells(flags[0], blocks, far["own"])
 
     far["a"], far["b"], far["c"] = tie([far["a"], far["b"], far["c"]], token, near_v)
     far["d"] = move(far["a"], -1, 0)
@@ -373,8 +421,12 @@
     sums, *parts = tie([sums, *parts], *returned2)
     returned = returned1 + returned2 + give_back(group3, parts)
 
-    kept = sums[:SIDE] + swap(sums[SIDE:])
-    summed = kept[0] + (turn(kept[1], 3) + turn(kept[2], 2) + turn(kept[3], 1))
+    layer, core = here_col // CORES, here_col % CORES
+    halves = sums.reshape(SIDE, CORES, ACC, BLOCK)
+    mine = lax.dynamic_index_in_dim(halves, core, 1, keepdims=False)
+    kept = mine + swap(lax.dynamic_index_in_dim(halves, 1 - core, 1, keepdims=False))
+    layers = [lax.dynamic_index_in_dim(kept, (layer - k) % SIDE, 0, keepdims=False) for k in range(SIDE)]
+    summed = layers[0] + (turn(layers[1], 3) + turn(layers[2], 2) + turn(layers[3], 1))
     totals, degrees = summed[0:EIGS], summed[EIGS : EIGS + 1]
     for part in returned:
         part = part.astype(jnp.float32)

time: 188 us -> 190 us (1.011)
  Pallas kernels: 49.4 us -> 47.4 us
    pallas_call x4, Pallas kernels: 41.8 us -> 39.8 us  [the longest x3 30.3 us: cells(): pl.pallas_call(functools.partial(cells_kernel, count), out_shape=[SUMS] +...]
    all_to_all x1, blocking collectives: 25 us -> 27 us  [per_device(): gram = jnp.sum(lax.all_to_all(everyone, 'row', 0, 0), axis=0)]
  transfers between devices with their start and end apart: 26 -> 26, of which waited for: 12 -> 12; matrix products, arithmetic and copies ran while one was open for 2% -> 2% of each run, Pallas kernels for 22% -> 21%
where the time goes in v7:
time: 190 us; the launch traced here: 189 us
  starting transfers between devices  48.9 us (26%)
  Pallas kernels  47.4 us (25%)
  blocking collectives  43.3 us (23%)
  waiting for transfers between devices  35.1 us (18%)
  local copies, waits for them, and re-layouts  10.1 us (5%)
  other arithmetic  3.11 us (2%)
    pallas_call x3, Pallas kernels, cells(): pl.pallas_call(functools.partial(cells_kernel, count), out_shape=[SUMS] +...  30.3 us
    all_to_all x1, blocking collectives, per_device(): gram = jnp.sum(lax.all_to_all(everyone, 'row', 0, 0), axis=0)  27 us
    ppermute x9, starting transfers between devices, give_back(): returned.append(lax.ppermute(part, 'row', back))  22.7 us
    ppermute x9, starting transfers between devices, move(): return lax.ppermute(array, 'row', shift(dy, dx, keep))  17.7 us
    all_gather x1, blocking collectives, per_device(): near_v = lax.all_gather(vectors, 'col')  16.4 us
    ppermute x9, waiting for transfers between devices, give_back(): returned.append(lax.ppermute(part, 'row', back))  15.5 us
    ppermute x9, waiting for transfers between devices, move(): return lax.ppermute(array, 'row', shift(dy, dx, keep))  13.3 us
    pallas_call x1, Pallas kernels, own_cells(): pl.pallas_call(own_kernel, out_shape=[SUMS, NORM, ROW, TOKEN], grid_spec=...  9.51 us
  transfers between devices with their start and end apart: 26, of which 12 were waited for; matrix products, arithmetic and copies ran while one was open for 2% of the time, Pallas kernels for 21%

profile of v7, /device:TPU:0, one launch (start us, length us, event | category | flops | bytes accessed | tf_op | source)
XLA Modules:
  0.0 189.0 jit_solution(2145481571239566690)
XLA Ops:
  0.0 2.6 %payload.1.far_ref = bf16[560,1024]{1,0:T(8,128)(2,1)} custom-call(s32[1]{0:T(128)} %bitcast.14.index_ref, bf16[8,512,1024]{2,1,0:T(8,128)(2,1)} %bitcast.37, bf16[64,512]{1,0:T(8,128)(2,1)} %v_ref.1), custom_call_target="tpu_custom_call" | custom-call | tf_op jit(solution)/shard_map/payload/pallas_call | solution.py:78
  2.6 5.3 %collective-permute-start.2 = (bf16[560,1024]{1,0:T(8,128)(2,1)}, bf16[560,1024]{1,0:T(8,128)(2,1)S(1)}, u32[]{:S(2)}, u32[]{:S(2)}) collective-permute-start(bf16[560,1024]{1,0:T(8,128)(2,1)} %payload.1.far_ref), channel_id=1, source_target_pairs={{0,120},{8,96},{16,104},{24,112},{32,24},{40,0},{48,8},{56,16},{64... | collective-permute-start | bytes 3440648 | tf_op jit(solution)/shard_map/ppermute | solution.py:354
  9.8 9.5 %cells_own.1 = (f32[8,72,512]{2,1,0:T(8,128)}, f32[8,512,128]{2,1,0:T(8,128)}, f32[8,8,512]{2,1,0:T(8,128)}, f32[8,128]{1,0:T(8,128)}) custom-call(s32[8]{0:T(128)} %slice_reduce_fusion.flags_ref, bf16[8,512,1024]{2,1,0:T(8,128)(2,1)} %bitcast.38, bf16[560,1024]{1,0:T(8,128)(2,1)} %payload.1.far_ref), custom_call_target="tpu_custom_call" | custom-call | flops 2147483648 | bytes 13631488 | tf_op jit(solution)/shard_map/cells_own/pallas_call | solution.py:229
  19.3 16.4 %all-gather = bf16[512,512]{1,0:T(8,128)(2,1)} all-gather(bf16[64,512]{1,0:T(8,128)(2,1)S(1)} %copy-done.22), channel_id=2, replica_groups=mesh['row'=16,'col'=8] {'col'}, dimensions={0}, use_global_device_ids=true | all-gather | bytes 589824 | tf_op jit(solution)/shard_map/all_gather | solution.py:400
  38.0 3.2 %collective-permute-start.4 = (bf16[560,1024]{1,0:T(8,128)(2,1)}, bf16[560,1024]{1,0:T(8,128)(2,1)}, u32[]{:S(2)}, u32[]{:S(2)}) collective-permute-start(bf16[560,1024]{1,0:T(8,128)(2,1)} %get-tuple-element.41.refs_2_), channel_id=1, source_target_pairs={{0,24},{8,0},{16,8},{24,16},{32,56},{40,32},{48,40},{56,48},{64,88... | collective-permute-start | bytes 3440648 | tf_op jit(solution)/shard_map/ppermute | solution.py:354
  43.2 5.4 %collective-permute-start.5 = (bf16[560,1024]{1,0:T(8,128)(2,1)}, bf16[560,1024]{1,0:T(8,128)(2,1)S(1)}, u32[]{:S(2)}, u32[]{:S(2)}) collective-permute-start(bf16[560,1024]{1,0:T(8,128)(2,1)} %get-tuple-element.42.refs_0_), channel_id=1, source_target_pairs={{0,96},{8,104},{16,112},{24,120},{32,0},{40,8},{48,16},{56,24},{64... | collective-permute-start | bytes 3440648 | tf_op jit(solution)/shard_map/ppermute | solution.py:354
  49.3 11.3 %cells.3 = (f32[8,72,512]{2,1,0:T(8,128)}, bf16[80,512]{1,0:T(8,128)(2,1)}, bf16[80,512]{1,0:T(8,128)(2,1)}, bf16[80,512]{1,0:T(8,128)(2,1)}, f32[8,128]{1,0:T(8,128)}) custom-call(s32[24]{0:T(128)} %reshape.212.flags_ref, bf16[8,512,1024]{2,1,0:T(8,128)(2,1)} %bitcast.39, bf16[8,64,512]{2,1,0:T(8,128)(2,1)} %bitcast.45, ...), custom_call_target="tpu_custom_call", output_to_operand_aliasing={{0}: (8, {})} | custom-call | flops 6442450944 | bytes 15728640 | tf_op jit(solution)/shard_map/cells/pallas_call | solution.py:268
  60.7 8.5 %collective-permute-done.3.refs_0_ = bf16[560,1024]{1,0:T(8,128)(2,1)S(1)} collective-permute-done((bf16[560,1024]{1,0:T(8,128)(2,1)}, bf16[560,1024]{1,0:T(8,128)(2,1)S(1)}, u32[]{:S(2)}, u32[]{:S(2)}) %collective-permute-start.3) | collective-permute-done | bytes 1146912 | tf_op jit(solution)/shard_map/ppermute | solution.py:354
  69.2 2.4 %collective-permute-done.6.refs_7_.refs_1_ = bf16[560,1024]{1,0:T(8,128)(2,1)S(1)} collective-permute-done((bf16[560,1024]{1,0:T(8,128)(2,1)}, bf16[560,1024]{1,0:T(8,128)(2,1)S(1)}, u32[]{:S(2)}, u32[]{:S(2)}) %collective-permute-start.6) | collective-permute-done | bytes 1146912 | tf_op jit(solution)/shard_map/ppermute | solution.py:354
  71.5 2.1 %collective-permute-done.5.refs_6_.refs_0_ = bf16[560,1024]{1,0:T(8,128)(2,1)S(1)} collective-permute-done((bf16[560,1024]{1,0:T(8,128)(2,1)}, bf16[560,1024]{1,0:T(8,128)(2,1)S(1)}, u32[]{:S(2)}, u32[]{:S(2)}) %collective-permute-start.5) | collective-permute-done | bytes 1146912 | tf_op jit(solution)/shard_map/ppermute | solution.py:354
  77.4 3.2 %collective-permute-start.9 = (bf16[80,512]{1,0:T(8,128)(2,1)}, bf16[80,512]{1,0:T(8,128)(2,1)S(1)}, u32[]{:S(2)}, u32[]{:S(2)}) collective-permute-start(bf16[80,512]{1,0:T(8,128)(2,1)} %get-tuple-element.56), channel_id=1, source_target_pairs={{8,0},{16,8},{24,16},{0,24},{40,32},{48,40},{56,48},{32,56},{72,64... | collective-permute-start | bytes 245768 | tf_op jit(solution)/shard_map/ppermute | solution.py:397
  80.6 3.3 %collective-permute-start.10 = (bf16[80,512]{1,0:T(8,128)(2,1)}, bf16[80,512]{1,0:T(8,128)(2,1)S(1)}, u32[]{:S(2)}, u32[]{:S(2)}) collective-permute-start(bf16[80,512]{1,0:T(8,128)(2,1)} %get-tuple-element.57), channel_id=1, source_target_pairs={{32,0},{40,8},{48,16},{56,24},{64,32},{72,40},{80,48},{88,56},{96,... | collective-permute-start | bytes 245768 | tf_op jit(solution)/shard_map/ppermute | solution.py:397
  83.9 9.9 %cells.4 = (f32[8,72,512]{2,1,0:T(8,128)}, bf16[80,512]{1,0:T(8,128)(2,1)}, bf16[80,512]{1,0:T(8,128)(2,1)}, bf16[80,512]{1,0:T(8,128)(2,1)}, f32[8,128]{1,0:T(8,128)}) custom-call(s32[24]{0:T(128)} %reshape.213.flags_ref, bf16[8,512,1024]{2,1,0:T(8,128)(2,1)} %bitcast.40, bf16[8,64,512]{2,1,0:T(8,128)(2,1)} %bitcast.46, ...), custom_call_target="tpu_custom_call", output_to_operand_aliasing={{0}: (8, {})} | custom-call | flops 6442450944 | bytes 15728640 | tf_op jit(solution)/shard_map/cells/pallas_call | solution.py:268
  93.9 11.5 %collective-permute-done.10.refs_6_ = bf16[80,512]{1,0:T(8,128)(2,1)S(1)} collective-permute-done((bf16[80,512]{1,0:T(8,128)(2,1)}, bf16[80,512]{1,0:T(8,128)(2,1)S(1)}, u32[]{:S(2)}, u32[]{:S(2)}) %collective-permute-start.10) | collective-permute-done | bytes 81952 | tf_op jit(solution)/shard_map/ppermute | solution.py:397
  105.3 2.3 %collective-permute-done.11.refs_7_ = bf16[80,512]{1,0:T(8,128)(2,1)S(1)} collective-permute-done((bf16[80,512]{1,0:T(8,128)(2,1)}, bf16[80,512]{1,0:T(8,128)(2,1)S(1)}, u32[]{:S(2)}, u32[]{:S(2)}) %collective-permute-start.11) | collective-permute-done | bytes 81952 | tf_op jit(solution)/shard_map/ppermute | solution.py:397
  109.1 2.1 %collective-permute-start.12 = (bf16[80,512]{1,0:T(8,128)(2,1)}, bf16[80,512]{1,0:T(8,128)(2,1)S(1)}, u32[]{:S(2)}, u32[]{:S(2)}) collective-permute-start(bf16[80,512]{1,0:T(8,128)(2,1)} %get-tuple-element.66), channel_id=1, source_target_pairs={{104,0},{112,8},{120,16},{96,24},{8,32},{16,40},{24,48},{0,56},{40... | collective-permute-start | bytes 245768 | tf_op jit(solution)/shard_map/ppermute | solution.py:397
  111.5 4.4 %collective-permute-start.14 = (bf16[80,512]{1,0:T(8,128)(2,1)}, bf16[80,512]{1,0:T(8,128)(2,1)S(1)}, u32[]{:S(2)}, u32[]{:S(2)}) collective-permute-start(bf16[80,512]{1,0:T(8,128)(2,1)} %get-tuple-element.68), channel_id=1, source_target_pairs={{0,64},{8,72},{16,80},{24,88},{32,96},{40,104},{48,112},{56,120},{... | collective-permute-start | bytes 245768 | tf_op jit(solution)/shard_map/ppermute | solution.py:397
  115.9 9.0 %cells.5 = (f32[8,72,512]{2,1,0:T(8,128)}, bf16[80,512]{1,0:T(8,128)(2,1)}, bf16[80,512]{1,0:T(8,128)(2,1)}, bf16[80,512]{1,0:T(8,128)(2,1)}, f32[8,128]{1,0:T(8,128)}) custom-call(s32[24]{0:T(128)} %reshape.210.flags_ref, bf16[8,512,1024]{2,1,0:T(8,128)(2,1)} %bitcast.41, bf16[8,64,512]{2,1,0:T(8,128)(2,1)} %bitcast.47, ...), custom_call_target="tpu_custom_call", output_to_operand_aliasing={{0}: (8, {})} | custom-call | flops 6442450944 | bytes 15728640 | tf_op jit(solution)/shard_map/cells/pallas_call | solution.py:268
  127.0 2.5 %collective-permute-start.19 = (bf16[80,512]{1,0:T(8,128)(2,1)S(1)}, bf16[80,512]{1,0:T(8,128)(2,1)S(1)}, u32[]{:S(2)}, u32[]{:S(2)}) collective-permute-start(bf16[80,512]{1,0:T(8,128)(2,1)S(1)} %copy-done.23), channel_id=1, source_target_pairs={{72,0},{80,8},{88,16},{64,24},{104,32},{112,40},{120,48},{96,56},{... | collective-permute-start | bytes 245768 | tf_op jit(solution)/shard_map/ppermute | solution.py:397
  131.3 2.5 %collective-permute-start.18 = (f32[72,512]{1,0:T(8,128)S(1)}, f32[72,512]{1,0:T(8,128)S(1)}, u32[]{:S(2)}, u32[]{:S(2)}) collective-permute-start(f32[72,512]{1,0:T(8,128)S(1)} %get-tuple-element.74), channel_id=1, source_target_pairs={{0,2},{1,3},{2,4},{3,5},{4,6},{5,7},{6,0},{7,1},{8,10},{9,11},{10,... | collective-permute-start | bytes 442376 | tf_op jit(solution)/shard_map/ppermute | solution.py:357
  134.5 5.1 %collective-permute-start.20 = (bf16[80,512]{1,0:T(8,128)(2,1)S(1)}, bf16[80,512]{1,0:T(8,128)(2,1)S(1)}, u32[]{:S(2)}, u32[]{:S(2)}) collective-permute-start(bf16[80,512]{1,0:T(8,128)(2,1)S(1)} %copy-done.24), channel_id=1, source_target_pairs={{0,16},{8,24},{32,48},{40,56},{64,80},{72,88},{96,112},{104,120},{... | collective-permute-start | bytes 245768 | tf_op jit(solution)/shard_map/ppermute | solution.py:397
  149.4 3.1 %collective-permute-done.24 = f32[64,64]{1,0:T(8,128)S(1)} collective-permute-done((f32[64,64]{1,0:T(8,128)S(1)}, f32[64,64]{1,0:T(8,128)S(1)}, u32[]{:S(2)}, u32[]{:S(2)}) %collective-permute-start.24) | collective-permute-done | bytes 16416 | tf_op jit(solution)/shard_map/ppermute | solution.py:357
  154.4 27.0 %all_to_all.5 = f32[16,1,4096]{2,1,0:T(1,128)S(1)} all-to-all(f32[16,1,4096]{2,1,0:T(1,128)S(1)} %reshape.219), channel_id=1, replica_groups=mesh['row'=16,'col'=8] {'row'}, dimensions={0} | all-to-all | bytes 524288 | tf_op jit(solution)/shard_map/all_to_all | solution.py:441
  184.0 5.0 %solve.1 = f32[64,512]{1,0:T(8,128)} custom-call(f32[64,64]{1,0:T(8,128)} %reduce_sum.9.gram_ref, f32[64,512]{1,0:T(8,128)} %copy-done.1), custom_call_target="tpu_custom_call" | custom-call | tf_op jit(solution)/shard_map/solve/pallas_call | solution.py:338
  (145 shorter events, 30.8 us)
Async XLA Ops:
  2.6 33.1 %collective-permute-start.2 = (bf16[560,1024]{1,0:T(8,128)(2,1)}, bf16[560,1024]{1,0:T(8,128)(2,1)S(1)}, u32[]{:S(2)}, u32[]{:S(2)}) collective-permute-start(bf16[560,1024]{1,0:T(8,128)(2,1)} %payload.1.far_ref), channel_id=1, source_target_pairs={{0,120},{8,96},{16,104},{24,112},{32,24},{40,0},{48,8},{56,16},{64... | collective-permute-start | bytes 3440648 | tf_op jit(solution)/shard_map/ppermute | solution.py:354
  7.9 28.1 %collective-permute-start.1 = (bf16[560,1024]{1,0:T(8,128)(2,1)}, bf16[560,1024]{1,0:T(8,128)(2,1)S(1)}, u32[]{:S(2)}, u32[]{:S(2)}) collective-permute-start(bf16[560,1024]{1,0:T(8,128)(2,1)} %payload.1.far_ref), channel_id=1, source_target_pairs={{0,32},{8,40},{16,48},{24,56},{32,64},{40,72},{48,80},{56,88},{64,... | collective-permute-start | bytes 3440648 | tf_op jit(solution)/shard_map/ppermute | solution.py:354
  7.9 28.1 %collective-permute-start = (bf16[560,1024]{1,0:T(8,128)(2,1)}, bf16[560,1024]{1,0:T(8,128)(2,1)S(1)}, u32[]{:S(2)}, u32[]{:S(2)}) collective-permute-start(bf16[560,1024]{1,0:T(8,128)(2,1)} %payload.1.far_ref), channel_id=1, source_target_pairs={{0,8},{8,16},{16,24},{24,0},{32,40},{40,48},{48,56},{56,32},{64,72... | collective-permute-start | bytes 3440648 | tf_op jit(solution)/shard_map/ppermute | solution.py:354
  37.5 31.7 %collective-permute-start.3 = (bf16[560,1024]{1,0:T(8,128)(2,1)}, bf16[560,1024]{1,0:T(8,128)(2,1)S(1)}, u32[]{:S(2)}, u32[]{:S(2)}) collective-permute-start(bf16[560,1024]{1,0:T(8,128)(2,1)} %get-tuple-element.40.refs_1_), channel_id=1, source_target_pairs={{0,32},{8,40},{16,48},{24,56},{32,64},{40,72},{48,80},{56,88},{64,... | collective-permute-start | bytes 3440648 | tf_op jit(solution)/shard_map/ppermute | solution.py:354
  38.0 31.1 %collective-permute-start.4 = (bf16[560,1024]{1,0:T(8,128)(2,1)}, bf16[560,1024]{1,0:T(8,128)(2,1)}, u32[]{:S(2)}, u32[]{:S(2)}) collective-permute-start(bf16[560,1024]{1,0:T(8,128)(2,1)} %get-tuple-element.41.refs_2_), channel_id=1, source_target_pairs={{0,24},{8,0},{16,8},{24,16},{32,56},{40,32},{48,40},{56,48},{64,88... | collective-permute-start | bytes 3440648 | tf_op jit(solution)/shard_map/ppermute | solution.py:354
  41.3 30.3 %collective-permute-start.6 = (bf16[560,1024]{1,0:T(8,128)(2,1)}, bf16[560,1024]{1,0:T(8,128)(2,1)S(1)}, u32[]{:S(2)}, u32[]{:S(2)}) collective-permute-start(bf16[560,1024]{1,0:T(8,128)(2,1)} %get-tuple-element.42.refs_0_), channel_id=1, source_target_pairs={{0,8},{24,0},{32,40},{56,32},{64,72},{88,64},{96,104},{120,96},{1,... | collective-permute-start | bytes 3440648 | tf_op jit(solution)/shard_map/ppermute | solution.py:354
  43.2 30.4 %collective-permute-start.5 = (bf16[560,1024]{1,0:T(8,128)(2,1)}, bf16[560,1024]{1,0:T(8,128)(2,1)S(1)}, u32[]{:S(2)}, u32[]{:S(2)}) collective-permute-start(bf16[560,1024]{1,0:T(8,128)(2,1)} %get-tuple-element.42.refs_0_), channel_id=1, source_target_pairs={{0,96},{8,104},{16,112},{24,120},{32,0},{40,8},{48,16},{56,24},{64... | collective-permute-start | bytes 3440648 | tf_op jit(solution)/shard_map/ppermute | solution.py:354
  74.7 32.9 %collective-permute-start.7 = (bf16[560,1024]{1,0:T(8,128)(2,1)}, bf16[560,1024]{1,0:T(8,128)(2,1)S(1)}, u32[]{:S(2)}, u32[]{:S(2)}) collective-permute-start(bf16[560,1024]{1,0:T(8,128)(2,1)} %get-tuple-element.50.refs_2_), channel_id=1, source_target_pairs={{0,8},{8,16},{16,24},{24,0},{32,40},{40,48},{48,56},{56,32},{64,72... | collective-permute-start | bytes 3440648 | tf_op jit(solution)/shard_map/ppermute | solution.py:354
  74.7 32.9 %collective-permute-start.8 = (bf16[560,1024]{1,0:T(8,128)(2,1)}, bf16[560,1024]{1,0:T(8,128)(2,1)S(1)}, u32[]{:S(2)}, u32[]{:S(2)}) collective-permute-start(bf16[560,1024]{1,0:T(8,128)(2,1)} %get-tuple-element.51.refs_1_), channel_id=1, source_target_pairs={{32,0},{40,8},{48,16},{56,24},{64,32},{72,40},{80,48},{88,56},{33,... | collective-permute-start | bytes 3440648 | tf_op jit(solution)/shard_map/ppermute | solution.py:354
  77.4 16.5 %collective-permute-start.9 = (bf16[80,512]{1,0:T(8,128)(2,1)}, bf16[80,512]{1,0:T(8,128)(2,1)S(1)}, u32[]{:S(2)}, u32[]{:S(2)}) collective-permute-start(bf16[80,512]{1,0:T(8,128)(2,1)} %get-tuple-element.56), channel_id=1, source_target_pairs={{8,0},{16,8},{24,16},{0,24},{40,32},{48,40},{56,48},{32,56},{72,64... | collective-permute-start | bytes 245768 | tf_op jit(solution)/shard_map/ppermute | solution.py:397
  80.6 24.7 %collective-permute-start.10 = (bf16[80,512]{1,0:T(8,128)(2,1)}, bf16[80,512]{1,0:T(8,128)(2,1)S(1)}, u32[]{:S(2)}, u32[]{:S(2)}) collective-permute-start(bf16[80,512]{1,0:T(8,128)(2,1)} %get-tuple-element.57), channel_id=1, source_target_pairs={{32,0},{40,8},{48,16},{56,24},{64,32},{72,40},{80,48},{88,56},{96,... | collective-permute-start | bytes 245768 | tf_op jit(solution)/shard_map/ppermute | solution.py:397
  83.9 23.7 %collective-permute-start.11 = (bf16[80,512]{1,0:T(8,128)(2,1)}, bf16[80,512]{1,0:T(8,128)(2,1)S(1)}, u32[]{:S(2)}, u32[]{:S(2)}) collective-permute-start(bf16[80,512]{1,0:T(8,128)(2,1)} %get-tuple-element.58), channel_id=1, source_target_pairs={{120,0},{96,8},{104,16},{112,24},{24,32},{0,40},{8,48},{16,56},{56... | collective-permute-start | bytes 245768 | tf_op jit(solution)/shard_map/ppermute | solution.py:397
  109.1 15.9 %collective-permute-start.12 = (bf16[80,512]{1,0:T(8,128)(2,1)}, bf16[80,512]{1,0:T(8,128)(2,1)S(1)}, u32[]{:S(2)}, u32[]{:S(2)}) collective-permute-start(bf16[80,512]{1,0:T(8,128)(2,1)} %get-tuple-element.66), channel_id=1, source_target_pairs={{104,0},{112,8},{120,16},{96,24},{8,32},{16,40},{24,48},{0,56},{40... | collective-permute-start | bytes 245768 | tf_op jit(solution)/shard_map/ppermute | solution.py:397
  111.2 13.8 %collective-permute-start.13 = (bf16[80,512]{1,0:T(8,128)(2,1)}, bf16[80,512]{1,0:T(8,128)(2,1)S(1)}, u32[]{:S(2)}, u32[]{:S(2)}) collective-permute-start(bf16[80,512]{1,0:T(8,128)(2,1)} %get-tuple-element.67), channel_id=1, source_target_pairs={{112,0},{120,8},{96,16},{104,24},{16,32},{24,40},{0,48},{8,56},{48... | collective-permute-start | bytes 245768 | tf_op jit(solution)/shard_map/ppermute | solution.py:397
  111.5 13.4 %collective-permute-start.14 = (bf16[80,512]{1,0:T(8,128)(2,1)}, bf16[80,512]{1,0:T(8,128)(2,1)S(1)}, u32[]{:S(2)}, u32[]{:S(2)}) collective-permute-start(bf16[80,512]{1,0:T(8,128)(2,1)} %get-tuple-element.68), channel_id=1, source_target_pairs={{0,64},{8,72},{16,80},{24,88},{32,96},{40,104},{48,112},{56,120},{... | collective-permute-start | bytes 245768 | tf_op jit(solution)/shard_map/ppermute | solution.py:397
  127.0 12.6 %collective-permute-start.19 = (bf16[80,512]{1,0:T(8,128)(2,1)S(1)}, bf16[80,512]{1,0:T(8,128)(2,1)S(1)}, u32[]{:S(2)}, u32[]{:S(2)}) collective-permute-start(bf16[80,512]{1,0:T(8,128)(2,1)S(1)} %copy-done.23), channel_id=1, source_target_pairs={{72,0},{80,8},{88,16},{64,24},{104,32},{112,40},{120,48},{96,56},{... | collective-permute-start | bytes 245768 | tf_op jit(solution)/shard_map/ppermute | solution.py:397
  129.7 13.7 %collective-permute-start.17 = (f32[72,512]{1,0:T(8,128)S(1)}, f32[72,512]{1,0:T(8,128)S(1)}, u32[]{:S(2)}, u32[]{:S(2)}) collective-permute-start(f32[72,512]{1,0:T(8,128)S(1)} %get-tuple-element.73), channel_id=1, source_target_pairs={{0,4},{1,5},{2,6},{3,7},{4,0},{5,1},{6,2},{7,3},{8,12},{9,13},{10,... | collective-permute-start | bytes 442376 | tf_op jit(solution)/shard_map/ppermute | solution.py:357
  131.3 12.2 %collective-permute-start.18 = (f32[72,512]{1,0:T(8,128)S(1)}, f32[72,512]{1,0:T(8,128)S(1)}, u32[]{:S(2)}, u32[]{:S(2)}) collective-permute-start(f32[72,512]{1,0:T(8,128)S(1)} %get-tuple-element.74), channel_id=1, source_target_pairs={{0,2},{1,3},{2,4},{3,5},{4,6},{5,7},{6,0},{7,1},{8,10},{9,11},{10,... | collective-permute-start | bytes 442376 | tf_op jit(solution)/shard_map/ppermute | solution.py:357
  133.7 9.7 %collective-permute-start.16 = (f32[72,512]{1,0:T(8,128)S(1)}, f32[72,512]{1,0:T(8,128)S(1)}, u32[]{:S(2)}, u32[]{:S(2)}) collective-permute-start(f32[72,512]{1,0:T(8,128)S(1)} %get-tuple-element.75), channel_id=1, source_target_pairs={{0,6},{1,7},{2,0},{3,1},{4,2},{5,3},{6,4},{7,5},{8,14},{9,15},{10,... | collective-permute-start | bytes 442376 | tf_op jit(solution)/shard_map/ppermute | solution.py:357
  134.5 7.8 %collective-permute-start.20 = (bf16[80,512]{1,0:T(8,128)(2,1)S(1)}, bf16[80,512]{1,0:T(8,128)(2,1)S(1)}, u32[]{:S(2)}, u32[]{:S(2)}) collective-permute-start(bf16[80,512]{1,0:T(8,128)(2,1)S(1)} %copy-done.24), channel_id=1, source_target_pairs={{0,16},{8,24},{32,48},{40,56},{64,80},{72,88},{96,112},{104,120},{... | collective-permute-start | bytes 245768 | tf_op jit(solution)/shard_map/ppermute | solution.py:397
  139.6 3.8 %collective-permute-start.21 = (bf16[80,512]{1,0:T(8,128)(2,1)S(1)}, bf16[80,512]{1,0:T(8,128)(2,1)S(1)}, u32[]{:S(2)}, u32[]{:S(2)}) collective-permute-start(bf16[80,512]{1,0:T(8,128)(2,1)S(1)} %copy-done.25), channel_id=1, source_target_pairs={{16,64},{24,72},{0,80},{8,88},{48,96},{56,104},{32,112},{40,120},{... | collective-permute-start | bytes 245768 | tf_op jit(solution)/shard_map/ppermute | solution.py:397
  145.2 4.2 %collective-permute-start.25 = (f32[64,64]{1,0:T(8,128)S(1)}, f32[64,64]{1,0:T(8,128)S(1)}, u32[]{:S(2)}, u32[]{:S(2)}) collective-permute-start(f32[64,64]{1,0:T(8,128)S(1)} %add.404), channel_id=1, source_target_pairs={{0,6},{1,7},{2,0},{3,1},{4,2},{5,3},{6,4},{7,5},{8,14},{9,15},{10,... | collective-permute-start | bytes 49160 | tf_op jit(solution)/shard_map/ppermute | solution.py:357
  147.1 5.4 %collective-permute-start.24 = (f32[64,64]{1,0:T(8,128)S(1)}, f32[64,64]{1,0:T(8,128)S(1)}, u32[]{:S(2)}, u32[]{:S(2)}) collective-permute-start(f32[64,64]{1,0:T(8,128)S(1)} %add.404), channel_id=1, source_target_pairs={{0,4},{1,5},{2,6},{3,7},{4,0},{5,1},{6,2},{7,3},{8,12},{9,13},{10,... | collective-permute-start | bytes 49160 | tf_op jit(solution)/shard_map/ppermute | solution.py:357
  148.8 5.1 %collective-permute-start.23 = (f32[64,64]{1,0:T(8,128)S(1)}, f32[64,64]{1,0:T(8,128)S(1)}, u32[]{:S(2)}, u32[]{:S(2)}) collective-permute-start(f32[64,64]{1,0:T(8,128)S(1)} %add.404), channel_id=1, source_target_pairs={{0,2},{1,3},{2,4},{3,5},{4,6},{5,7},{6,0},{7,1},{8,10},{9,11},{10,... | collective-permute-start | bytes 49160 | tf_op jit(solution)/shard_map/ppermute | solution.py:357
  (29 other events, 193.1 us)

commit v8 on v7

--- a/solution.py
+++ b/solution.py
@@ -50,7 +50,7 @@
     "d": ((-1, 1), None),
     "e": ((-1, -2), None),
     "h": ((2, 0), top_half),
-    "f": ((2, 1), None),
+    "f": ((-2, -1), None),
     "g": ((0, 2), left_half),
     "k": ((2, 2), top_half),
 }
@@ -404,14 +404,14 @@
     far["d"] = move(far["a"], -1, 0)
     far["e"] = move(far["c"], 0, -1)
     far["g"] = move(far["a"], 0, 1, left_half)
-    far["h"] = move(far["b"], 1, 0)
+    far["h"] = move(far["b"], 1, 0, top_half)
+    far["f"] = move(far["c"], -1, 0)
     group1, group2, group3 = ("a", "b", "c"), ("d", "e", "h"), ("f", "g", "k")
     sums, parts, token = work(group1, sums)
 
-    far["h"], far["e"], *parts = tie([far["h"], far["e"], *parts], token, far["d"], far["g"])
-    far["f"] = move(far["h"], 0, 1)
+    far["e"], *parts = tie([far["e"], *parts], token, far["d"], far["h"], far["g"])
+    returned1 = give_back(group1, parts)
     far["k"] = move(far["e"], -1, 0, top_half)
-    returned1 = give_back(group1, parts)
     sums, parts, token = work(group2, sums)
 
     far["f"], far["k"], *parts = tie([far["f"], far["k"], *parts], *returned1)

time: 190 us -> 204 us (1.074)
  waiting for transfers between devices: 35.1 us -> 51.7 us
    ppermute x9, waiting for transfers between devices: 15.5 us -> 25.4 us  [give_back(): returned.append(lax.ppermute(part, 'row', back))]
    ppermute x9, waiting for transfers between devices: 13.3 us -> 19.5 us  [move(): return lax.ppermute(array, 'row', shift(dy, dx, keep))]
    unnamed x57 -> x55, local copies, waits for them, and re-layouts: 5.2 us -> 4.91 us
  transfers between devices with their start and end apart: 26 -> 26, of which waited for: 12 -> 13; matrix products, arithmetic and copies ran while one was open for 2% -> 2% of each run, Pallas kernels for 21% -> 19%
where the time goes in v8:
time: 204 us
  waiting for transfers between devices  51.7 us (25%)
  starting transfers between devices  50.1 us (25%)
  Pallas kernels  46.2 us (23%)
  blocking collectives  41.7 us (20%)
  local copies, waits for them, and re-layouts  9.93 us (5%)
  other arithmetic  3.1 us (2%)
    pallas_call x3, Pallas kernels, cells(): pl.pallas_call(functools.partial(cells_kernel, count), out_shape=[SUMS] +...  29.1 us
    ppermute x9, waiting for transfers between devices, give_back(): returned.append(lax.ppermute(part, 'row', back))  25.4 us
    all_to_all x1, blocking collectives, per_device(): gram = jnp.sum(lax.all_to_all(everyone, 'row', 0, 0), axis=0)  25.4 us
    ppermute x9, starting transfers between devices, give_back(): returned.append(lax.ppermute(part, 'row', back))  23 us
    ppermute x9, waiting for transfers between devices, move(): return lax.ppermute(array, 'row', shift(dy, dx, keep))  19.5 us
    ppermute x9, starting transfers between devices, move(): return lax.ppermute(array, 'row', shift(dy, dx, keep))  18.5 us
    all_gather x1, blocking collectives, per_device(): near_v = lax.all_gather(vectors, 'col')  16.3 us
    pallas_call x1, Pallas kernels, own_cells(): pl.pallas_call(own_kernel, out_shape=[SUMS, NORM, ROW, TOKEN], grid_spec=...  9.53 us
  transfers between devices with their start and end apart: 26, of which 13 were waited for; matrix products, arithmetic and copies ran while one was open for 2% of the time, Pallas kernels for 19%

profile of v8, /device:TPU:0, one launch (start us, length us, event | category | flops | bytes accessed | tf_op | source)
XLA Modules:
  0.0 203.6 jit_solution(2686285097623401286)
XLA Ops:
  0.0 2.6 %payload.1.far_ref = bf16[560,1024]{1,0:T(8,128)(2,1)} custom-call(s32[1]{0:T(128)} %bitcast.14.index_ref, bf16[8,512,1024]{2,1,0:T(8,128)(2,1)} %bitcast.37, bf16[64,512]{1,0:T(8,128)(2,1)} %v_ref.1), custom_call_target="tpu_custom_call" | custom-call | tf_op jit(solution)/shard_map/payload/pallas_call | solution.py:78
  2.6 5.3 %collective-permute-start.2 = (bf16[560,1024]{1,0:T(8,128)(2,1)}, bf16[560,1024]{1,0:T(8,128)(2,1)S(1)}, u32[]{:S(2)}, u32[]{:S(2)}) collective-permute-start(bf16[560,1024]{1,0:T(8,128)(2,1)} %payload.1.far_ref), channel_id=1, source_target_pairs={{0,120},{8,96},{16,104},{24,112},{32,24},{40,0},{48,8},{56,16},{64... | collective-permute-start | bytes 3440648 | tf_op jit(solution)/shard_map/ppermute | solution.py:354
  9.8 9.5 %cells_own.1 = (f32[8,72,512]{2,1,0:T(8,128)}, f32[8,512,128]{2,1,0:T(8,128)}, f32[8,8,512]{2,1,0:T(8,128)}, f32[8,128]{1,0:T(8,128)}) custom-call(s32[8]{0:T(128)} %slice_reduce_fusion.flags_ref, bf16[8,512,1024]{2,1,0:T(8,128)(2,1)} %bitcast.38, bf16[560,1024]{1,0:T(8,128)(2,1)} %payload.1.far_ref), custom_call_target="tpu_custom_call" | custom-call | flops 2147483648 | bytes 13631488 | tf_op jit(solution)/shard_map/cells_own/pallas_call | solution.py:229
  19.3 16.3 %all-gather = bf16[512,512]{1,0:T(8,128)(2,1)} all-gather(bf16[64,512]{1,0:T(8,128)(2,1)S(1)} %copy-done.21), channel_id=2, replica_groups=mesh['row'=16,'col'=8] {'col'}, dimensions={0}, use_global_device_ids=true | all-gather | bytes 589824 | tf_op jit(solution)/shard_map/all_gather | solution.py:400
  37.5 2.5 %collective-permute-start.6 = (bf16[560,1024]{1,0:T(8,128)(2,1)}, bf16[560,1024]{1,0:T(8,128)(2,1)S(1)}, u32[]{:S(2)}, u32[]{:S(2)}) collective-permute-start(bf16[560,1024]{1,0:T(8,128)(2,1)} %get-tuple-element.41.refs_1_), channel_id=1, source_target_pairs={{0,32},{8,40},{16,48},{24,56},{96,0},{104,8},{112,16},{120,24},{1,... | collective-permute-start | bytes 3440648 | tf_op jit(solution)/shard_map/ppermute | solution.py:354
  40.0 3.3 %collective-permute-start.4 = (bf16[560,1024]{1,0:T(8,128)(2,1)}, bf16[560,1024]{1,0:T(8,128)(2,1)}, u32[]{:S(2)}, u32[]{:S(2)}) collective-permute-start(bf16[560,1024]{1,0:T(8,128)(2,1)} %get-tuple-element.39.refs_2_), channel_id=1, source_target_pairs={{0,24},{8,0},{16,8},{24,16},{32,56},{40,32},{48,40},{56,48},{64,88... | collective-permute-start | bytes 3440648 | tf_op jit(solution)/shard_map/ppermute | solution.py:354
  45.2 4.0 %collective-permute-start.5 = (bf16[560,1024]{1,0:T(8,128)(2,1)}, bf16[560,1024]{1,0:T(8,128)(2,1)S(1)}, u32[]{:S(2)}, u32[]{:S(2)}) collective-permute-start(bf16[560,1024]{1,0:T(8,128)(2,1)} %get-tuple-element.40.refs_0_), channel_id=1, source_target_pairs={{0,96},{8,104},{16,112},{24,120},{32,0},{40,8},{48,16},{56,24},{64... | collective-permute-start | bytes 3440648 | tf_op jit(solution)/shard_map/ppermute | solution.py:354
  50.0 10.3 %cells.3 = (f32[8,72,512]{2,1,0:T(8,128)}, bf16[80,512]{1,0:T(8,128)(2,1)}, bf16[80,512]{1,0:T(8,128)(2,1)}, bf16[80,512]{1,0:T(8,128)(2,1)}, f32[8,128]{1,0:T(8,128)}) custom-call(s32[24]{0:T(128)} %reshape.212.flags_ref, bf16[8,512,1024]{2,1,0:T(8,128)(2,1)} %bitcast.39, bf16[8,64,512]{2,1,0:T(8,128)(2,1)} %bitcast.45, ...), custom_call_target="tpu_custom_call", output_to_operand_aliasing={{0}: (8, {})} | custom-call | flops 6442450944 | bytes 15728640 | tf_op jit(solution)/shard_map/cells/pallas_call | solution.py:268
  60.3 10.5 %collective-permute-done.6.refs_6_.refs_2_ = bf16[560,1024]{1,0:T(8,128)(2,1)S(1)} collective-permute-done((bf16[560,1024]{1,0:T(8,128)(2,1)}, bf16[560,1024]{1,0:T(8,128)(2,1)S(1)}, u32[]{:S(2)}, u32[]{:S(2)}) %collective-permute-start.6) | collective-permute-done | bytes 1146912 | tf_op jit(solution)/shard_map/ppermute | solution.py:354
  70.8 2.7 %collective-permute-done.7.refs_7_.refs_1_ = bf16[560,1024]{1,0:T(8,128)(2,1)S(1)} collective-permute-done((bf16[560,1024]{1,0:T(8,128)(2,1)}, bf16[560,1024]{1,0:T(8,128)(2,1)S(1)}, u32[]{:S(2)}, u32[]{:S(2)}) %collective-permute-start.7) | collective-permute-done | bytes 1146912 | tf_op jit(solution)/shard_map/ppermute | solution.py:354
  79.2 3.3 %collective-permute-start.9 = (bf16[80,512]{1,0:T(8,128)(2,1)}, bf16[80,512]{1,0:T(8,128)(2,1)S(1)}, u32[]{:S(2)}, u32[]{:S(2)}) collective-permute-start(bf16[80,512]{1,0:T(8,128)(2,1)} %get-tuple-element.54), channel_id=1, source_target_pairs={{8,0},{16,8},{24,16},{0,24},{40,32},{48,40},{56,48},{32,56},{72,64... | collective-permute-start | bytes 245768 | tf_op jit(solution)/shard_map/ppermute | solution.py:397
  82.6 3.0 %collective-permute-start.10 = (bf16[80,512]{1,0:T(8,128)(2,1)}, bf16[80,512]{1,0:T(8,128)(2,1)S(1)}, u32[]{:S(2)}, u32[]{:S(2)}) collective-permute-start(bf16[80,512]{1,0:T(8,128)(2,1)} %get-tuple-element.55), channel_id=1, source_target_pairs={{32,0},{40,8},{48,16},{56,24},{64,32},{72,40},{80,48},{88,56},{96,... | collective-permute-start | bytes 245768 | tf_op jit(solution)/shard_map/ppermute | solution.py:397
  85.6 9.9 %cells.4 = (f32[8,72,512]{2,1,0:T(8,128)}, bf16[80,512]{1,0:T(8,128)(2,1)}, bf16[80,512]{1,0:T(8,128)(2,1)}, bf16[80,512]{1,0:T(8,128)(2,1)}, f32[8,128]{1,0:T(8,128)}) custom-call(s32[24]{0:T(128)} %reshape.213.flags_ref, bf16[8,512,1024]{2,1,0:T(8,128)(2,1)} %bitcast.40, bf16[8,64,512]{2,1,0:T(8,128)(2,1)} %bitcast.46, ...), custom_call_target="tpu_custom_call", output_to_operand_aliasing={{0}: (8, {})} | custom-call | flops 6442450944 | bytes 15728640 | tf_op jit(solution)/shard_map/cells/pallas_call | solution.py:268
  95.5 4.3 %collective-permute-done.3.refs_0_ = bf16[560,1024]{1,0:T(8,128)(2,1)} collective-permute-done((bf16[560,1024]{1,0:T(8,128)(2,1)}, bf16[560,1024]{1,0:T(8,128)(2,1)}, u32[]{:S(2)}, u32[]{:S(2)}) %collective-permute-start.3) | collective-permute-done | bytes 1146912 | tf_op jit(solution)/shard_map/ppermute | solution.py:354
  99.8 23.6 %collective-permute-done.10.refs_6_ = bf16[80,512]{1,0:T(8,128)(2,1)S(1)} collective-permute-done((bf16[80,512]{1,0:T(8,128)(2,1)}, bf16[80,512]{1,0:T(8,128)(2,1)S(1)}, u32[]{:S(2)}, u32[]{:S(2)}) %collective-permute-start.10) | collective-permute-done | bytes 81952 | tf_op jit(solution)/shard_map/ppermute | solution.py:397
  124.4 3.3 %collective-permute-start.12 = (bf16[80,512]{1,0:T(8,128)(2,1)}, bf16[80,512]{1,0:T(8,128)(2,1)S(1)}, u32[]{:S(2)}, u32[]{:S(2)}) collective-permute-start(bf16[80,512]{1,0:T(8,128)(2,1)} %get-tuple-element.64), channel_id=1, source_target_pairs={{104,0},{112,8},{120,16},{96,24},{8,32},{16,40},{24,48},{0,56},{40... | collective-permute-start | bytes 245768 | tf_op jit(solution)/shard_map/ppermute | solution.py:397
  127.7 2.7 %collective-permute-start.14 = (bf16[80,512]{1,0:T(8,128)(2,1)}, bf16[80,512]{1,0:T(8,128)(2,1)S(1)}, u32[]{:S(2)}, u32[]{:S(2)}) collective-permute-start(bf16[80,512]{1,0:T(8,128)(2,1)} %get-tuple-element.66), channel_id=1, source_target_pairs={{0,64},{8,72},{16,80},{24,88},{32,96},{40,104},{48,112},{56,120},{... | collective-permute-start | bytes 245768 | tf_op jit(solution)/shard_map/ppermute | solution.py:397
  130.3 8.9 %cells.5 = (f32[8,72,512]{2,1,0:T(8,128)}, bf16[80,512]{1,0:T(8,128)(2,1)}, bf16[80,512]{1,0:T(8,128)(2,1)}, bf16[80,512]{1,0:T(8,128)(2,1)}, f32[8,128]{1,0:T(8,128)}) custom-call(s32[24]{0:T(128)} %reshape.210.flags_ref, bf16[8,512,1024]{2,1,0:T(8,128)(2,1)} %bitcast.41, bf16[8,64,512]{2,1,0:T(8,128)(2,1)} %bitcast.47, ...), custom_call_target="tpu_custom_call", output_to_operand_aliasing={{0}: (8, {})} | custom-call | flops 6442450944 | bytes 15728640 | tf_op jit(solution)/shard_map/cells/pallas_call | solution.py:268
  143.5 2.0 collective-permute-start.17
  145.4 2.4 %collective-permute-start.18 = (f32[72,512]{1,0:T(8,128)S(1)}, f32[72,512]{1,0:T(8,128)S(1)}, u32[]{:S(2)}, u32[]{:S(2)}) collective-permute-start(f32[72,512]{1,0:T(8,128)S(1)} %get-tuple-element.72), channel_id=1, source_target_pairs={{0,2},{1,3},{2,4},{3,5},{4,6},{5,7},{6,0},{7,1},{8,10},{9,11},{10,... | collective-permute-start | bytes 442376 | tf_op jit(solution)/shard_map/ppermute | solution.py:357
  148.7 7.8 %collective-permute-start.20 = (bf16[80,512]{1,0:T(8,128)(2,1)S(1)}, bf16[80,512]{1,0:T(8,128)(2,1)S(1)}, u32[]{:S(2)}, u32[]{:S(2)}) collective-permute-start(bf16[80,512]{1,0:T(8,128)(2,1)S(1)} %copy-done.23), channel_id=1, source_target_pairs={{0,16},{8,24},{32,48},{40,56},{64,80},{72,88},{96,112},{104,120},{... | collective-permute-start | bytes 245768 | tf_op jit(solution)/shard_map/ppermute | solution.py:397
  166.0 3.1 %collective-permute-done.24 = f32[64,64]{1,0:T(8,128)S(1)} collective-permute-done((f32[64,64]{1,0:T(8,128)S(1)}, f32[64,64]{1,0:T(8,128)S(1)}, u32[]{:S(2)}, u32[]{:S(2)}) %collective-permute-start.24) | collective-permute-done | bytes 16416 | tf_op jit(solution)/shard_map/ppermute | solution.py:357
  170.6 25.4 %all_to_all.5 = f32[16,1,4096]{2,1,0:T(1,128)S(1)} all-to-all(f32[16,1,4096]{2,1,0:T(1,128)S(1)} %reshape.219), channel_id=1, replica_groups=mesh['row'=16,'col'=8] {'row'}, dimensions={0} | all-to-all | bytes 524288 | tf_op jit(solution)/shard_map/all_to_all | solution.py:441
  198.6 5.0 %solve.1 = f32[64,512]{1,0:T(8,128)} custom-call(f32[64,64]{1,0:T(8,128)} %reduce_sum.9.gram_ref, f32[64,512]{1,0:T(8,128)} %copy-done.1), custom_call_target="tpu_custom_call" | custom-call | tf_op jit(solution)/shard_map/solve/pallas_call | solution.py:338
  (143 shorter events, 31.3 us)
Async XLA Ops:
  2.6 33.1 %collective-permute-start.2 = (bf16[560,1024]{1,0:T(8,128)(2,1)}, bf16[560,1024]{1,0:T(8,128)(2,1)S(1)}, u32[]{:S(2)}, u32[]{:S(2)}) collective-permute-start(bf16[560,1024]{1,0:T(8,128)(2,1)} %payload.1.far_ref), channel_id=1, source_target_pairs={{0,120},{8,96},{16,104},{24,112},{32,24},{40,0},{48,8},{56,16},{64... | collective-permute-start | bytes 3440648 | tf_op jit(solution)/shard_map/ppermute | solution.py:354
  7.9 28.1 %collective-permute-start.1 = (bf16[560,1024]{1,0:T(8,128)(2,1)}, bf16[560,1024]{1,0:T(8,128)(2,1)S(1)}, u32[]{:S(2)}, u32[]{:S(2)}) collective-permute-start(bf16[560,1024]{1,0:T(8,128)(2,1)} %payload.1.far_ref), channel_id=1, source_target_pairs={{0,32},{8,40},{16,48},{24,56},{32,64},{40,72},{48,80},{56,88},{64,... | collective-permute-start | bytes 3440648 | tf_op jit(solution)/shard_map/ppermute | solution.py:354
  7.9 28.1 %collective-permute-start = (bf16[560,1024]{1,0:T(8,128)(2,1)}, bf16[560,1024]{1,0:T(8,128)(2,1)S(1)}, u32[]{:S(2)}, u32[]{:S(2)}) collective-permute-start(bf16[560,1024]{1,0:T(8,128)(2,1)} %payload.1.far_ref), channel_id=1, source_target_pairs={{0,8},{8,16},{16,24},{24,0},{32,40},{40,48},{48,56},{56,32},{64,72... | collective-permute-start | bytes 3440648 | tf_op jit(solution)/shard_map/ppermute | solution.py:354
  37.5 33.3 %collective-permute-start.6 = (bf16[560,1024]{1,0:T(8,128)(2,1)}, bf16[560,1024]{1,0:T(8,128)(2,1)S(1)}, u32[]{:S(2)}, u32[]{:S(2)}) collective-permute-start(bf16[560,1024]{1,0:T(8,128)(2,1)} %get-tuple-element.41.refs_1_), channel_id=1, source_target_pairs={{0,32},{8,40},{16,48},{24,56},{96,0},{104,8},{112,16},{120,24},{1,... | collective-permute-start | bytes 3440648 | tf_op jit(solution)/shard_map/ppermute | solution.py:354
  40.0 30.9 %collective-permute-start.4 = (bf16[560,1024]{1,0:T(8,128)(2,1)}, bf16[560,1024]{1,0:T(8,128)(2,1)}, u32[]{:S(2)}, u32[]{:S(2)}) collective-permute-start(bf16[560,1024]{1,0:T(8,128)(2,1)} %get-tuple-element.39.refs_2_), channel_id=1, source_target_pairs={{0,24},{8,0},{16,8},{24,16},{32,56},{40,32},{48,40},{56,48},{64,88... | collective-permute-start | bytes 3440648 | tf_op jit(solution)/shard_map/ppermute | solution.py:354
  43.3 30.3 %collective-permute-start.7 = (bf16[560,1024]{1,0:T(8,128)(2,1)}, bf16[560,1024]{1,0:T(8,128)(2,1)S(1)}, u32[]{:S(2)}, u32[]{:S(2)}) collective-permute-start(bf16[560,1024]{1,0:T(8,128)(2,1)} %get-tuple-element.40.refs_0_), channel_id=1, source_target_pairs={{0,8},{24,0},{32,40},{56,32},{64,72},{88,64},{96,104},{120,96},{1,... | collective-permute-start | bytes 3440648 | tf_op jit(solution)/shard_map/ppermute | solution.py:354
  45.2 30.0 %collective-permute-start.5 = (bf16[560,1024]{1,0:T(8,128)(2,1)}, bf16[560,1024]{1,0:T(8,128)(2,1)S(1)}, u32[]{:S(2)}, u32[]{:S(2)}) collective-permute-start(bf16[560,1024]{1,0:T(8,128)(2,1)} %get-tuple-element.40.refs_0_), channel_id=1, source_target_pairs={{0,96},{8,104},{16,112},{24,120},{32,0},{40,8},{48,16},{56,24},{64... | collective-permute-start | bytes 3440648 | tf_op jit(solution)/shard_map/ppermute | solution.py:354
  49.9 49.8 %collective-permute-start.3 = (bf16[560,1024]{1,0:T(8,128)(2,1)}, bf16[560,1024]{1,0:T(8,128)(2,1)}, u32[]{:S(2)}, u32[]{:S(2)}) collective-permute-start(bf16[560,1024]{1,0:T(8,128)(2,1)} %get-tuple-element.39.refs_2_), channel_id=1, source_target_pairs={{0,96},{8,104},{16,112},{24,120},{32,0},{40,8},{48,16},{56,24},{64... | collective-permute-start | bytes 3440648 | tf_op jit(solution)/shard_map/ppermute | solution.py:354
  76.3 47.1 %collective-permute-start.8 = (bf16[560,1024]{1,0:T(8,128)(2,1)}, bf16[560,1024]{1,0:T(8,128)(2,1)S(1)}, u32[]{:S(2)}, u32[]{:S(2)}) collective-permute-start(bf16[560,1024]{1,0:T(8,128)(2,1)} %get-tuple-element.49.refs_1_), channel_id=1, source_target_pairs={{32,0},{40,8},{48,16},{56,24},{64,32},{72,40},{80,48},{88,56},{33,... | collective-permute-start | bytes 3440648 | tf_op jit(solution)/shard_map/ppermute | solution.py:354
  79.2 20.5 %collective-permute-start.9 = (bf16[80,512]{1,0:T(8,128)(2,1)}, bf16[80,512]{1,0:T(8,128)(2,1)S(1)}, u32[]{:S(2)}, u32[]{:S(2)}) collective-permute-start(bf16[80,512]{1,0:T(8,128)(2,1)} %get-tuple-element.54), channel_id=1, source_target_pairs={{8,0},{16,8},{24,16},{0,24},{40,32},{48,40},{56,48},{32,56},{72,64... | collective-permute-start | bytes 245768 | tf_op jit(solution)/shard_map/ppermute | solution.py:397
  82.6 40.7 %collective-permute-start.10 = (bf16[80,512]{1,0:T(8,128)(2,1)}, bf16[80,512]{1,0:T(8,128)(2,1)S(1)}, u32[]{:S(2)}, u32[]{:S(2)}) collective-permute-start(bf16[80,512]{1,0:T(8,128)(2,1)} %get-tuple-element.55), channel_id=1, source_target_pairs={{32,0},{40,8},{48,16},{56,24},{64,32},{72,40},{80,48},{88,56},{96,... | collective-permute-start | bytes 245768 | tf_op jit(solution)/shard_map/ppermute | solution.py:397
  85.6 37.7 %collective-permute-start.11 = (bf16[80,512]{1,0:T(8,128)(2,1)}, bf16[80,512]{1,0:T(8,128)(2,1)S(1)}, u32[]{:S(2)}, u32[]{:S(2)}) collective-permute-start(bf16[80,512]{1,0:T(8,128)(2,1)} %get-tuple-element.56), channel_id=1, source_target_pairs={{120,0},{96,8},{104,16},{112,24},{24,32},{0,40},{8,48},{16,56},{56... | collective-permute-start | bytes 245768 | tf_op jit(solution)/shard_map/ppermute | solution.py:397
  124.4 14.9 %collective-permute-start.12 = (bf16[80,512]{1,0:T(8,128)(2,1)}, bf16[80,512]{1,0:T(8,128)(2,1)S(1)}, u32[]{:S(2)}, u32[]{:S(2)}) collective-permute-start(bf16[80,512]{1,0:T(8,128)(2,1)} %get-tuple-element.64), channel_id=1, source_target_pairs={{104,0},{112,8},{120,16},{96,24},{8,32},{16,40},{24,48},{0,56},{40... | collective-permute-start | bytes 245768 | tf_op jit(solution)/shard_map/ppermute | solution.py:397
  127.7 11.6 %collective-permute-start.13 = (bf16[80,512]{1,0:T(8,128)(2,1)}, bf16[80,512]{1,0:T(8,128)(2,1)S(1)}, u32[]{:S(2)}, u32[]{:S(2)}) collective-permute-start(bf16[80,512]{1,0:T(8,128)(2,1)} %get-tuple-element.65), channel_id=1, source_target_pairs={{112,0},{120,8},{96,16},{104,24},{16,32},{24,40},{0,48},{8,56},{48... | collective-permute-start | bytes 245768 | tf_op jit(solution)/shard_map/ppermute | solution.py:397
  127.7 11.7 %collective-permute-start.14 = (bf16[80,512]{1,0:T(8,128)(2,1)}, bf16[80,512]{1,0:T(8,128)(2,1)S(1)}, u32[]{:S(2)}, u32[]{:S(2)}) collective-permute-start(bf16[80,512]{1,0:T(8,128)(2,1)} %get-tuple-element.66), channel_id=1, source_target_pairs={{0,64},{8,72},{16,80},{24,88},{32,96},{40,104},{48,112},{56,120},{... | collective-permute-start | bytes 245768 | tf_op jit(solution)/shard_map/ppermute | solution.py:397
  141.4 15.0 %collective-permute-start.19 = (bf16[80,512]{1,0:T(8,128)(2,1)S(1)}, bf16[80,512]{1,0:T(8,128)(2,1)S(1)}, u32[]{:S(2)}, u32[]{:S(2)}) collective-permute-start(bf16[80,512]{1,0:T(8,128)(2,1)S(1)} %copy-done.22), channel_id=1, source_target_pairs={{88,0},{64,8},{72,16},{80,24},{120,32},{96,40},{104,48},{112,56},{... | collective-permute-start | bytes 245768 | tf_op jit(solution)/shard_map/ppermute | solution.py:397
  143.5 16.6 %collective-permute-start.17 = (f32[72,512]{1,0:T(8,128)S(1)}, f32[72,512]{1,0:T(8,128)S(1)}, u32[]{:S(2)}, u32[]{:S(2)}) collective-permute-start(f32[72,512]{1,0:T(8,128)S(1)} %get-tuple-element.71), channel_id=1, source_target_pairs={{0,4},{1,5},{2,6},{3,7},{4,0},{5,1},{6,2},{7,3},{8,12},{9,13},{10,... | collective-permute-start | bytes 442376 | tf_op jit(solution)/shard_map/ppermute | solution.py:357
  145.4 14.7 %collective-permute-start.18 = (f32[72,512]{1,0:T(8,128)S(1)}, f32[72,512]{1,0:T(8,128)S(1)}, u32[]{:S(2)}, u32[]{:S(2)}) collective-permute-start(f32[72,512]{1,0:T(8,128)S(1)} %get-tuple-element.72), channel_id=1, source_target_pairs={{0,2},{1,3},{2,4},{3,5},{4,6},{5,7},{6,0},{7,1},{8,10},{9,11},{10,... | collective-permute-start | bytes 442376 | tf_op jit(solution)/shard_map/ppermute | solution.py:357
  147.8 12.3 %collective-permute-start.16 = (f32[72,512]{1,0:T(8,128)S(1)}, f32[72,512]{1,0:T(8,128)S(1)}, u32[]{:S(2)}, u32[]{:S(2)}) collective-permute-start(f32[72,512]{1,0:T(8,128)S(1)} %get-tuple-element.73), channel_id=1, source_target_pairs={{0,6},{1,7},{2,0},{3,1},{4,2},{5,3},{6,4},{7,5},{8,14},{9,15},{10,... | collective-permute-start | bytes 442376 | tf_op jit(solution)/shard_map/ppermute | solution.py:357
  148.7 10.4 %collective-permute-start.20 = (bf16[80,512]{1,0:T(8,128)(2,1)S(1)}, bf16[80,512]{1,0:T(8,128)(2,1)S(1)}, u32[]{:S(2)}, u32[]{:S(2)}) collective-permute-start(bf16[80,512]{1,0:T(8,128)(2,1)S(1)} %copy-done.23), channel_id=1, source_target_pairs={{0,16},{8,24},{32,48},{40,56},{64,80},{72,88},{96,112},{104,120},{... | collective-permute-start | bytes 245768 | tf_op jit(solution)/shard_map/ppermute | solution.py:397
  156.5 3.6 %collective-permute-start.21 = (bf16[80,512]{1,0:T(8,128)(2,1)S(1)}, bf16[80,512]{1,0:T(8,128)(2,1)S(1)}, u32[]{:S(2)}, u32[]{:S(2)}) collective-permute-start(bf16[80,512]{1,0:T(8,128)(2,1)S(1)} %copy-done.24), channel_id=1, source_target_pairs={{16,64},{24,72},{0,80},{8,88},{48,96},{56,104},{32,112},{40,120},{... | collective-permute-start | bytes 245768 | tf_op jit(solution)/shard_map/ppermute | solution.py:397
  161.9 4.1 %collective-permute-start.25 = (f32[64,64]{1,0:T(8,128)S(1)}, f32[64,64]{1,0:T(8,128)S(1)}, u32[]{:S(2)}, u32[]{:S(2)}) collective-permute-start(f32[64,64]{1,0:T(8,128)S(1)} %add.408), channel_id=1, source_target_pairs={{0,6},{1,7},{2,0},{3,1},{4,2},{5,3},{6,4},{7,5},{8,14},{9,15},{10,... | collective-permute-start | bytes 49160 | tf_op jit(solution)/shard_map/ppermute | solution.py:357
  163.7 5.5 %collective-permute-start.24 = (f32[64,64]{1,0:T(8,128)S(1)}, f32[64,64]{1,0:T(8,128)S(1)}, u32[]{:S(2)}, u32[]{:S(2)}) collective-permute-start(f32[64,64]{1,0:T(8,128)S(1)} %add.408), channel_id=1, source_target_pairs={{0,4},{1,5},{2,6},{3,7},{4,0},{5,1},{6,2},{7,3},{8,12},{9,13},{10,... | collective-permute-start | bytes 49160 | tf_op jit(solution)/shard_map/ppermute | solution.py:357
  165.1 5.1 %collective-permute-start.23 = (f32[64,64]{1,0:T(8,128)S(1)}, f32[64,64]{1,0:T(8,128)S(1)}, u32[]{:S(2)}, u32[]{:S(2)}) collective-permute-start(f32[64,64]{1,0:T(8,128)S(1)} %add.408), channel_id=1, source_target_pairs={{0,2},{1,3},{2,4},{3,5},{4,6},{5,7},{6,0},{7,1},{8,10},{9,11},{10,... | collective-permute-start | bytes 49160 | tf_op jit(solution)/shard_map/ppermute | solution.py:357
  (28 other events, 214.7 us)

commit v9 on v7

--- a/solution.py
+++ b/solution.py
@@ -411,15 +411,16 @@
     far["h"], far["e"], *parts = tie([far["h"], far["e"], *parts], token, far["d"], far["g"])
     far["f"] = move(far["h"], 0, 1)
     far["k"] = move(far["e"], -1, 0, top_half)
-    returned1 = give_back(group1, parts)
+    returned = give_back(("a",), parts[0:1])
+    later = parts[1:]
     sums, parts, token = work(group2, sums)
 
-    far["f"], far["k"], *parts = tie([far["f"], far["k"], *parts], *returned1)
-    returned2 = give_back(group2, parts)
+    far["f"], far["k"], *parts = tie([far["f"], far["k"], *later, *parts], *returned)
+    returned += give_back(("b", "c", *group2), parts)
     sums, parts, token = work(group3, sums)
 
-    sums, *parts = tie([sums, *parts], *returned2)
-    returned = returned1 + returned2 + give_back(group3, parts)
+    sums, *parts = tie([sums, *parts], *returned[1:])
+    returned += give_back(group3, parts)
 
     layer, core = here_col // CORES, here_col % CORES
     halves = sums.reshape(SIDE, CORES, ACC, BLOCK)

time: 190 us -> 189 us (level)
    ppermute x9, waiting for transfers between devices: 15.5 us -> 1.81 us  [give_back(): returned.append(lax.ppermute(part, 'row', back))]
    ppermute x9, waiting for transfers between devices: 13.3 us -> 26.3 us  [move(): return lax.ppermute(array, 'row', shift(dy, dx, keep))]
  transfers between devices with their start and end apart: 26 -> 26, of which waited for: 12 -> 13; matrix products, arithmetic and copies ran while one was open for 2% -> 2% of each run, Pallas kernels for 21% -> 21%
where the time goes in v9:
time: 189 us; the launch traced here: 188 us
  starting transfers between devices  48.4 us (26%)
  Pallas kernels  47.1 us (25%)
  blocking collectives  42 us (22%)
  waiting for transfers between devices  36.2 us (19%)
  local copies, waits for them, and re-layouts  9.83 us (5%)
  other arithmetic  3.11 us (2%)
    pallas_call x3, Pallas kernels, cells(): pl.pallas_call(functools.partial(cells_kernel, count), out_shape=[SUMS] +...  30 us
    ppermute x9, waiting for transfers between devices, move(): return lax.ppermute(array, 'row', shift(dy, dx, keep))  26.3 us
    all_to_all x1, blocking collectives, per_device(): gram = jnp.sum(lax.all_to_all(everyone, 'row', 0, 0), axis=0)  25.6 us
    ppermute x9, starting transfers between devices, give_back(): returned.append(lax.ppermute(part, 'row', back))  22.8 us
    ppermute x9, starting transfers between devices, move(): return lax.ppermute(array, 'row', shift(dy, dx, keep))  17.7 us
    all_gather x1, blocking collectives, per_device(): near_v = lax.all_gather(vectors, 'col')  16.4 us
    pallas_call x1, Pallas kernels, own_cells(): pl.pallas_call(own_kernel, out_shape=[SUMS, NORM, ROW, TOKEN], grid_spec=...  9.51 us
    ppermute x6, starting transfers between devices, turn(): lax.ppermute(array, 'col', [(i, (i + by * CORES) % COLS) for i in range(C...  7.77 us
  transfers between devices with their start and end apart: 26, of which 13 were waited for; matrix products, arithmetic and copies ran while one was open for 2% of the time, Pallas kernels for 21%

profile of v9, /device:TPU:0, one launch (start us, length us, event | category | flops | bytes accessed | tf_op | source)
XLA Modules:
  0.0 187.6 jit_solution(490821456281387723)
XLA Ops:
  0.0 2.6 %payload.1.far_ref = bf16[560,1024]{1,0:T(8,128)(2,1)} custom-call(s32[1]{0:T(128)} %bitcast.14.index_ref, bf16[8,512,1024]{2,1,0:T(8,128)(2,1)} %bitcast.37, bf16[64,512]{1,0:T(8,128)(2,1)} %v_ref.1), custom_call_target="tpu_custom_call" | custom-call | tf_op jit(solution)/shard_map/payload/pallas_call | solution.py:78
  2.6 5.3 %collective-permute-start.2 = (bf16[560,1024]{1,0:T(8,128)(2,1)}, bf16[560,1024]{1,0:T(8,128)(2,1)S(1)}, u32[]{:S(2)}, u32[]{:S(2)}) collective-permute-start(bf16[560,1024]{1,0:T(8,128)(2,1)} %payload.1.far_ref), channel_id=1, source_target_pairs={{0,120},{8,96},{16,104},{24,112},{32,24},{40,0},{48,8},{56,16},{64... | collective-permute-start | bytes 3440648 | tf_op jit(solution)/shard_map/ppermute | solution.py:354
  9.8 9.5 %cells_own.1 = (f32[8,72,512]{2,1,0:T(8,128)}, f32[8,512,128]{2,1,0:T(8,128)}, f32[8,8,512]{2,1,0:T(8,128)}, f32[8,128]{1,0:T(8,128)}) custom-call(s32[8]{0:T(128)} %slice_reduce_fusion.flags_ref, bf16[8,512,1024]{2,1,0:T(8,128)(2,1)} %bitcast.38, bf16[560,1024]{1,0:T(8,128)(2,1)} %payload.1.far_ref), custom_call_target="tpu_custom_call" | custom-call | flops 2147483648 | bytes 13631488 | tf_op jit(solution)/shard_map/cells_own/pallas_call | solution.py:229
  19.4 16.4 %all-gather = bf16[512,512]{1,0:T(8,128)(2,1)} all-gather(bf16[64,512]{1,0:T(8,128)(2,1)S(1)} %copy-done.22), channel_id=2, replica_groups=mesh['row'=16,'col'=8] {'col'}, dimensions={0}, use_global_device_ids=true | all-gather | bytes 589824 | tf_op jit(solution)/shard_map/all_gather | solution.py:400
  38.1 3.2 %collective-permute-start.4 = (bf16[560,1024]{1,0:T(8,128)(2,1)}, bf16[560,1024]{1,0:T(8,128)(2,1)}, u32[]{:S(2)}, u32[]{:S(2)}) collective-permute-start(bf16[560,1024]{1,0:T(8,128)(2,1)} %get-tuple-element.43.refs_2_), channel_id=1, source_target_pairs={{0,24},{8,0},{16,8},{24,16},{32,56},{40,32},{48,40},{56,48},{64,88... | collective-permute-start | bytes 3440648 | tf_op jit(solution)/shard_map/ppermute | solution.py:354
  41.3 1.9 %collective-permute-start.6 = (bf16[560,1024]{1,0:T(8,128)(2,1)}, bf16[560,1024]{1,0:T(8,128)(2,1)S(1)}, u32[]{:S(2)}, u32[]{:S(2)}) collective-permute-start(bf16[560,1024]{1,0:T(8,128)(2,1)} %get-tuple-element.44.refs_0_), channel_id=1, source_target_pairs={{0,8},{24,0},{32,40},{56,32},{64,72},{88,64},{96,104},{120,96},{1,... | collective-permute-start | bytes 3440648 | tf_op jit(solution)/shard_map/ppermute | solution.py:354
  43.2 5.4 %collective-permute-start.5 = (bf16[560,1024]{1,0:T(8,128)(2,1)}, bf16[560,1024]{1,0:T(8,128)(2,1)S(1)}, u32[]{:S(2)}, u32[]{:S(2)}) collective-permute-start(bf16[560,1024]{1,0:T(8,128)(2,1)} %get-tuple-element.44.refs_0_), channel_id=1, source_target_pairs={{0,96},{8,104},{16,112},{24,120},{32,0},{40,8},{48,16},{56,24},{64... | collective-permute-start | bytes 3440648 | tf_op jit(solution)/shard_map/ppermute | solution.py:354
  49.3 11.1 %cells.3 = (f32[8,72,512]{2,1,0:T(8,128)}, bf16[80,512]{1,0:T(8,128)(2,1)}, bf16[80,512]{1,0:T(8,128)(2,1)}, bf16[80,512]{1,0:T(8,128)(2,1)}, f32[8,128]{1,0:T(8,128)}) custom-call(s32[24]{0:T(128)} %reshape.212.flags_ref, bf16[8,512,1024]{2,1,0:T(8,128)(2,1)} %bitcast.39, bf16[8,64,512]{2,1,0:T(8,128)(2,1)} %bitcast.45, ...), custom_call_target="tpu_custom_call", output_to_operand_aliasing={{0}: (8, {})} | custom-call | flops 6442450944 | bytes 15728640 | tf_op jit(solution)/shard_map/cells/pallas_call | solution.py:268
  60.5 10.0 %collective-permute-done.3.refs_0_ = bf16[560,1024]{1,0:T(8,128)(2,1)S(1)} collective-permute-done((bf16[560,1024]{1,0:T(8,128)(2,1)}, bf16[560,1024]{1,0:T(8,128)(2,1)S(1)}, u32[]{:S(2)}, u32[]{:S(2)}) %collective-permute-start.3) | collective-permute-done | bytes 1146912 | tf_op jit(solution)/shard_map/ppermute | solution.py:354
  71.6 2.1 %collective-permute-done.5.refs_6_.refs_0_ = bf16[560,1024]{1,0:T(8,128)(2,1)S(1)} collective-permute-done((bf16[560,1024]{1,0:T(8,128)(2,1)}, bf16[560,1024]{1,0:T(8,128)(2,1)S(1)}, u32[]{:S(2)}, u32[]{:S(2)}) %collective-permute-start.5) | collective-permute-done | bytes 1146912 | tf_op jit(solution)/shard_map/ppermute | solution.py:354
  77.4 3.2 %collective-permute-start.9 = (bf16[80,512]{1,0:T(8,128)(2,1)}, bf16[80,512]{1,0:T(8,128)(2,1)S(1)}, u32[]{:S(2)}, u32[]{:S(2)}) collective-permute-start(bf16[80,512]{1,0:T(8,128)(2,1)} %get-tuple-element.60), channel_id=1, source_target_pairs={{8,0},{16,8},{24,16},{0,24},{40,32},{48,40},{56,48},{32,56},{72,64... | collective-permute-start | bytes 245768 | tf_op jit(solution)/shard_map/ppermute | solution.py:397
  80.6 9.9 %cells.4 = (f32[8,72,512]{2,1,0:T(8,128)}, bf16[80,512]{1,0:T(8,128)(2,1)}, bf16[80,512]{1,0:T(8,128)(2,1)}, bf16[80,512]{1,0:T(8,128)(2,1)}, f32[8,128]{1,0:T(8,128)}) custom-call(s32[24]{0:T(128)} %reshape.213.flags_ref, bf16[8,512,1024]{2,1,0:T(8,128)(2,1)} %bitcast.40, bf16[8,64,512]{2,1,0:T(8,128)(2,1)} %bitcast.46, ...), custom_call_target="tpu_custom_call", output_to_operand_aliasing={{0}: (8, {})} | custom-call | flops 6442450944 | bytes 15728640 | tf_op jit(solution)/shard_map/cells/pallas_call | solution.py:268
  90.6 12.0 %collective-permute-done.7.refs_0_ = bf16[560,1024]{1,0:T(8,128)(2,1)S(1)} collective-permute-done((bf16[560,1024]{1,0:T(8,128)(2,1)}, bf16[560,1024]{1,0:T(8,128)(2,1)S(1)}, u32[]{:S(2)}, u32[]{:S(2)}) %collective-permute-start.7) | collective-permute-done | bytes 1146912 | tf_op jit(solution)/shard_map/ppermute | solution.py:354
  104.3 3.5 %collective-permute-start.10 = (bf16[80,512]{1,0:T(8,128)(2,1)}, bf16[80,512]{1,0:T(8,128)(2,1)S(1)}, u32[]{:S(2)}, u32[]{:S(2)}) collective-permute-start(bf16[80,512]{1,0:T(8,128)(2,1)} %get-tuple-element.68), channel_id=1, source_target_pairs={{32,0},{40,8},{48,16},{56,24},{64,32},{72,40},{80,48},{88,56},{96,... | collective-permute-start | bytes 245768 | tf_op jit(solution)/shard_map/ppermute | solution.py:397
  107.9 2.9 %collective-permute-start.12 = (bf16[80,512]{1,0:T(8,128)(2,1)}, bf16[80,512]{1,0:T(8,128)(2,1)S(1)}, u32[]{:S(2)}, u32[]{:S(2)}) collective-permute-start(bf16[80,512]{1,0:T(8,128)(2,1)} %get-tuple-element.70), channel_id=1, source_target_pairs={{104,0},{112,8},{120,16},{96,24},{8,32},{16,40},{24,48},{0,56},{40... | collective-permute-start | bytes 245768 | tf_op jit(solution)/shard_map/ppermute | solution.py:397
  112.0 5.4 %collective-permute-start.14 = (bf16[80,512]{1,0:T(8,128)(2,1)}, bf16[80,512]{1,0:T(8,128)(2,1)S(1)}, u32[]{:S(2)}, u32[]{:S(2)}) collective-permute-start(bf16[80,512]{1,0:T(8,128)(2,1)} %get-tuple-element.72), channel_id=1, source_target_pairs={{0,64},{8,72},{16,80},{24,88},{32,96},{40,104},{48,112},{56,120},{... | collective-permute-start | bytes 245768 | tf_op jit(solution)/shard_map/ppermute | solution.py:397
  117.4 9.0 %cells.5 = (f32[8,72,512]{2,1,0:T(8,128)}, bf16[80,512]{1,0:T(8,128)(2,1)}, bf16[80,512]{1,0:T(8,128)(2,1)}, bf16[80,512]{1,0:T(8,128)(2,1)}, f32[8,128]{1,0:T(8,128)}) custom-call(s32[24]{0:T(128)} %reshape.210.flags_ref, bf16[8,512,1024]{2,1,0:T(8,128)(2,1)} %bitcast.41, bf16[8,64,512]{2,1,0:T(8,128)(2,1)} %bitcast.47, ...), custom_call_target="tpu_custom_call", output_to_operand_aliasing={{0}: (8, {})} | custom-call | flops 6442450944 | bytes 15728640 | tf_op jit(solution)/shard_map/cells/pallas_call | solution.py:268
  128.7 1.8 collective-permute-done.15
  130.7 1.5 collective-permute-start.17
  132.2 2.5 %collective-permute-start.18 = (f32[72,512]{1,0:T(8,128)S(1)}, f32[72,512]{1,0:T(8,128)S(1)}, u32[]{:S(2)}, u32[]{:S(2)}) collective-permute-start(f32[72,512]{1,0:T(8,128)S(1)} %get-tuple-element.78), channel_id=1, source_target_pairs={{0,2},{1,3},{2,4},{3,5},{4,6},{5,7},{6,0},{7,1},{8,10},{9,11},{10,... | collective-permute-start | bytes 442376 | tf_op jit(solution)/shard_map/ppermute | solution.py:357
  135.4 5.2 %collective-permute-start.20 = (bf16[80,512]{1,0:T(8,128)(2,1)S(1)}, bf16[80,512]{1,0:T(8,128)(2,1)S(1)}, u32[]{:S(2)}, u32[]{:S(2)}) collective-permute-start(bf16[80,512]{1,0:T(8,128)(2,1)S(1)} %copy-done.24), channel_id=1, source_target_pairs={{0,16},{8,24},{32,48},{40,56},{64,80},{72,88},{96,112},{104,120},{... | collective-permute-start | bytes 245768 | tf_op jit(solution)/shard_map/ppermute | solution.py:397
  149.7 3.2 %collective-permute-done.24 = f32[64,64]{1,0:T(8,128)S(1)} collective-permute-done((f32[64,64]{1,0:T(8,128)S(1)}, f32[64,64]{1,0:T(8,128)S(1)}, u32[]{:S(2)}, u32[]{:S(2)}) %collective-permute-start.24) | collective-permute-done | bytes 16416 | tf_op jit(solution)/shard_map/ppermute | solution.py:357
  154.3 25.6 %all_to_all.5 = f32[16,1,4096]{2,1,0:T(1,128)S(1)} all-to-all(f32[16,1,4096]{2,1,0:T(1,128)S(1)} %reshape.219), channel_id=1, replica_groups=mesh['row'=16,'col'=8] {'row'}, dimensions={0} | all-to-all | bytes 524288 | tf_op jit(solution)/shard_map/all_to_all | solution.py:442
  182.6 5.0 %solve.1 = f32[64,512]{1,0:T(8,128)} custom-call(f32[64,64]{1,0:T(8,128)} %reduce_sum.9.gram_ref, f32[64,512]{1,0:T(8,128)} %copy-done.1), custom_call_target="tpu_custom_call" | custom-call | tf_op jit(solution)/shard_map/solve/pallas_call | solution.py:338
  (145 shorter events, 28.7 us)
Async XLA Ops:
  2.6 33.1 %collective-permute-start.2 = (bf16[560,1024]{1,0:T(8,128)(2,1)}, bf16[560,1024]{1,0:T(8,128)(2,1)S(1)}, u32[]{:S(2)}, u32[]{:S(2)}) collective-permute-start(bf16[560,1024]{1,0:T(8,128)(2,1)} %payload.1.far_ref), channel_id=1, source_target_pairs={{0,120},{8,96},{16,104},{24,112},{32,24},{40,0},{48,8},{56,16},{64... | collective-permute-start | bytes 3440648 | tf_op jit(solution)/shard_map/ppermute | solution.py:354
  7.9 28.1 %collective-permute-start.1 = (bf16[560,1024]{1,0:T(8,128)(2,1)}, bf16[560,1024]{1,0:T(8,128)(2,1)S(1)}, u32[]{:S(2)}, u32[]{:S(2)}) collective-permute-start(bf16[560,1024]{1,0:T(8,128)(2,1)} %payload.1.far_ref), channel_id=1, source_target_pairs={{0,32},{8,40},{16,48},{24,56},{32,64},{40,72},{48,80},{56,88},{64,... | collective-permute-start | bytes 3440648 | tf_op jit(solution)/shard_map/ppermute | solution.py:354
  7.9 28.1 %collective-permute-start = (bf16[560,1024]{1,0:T(8,128)(2,1)}, bf16[560,1024]{1,0:T(8,128)(2,1)S(1)}, u32[]{:S(2)}, u32[]{:S(2)}) collective-permute-start(bf16[560,1024]{1,0:T(8,128)(2,1)} %payload.1.far_ref), channel_id=1, source_target_pairs={{0,8},{8,16},{16,24},{24,0},{32,40},{40,48},{48,56},{56,32},{64,72... | collective-permute-start | bytes 3440648 | tf_op jit(solution)/shard_map/ppermute | solution.py:354
  37.5 32.9 %collective-permute-start.3 = (bf16[560,1024]{1,0:T(8,128)(2,1)}, bf16[560,1024]{1,0:T(8,128)(2,1)S(1)}, u32[]{:S(2)}, u32[]{:S(2)}) collective-permute-start(bf16[560,1024]{1,0:T(8,128)(2,1)} %get-tuple-element.42.refs_1_), channel_id=1, source_target_pairs={{0,32},{8,40},{16,48},{24,56},{32,64},{40,72},{48,80},{56,88},{64,... | collective-permute-start | bytes 3440648 | tf_op jit(solution)/shard_map/ppermute | solution.py:354
  38.1 32.3 %collective-permute-start.4 = (bf16[560,1024]{1,0:T(8,128)(2,1)}, bf16[560,1024]{1,0:T(8,128)(2,1)}, u32[]{:S(2)}, u32[]{:S(2)}) collective-permute-start(bf16[560,1024]{1,0:T(8,128)(2,1)} %get-tuple-element.43.refs_2_), channel_id=1, source_target_pairs={{0,24},{8,0},{16,8},{24,16},{32,56},{40,32},{48,40},{56,48},{64,88... | collective-permute-start | bytes 3440648 | tf_op jit(solution)/shard_map/ppermute | solution.py:354
  41.3 30.3 %collective-permute-start.6 = (bf16[560,1024]{1,0:T(8,128)(2,1)}, bf16[560,1024]{1,0:T(8,128)(2,1)S(1)}, u32[]{:S(2)}, u32[]{:S(2)}) collective-permute-start(bf16[560,1024]{1,0:T(8,128)(2,1)} %get-tuple-element.44.refs_0_), channel_id=1, source_target_pairs={{0,8},{24,0},{32,40},{56,32},{64,72},{88,64},{96,104},{120,96},{1,... | collective-permute-start | bytes 3440648 | tf_op jit(solution)/shard_map/ppermute | solution.py:354
  43.2 30.4 %collective-permute-start.5 = (bf16[560,1024]{1,0:T(8,128)(2,1)}, bf16[560,1024]{1,0:T(8,128)(2,1)S(1)}, u32[]{:S(2)}, u32[]{:S(2)}) collective-permute-start(bf16[560,1024]{1,0:T(8,128)(2,1)} %get-tuple-element.44.refs_0_), channel_id=1, source_target_pairs={{0,96},{8,104},{16,112},{24,120},{32,0},{40,8},{48,16},{56,24},{64... | collective-permute-start | bytes 3440648 | tf_op jit(solution)/shard_map/ppermute | solution.py:354
  74.7 27.8 %collective-permute-start.7 = (bf16[560,1024]{1,0:T(8,128)(2,1)}, bf16[560,1024]{1,0:T(8,128)(2,1)S(1)}, u32[]{:S(2)}, u32[]{:S(2)}) collective-permute-start(bf16[560,1024]{1,0:T(8,128)(2,1)} %get-tuple-element.52.refs_2_), channel_id=1, source_target_pairs={{0,8},{8,16},{16,24},{24,0},{32,40},{40,48},{48,56},{56,32},{64,72... | collective-permute-start | bytes 3440648 | tf_op jit(solution)/shard_map/ppermute | solution.py:354
  74.7 28.5 %collective-permute-start.8 = (bf16[560,1024]{1,0:T(8,128)(2,1)}, bf16[560,1024]{1,0:T(8,128)(2,1)S(1)}, u32[]{:S(2)}, u32[]{:S(2)}) collective-permute-start(bf16[560,1024]{1,0:T(8,128)(2,1)} %get-tuple-element.53.refs_1_), channel_id=1, source_target_pairs={{32,0},{40,8},{48,16},{56,24},{64,32},{72,40},{80,48},{88,56},{33,... | collective-permute-start | bytes 3440648 | tf_op jit(solution)/shard_map/ppermute | solution.py:354
  77.4 13.1 %collective-permute-start.9 = (bf16[80,512]{1,0:T(8,128)(2,1)}, bf16[80,512]{1,0:T(8,128)(2,1)S(1)}, u32[]{:S(2)}, u32[]{:S(2)}) collective-permute-start(bf16[80,512]{1,0:T(8,128)(2,1)} %get-tuple-element.60), channel_id=1, source_target_pairs={{8,0},{16,8},{24,16},{0,24},{40,32},{48,40},{56,48},{32,56},{72,64... | collective-permute-start | bytes 245768 | tf_op jit(solution)/shard_map/ppermute | solution.py:397
  104.3 22.1 %collective-permute-start.10 = (bf16[80,512]{1,0:T(8,128)(2,1)}, bf16[80,512]{1,0:T(8,128)(2,1)S(1)}, u32[]{:S(2)}, u32[]{:S(2)}) collective-permute-start(bf16[80,512]{1,0:T(8,128)(2,1)} %get-tuple-element.68), channel_id=1, source_target_pairs={{32,0},{40,8},{48,16},{56,24},{64,32},{72,40},{80,48},{88,56},{96,... | collective-permute-start | bytes 245768 | tf_op jit(solution)/shard_map/ppermute | solution.py:397
  107.9 18.6 %collective-permute-start.11 = (bf16[80,512]{1,0:T(8,128)(2,1)}, bf16[80,512]{1,0:T(8,128)(2,1)S(1)}, u32[]{:S(2)}, u32[]{:S(2)}) collective-permute-start(bf16[80,512]{1,0:T(8,128)(2,1)} %get-tuple-element.69), channel_id=1, source_target_pairs={{120,0},{96,8},{104,16},{112,24},{24,32},{0,40},{8,48},{16,56},{56... | collective-permute-start | bytes 245768 | tf_op jit(solution)/shard_map/ppermute | solution.py:397
  107.9 18.6 %collective-permute-start.12 = (bf16[80,512]{1,0:T(8,128)(2,1)}, bf16[80,512]{1,0:T(8,128)(2,1)S(1)}, u32[]{:S(2)}, u32[]{:S(2)}) collective-permute-start(bf16[80,512]{1,0:T(8,128)(2,1)} %get-tuple-element.70), channel_id=1, source_target_pairs={{104,0},{112,8},{120,16},{96,24},{8,32},{16,40},{24,48},{0,56},{40... | collective-permute-start | bytes 245768 | tf_op jit(solution)/shard_map/ppermute | solution.py:397
  110.8 15.7 %collective-permute-start.13 = (bf16[80,512]{1,0:T(8,128)(2,1)}, bf16[80,512]{1,0:T(8,128)(2,1)S(1)}, u32[]{:S(2)}, u32[]{:S(2)}) collective-permute-start(bf16[80,512]{1,0:T(8,128)(2,1)} %get-tuple-element.71), channel_id=1, source_target_pairs={{112,0},{120,8},{96,16},{104,24},{16,32},{24,40},{0,48},{8,56},{48... | collective-permute-start | bytes 245768 | tf_op jit(solution)/shard_map/ppermute | solution.py:397
  112.0 14.5 %collective-permute-start.14 = (bf16[80,512]{1,0:T(8,128)(2,1)}, bf16[80,512]{1,0:T(8,128)(2,1)S(1)}, u32[]{:S(2)}, u32[]{:S(2)}) collective-permute-start(bf16[80,512]{1,0:T(8,128)(2,1)} %get-tuple-element.72), channel_id=1, source_target_pairs={{0,64},{8,72},{16,80},{24,88},{32,96},{40,104},{48,112},{56,120},{... | collective-permute-start | bytes 245768 | tf_op jit(solution)/shard_map/ppermute | solution.py:397
  128.6 12.0 %collective-permute-start.19 = (bf16[80,512]{1,0:T(8,128)(2,1)S(1)}, bf16[80,512]{1,0:T(8,128)(2,1)S(1)}, u32[]{:S(2)}, u32[]{:S(2)}) collective-permute-start(bf16[80,512]{1,0:T(8,128)(2,1)S(1)} %copy-done.23), channel_id=1, source_target_pairs={{72,0},{80,8},{88,16},{64,24},{104,32},{112,40},{120,48},{96,56},{... | collective-permute-start | bytes 245768 | tf_op jit(solution)/shard_map/ppermute | solution.py:397
  130.7 13.3 %collective-permute-start.17 = (f32[72,512]{1,0:T(8,128)S(1)}, f32[72,512]{1,0:T(8,128)S(1)}, u32[]{:S(2)}, u32[]{:S(2)}) collective-permute-start(f32[72,512]{1,0:T(8,128)S(1)} %get-tuple-element.77), channel_id=1, source_target_pairs={{0,4},{1,5},{2,6},{3,7},{4,0},{5,1},{6,2},{7,3},{8,12},{9,13},{10,... | collective-permute-start | bytes 442376 | tf_op jit(solution)/shard_map/ppermute | solution.py:357
  132.2 11.8 %collective-permute-start.18 = (f32[72,512]{1,0:T(8,128)S(1)}, f32[72,512]{1,0:T(8,128)S(1)}, u32[]{:S(2)}, u32[]{:S(2)}) collective-permute-start(f32[72,512]{1,0:T(8,128)S(1)} %get-tuple-element.78), channel_id=1, source_target_pairs={{0,2},{1,3},{2,4},{3,5},{4,6},{5,7},{6,0},{7,1},{8,10},{9,11},{10,... | collective-permute-start | bytes 442376 | tf_op jit(solution)/shard_map/ppermute | solution.py:357
  134.6 9.4 %collective-permute-start.16 = (f32[72,512]{1,0:T(8,128)S(1)}, f32[72,512]{1,0:T(8,128)S(1)}, u32[]{:S(2)}, u32[]{:S(2)}) collective-permute-start(f32[72,512]{1,0:T(8,128)S(1)} %get-tuple-element.79), channel_id=1, source_target_pairs={{0,6},{1,7},{2,0},{3,1},{4,2},{5,3},{6,4},{7,5},{8,14},{9,15},{10,... | collective-permute-start | bytes 442376 | tf_op jit(solution)/shard_map/ppermute | solution.py:357
  135.4 7.6 %collective-permute-start.20 = (bf16[80,512]{1,0:T(8,128)(2,1)S(1)}, bf16[80,512]{1,0:T(8,128)(2,1)S(1)}, u32[]{:S(2)}, u32[]{:S(2)}) collective-permute-start(bf16[80,512]{1,0:T(8,128)(2,1)S(1)} %copy-done.24), channel_id=1, source_target_pairs={{0,16},{8,24},{32,48},{40,56},{64,80},{72,88},{96,112},{104,120},{... | collective-permute-start | bytes 245768 | tf_op jit(solution)/shard_map/ppermute | solution.py:397
  140.6 3.3 %collective-permute-start.21 = (bf16[80,512]{1,0:T(8,128)(2,1)S(1)}, bf16[80,512]{1,0:T(8,128)(2,1)S(1)}, u32[]{:S(2)}, u32[]{:S(2)}) collective-permute-start(bf16[80,512]{1,0:T(8,128)(2,1)S(1)} %copy-done.25), channel_id=1, source_target_pairs={{16,64},{24,72},{0,80},{8,88},{48,96},{56,104},{32,112},{40,120},{... | collective-permute-start | bytes 245768 | tf_op jit(solution)/shard_map/ppermute | solution.py:397
  145.8 3.9 %collective-permute-start.25 = (f32[64,64]{1,0:T(8,128)S(1)}, f32[64,64]{1,0:T(8,128)S(1)}, u32[]{:S(2)}, u32[]{:S(2)}) collective-permute-start(f32[64,64]{1,0:T(8,128)S(1)} %add.404), channel_id=1, source_target_pairs={{0,6},{1,7},{2,0},{3,1},{4,2},{5,3},{6,4},{7,5},{8,14},{9,15},{10,... | collective-permute-start | bytes 49160 | tf_op jit(solution)/shard_map/ppermute | solution.py:357
  147.3 5.6 %collective-permute-start.24 = (f32[64,64]{1,0:T(8,128)S(1)}, f32[64,64]{1,0:T(8,128)S(1)}, u32[]{:S(2)}, u32[]{:S(2)}) collective-permute-start(f32[64,64]{1,0:T(8,128)S(1)} %add.404), channel_id=1, source_target_pairs={{0,4},{1,5},{2,6},{3,7},{4,0},{5,1},{6,2},{7,3},{8,12},{9,13},{10,... | collective-permute-start | bytes 49160 | tf_op jit(solution)/shard_map/ppermute | solution.py:357
  148.8 5.1 %collective-permute-start.23 = (f32[64,64]{1,0:T(8,128)S(1)}, f32[64,64]{1,0:T(8,128)S(1)}, u32[]{:S(2)}, u32[]{:S(2)}) collective-permute-start(f32[64,64]{1,0:T(8,128)S(1)} %add.404), channel_id=1, source_target_pairs={{0,2},{1,3},{2,4},{3,5},{4,6},{5,7},{6,0},{7,1},{8,10},{9,11},{10,... | collective-permute-start | bytes 49160 | tf_op jit(solution)/shard_map/ppermute | solution.py:357
  (29 other events, 181.2 us)

commit v10 on v9

--- a/solution.py
+++ b/solution.py
@@ -168,7 +168,7 @@
                 x_ref[near], far_ref[at, to : to + 256, :], NT, preferred_element_type=jnp.float32
             )
             p_ref[:, to : to + 256] = jnp.exp2(scores * columns * far[:, to : to + 256]).astype(jnp.bfloat16)
-        vectors = jnp.concatenate([v_ref[near], jnp.ones((16, BLOCK), jnp.bfloat16)], axis=0)
+        vectors = jnp.concatenate([v_ref[near].astype(jnp.bfloat16), jnp.ones((16, BLOCK), jnp.bfloat16)], axis=0)
         part = jnp.dot(vectors, p_ref[...], preferred_element_type=jnp.float32)
         far_sums_ref[at] += part[0:ACC, :]
         if both:
@@ -184,15 +184,16 @@
 
         for copy in near_copies(near):
             copy.wait()
-        for at in range(count):
-
-            @pl.when(near == 0)
-            def _():
-                if at == 0:
-                    row_copy.wait()
+
+        @pl.when(near == 0)
+        def _():
+            row_copy.wait()
+            for at in range(count):
                 far_copies[at].wait()
                 column_ref[at] = jnp.broadcast_to(side_norms(far_ref[at, BLOCK:PAYLOAD, :]), (128, BLOCK)).T
 
+        @pl.loop(0, count)
+        def _(at):
             flag = flags_ref[at * COLS + near]
             pl.when(flag == 1)(functools.partial(forward_only, at, near))
             pl.when(flag == 2)(functools.partial(backward, at, near, False))
@@ -254,7 +255,7 @@
     count = len(fars)
     buffers = [
         ((COLS, BLOCK, WIDTH), jnp.bfloat16),
-        ((COLS, EIGS, BLOCK), jnp.bfloat16),
+        ((COLS, EIGS, BLOCK), jnp.float32),
         ((count, PAYLOAD, WIDTH), jnp.bfloat16),
         ((COLS, BLOCK, 128), jnp.float32),
         ((COLS, 8, BLOCK), jnp.float32),
@@ -397,10 +398,10 @@
             returned.append(lax.ppermute(part, "row", back))
         return returned
 
-    near_v = lax.all_gather(vectors, "col")
+    near_v = lax.all_gather(vectors.astype(jnp.float32), "col")
     sums, norms, rows, token = own_cells(flags[0], blocks, far["own"])
 
-    far["a"], far["b"], far["c"] = tie([far["a"], far["b"], far["c"]], token, near_v)
+    far["a"], far["b"], far["c"] = tie([far["a"], far["b"], far["c"]], token)
     far["d"] = move(far["a"], -1, 0)
     far["e"] = move(far["c"], 0, -1)
     far["g"] = move(far["a"], 0, 1, left_half)

time: 189 us -> 195 us (1.032)
  blocking collectives: 42 us -> 25.5 us
  between operations: 0.7 us -> 14.3 us
  waiting for transfers between devices: 36.2 us -> 47.3 us
  starting transfers between devices: 48.4 us -> 45.2 us
    all_gather x1 -> x0, blocking collectives: 16.4 us -> none  [per_device(): near_v = lax.all_gather(vectors, 'col')]
    ppermute x9, waiting for transfers between devices: 26.3 us -> 37.5 us  [move(): return lax.ppermute(array, 'row', shift(dy, dx, keep))]
    ppermute x9, starting transfers between devices: 17.7 us -> 13.8 us  [move(): return lax.ppermute(array, 'row', shift(dy, dx, keep))]
  transfers between devices with their start and end apart: 26 -> 27, of which waited for: 13 -> 13; matrix products, arithmetic and copies ran while one was open for 2% -> 2% of each run, Pallas kernels for 21% -> 21%
where the time goes in v10:
time: 195 us; the launch traced here: 193 us
  Pallas kernels  47.3 us (24%)
  waiting for transfers between devices  47.3 us (24%)
  starting transfers between devices  45.2 us (23%)
  blocking collectives  25.5 us (13%)
  between operations  14.3 us (7%)
  local copies, waits for them, and re-layouts  9.94 us (5%)
  other arithmetic  3.77 us (2%)
    ppermute x9, waiting for transfers between devices, move(): return lax.ppermute(array, 'row', shift(dy, dx, keep))  37.5 us
    pallas_call x3, Pallas kernels, cells(): pl.pallas_call(functools.partial(cells_kernel, count), out_shape=[SUMS] +...  30.2 us
    all_to_all x1, blocking collectives, per_device(): gram = jnp.sum(lax.all_to_all(everyone, 'row', 0, 0), axis=0)  25.5 us
    ppermute x9, starting transfers between devices, give_back(): returned.append(lax.ppermute(part, 'row', back))  22 us
    ppermute x9, starting transfers between devices, move(): return lax.ppermute(array, 'row', shift(dy, dx, keep))  13.8 us
    pallas_call x1, Pallas kernels, own_cells(): pl.pallas_call(own_kernel, out_shape=[SUMS, NORM, ROW, TOKEN], grid_spec=...  9.45 us
    ppermute x6, starting transfers between devices, turn(): lax.ppermute(array, 'col', [(i, (i + by * CORES) % COLS) for i in range(C...  9.21 us
    ppermute x6, waiting for transfers between devices, turn(): lax.ppermute(array, 'col', [(i, (i + by * CORES) % COLS) for i in range(C...  4.98 us
  transfers between devices with their start and end apart: 27, of which 13 were waited for; matrix products, arithmetic and copies ran while one was open for 2% of the time, Pallas kernels for 21%

profile of v10, /device:TPU:0, one launch (start us, length us, event | category | flops | bytes accessed | tf_op | source)
XLA Modules:
  0.0 193.5 jit_solution(3301223960218822678)
XLA Ops:
  6.5 2.6 %payload.1.far_ref = bf16[560,1024]{1,0:T(8,128)(2,1)} custom-call(s32[1]{0:T(128)} %bitcast.14.index_ref, bf16[8,512,1024]{2,1,0:T(8,128)(2,1)} %bitcast.37, bf16[64,512]{1,0:T(8,128)(2,1)} %v_ref.1), custom_call_target="tpu_custom_call" | custom-call | tf_op jit(solution)/shard_map/payload/pallas_call | solution.py:78
  9.2 5.3 %collective-permute-start.2 = (bf16[560,1024]{1,0:T(8,128)(2,1)}, bf16[560,1024]{1,0:T(8,128)(2,1)S(1)}, u32[]{:S(2)}, u32[]{:S(2)}) collective-permute-start(bf16[560,1024]{1,0:T(8,128)(2,1)} %payload.1.far_ref), channel_id=1, source_target_pairs={{0,120},{8,96},{16,104},{24,112},{32,24},{40,0},{48,8},{56,16},{64... | collective-permute-start | bytes 3440648 | tf_op jit(solution)/shard_map/ppermute | solution.py:355
  17.3 9.5 %cells_own.1 = (f32[8,72,512]{2,1,0:T(8,128)}, f32[8,512,128]{2,1,0:T(8,128)}, f32[8,8,512]{2,1,0:T(8,128)}, f32[8,128]{1,0:T(8,128)}) custom-call(s32[8]{0:T(128)} %slice_reduce_fusion.flags_ref, bf16[8,512,1024]{2,1,0:T(8,128)(2,1)} %bitcast.38, bf16[560,1024]{1,0:T(8,128)(2,1)} %payload.1.far_ref), custom_call_target="tpu_custom_call" | custom-call | flops 2147483648 | bytes 13631488 | tf_op jit(solution)/shard_map/cells_own/pallas_call | solution.py:230
  26.7 12.6 %collective-permute-done.2.refs_2_ = bf16[560,1024]{1,0:T(8,128)(2,1)S(1)} collective-permute-done((bf16[560,1024]{1,0:T(8,128)(2,1)}, bf16[560,1024]{1,0:T(8,128)(2,1)S(1)}, u32[]{:S(2)}, u32[]{:S(2)}) %collective-permute-start.2) | collective-permute-done | bytes 1146912 | tf_op jit(solution)/shard_map/ppermute | solution.py:355
  39.3 3.3 %collective-permute-done.1.refs_1_ = bf16[560,1024]{1,0:T(8,128)(2,1)S(1)} collective-permute-done((bf16[560,1024]{1,0:T(8,128)(2,1)}, bf16[560,1024]{1,0:T(8,128)(2,1)S(1)}, u32[]{:S(2)}, u32[]{:S(2)}) %collective-permute-start.1) | collective-permute-done | bytes 1146912 | tf_op jit(solution)/shard_map/ppermute | solution.py:355
  44.9 3.1 %collective-permute-start.6 = (bf16[560,1024]{1,0:T(8,128)(2,1)}, bf16[560,1024]{1,0:T(8,128)(2,1)S(1)}, u32[]{:S(2)}, u32[]{:S(2)}) collective-permute-start(bf16[560,1024]{1,0:T(8,128)(2,1)} %get-tuple-element.44.refs_0_), channel_id=1, source_target_pairs={{0,8},{24,0},{32,40},{56,32},{64,72},{88,64},{96,104},{120,96},{1,... | collective-permute-start | bytes 3440648 | tf_op jit(solution)/shard_map/ppermute | solution.py:355
  48.0 3.3 %collective-permute-start.5 = (bf16[560,1024]{1,0:T(8,128)(2,1)}, bf16[560,1024]{1,0:T(8,128)(2,1)S(1)}, u32[]{:S(2)}, u32[]{:S(2)}) collective-permute-start(bf16[560,1024]{1,0:T(8,128)(2,1)} %get-tuple-element.44.refs_0_), channel_id=1, source_target_pairs={{0,96},{8,104},{16,112},{24,120},{32,0},{40,8},{48,16},{56,24},{64... | collective-permute-start | bytes 3440648 | tf_op jit(solution)/shard_map/ppermute | solution.py:355
  52.1 11.0 %cells.3 = (f32[8,72,512]{2,1,0:T(8,128)}, bf16[80,512]{1,0:T(8,128)(2,1)}, bf16[80,512]{1,0:T(8,128)(2,1)}, bf16[80,512]{1,0:T(8,128)(2,1)}, f32[8,128]{1,0:T(8,128)}) custom-call(s32[24]{0:T(128)} %reshape.212.flags_ref, bf16[8,512,1024]{2,1,0:T(8,128)(2,1)} %bitcast.39, f32[8,64,512]{2,1,0:T(8,128)} %bitcast.45, ...), custom_call_target="tpu_custom_call", output_to_operand_aliasing={{0}: (8, {})} | custom-call | flops 6442450944 | bytes 15728640 | tf_op jit(solution)/shard_map/cells/pallas_call | solution.py:269
  63.1 8.2 %collective-permute-done.3.refs_0_ = bf16[560,1024]{1,0:T(8,128)(2,1)S(1)} collective-permute-done((bf16[560,1024]{1,0:T(8,128)(2,1)}, bf16[560,1024]{1,0:T(8,128)(2,1)S(1)}, u32[]{:S(2)}, u32[]{:S(2)}) %collective-permute-start.3) | collective-permute-done | bytes 1146912 | tf_op jit(solution)/shard_map/ppermute | solution.py:355
  71.3 2.4 %collective-permute-done.6.refs_7_.refs_1_ = bf16[560,1024]{1,0:T(8,128)(2,1)S(1)} collective-permute-done((bf16[560,1024]{1,0:T(8,128)(2,1)}, bf16[560,1024]{1,0:T(8,128)(2,1)S(1)}, u32[]{:S(2)}, u32[]{:S(2)}) %collective-permute-start.6) | collective-permute-done | bytes 1146912 | tf_op jit(solution)/shard_map/ppermute | solution.py:355
  77.9 3.2 %collective-permute-start.9 = (bf16[80,512]{1,0:T(8,128)(2,1)}, bf16[80,512]{1,0:T(8,128)(2,1)S(1)}, u32[]{:S(2)}, u32[]{:S(2)}) collective-permute-start(bf16[80,512]{1,0:T(8,128)(2,1)} %get-tuple-element.60), channel_id=1, source_target_pairs={{8,0},{16,8},{24,16},{0,24},{40,32},{48,40},{56,48},{32,56},{72,64... | collective-permute-start | bytes 245768 | tf_op jit(solution)/shard_map/ppermute | solution.py:398
  81.1 10.1 %cells.4 = (f32[8,72,512]{2,1,0:T(8,128)}, bf16[80,512]{1,0:T(8,128)(2,1)}, bf16[80,512]{1,0:T(8,128)(2,1)}, bf16[80,512]{1,0:T(8,128)(2,1)}, f32[8,128]{1,0:T(8,128)}) custom-call(s32[24]{0:T(128)} %reshape.213.flags_ref, bf16[8,512,1024]{2,1,0:T(8,128)(2,1)} %bitcast.40, f32[8,64,512]{2,1,0:T(8,128)} %bitcast.46, ...), custom_call_target="tpu_custom_call", output_to_operand_aliasing={{0}: (8, {})} | custom-call | flops 6442450944 | bytes 15728640 | tf_op jit(solution)/shard_map/cells/pallas_call | solution.py:269
  91.3 9.9 %collective-permute-done.7.refs_0_ = bf16[560,1024]{1,0:T(8,128)(2,1)S(1)} collective-permute-done((bf16[560,1024]{1,0:T(8,128)(2,1)}, bf16[560,1024]{1,0:T(8,128)(2,1)S(1)}, u32[]{:S(2)}, u32[]{:S(2)}) %collective-permute-start.7) | collective-permute-done | bytes 1146912 | tf_op jit(solution)/shard_map/ppermute | solution.py:355
  102.9 2.7 %collective-permute-start.10 = (bf16[80,512]{1,0:T(8,128)(2,1)}, bf16[80,512]{1,0:T(8,128)(2,1)S(1)}, u32[]{:S(2)}, u32[]{:S(2)}) collective-permute-start(bf16[80,512]{1,0:T(8,128)(2,1)} %get-tuple-element.68), channel_id=1, source_target_pairs={{32,0},{40,8},{48,16},{56,24},{64,32},{72,40},{80,48},{88,56},{96,... | collective-permute-start | bytes 245768 | tf_op jit(solution)/shard_map/ppermute | solution.py:398
  105.6 4.1 %collective-permute-start.12 = (bf16[80,512]{1,0:T(8,128)(2,1)}, bf16[80,512]{1,0:T(8,128)(2,1)S(1)}, u32[]{:S(2)}, u32[]{:S(2)}) collective-permute-start(bf16[80,512]{1,0:T(8,128)(2,1)} %get-tuple-element.70), channel_id=1, source_target_pairs={{104,0},{112,8},{120,16},{96,24},{8,32},{16,40},{24,48},{0,56},{40... | collective-permute-start | bytes 245768 | tf_op jit(solution)/shard_map/ppermute | solution.py:398
  109.8 5.2 %collective-permute-start.14 = (bf16[80,512]{1,0:T(8,128)(2,1)}, bf16[80,512]{1,0:T(8,128)(2,1)S(1)}, u32[]{:S(2)}, u32[]{:S(2)}) collective-permute-start(bf16[80,512]{1,0:T(8,128)(2,1)} %get-tuple-element.72), channel_id=1, source_target_pairs={{0,64},{8,72},{16,80},{24,88},{32,96},{40,104},{48,112},{56,120},{... | collective-permute-start | bytes 245768 | tf_op jit(solution)/shard_map/ppermute | solution.py:398
  115.0 9.2 %cells.5 = (f32[8,72,512]{2,1,0:T(8,128)}, bf16[80,512]{1,0:T(8,128)(2,1)}, bf16[80,512]{1,0:T(8,128)(2,1)}, bf16[80,512]{1,0:T(8,128)(2,1)}, f32[8,128]{1,0:T(8,128)}) custom-call(s32[24]{0:T(128)} %reshape.210.flags_ref, bf16[8,512,1024]{2,1,0:T(8,128)(2,1)} %bitcast.41, f32[8,64,512]{2,1,0:T(8,128)} %bitcast.47, ...), custom_call_target="tpu_custom_call", output_to_operand_aliasing={{0}: (8, {})} | custom-call | flops 6442450944 | bytes 15728640 | tf_op jit(solution)/shard_map/cells/pallas_call | solution.py:269
  128.5 4.0 %collective-permute-start.17 = (f32[72,512]{1,0:T(8,128)S(1)}, f32[72,512]{1,0:T(8,128)S(1)}, u32[]{:S(2)}, u32[]{:S(2)}) collective-permute-start(f32[72,512]{1,0:T(8,128)S(1)} %get-tuple-element.77), channel_id=1, source_target_pairs={{0,4},{1,5},{2,6},{3,7},{4,0},{5,1},{6,2},{7,3},{8,12},{9,13},{10,... | collective-permute-start | bytes 442376 | tf_op jit(solution)/shard_map/ppermute | solution.py:358
  133.4 2.2 %collective-permute-start.16 = (f32[72,512]{1,0:T(8,128)S(1)}, f32[72,512]{1,0:T(8,128)S(1)}, u32[]{:S(2)}, u32[]{:S(2)}) collective-permute-start(f32[72,512]{1,0:T(8,128)S(1)} %get-tuple-element.79), channel_id=1, source_target_pairs={{0,6},{1,7},{2,0},{3,1},{4,2},{5,3},{6,4},{7,5},{8,14},{9,15},{10,... | collective-permute-start | bytes 442376 | tf_op jit(solution)/shard_map/ppermute | solution.py:358
  135.7 4.2 %collective-permute-start.20 = (bf16[80,512]{1,0:T(8,128)(2,1)S(1)}, bf16[80,512]{1,0:T(8,128)(2,1)S(1)}, u32[]{:S(2)}, u32[]{:S(2)}) collective-permute-start(bf16[80,512]{1,0:T(8,128)(2,1)S(1)} %copy-done.24), channel_id=1, source_target_pairs={{0,16},{8,24},{32,48},{40,56},{64,80},{72,88},{96,112},{104,120},{... | collective-permute-start | bytes 245768 | tf_op jit(solution)/shard_map/ppermute | solution.py:398
  139.9 2.3 %collective-permute-start.21 = (bf16[80,512]{1,0:T(8,128)(2,1)S(1)}, bf16[80,512]{1,0:T(8,128)(2,1)S(1)}, u32[]{:S(2)}, u32[]{:S(2)}) collective-permute-start(bf16[80,512]{1,0:T(8,128)(2,1)S(1)} %copy-done.25), channel_id=1, source_target_pairs={{16,64},{24,72},{0,80},{8,88},{48,96},{56,104},{32,112},{40,120},{... | collective-permute-start | bytes 245768 | tf_op jit(solution)/shard_map/ppermute | solution.py:398
  148.1 1.9 collective-permute-done.25
  153.5 25.5 %all_to_all.5 = f32[16,1,4096]{2,1,0:T(1,128)S(1)} all-to-all(f32[16,1,4096]{2,1,0:T(1,128)S(1)} %reshape.220), channel_id=1, replica_groups=mesh['row'=16,'col'=8] {'row'}, dimensions={0} | all-to-all | bytes 524288 | tf_op jit(solution)/shard_map/all_to_all | solution.py:443
  181.7 5.0 %solve.1 = f32[64,512]{1,0:T(8,128)} custom-call(f32[64,64]{1,0:T(8,128)} %reduce_sum.9.gram_ref, f32[64,512]{1,0:T(8,128)} %copy-done.1), custom_call_target="tpu_custom_call" | custom-call | tf_op jit(solution)/shard_map/solve/pallas_call | solution.py:339
  (148 shorter events, 28.5 us)
Async XLA Ops:
  6.5 45.6 %all-gather.3.cloned.1.call-start = ((), (), s32[]{:S(2)}) async-start(), calls=%async_computation.1 | async-start | bytes 1179648 | tf_op jit(solution)/shard_map/all_gather | solution.py:401
  9.2 30.1 %collective-permute-start.2 = (bf16[560,1024]{1,0:T(8,128)(2,1)}, bf16[560,1024]{1,0:T(8,128)(2,1)S(1)}, u32[]{:S(2)}, u32[]{:S(2)}) collective-permute-start(bf16[560,1024]{1,0:T(8,128)(2,1)} %payload.1.far_ref), channel_id=1, source_target_pairs={{0,120},{8,96},{16,104},{24,112},{32,24},{40,0},{48,8},{56,16},{64... | collective-permute-start | bytes 3440648 | tf_op jit(solution)/shard_map/ppermute | solution.py:355
  14.5 28.1 %collective-permute-start.1 = (bf16[560,1024]{1,0:T(8,128)(2,1)}, bf16[560,1024]{1,0:T(8,128)(2,1)S(1)}, u32[]{:S(2)}, u32[]{:S(2)}) collective-permute-start(bf16[560,1024]{1,0:T(8,128)(2,1)} %payload.1.far_ref), channel_id=1, source_target_pairs={{0,32},{8,40},{16,48},{24,56},{32,64},{40,72},{48,80},{56,88},{64,... | collective-permute-start | bytes 3440648 | tf_op jit(solution)/shard_map/ppermute | solution.py:355
  14.5 28.1 %collective-permute-start = (bf16[560,1024]{1,0:T(8,128)(2,1)}, bf16[560,1024]{1,0:T(8,128)(2,1)S(1)}, u32[]{:S(2)}, u32[]{:S(2)}) collective-permute-start(bf16[560,1024]{1,0:T(8,128)(2,1)} %payload.1.far_ref), channel_id=1, source_target_pairs={{0,8},{8,16},{16,24},{24,0},{32,40},{40,48},{48,56},{56,32},{64,72... | collective-permute-start | bytes 3440648 | tf_op jit(solution)/shard_map/ppermute | solution.py:355
  44.1 27.2 %collective-permute-start.3 = (bf16[560,1024]{1,0:T(8,128)(2,1)}, bf16[560,1024]{1,0:T(8,128)(2,1)S(1)}, u32[]{:S(2)}, u32[]{:S(2)}) collective-permute-start(bf16[560,1024]{1,0:T(8,128)(2,1)} %get-tuple-element.42.refs_1_), channel_id=1, source_target_pairs={{0,32},{8,40},{16,48},{24,56},{32,64},{40,72},{48,80},{56,88},{64,... | collective-permute-start | bytes 3440648 | tf_op jit(solution)/shard_map/ppermute | solution.py:355
  44.1 27.2 %collective-permute-start.4 = (bf16[560,1024]{1,0:T(8,128)(2,1)}, bf16[560,1024]{1,0:T(8,128)(2,1)}, u32[]{:S(2)}, u32[]{:S(2)}) collective-permute-start(bf16[560,1024]{1,0:T(8,128)(2,1)} %get-tuple-element.43.refs_2_), channel_id=1, source_target_pairs={{0,24},{8,0},{16,8},{24,16},{32,56},{40,32},{48,40},{56,48},{64,88... | collective-permute-start | bytes 3440648 | tf_op jit(solution)/shard_map/ppermute | solution.py:355
  44.9 28.8 %collective-permute-start.6 = (bf16[560,1024]{1,0:T(8,128)(2,1)}, bf16[560,1024]{1,0:T(8,128)(2,1)S(1)}, u32[]{:S(2)}, u32[]{:S(2)}) collective-permute-start(bf16[560,1024]{1,0:T(8,128)(2,1)} %get-tuple-element.44.refs_0_), channel_id=1, source_target_pairs={{0,8},{24,0},{32,40},{56,32},{64,72},{88,64},{96,104},{120,96},{1,... | collective-permute-start | bytes 3440648 | tf_op jit(solution)/shard_map/ppermute | solution.py:355
  48.0 26.1 %collective-permute-start.5 = (bf16[560,1024]{1,0:T(8,128)(2,1)}, bf16[560,1024]{1,0:T(8,128)(2,1)S(1)}, u32[]{:S(2)}, u32[]{:S(2)}) collective-permute-start(bf16[560,1024]{1,0:T(8,128)(2,1)} %get-tuple-element.44.refs_0_), channel_id=1, source_target_pairs={{0,96},{8,104},{16,112},{24,120},{32,0},{40,8},{48,16},{56,24},{64... | collective-permute-start | bytes 3440648 | tf_op jit(solution)/shard_map/ppermute | solution.py:355
  75.2 26.0 %collective-permute-start.7 = (bf16[560,1024]{1,0:T(8,128)(2,1)}, bf16[560,1024]{1,0:T(8,128)(2,1)S(1)}, u32[]{:S(2)}, u32[]{:S(2)}) collective-permute-start(bf16[560,1024]{1,0:T(8,128)(2,1)} %get-tuple-element.52.refs_2_), channel_id=1, source_target_pairs={{0,8},{8,16},{16,24},{24,0},{32,40},{40,48},{48,56},{56,32},{64,72... | collective-permute-start | bytes 3440648 | tf_op jit(solution)/shard_map/ppermute | solution.py:355
  75.2 26.7 %collective-permute-start.8 = (bf16[560,1024]{1,0:T(8,128)(2,1)}, bf16[560,1024]{1,0:T(8,128)(2,1)S(1)}, u32[]{:S(2)}, u32[]{:S(2)}) collective-permute-start(bf16[560,1024]{1,0:T(8,128)(2,1)} %get-tuple-element.53.refs_1_), channel_id=1, source_target_pairs={{32,0},{40,8},{48,16},{56,24},{64,32},{72,40},{80,48},{88,56},{33,... | collective-permute-start | bytes 3440648 | tf_op jit(solution)/shard_map/ppermute | solution.py:355
  77.9 13.4 %collective-permute-start.9 = (bf16[80,512]{1,0:T(8,128)(2,1)}, bf16[80,512]{1,0:T(8,128)(2,1)S(1)}, u32[]{:S(2)}, u32[]{:S(2)}) collective-permute-start(bf16[80,512]{1,0:T(8,128)(2,1)} %get-tuple-element.60), channel_id=1, source_target_pairs={{8,0},{16,8},{24,16},{0,24},{40,32},{48,40},{56,48},{32,56},{72,64... | collective-permute-start | bytes 245768 | tf_op jit(solution)/shard_map/ppermute | solution.py:398
  102.9 21.3 %collective-permute-start.10 = (bf16[80,512]{1,0:T(8,128)(2,1)}, bf16[80,512]{1,0:T(8,128)(2,1)S(1)}, u32[]{:S(2)}, u32[]{:S(2)}) collective-permute-start(bf16[80,512]{1,0:T(8,128)(2,1)} %get-tuple-element.68), channel_id=1, source_target_pairs={{32,0},{40,8},{48,16},{56,24},{64,32},{72,40},{80,48},{88,56},{96,... | collective-permute-start | bytes 245768 | tf_op jit(solution)/shard_map/ppermute | solution.py:398
  105.6 18.6 %collective-permute-start.11 = (bf16[80,512]{1,0:T(8,128)(2,1)}, bf16[80,512]{1,0:T(8,128)(2,1)S(1)}, u32[]{:S(2)}, u32[]{:S(2)}) collective-permute-start(bf16[80,512]{1,0:T(8,128)(2,1)} %get-tuple-element.69), channel_id=1, source_target_pairs={{120,0},{96,8},{104,16},{112,24},{24,32},{0,40},{8,48},{16,56},{56... | collective-permute-start | bytes 245768 | tf_op jit(solution)/shard_map/ppermute | solution.py:398
  105.6 18.6 %collective-permute-start.12 = (bf16[80,512]{1,0:T(8,128)(2,1)}, bf16[80,512]{1,0:T(8,128)(2,1)S(1)}, u32[]{:S(2)}, u32[]{:S(2)}) collective-permute-start(bf16[80,512]{1,0:T(8,128)(2,1)} %get-tuple-element.70), channel_id=1, source_target_pairs={{104,0},{112,8},{120,16},{96,24},{8,32},{16,40},{24,48},{0,56},{40... | collective-permute-start | bytes 245768 | tf_op jit(solution)/shard_map/ppermute | solution.py:398
  109.7 14.6 %collective-permute-start.13 = (bf16[80,512]{1,0:T(8,128)(2,1)}, bf16[80,512]{1,0:T(8,128)(2,1)S(1)}, u32[]{:S(2)}, u32[]{:S(2)}) collective-permute-start(bf16[80,512]{1,0:T(8,128)(2,1)} %get-tuple-element.71), channel_id=1, source_target_pairs={{112,0},{120,8},{96,16},{104,24},{16,32},{24,40},{0,48},{8,56},{48... | collective-permute-start | bytes 245768 | tf_op jit(solution)/shard_map/ppermute | solution.py:398
  109.8 14.4 %collective-permute-start.14 = (bf16[80,512]{1,0:T(8,128)(2,1)}, bf16[80,512]{1,0:T(8,128)(2,1)S(1)}, u32[]{:S(2)}, u32[]{:S(2)}) collective-permute-start(bf16[80,512]{1,0:T(8,128)(2,1)} %get-tuple-element.72), channel_id=1, source_target_pairs={{0,64},{8,72},{16,80},{24,88},{32,96},{40,104},{48,112},{56,120},{... | collective-permute-start | bytes 245768 | tf_op jit(solution)/shard_map/ppermute | solution.py:398
  126.4 13.5 %collective-permute-start.19 = (bf16[80,512]{1,0:T(8,128)(2,1)S(1)}, bf16[80,512]{1,0:T(8,128)(2,1)S(1)}, u32[]{:S(2)}, u32[]{:S(2)}) collective-permute-start(bf16[80,512]{1,0:T(8,128)(2,1)S(1)} %copy-done.23), channel_id=1, source_target_pairs={{72,0},{80,8},{88,16},{64,24},{104,32},{112,40},{120,48},{96,56},{... | collective-permute-start | bytes 245768 | tf_op jit(solution)/shard_map/ppermute | solution.py:398
  128.5 15.8 %collective-permute-start.17 = (f32[72,512]{1,0:T(8,128)S(1)}, f32[72,512]{1,0:T(8,128)S(1)}, u32[]{:S(2)}, u32[]{:S(2)}) collective-permute-start(f32[72,512]{1,0:T(8,128)S(1)} %get-tuple-element.77), channel_id=1, source_target_pairs={{0,4},{1,5},{2,6},{3,7},{4,0},{5,1},{6,2},{7,3},{8,12},{9,13},{10,... | collective-permute-start | bytes 442376 | tf_op jit(solution)/shard_map/ppermute | solution.py:358
  132.4 11.9 %collective-permute-start.18 = (f32[72,512]{1,0:T(8,128)S(1)}, f32[72,512]{1,0:T(8,128)S(1)}, u32[]{:S(2)}, u32[]{:S(2)}) collective-permute-start(f32[72,512]{1,0:T(8,128)S(1)} %get-tuple-element.78), channel_id=1, source_target_pairs={{0,2},{1,3},{2,4},{3,5},{4,6},{5,7},{6,0},{7,1},{8,10},{9,11},{10,... | collective-permute-start | bytes 442376 | tf_op jit(solution)/shard_map/ppermute | solution.py:358
  133.4 10.9 %collective-permute-start.16 = (f32[72,512]{1,0:T(8,128)S(1)}, f32[72,512]{1,0:T(8,128)S(1)}, u32[]{:S(2)}, u32[]{:S(2)}) collective-permute-start(f32[72,512]{1,0:T(8,128)S(1)} %get-tuple-element.79), channel_id=1, source_target_pairs={{0,6},{1,7},{2,0},{3,1},{4,2},{5,3},{6,4},{7,5},{8,14},{9,15},{10,... | collective-permute-start | bytes 442376 | tf_op jit(solution)/shard_map/ppermute | solution.py:358
  135.7 6.8 %collective-permute-start.20 = (bf16[80,512]{1,0:T(8,128)(2,1)S(1)}, bf16[80,512]{1,0:T(8,128)(2,1)S(1)}, u32[]{:S(2)}, u32[]{:S(2)}) collective-permute-start(bf16[80,512]{1,0:T(8,128)(2,1)S(1)} %copy-done.24), channel_id=1, source_target_pairs={{0,16},{8,24},{32,48},{40,56},{64,80},{72,88},{96,112},{104,120},{... | collective-permute-start | bytes 245768 | tf_op jit(solution)/shard_map/ppermute | solution.py:398
  139.9 4.4 %collective-permute-start.21 = (bf16[80,512]{1,0:T(8,128)(2,1)S(1)}, bf16[80,512]{1,0:T(8,128)(2,1)S(1)}, u32[]{:S(2)}, u32[]{:S(2)}) collective-permute-start(bf16[80,512]{1,0:T(8,128)(2,1)S(1)} %copy-done.25), channel_id=1, source_target_pairs={{16,64},{24,72},{0,80},{8,88},{48,96},{56,104},{32,112},{40,120},{... | collective-permute-start | bytes 245768 | tf_op jit(solution)/shard_map/ppermute | solution.py:398
  146.1 5.5 %collective-permute-start.24 = (f32[64,64]{1,0:T(8,128)S(1)}, f32[64,64]{1,0:T(8,128)S(1)}, u32[]{:S(2)}, u32[]{:S(2)}) collective-permute-start(f32[64,64]{1,0:T(8,128)S(1)} %add.404), channel_id=1, source_target_pairs={{0,4},{1,5},{2,6},{3,7},{4,0},{5,1},{6,2},{7,3},{8,12},{9,13},{10,... | collective-permute-start | bytes 49160 | tf_op jit(solution)/shard_map/ppermute | solution.py:358
  148.0 5.1 %collective-permute-start.23 = (f32[64,64]{1,0:T(8,128)S(1)}, f32[64,64]{1,0:T(8,128)S(1)}, u32[]{:S(2)}, u32[]{:S(2)}) collective-permute-start(f32[64,64]{1,0:T(8,128)S(1)} %add.404), channel_id=1, source_target_pairs={{0,2},{1,3},{2,4},{3,5},{4,6},{5,7},{6,0},{7,1},{8,10},{9,11},{10,... | collective-permute-start | bytes 49160 | tf_op jit(solution)/shard_map/ppermute | solution.py:358
  (30 other events, 200.7 us)
Sparse Core Ops, SparseCore 0:
  15.3 26.1 all-gather.2

commit v11 on v10

--- a/solution.py
+++ b/solution.py
@@ -168,7 +168,7 @@
                 x_ref[near], far_ref[at, to : to + 256, :], NT, preferred_element_type=jnp.float32
             )
             p_ref[:, to : to + 256] = jnp.exp2(scores * columns * far[:, to : to + 256]).astype(jnp.bfloat16)
-        vectors = jnp.concatenate([v_ref[near].astype(jnp.bfloat16), jnp.ones((16, BLOCK), jnp.bfloat16)], axis=0)
+        vectors = jnp.concatenate([v_ref[near], jnp.ones((16, BLOCK), jnp.bfloat16)], axis=0)
         part = jnp.dot(vectors, p_ref[...], preferred_element_type=jnp.float32)
         far_sums_ref[at] += part[0:ACC, :]
         if both:
@@ -255,7 +255,7 @@
     count = len(fars)
     buffers = [
         ((COLS, BLOCK, WIDTH), jnp.bfloat16),
-        ((COLS, EIGS, BLOCK), jnp.float32),
+        ((COLS, EIGS, BLOCK), jnp.bfloat16),
         ((count, PAYLOAD, WIDTH), jnp.bfloat16),
         ((COLS, BLOCK, 128), jnp.float32),
         ((COLS, 8, BLOCK), jnp.float32),
@@ -398,10 +398,10 @@
             returned.append(lax.ppermute(part, "row", back))
         return returned
 
-    near_v = lax.all_gather(vectors.astype(jnp.float32), "col")
+    near_v = lax.all_to_all(jnp.broadcast_to(vectors, (COLS, EIGS, BLOCK)), "col", 0, 0)
     sums, norms, rows, token = own_cells(flags[0], blocks, far["own"])
 
-    far["a"], far["b"], far["c"] = tie([far["a"], far["b"], far["c"]], token)
+    far["a"], far["b"], far["c"] = tie([far["a"], far["b"], far["c"]], token, near_v)
     far["d"] = move(far["a"], -1, 0)
     far["e"] = move(far["c"], 0, -1)
     far["g"] = move(far["a"], 0, 1, left_half)

time: 195 us -> 182 us (0.933)
  between operations: 14.3 us -> 0.71 us
  starting transfers between devices: 45.2 us -> 51 us
  waiting for transfers between devices: 47.3 us -> 42.8 us
  blocking collectives: 25.5 us -> 27.6 us
    all_to_all x0 -> x1, starting transfers between devices: none -> 5.31 us  [per_device(): lax.all_to_all(jnp.broadcast_to(vectors, (COLS, EIGS, BLOCK)), 'col', 0, 0)]
    ppermute x9, waiting for transfers between devices: 37.5 us -> 32.9 us  [move(): return lax.ppermute(array, 'row', shift(dy, dx, keep))]
    all_to_all x1, blocking collectives: 25.5 us -> 27.6 us  [per_device(): gram = jnp.sum(lax.all_to_all(everyone, 'row', 0, 0), axis=0)]
  transfers between devices with their start and end apart: 27 -> 27, of which waited for: 13 -> 15; matrix products, arithmetic and copies ran while one was open for 2% -> 3% of each run, Pallas kernels for 21% -> 21%
where the time goes in v11:
time: 182 us
  starting transfers between devices  51 us (28%)
  Pallas kernels  46.5 us (26%)
  waiting for transfers between devices  42.8 us (24%)
  blocking collectives  27.6 us (15%)
  local copies, waits for them, and re-layouts  10.2 us (6%)
  other arithmetic  3.11 us (2%)
    ppermute x9, waiting for transfers between devices, move(): return lax.ppermute(array, 'row', shift(dy, dx, keep))  32.9 us
    pallas_call x3, Pallas kernels, cells(): pl.pallas_call(functools.partial(cells_kernel, count), out_shape=[SUMS] +...  29.5 us
    all_to_all x1, blocking collectives, per_device(): gram = jnp.sum(lax.all_to_all(everyone, 'row', 0, 0), axis=0)  27.6 us
    ppermute x9, starting transfers between devices, give_back(): returned.append(lax.ppermute(part, 'row', back))  22 us
    ppermute x9, starting transfers between devices, move(): return lax.ppermute(array, 'row', shift(dy, dx, keep))  13.8 us
    ppermute x6, starting transfers between devices, turn(): lax.ppermute(array, 'col', [(i, (i + by * CORES) % COLS) for i in range(C...  9.74 us
    pallas_call x1, Pallas kernels, own_cells(): pl.pallas_call(own_kernel, out_shape=[SUMS, NORM, ROW, TOKEN], grid_spec=...  9.43 us
    all_to_all x1, starting transfers between devices, per_device(): lax.all_to_all(jnp.broadcast_to(vectors, (COLS, EIGS, BLOCK)), 'col', 0, 0)  5.31 us
  transfers between devices with their start and end apart: 27, of which 15 were waited for; matrix products, arithmetic and copies ran while one was open for 3% of the time, Pallas kernels for 21%

profile of v11, /device:TPU:0, one launch (start us, length us, event | category | flops | bytes accessed | tf_op | source)
XLA Modules:
  0.0 182.3 jit_solution(5913877248735267422)
XLA Ops:
  0.0 2.6 %payload.1.far_ref = bf16[560,1024]{1,0:T(8,128)(2,1)} custom-call(s32[1]{0:T(128)} %bitcast.13.index_ref, bf16[8,512,1024]{2,1,0:T(8,128)(2,1)} %bitcast.36, bf16[64,512]{1,0:T(8,128)(2,1)} %v_ref.1), custom_call_target="tpu_custom_call" | custom-call | tf_op jit(solution)/shard_map/payload/pallas_call | solution.py:78
  2.6 5.3 %collective-permute-start.2 = (bf16[560,1024]{1,0:T(8,128)(2,1)}, bf16[560,1024]{1,0:T(8,128)(2,1)S(1)}, u32[]{:S(2)}, u32[]{:S(2)}) collective-permute-start(bf16[560,1024]{1,0:T(8,128)(2,1)} %payload.1.far_ref), channel_id=1, source_target_pairs={{0,120},{8,96},{16,104},{24,112},{32,24},{40,0},{48,8},{56,16},{64... | collective-permute-start | bytes 3440648 | tf_op jit(solution)/shard_map/ppermute | solution.py:355
  8.8 5.3 %all-to-all-start = ((bf16[8,64,512]{2,1,0:T(8,128)(2,1)}), bf16[8,64,512]{2,1,0:T(8,128)(2,1)S(1)}, u32[]{:S(2)}, u32[]{:S(2)}) async-start(bf16[8,64,512]{2,1,0:T(8,128)(2,1)} %broadcast_in_dim.8), calls=%async_computation | async-start | bytes 1048576 | tf_op jit(solution)/shard_map/all_to_all | solution.py:401
  15.9 9.4 %cells_own.1 = (f32[8,72,512]{2,1,0:T(8,128)}, f32[8,512,128]{2,1,0:T(8,128)}, f32[8,8,512]{2,1,0:T(8,128)}, f32[8,128]{1,0:T(8,128)}) custom-call(s32[8]{0:T(128)} %slice_reduce_fusion.flags_ref, bf16[8,512,1024]{2,1,0:T(8,128)(2,1)} %bitcast.37, bf16[560,1024]{1,0:T(8,128)(2,1)} %payload.1.far_ref), custom_call_target="tpu_custom_call" | custom-call | flops 2147483648 | bytes 13631488 | tf_op jit(solution)/shard_map/cells_own/pallas_call | solution.py:230
  25.4 7.4 %collective-permute-done.2.refs_2_ = bf16[560,1024]{1,0:T(8,128)(2,1)S(1)} collective-permute-done((bf16[560,1024]{1,0:T(8,128)(2,1)}, bf16[560,1024]{1,0:T(8,128)(2,1)S(1)}, u32[]{:S(2)}, u32[]{:S(2)}) %collective-permute-start.2) | collective-permute-done | bytes 1146912 | tf_op jit(solution)/shard_map/ppermute | solution.py:355
  32.8 3.3 %collective-permute-done.1.refs_1_ = bf16[560,1024]{1,0:T(8,128)(2,1)S(1)} collective-permute-done((bf16[560,1024]{1,0:T(8,128)(2,1)}, bf16[560,1024]{1,0:T(8,128)(2,1)S(1)}, u32[]{:S(2)}, u32[]{:S(2)}) %collective-permute-start.1) | collective-permute-done | bytes 1146912 | tf_op jit(solution)/shard_map/ppermute | solution.py:355
  38.0 3.1 %collective-permute-start.6 = (bf16[560,1024]{1,0:T(8,128)(2,1)}, bf16[560,1024]{1,0:T(8,128)(2,1)S(1)}, u32[]{:S(2)}, u32[]{:S(2)}) collective-permute-start(bf16[560,1024]{1,0:T(8,128)(2,1)} %get-tuple-element.44.refs_0_), channel_id=1, source_target_pairs={{0,8},{24,0},{32,40},{56,32},{64,72},{88,64},{96,104},{120,96},{1,... | collective-permute-start | bytes 3440648 | tf_op jit(solution)/shard_map/ppermute | solution.py:355
  41.1 3.3 %collective-permute-start.5 = (bf16[560,1024]{1,0:T(8,128)(2,1)}, bf16[560,1024]{1,0:T(8,128)(2,1)S(1)}, u32[]{:S(2)}, u32[]{:S(2)}) collective-permute-start(bf16[560,1024]{1,0:T(8,128)(2,1)} %get-tuple-element.44.refs_0_), channel_id=1, source_target_pairs={{0,96},{8,104},{16,112},{24,120},{32,0},{40,8},{48,16},{56,24},{64... | collective-permute-start | bytes 3440648 | tf_op jit(solution)/shard_map/ppermute | solution.py:355
  45.2 10.6 %cells.3 = (f32[8,72,512]{2,1,0:T(8,128)}, bf16[80,512]{1,0:T(8,128)(2,1)}, bf16[80,512]{1,0:T(8,128)(2,1)}, bf16[80,512]{1,0:T(8,128)(2,1)}, f32[8,128]{1,0:T(8,128)}) custom-call(s32[24]{0:T(128)} %reshape.212.flags_ref, bf16[8,512,1024]{2,1,0:T(8,128)(2,1)} %bitcast.38, bf16[8,64,512]{2,1,0:T(8,128)(2,1)} %copy-done.1, ...), custom_call_target="tpu_custom_call", output_to_operand_aliasing={{0}: (8, {})} | custom-call | flops 6442450944 | bytes 15728640 | tf_op jit(solution)/shard_map/cells/pallas_call | solution.py:269
  55.8 8.7 %collective-permute-done.3.refs_0_ = bf16[560,1024]{1,0:T(8,128)(2,1)S(1)} collective-permute-done((bf16[560,1024]{1,0:T(8,128)(2,1)}, bf16[560,1024]{1,0:T(8,128)(2,1)S(1)}, u32[]{:S(2)}, u32[]{:S(2)}) %collective-permute-start.3) | collective-permute-done | bytes 1146912 | tf_op jit(solution)/shard_map/ppermute | solution.py:355
  64.5 2.3 %collective-permute-done.6.refs_7_.refs_1_ = bf16[560,1024]{1,0:T(8,128)(2,1)S(1)} collective-permute-done((bf16[560,1024]{1,0:T(8,128)(2,1)}, bf16[560,1024]{1,0:T(8,128)(2,1)S(1)}, u32[]{:S(2)}, u32[]{:S(2)}) %collective-permute-start.6) | collective-permute-done | bytes 1146912 | tf_op jit(solution)/shard_map/ppermute | solution.py:355
  71.0 3.2 %collective-permute-start.9 = (bf16[80,512]{1,0:T(8,128)(2,1)}, bf16[80,512]{1,0:T(8,128)(2,1)S(1)}, u32[]{:S(2)}, u32[]{:S(2)}) collective-permute-start(bf16[80,512]{1,0:T(8,128)(2,1)} %get-tuple-element.60), channel_id=1, source_target_pairs={{8,0},{16,8},{24,16},{0,24},{40,32},{48,40},{56,48},{32,56},{72,64... | collective-permute-start | bytes 245768 | tf_op jit(solution)/shard_map/ppermute | solution.py:398
  74.3 9.9 %cells.4 = (f32[8,72,512]{2,1,0:T(8,128)}, bf16[80,512]{1,0:T(8,128)(2,1)}, bf16[80,512]{1,0:T(8,128)(2,1)}, bf16[80,512]{1,0:T(8,128)(2,1)}, f32[8,128]{1,0:T(8,128)}) custom-call(s32[24]{0:T(128)} %reshape.213.flags_ref, bf16[8,512,1024]{2,1,0:T(8,128)(2,1)} %bitcast.39, bf16[8,64,512]{2,1,0:T(8,128)(2,1)} %copy-done.1, ...), custom_call_target="tpu_custom_call", output_to_operand_aliasing={{0}: (8, {})} | custom-call | flops 6442450944 | bytes 15728640 | tf_op jit(solution)/shard_map/cells/pallas_call | solution.py:269
  84.2 10.0 %collective-permute-done.7.refs_0_ = bf16[560,1024]{1,0:T(8,128)(2,1)S(1)} collective-permute-done((bf16[560,1024]{1,0:T(8,128)(2,1)}, bf16[560,1024]{1,0:T(8,128)(2,1)S(1)}, u32[]{:S(2)}, u32[]{:S(2)}) %collective-permute-start.7) | collective-permute-done | bytes 1146912 | tf_op jit(solution)/shard_map/ppermute | solution.py:355
  95.9 3.0 %collective-permute-start.10 = (bf16[80,512]{1,0:T(8,128)(2,1)}, bf16[80,512]{1,0:T(8,128)(2,1)S(1)}, u32[]{:S(2)}, u32[]{:S(2)}) collective-permute-start(bf16[80,512]{1,0:T(8,128)(2,1)} %get-tuple-element.68), channel_id=1, source_target_pairs={{32,0},{40,8},{48,16},{56,24},{64,32},{72,40},{80,48},{88,56},{96,... | collective-permute-start | bytes 245768 | tf_op jit(solution)/shard_map/ppermute | solution.py:398
  98.9 3.9 %collective-permute-start.12 = (bf16[80,512]{1,0:T(8,128)(2,1)}, bf16[80,512]{1,0:T(8,128)(2,1)S(1)}, u32[]{:S(2)}, u32[]{:S(2)}) collective-permute-start(bf16[80,512]{1,0:T(8,128)(2,1)} %get-tuple-element.70), channel_id=1, source_target_pairs={{104,0},{112,8},{120,16},{96,24},{8,32},{16,40},{24,48},{0,56},{40... | collective-permute-start | bytes 245768 | tf_op jit(solution)/shard_map/ppermute | solution.py:398
  102.9 5.2 %collective-permute-start.14 = (bf16[80,512]{1,0:T(8,128)(2,1)}, bf16[80,512]{1,0:T(8,128)(2,1)S(1)}, u32[]{:S(2)}, u32[]{:S(2)}) collective-permute-start(bf16[80,512]{1,0:T(8,128)(2,1)} %get-tuple-element.72), channel_id=1, source_target_pairs={{0,64},{8,72},{16,80},{24,88},{32,96},{40,104},{48,112},{56,120},{... | collective-permute-start | bytes 245768 | tf_op jit(solution)/shard_map/ppermute | solution.py:398
  108.1 9.0 %cells.5 = (f32[8,72,512]{2,1,0:T(8,128)}, bf16[80,512]{1,0:T(8,128)(2,1)}, bf16[80,512]{1,0:T(8,128)(2,1)}, bf16[80,512]{1,0:T(8,128)(2,1)}, f32[8,128]{1,0:T(8,128)}) custom-call(s32[24]{0:T(128)} %reshape.210.flags_ref, bf16[8,512,1024]{2,1,0:T(8,128)(2,1)} %bitcast.40, bf16[8,64,512]{2,1,0:T(8,128)(2,1)} %copy-done.1, ...), custom_call_target="tpu_custom_call", output_to_operand_aliasing={{0}: (8, {})} | custom-call | flops 6442450944 | bytes 15728640 | tf_op jit(solution)/shard_map/cells/pallas_call | solution.py:269
  121.4 4.0 %collective-permute-start.17 = (f32[72,512]{1,0:T(8,128)S(1)}, f32[72,512]{1,0:T(8,128)S(1)}, u32[]{:S(2)}, u32[]{:S(2)}) collective-permute-start(f32[72,512]{1,0:T(8,128)S(1)} %get-tuple-element.77), channel_id=1, source_target_pairs={{0,4},{1,5},{2,6},{3,7},{4,0},{5,1},{6,2},{7,3},{8,12},{9,13},{10,... | collective-permute-start | bytes 442376 | tf_op jit(solution)/shard_map/ppermute | solution.py:358
  126.3 2.2 %collective-permute-start.16 = (f32[72,512]{1,0:T(8,128)S(1)}, f32[72,512]{1,0:T(8,128)S(1)}, u32[]{:S(2)}, u32[]{:S(2)}) collective-permute-start(f32[72,512]{1,0:T(8,128)S(1)} %get-tuple-element.79), channel_id=1, source_target_pairs={{0,6},{1,7},{2,0},{3,1},{4,2},{5,3},{6,4},{7,5},{8,14},{9,15},{10,... | collective-permute-start | bytes 442376 | tf_op jit(solution)/shard_map/ppermute | solution.py:358
  128.6 5.0 %collective-permute-start.20 = (bf16[80,512]{1,0:T(8,128)(2,1)S(1)}, bf16[80,512]{1,0:T(8,128)(2,1)S(1)}, u32[]{:S(2)}, u32[]{:S(2)}) collective-permute-start(bf16[80,512]{1,0:T(8,128)(2,1)S(1)} %copy-done.24), channel_id=1, source_target_pairs={{0,16},{8,24},{32,48},{40,56},{64,80},{72,88},{96,112},{104,120},{... | collective-permute-start | bytes 245768 | tf_op jit(solution)/shard_map/ppermute | solution.py:398
  139.1 2.4 %collective-permute-start.24 = (f32[64,64]{1,0:T(8,128)S(1)}, f32[64,64]{1,0:T(8,128)S(1)}, u32[]{:S(2)}, u32[]{:S(2)}) collective-permute-start(f32[64,64]{1,0:T(8,128)S(1)} %add.404), channel_id=1, source_target_pairs={{0,4},{1,5},{2,6},{3,7},{4,0},{5,1},{6,2},{7,3},{8,12},{9,13},{10,... | collective-permute-start | bytes 49160 | tf_op jit(solution)/shard_map/ppermute | solution.py:358
  147.0 27.6 %all_to_all.10 = f32[16,1,4096]{2,1,0:T(1,128)S(1)} all-to-all(f32[16,1,4096]{2,1,0:T(1,128)S(1)} %reshape.218), channel_id=1, replica_groups=mesh['row'=16,'col'=8] {'row'}, dimensions={0} | all-to-all | bytes 524288 | tf_op jit(solution)/shard_map/all_to_all | solution.py:443
  177.3 5.0 %solve.1 = f32[64,512]{1,0:T(8,128)} custom-call(f32[64,64]{1,0:T(8,128)} %reduce_sum.9.gram_ref, f32[64,512]{1,0:T(8,128)} %copy-done.2), custom_call_target="tpu_custom_call" | custom-call | tf_op jit(solution)/shard_map/solve/pallas_call | solution.py:339
  (147 shorter events, 29.9 us)
Async XLA Ops:
  2.6 30.1 %collective-permute-start.2 = (bf16[560,1024]{1,0:T(8,128)(2,1)}, bf16[560,1024]{1,0:T(8,128)(2,1)S(1)}, u32[]{:S(2)}, u32[]{:S(2)}) collective-permute-start(bf16[560,1024]{1,0:T(8,128)(2,1)} %payload.1.far_ref), channel_id=1, source_target_pairs={{0,120},{8,96},{16,104},{24,112},{32,24},{40,0},{48,8},{56,16},{64... | collective-permute-start | bytes 3440648 | tf_op jit(solution)/shard_map/ppermute | solution.py:355
  7.9 28.1 %collective-permute-start.1 = (bf16[560,1024]{1,0:T(8,128)(2,1)}, bf16[560,1024]{1,0:T(8,128)(2,1)S(1)}, u32[]{:S(2)}, u32[]{:S(2)}) collective-permute-start(bf16[560,1024]{1,0:T(8,128)(2,1)} %payload.1.far_ref), channel_id=1, source_target_pairs={{0,32},{8,40},{16,48},{24,56},{32,64},{40,72},{48,80},{56,88},{64,... | collective-permute-start | bytes 3440648 | tf_op jit(solution)/shard_map/ppermute | solution.py:355
  7.9 28.3 %collective-permute-start = (bf16[560,1024]{1,0:T(8,128)(2,1)}, bf16[560,1024]{1,0:T(8,128)(2,1)}, u32[]{:S(2)}, u32[]{:S(2)}) collective-permute-start(bf16[560,1024]{1,0:T(8,128)(2,1)} %payload.1.far_ref), channel_id=1, source_target_pairs={{0,8},{8,16},{16,24},{24,0},{32,40},{40,48},{48,56},{56,32},{64,72... | collective-permute-start | bytes 3440648 | tf_op jit(solution)/shard_map/ppermute | solution.py:355
  8.8 16.6 %all-to-all-start = ((bf16[8,64,512]{2,1,0:T(8,128)(2,1)}), bf16[8,64,512]{2,1,0:T(8,128)(2,1)S(1)}, u32[]{:S(2)}, u32[]{:S(2)}) async-start(bf16[8,64,512]{2,1,0:T(8,128)(2,1)} %broadcast_in_dim.8), calls=%async_computation | async-start | bytes 1048576 | tf_op jit(solution)/shard_map/all_to_all | solution.py:401
  37.1 27.3 %collective-permute-start.3 = (bf16[560,1024]{1,0:T(8,128)(2,1)}, bf16[560,1024]{1,0:T(8,128)(2,1)S(1)}, u32[]{:S(2)}, u32[]{:S(2)}) collective-permute-start(bf16[560,1024]{1,0:T(8,128)(2,1)} %get-tuple-element.42.refs_1_), channel_id=1, source_target_pairs={{0,32},{8,40},{16,48},{24,56},{32,64},{40,72},{48,80},{56,88},{64,... | collective-permute-start | bytes 3440648 | tf_op jit(solution)/shard_map/ppermute | solution.py:355
  37.1 27.3 %collective-permute-start.4 = (bf16[560,1024]{1,0:T(8,128)(2,1)}, bf16[560,1024]{1,0:T(8,128)(2,1)}, u32[]{:S(2)}, u32[]{:S(2)}) collective-permute-start(bf16[560,1024]{1,0:T(8,128)(2,1)} %get-tuple-element.43.refs_2_), channel_id=1, source_target_pairs={{0,24},{8,0},{16,8},{24,16},{32,56},{40,32},{48,40},{56,48},{64,88... | collective-permute-start | bytes 3440648 | tf_op jit(solution)/shard_map/ppermute | solution.py:355
  38.0 28.8 %collective-permute-start.6 = (bf16[560,1024]{1,0:T(8,128)(2,1)}, bf16[560,1024]{1,0:T(8,128)(2,1)S(1)}, u32[]{:S(2)}, u32[]{:S(2)}) collective-permute-start(bf16[560,1024]{1,0:T(8,128)(2,1)} %get-tuple-element.44.refs_0_), channel_id=1, source_target_pairs={{0,8},{24,0},{32,40},{56,32},{64,72},{88,64},{96,104},{120,96},{1,... | collective-permute-start | bytes 3440648 | tf_op jit(solution)/shard_map/ppermute | solution.py:355
  41.1 26.2 %collective-permute-start.5 = (bf16[560,1024]{1,0:T(8,128)(2,1)}, bf16[560,1024]{1,0:T(8,128)(2,1)S(1)}, u32[]{:S(2)}, u32[]{:S(2)}) collective-permute-start(bf16[560,1024]{1,0:T(8,128)(2,1)} %get-tuple-element.44.refs_0_), channel_id=1, source_target_pairs={{0,96},{8,104},{16,112},{24,120},{32,0},{40,8},{48,16},{56,24},{64... | collective-permute-start | bytes 3440648 | tf_op jit(solution)/shard_map/ppermute | solution.py:355
  68.3 25.9 %collective-permute-start.7 = (bf16[560,1024]{1,0:T(8,128)(2,1)}, bf16[560,1024]{1,0:T(8,128)(2,1)S(1)}, u32[]{:S(2)}, u32[]{:S(2)}) collective-permute-start(bf16[560,1024]{1,0:T(8,128)(2,1)} %get-tuple-element.52.refs_2_), channel_id=1, source_target_pairs={{0,8},{8,16},{16,24},{24,0},{32,40},{40,48},{48,56},{56,32},{64,72... | collective-permute-start | bytes 3440648 | tf_op jit(solution)/shard_map/ppermute | solution.py:355
  68.3 26.6 %collective-permute-start.8 = (bf16[560,1024]{1,0:T(8,128)(2,1)}, bf16[560,1024]{1,0:T(8,128)(2,1)S(1)}, u32[]{:S(2)}, u32[]{:S(2)}) collective-permute-start(bf16[560,1024]{1,0:T(8,128)(2,1)} %get-tuple-element.53.refs_1_), channel_id=1, source_target_pairs={{32,0},{40,8},{48,16},{56,24},{64,32},{72,40},{80,48},{88,56},{33,... | collective-permute-start | bytes 3440648 | tf_op jit(solution)/shard_map/ppermute | solution.py:355
  71.0 13.2 %collective-permute-start.9 = (bf16[80,512]{1,0:T(8,128)(2,1)}, bf16[80,512]{1,0:T(8,128)(2,1)S(1)}, u32[]{:S(2)}, u32[]{:S(2)}) collective-permute-start(bf16[80,512]{1,0:T(8,128)(2,1)} %get-tuple-element.60), channel_id=1, source_target_pairs={{8,0},{16,8},{24,16},{0,24},{40,32},{48,40},{56,48},{32,56},{72,64... | collective-permute-start | bytes 245768 | tf_op jit(solution)/shard_map/ppermute | solution.py:398
  95.9 21.2 %collective-permute-start.10 = (bf16[80,512]{1,0:T(8,128)(2,1)}, bf16[80,512]{1,0:T(8,128)(2,1)S(1)}, u32[]{:S(2)}, u32[]{:S(2)}) collective-permute-start(bf16[80,512]{1,0:T(8,128)(2,1)} %get-tuple-element.68), channel_id=1, source_target_pairs={{32,0},{40,8},{48,16},{56,24},{64,32},{72,40},{80,48},{88,56},{96,... | collective-permute-start | bytes 245768 | tf_op jit(solution)/shard_map/ppermute | solution.py:398
  98.9 18.2 %collective-permute-start.11 = (bf16[80,512]{1,0:T(8,128)(2,1)}, bf16[80,512]{1,0:T(8,128)(2,1)S(1)}, u32[]{:S(2)}, u32[]{:S(2)}) collective-permute-start(bf16[80,512]{1,0:T(8,128)(2,1)} %get-tuple-element.69), channel_id=1, source_target_pairs={{120,0},{96,8},{104,16},{112,24},{24,32},{0,40},{8,48},{16,56},{56... | collective-permute-start | bytes 245768 | tf_op jit(solution)/shard_map/ppermute | solution.py:398
  98.9 18.2 %collective-permute-start.12 = (bf16[80,512]{1,0:T(8,128)(2,1)}, bf16[80,512]{1,0:T(8,128)(2,1)S(1)}, u32[]{:S(2)}, u32[]{:S(2)}) collective-permute-start(bf16[80,512]{1,0:T(8,128)(2,1)} %get-tuple-element.70), channel_id=1, source_target_pairs={{104,0},{112,8},{120,16},{96,24},{8,32},{16,40},{24,48},{0,56},{40... | collective-permute-start | bytes 245768 | tf_op jit(solution)/shard_map/ppermute | solution.py:398
  102.8 14.4 %collective-permute-start.13 = (bf16[80,512]{1,0:T(8,128)(2,1)}, bf16[80,512]{1,0:T(8,128)(2,1)S(1)}, u32[]{:S(2)}, u32[]{:S(2)}) collective-permute-start(bf16[80,512]{1,0:T(8,128)(2,1)} %get-tuple-element.71), channel_id=1, source_target_pairs={{112,0},{120,8},{96,16},{104,24},{16,32},{24,40},{0,48},{8,56},{48... | collective-permute-start | bytes 245768 | tf_op jit(solution)/shard_map/ppermute | solution.py:398
  102.9 14.3 %collective-permute-start.14 = (bf16[80,512]{1,0:T(8,128)(2,1)}, bf16[80,512]{1,0:T(8,128)(2,1)S(1)}, u32[]{:S(2)}, u32[]{:S(2)}) collective-permute-start(bf16[80,512]{1,0:T(8,128)(2,1)} %get-tuple-element.72), channel_id=1, source_target_pairs={{0,64},{8,72},{16,80},{24,88},{32,96},{40,104},{48,112},{56,120},{... | collective-permute-start | bytes 245768 | tf_op jit(solution)/shard_map/ppermute | solution.py:398
  119.3 14.2 %collective-permute-start.19 = (bf16[80,512]{1,0:T(8,128)(2,1)S(1)}, bf16[80,512]{1,0:T(8,128)(2,1)S(1)}, u32[]{:S(2)}, u32[]{:S(2)}) collective-permute-start(bf16[80,512]{1,0:T(8,128)(2,1)S(1)} %copy-done.23), channel_id=1, source_target_pairs={{72,0},{80,8},{88,16},{64,24},{104,32},{112,40},{120,48},{96,56},{... | collective-permute-start | bytes 245768 | tf_op jit(solution)/shard_map/ppermute | solution.py:398
  121.4 15.8 %collective-permute-start.17 = (f32[72,512]{1,0:T(8,128)S(1)}, f32[72,512]{1,0:T(8,128)S(1)}, u32[]{:S(2)}, u32[]{:S(2)}) collective-permute-start(f32[72,512]{1,0:T(8,128)S(1)} %get-tuple-element.77), channel_id=1, source_target_pairs={{0,4},{1,5},{2,6},{3,7},{4,0},{5,1},{6,2},{7,3},{8,12},{9,13},{10,... | collective-permute-start | bytes 442376 | tf_op jit(solution)/shard_map/ppermute | solution.py:358
  125.3 11.8 %collective-permute-start.18 = (f32[72,512]{1,0:T(8,128)S(1)}, f32[72,512]{1,0:T(8,128)S(1)}, u32[]{:S(2)}, u32[]{:S(2)}) collective-permute-start(f32[72,512]{1,0:T(8,128)S(1)} %get-tuple-element.78), channel_id=1, source_target_pairs={{0,2},{1,3},{2,4},{3,5},{4,6},{5,7},{6,0},{7,1},{8,10},{9,11},{10,... | collective-permute-start | bytes 442376 | tf_op jit(solution)/shard_map/ppermute | solution.py:358
  126.3 10.8 %collective-permute-start.16 = (f32[72,512]{1,0:T(8,128)S(1)}, f32[72,512]{1,0:T(8,128)S(1)}, u32[]{:S(2)}, u32[]{:S(2)}) collective-permute-start(f32[72,512]{1,0:T(8,128)S(1)} %get-tuple-element.79), channel_id=1, source_target_pairs={{0,6},{1,7},{2,0},{3,1},{4,2},{5,3},{6,4},{7,5},{8,14},{9,15},{10,... | collective-permute-start | bytes 442376 | tf_op jit(solution)/shard_map/ppermute | solution.py:358
  128.6 7.6 %collective-permute-start.20 = (bf16[80,512]{1,0:T(8,128)(2,1)S(1)}, bf16[80,512]{1,0:T(8,128)(2,1)S(1)}, u32[]{:S(2)}, u32[]{:S(2)}) collective-permute-start(bf16[80,512]{1,0:T(8,128)(2,1)S(1)} %copy-done.24), channel_id=1, source_target_pairs={{0,16},{8,24},{32,48},{40,56},{64,80},{72,88},{96,112},{104,120},{... | collective-permute-start | bytes 245768 | tf_op jit(solution)/shard_map/ppermute | solution.py:398
  139.0 3.9 %collective-permute-start.25 = (f32[64,64]{1,0:T(8,128)S(1)}, f32[64,64]{1,0:T(8,128)S(1)}, u32[]{:S(2)}, u32[]{:S(2)}) collective-permute-start(f32[64,64]{1,0:T(8,128)S(1)} %add.404), channel_id=1, source_target_pairs={{0,6},{1,7},{2,0},{3,1},{4,2},{5,3},{6,4},{7,5},{8,14},{9,15},{10,... | collective-permute-start | bytes 49160 | tf_op jit(solution)/shard_map/ppermute | solution.py:358
  139.1 5.4 %collective-permute-start.24 = (f32[64,64]{1,0:T(8,128)S(1)}, f32[64,64]{1,0:T(8,128)S(1)}, u32[]{:S(2)}, u32[]{:S(2)}) collective-permute-start(f32[64,64]{1,0:T(8,128)S(1)} %add.404), channel_id=1, source_target_pairs={{0,4},{1,5},{2,6},{3,7},{4,0},{5,1},{6,2},{7,3},{8,12},{9,13},{10,... | collective-permute-start | bytes 49160 | tf_op jit(solution)/shard_map/ppermute | solution.py:358
  141.5 5.1 %collective-permute-start.23 = (f32[64,64]{1,0:T(8,128)S(1)}, f32[64,64]{1,0:T(8,128)S(1)}, u32[]{:S(2)}, u32[]{:S(2)}) collective-permute-start(f32[64,64]{1,0:T(8,128)S(1)} %add.404), channel_id=1, source_target_pairs={{0,2},{1,3},{2,4},{3,5},{4,6},{5,7},{6,0},{7,1},{8,10},{9,11},{10,... | collective-permute-start | bytes 49160 | tf_op jit(solution)/shard_map/ppermute | solution.py:358
  (30 other events, 215.5 us)

commit v12 on v11

--- a/solution.py
+++ b/solution.py
@@ -188,12 +188,14 @@
         @pl.when(near == 0)
         def _():
             row_copy.wait()
-            for at in range(count):
-                far_copies[at].wait()
-                column_ref[at] = jnp.broadcast_to(side_norms(far_ref[at, BLOCK:PAYLOAD, :]), (128, BLOCK)).T
 
         @pl.loop(0, count)
         def _(at):
+            @pl.when(near == 0)
+            def _():
+                pltpu.make_async_copy(far_hbms[0], far_ref.at[at], far_sem.at[at]).wait()
+                column_ref[at] = jnp.broadcast_to(side_norms(far_ref[at, BLOCK:PAYLOAD, :]), (128, BLOCK)).T
+
             flag = flags_ref[at * COLS + near]
             pl.when(flag == 1)(functools.partial(forward_only, at, near))
             pl.when(flag == 2)(functools.partial(backward, at, near, False))
@@ -402,10 +404,10 @@
     sums, norms, rows, token = own_cells(flags[0], blocks, far["own"])
 
     far["a"], far["b"], far["c"] = tie([far["a"], far["b"], far["c"]], token, near_v)
+    far["h"] = move(far["b"], 1, 0)
+    far["e"] = move(far["c"], 0, -1)
     far["d"] = move(far["a"], -1, 0)
-    far["e"] = move(far["c"], 0, -1)
     far["g"] = move(far["a"], 0, 1, left_half)
-    far["h"] = move(far["b"], 1, 0)
     group1, group2, group3 = ("a", "b", "c"), ("d", "e", "h"), ("f", "g", "k")
     sums, parts, token = work(group1, sums)
 

time: 182 us -> 182 us (level)
  no operation moved by 1% of the time
where the time goes in v12:
time: 182 us
  starting transfers between devices  50.8 us (28%)
  Pallas kernels  45.7 us (25%)
  waiting for transfers between devices  43.6 us (24%)
  blocking collectives  27.3 us (15%)
  local copies, waits for them, and re-layouts  10.2 us (6%)
  other arithmetic  3.11 us (2%)
    ppermute x9, waiting for transfers between devices, move(): return lax.ppermute(array, 'row', shift(dy, dx, keep))  33.7 us
    pallas_call x3, Pallas kernels, cells(): pl.pallas_call(functools.partial(cells_kernel, count), out_shape=[SUMS] +...  28.7 us
    all_to_all x1, blocking collectives, per_device(): gram = jnp.sum(lax.all_to_all(everyone, 'row', 0, 0), axis=0)  27.3 us
    ppermute x9, starting transfers between devices, give_back(): returned.append(lax.ppermute(part, 'row', back))  22.2 us
    ppermute x9, starting transfers between devices, move(): return lax.ppermute(array, 'row', shift(dy, dx, keep))  13.8 us
    pallas_call x1, Pallas kernels, own_cells(): pl.pallas_call(own_kernel, out_shape=[SUMS, NORM, ROW, TOKEN], grid_spec=...  9.43 us
    ppermute x6, starting transfers between devices, turn(): lax.ppermute(array, 'col', [(i, (i + by * CORES) % COLS) for i in range(C...  9.27 us
    all_to_all x1, starting transfers between devices, per_device(): lax.all_to_all(jnp.broadcast_to(vectors, (COLS, EIGS, BLOCK)), 'col', 0, 0)  5.31 us
  transfers between devices with their start and end apart: 27, of which 15 were waited for; matrix products, arithmetic and copies ran while one was open for 3% of the time, Pallas kernels for 21%

profile of v12, /device:TPU:0, one launch (start us, length us, event | category | flops | bytes accessed | tf_op | source)
XLA Modules:
  0.0 181.7 jit_solution(5483353039492639267)
XLA Ops:
  0.0 2.6 %payload.1.far_ref = bf16[560,1024]{1,0:T(8,128)(2,1)} custom-call(s32[1]{0:T(128)} %bitcast.13.index_ref, bf16[8,512,1024]{2,1,0:T(8,128)(2,1)} %bitcast.36, bf16[64,512]{1,0:T(8,128)(2,1)} %v_ref.1), custom_call_target="tpu_custom_call" | custom-call | tf_op jit(solution)/shard_map/payload/pallas_call | solution.py:78
  2.6 5.3 %collective-permute-start.2 = (bf16[560,1024]{1,0:T(8,128)(2,1)}, bf16[560,1024]{1,0:T(8,128)(2,1)S(1)}, u32[]{:S(2)}, u32[]{:S(2)}) collective-permute-start(bf16[560,1024]{1,0:T(8,128)(2,1)} %payload.1.far_ref), channel_id=1, source_target_pairs={{0,120},{8,96},{16,104},{24,112},{32,24},{40,0},{48,8},{56,16},{64... | collective-permute-start | bytes 3440648 | tf_op jit(solution)/shard_map/ppermute | solution.py:357
  8.8 5.3 %all-to-all-start = ((bf16[8,64,512]{2,1,0:T(8,128)(2,1)}), bf16[8,64,512]{2,1,0:T(8,128)(2,1)S(1)}, u32[]{:S(2)}, u32[]{:S(2)}) async-start(bf16[8,64,512]{2,1,0:T(8,128)(2,1)} %broadcast_in_dim.8), calls=%async_computation | async-start | bytes 1048576 | tf_op jit(solution)/shard_map/all_to_all | solution.py:403
  15.9 9.4 %cells_own.1 = (f32[8,72,512]{2,1,0:T(8,128)}, f32[8,512,128]{2,1,0:T(8,128)}, f32[8,8,512]{2,1,0:T(8,128)}, f32[8,128]{1,0:T(8,128)}) custom-call(s32[8]{0:T(128)} %slice_reduce_fusion.flags_ref, bf16[8,512,1024]{2,1,0:T(8,128)(2,1)} %bitcast.37, bf16[560,1024]{1,0:T(8,128)(2,1)} %payload.1.far_ref), custom_call_target="tpu_custom_call" | custom-call | flops 2147483648 | bytes 13631488 | tf_op jit(solution)/shard_map/cells_own/pallas_call | solution.py:232
  25.4 7.4 %collective-permute-done.2.refs_2_ = bf16[560,1024]{1,0:T(8,128)(2,1)S(1)} collective-permute-done((bf16[560,1024]{1,0:T(8,128)(2,1)}, bf16[560,1024]{1,0:T(8,128)(2,1)S(1)}, u32[]{:S(2)}, u32[]{:S(2)}) %collective-permute-start.2) | collective-permute-done | bytes 1146912 | tf_op jit(solution)/shard_map/ppermute | solution.py:357
  32.8 3.3 %collective-permute-done.1.refs_1_ = bf16[560,1024]{1,0:T(8,128)(2,1)S(1)} collective-permute-done((bf16[560,1024]{1,0:T(8,128)(2,1)}, bf16[560,1024]{1,0:T(8,128)(2,1)S(1)}, u32[]{:S(2)}, u32[]{:S(2)}) %collective-permute-start.1) | collective-permute-done | bytes 1146912 | tf_op jit(solution)/shard_map/ppermute | solution.py:357
  38.0 3.1 %collective-permute-start.6 = (bf16[560,1024]{1,0:T(8,128)(2,1)}, bf16[560,1024]{1,0:T(8,128)(2,1)S(1)}, u32[]{:S(2)}, u32[]{:S(2)}) collective-permute-start(bf16[560,1024]{1,0:T(8,128)(2,1)} %get-tuple-element.44.refs_0_), channel_id=1, source_target_pairs={{0,8},{24,0},{32,40},{56,32},{64,72},{88,64},{96,104},{120,96},{1,... | collective-permute-start | bytes 3440648 | tf_op jit(solution)/shard_map/ppermute | solution.py:357
  41.1 3.3 %collective-permute-start.5 = (bf16[560,1024]{1,0:T(8,128)(2,1)}, bf16[560,1024]{1,0:T(8,128)(2,1)S(1)}, u32[]{:S(2)}, u32[]{:S(2)}) collective-permute-start(bf16[560,1024]{1,0:T(8,128)(2,1)} %get-tuple-element.44.refs_0_), channel_id=1, source_target_pairs={{0,96},{8,104},{16,112},{24,120},{32,0},{40,8},{48,16},{56,24},{64... | collective-permute-start | bytes 3440648 | tf_op jit(solution)/shard_map/ppermute | solution.py:357
  45.2 9.9 %cells.3 = (f32[8,72,512]{2,1,0:T(8,128)}, bf16[80,512]{1,0:T(8,128)(2,1)}, bf16[80,512]{1,0:T(8,128)(2,1)}, bf16[80,512]{1,0:T(8,128)(2,1)}, f32[8,128]{1,0:T(8,128)}) custom-call(s32[24]{0:T(128)} %reshape.212.flags_ref, bf16[8,512,1024]{2,1,0:T(8,128)(2,1)} %bitcast.38, bf16[8,64,512]{2,1,0:T(8,128)(2,1)} %copy-done.1, ...), custom_call_target="tpu_custom_call", output_to_operand_aliasing={{0}: (8, {})} | custom-call | flops 6442450944 | bytes 15728640 | tf_op jit(solution)/shard_map/cells/pallas_call | solution.py:271
  55.1 9.4 %collective-permute-done.3.refs_0_ = bf16[560,1024]{1,0:T(8,128)(2,1)S(1)} collective-permute-done((bf16[560,1024]{1,0:T(8,128)(2,1)}, bf16[560,1024]{1,0:T(8,128)(2,1)S(1)}, u32[]{:S(2)}, u32[]{:S(2)}) %collective-permute-start.3) | collective-permute-done | bytes 1146912 | tf_op jit(solution)/shard_map/ppermute | solution.py:357
  64.5 2.3 %collective-permute-done.6.refs_7_.refs_1_ = bf16[560,1024]{1,0:T(8,128)(2,1)S(1)} collective-permute-done((bf16[560,1024]{1,0:T(8,128)(2,1)}, bf16[560,1024]{1,0:T(8,128)(2,1)S(1)}, u32[]{:S(2)}, u32[]{:S(2)}) %collective-permute-start.6) | collective-permute-done | bytes 1146912 | tf_op jit(solution)/shard_map/ppermute | solution.py:357
  71.0 3.2 %collective-permute-start.9 = (bf16[80,512]{1,0:T(8,128)(2,1)}, bf16[80,512]{1,0:T(8,128)(2,1)S(1)}, u32[]{:S(2)}, u32[]{:S(2)}) collective-permute-start(bf16[80,512]{1,0:T(8,128)(2,1)} %get-tuple-element.60), channel_id=1, source_target_pairs={{8,0},{16,8},{24,16},{0,24},{40,32},{48,40},{56,48},{32,56},{72,64... | collective-permute-start | bytes 245768 | tf_op jit(solution)/shard_map/ppermute | solution.py:400
  74.3 9.9 %cells.4 = (f32[8,72,512]{2,1,0:T(8,128)}, bf16[80,512]{1,0:T(8,128)(2,1)}, bf16[80,512]{1,0:T(8,128)(2,1)}, bf16[80,512]{1,0:T(8,128)(2,1)}, f32[8,128]{1,0:T(8,128)}) custom-call(s32[24]{0:T(128)} %reshape.213.flags_ref, bf16[8,512,1024]{2,1,0:T(8,128)(2,1)} %bitcast.39, bf16[8,64,512]{2,1,0:T(8,128)(2,1)} %copy-done.1, ...), custom_call_target="tpu_custom_call", output_to_operand_aliasing={{0}: (8, {})} | custom-call | flops 6442450944 | bytes 15728640 | tf_op jit(solution)/shard_map/cells/pallas_call | solution.py:271
  84.2 10.0 %collective-permute-done.7.refs_0_ = bf16[560,1024]{1,0:T(8,128)(2,1)S(1)} collective-permute-done((bf16[560,1024]{1,0:T(8,128)(2,1)}, bf16[560,1024]{1,0:T(8,128)(2,1)S(1)}, u32[]{:S(2)}, u32[]{:S(2)}) %collective-permute-start.7) | collective-permute-done | bytes 1146912 | tf_op jit(solution)/shard_map/ppermute | solution.py:357
  95.9 3.0 %collective-permute-start.10 = (bf16[80,512]{1,0:T(8,128)(2,1)}, bf16[80,512]{1,0:T(8,128)(2,1)S(1)}, u32[]{:S(2)}, u32[]{:S(2)}) collective-permute-start(bf16[80,512]{1,0:T(8,128)(2,1)} %get-tuple-element.68), channel_id=1, source_target_pairs={{32,0},{40,8},{48,16},{56,24},{64,32},{72,40},{80,48},{88,56},{96,... | collective-permute-start | bytes 245768 | tf_op jit(solution)/shard_map/ppermute | solution.py:400
  98.9 2.8 %collective-permute-start.12 = (bf16[80,512]{1,0:T(8,128)(2,1)}, bf16[80,512]{1,0:T(8,128)(2,1)S(1)}, u32[]{:S(2)}, u32[]{:S(2)}) collective-permute-start(bf16[80,512]{1,0:T(8,128)(2,1)} %get-tuple-element.70), channel_id=1, source_target_pairs={{104,0},{112,8},{120,16},{96,24},{8,32},{16,40},{24,48},{0,56},{40... | collective-permute-start | bytes 245768 | tf_op jit(solution)/shard_map/ppermute | solution.py:400
  102.9 5.2 %collective-permute-start.14 = (bf16[80,512]{1,0:T(8,128)(2,1)}, bf16[80,512]{1,0:T(8,128)(2,1)S(1)}, u32[]{:S(2)}, u32[]{:S(2)}) collective-permute-start(bf16[80,512]{1,0:T(8,128)(2,1)} %get-tuple-element.72), channel_id=1, source_target_pairs={{0,64},{8,72},{16,80},{24,88},{32,96},{40,104},{48,112},{56,120},{... | collective-permute-start | bytes 245768 | tf_op jit(solution)/shard_map/ppermute | solution.py:400
  108.1 9.0 %cells.5 = (f32[8,72,512]{2,1,0:T(8,128)}, bf16[80,512]{1,0:T(8,128)(2,1)}, bf16[80,512]{1,0:T(8,128)(2,1)}, bf16[80,512]{1,0:T(8,128)(2,1)}, f32[8,128]{1,0:T(8,128)}) custom-call(s32[24]{0:T(128)} %reshape.210.flags_ref, bf16[8,512,1024]{2,1,0:T(8,128)(2,1)} %bitcast.40, bf16[8,64,512]{2,1,0:T(8,128)(2,1)} %copy-done.1, ...), custom_call_target="tpu_custom_call", output_to_operand_aliasing={{0}: (8, {})} | custom-call | flops 6442450944 | bytes 15728640 | tf_op jit(solution)/shard_map/cells/pallas_call | solution.py:271
  121.3 4.0 %collective-permute-start.17 = (f32[72,512]{1,0:T(8,128)S(1)}, f32[72,512]{1,0:T(8,128)S(1)}, u32[]{:S(2)}, u32[]{:S(2)}) collective-permute-start(f32[72,512]{1,0:T(8,128)S(1)} %get-tuple-element.77), channel_id=1, source_target_pairs={{0,4},{1,5},{2,6},{3,7},{4,0},{5,1},{6,2},{7,3},{8,12},{9,13},{10,... | collective-permute-start | bytes 442376 | tf_op jit(solution)/shard_map/ppermute | solution.py:360
  126.3 2.2 %collective-permute-start.16 = (f32[72,512]{1,0:T(8,128)S(1)}, f32[72,512]{1,0:T(8,128)S(1)}, u32[]{:S(2)}, u32[]{:S(2)}) collective-permute-start(f32[72,512]{1,0:T(8,128)S(1)} %get-tuple-element.79), channel_id=1, source_target_pairs={{0,6},{1,7},{2,0},{3,1},{4,2},{5,3},{6,4},{7,5},{8,14},{9,15},{10,... | collective-permute-start | bytes 442376 | tf_op jit(solution)/shard_map/ppermute | solution.py:360
  128.5 5.5 %collective-permute-start.20 = (bf16[80,512]{1,0:T(8,128)(2,1)S(1)}, bf16[80,512]{1,0:T(8,128)(2,1)S(1)}, u32[]{:S(2)}, u32[]{:S(2)}) collective-permute-start(bf16[80,512]{1,0:T(8,128)(2,1)S(1)} %copy-done.24), channel_id=1, source_target_pairs={{0,16},{8,24},{32,48},{40,56},{64,80},{72,88},{96,112},{104,120},{... | collective-permute-start | bytes 245768 | tf_op jit(solution)/shard_map/ppermute | solution.py:400
  139.4 1.9 %collective-permute-start.24 = (f32[64,64]{1,0:T(8,128)S(1)}, f32[64,64]{1,0:T(8,128)S(1)}, u32[]{:S(2)}, u32[]{:S(2)}) collective-permute-start(f32[64,64]{1,0:T(8,128)S(1)} %add.404), channel_id=1, source_target_pairs={{0,4},{1,5},{2,6},{3,7},{4,0},{5,1},{6,2},{7,3},{8,12},{9,13},{10,... | collective-permute-start | bytes 49160 | tf_op jit(solution)/shard_map/ppermute | solution.py:360
  146.8 27.3 %all_to_all.10 = f32[16,1,4096]{2,1,0:T(1,128)S(1)} all-to-all(f32[16,1,4096]{2,1,0:T(1,128)S(1)} %reshape.218), channel_id=1, replica_groups=mesh['row'=16,'col'=8] {'row'}, dimensions={0} | all-to-all | bytes 524288 | tf_op jit(solution)/shard_map/all_to_all | solution.py:445
  176.7 5.0 %solve.1 = f32[64,512]{1,0:T(8,128)} custom-call(f32[64,64]{1,0:T(8,128)} %reduce_sum.9.gram_ref, f32[64,512]{1,0:T(8,128)} %copy-done.2), custom_call_target="tpu_custom_call" | custom-call | tf_op jit(solution)/shard_map/solve/pallas_call | solution.py:341
  (147 shorter events, 30.8 us)
Async XLA Ops:
  2.6 30.1 %collective-permute-start.2 = (bf16[560,1024]{1,0:T(8,128)(2,1)}, bf16[560,1024]{1,0:T(8,128)(2,1)S(1)}, u32[]{:S(2)}, u32[]{:S(2)}) collective-permute-start(bf16[560,1024]{1,0:T(8,128)(2,1)} %payload.1.far_ref), channel_id=1, source_target_pairs={{0,120},{8,96},{16,104},{24,112},{32,24},{40,0},{48,8},{56,16},{64... | collective-permute-start | bytes 3440648 | tf_op jit(solution)/shard_map/ppermute | solution.py:357
  7.9 28.1 %collective-permute-start.1 = (bf16[560,1024]{1,0:T(8,128)(2,1)}, bf16[560,1024]{1,0:T(8,128)(2,1)S(1)}, u32[]{:S(2)}, u32[]{:S(2)}) collective-permute-start(bf16[560,1024]{1,0:T(8,128)(2,1)} %payload.1.far_ref), channel_id=1, source_target_pairs={{0,32},{8,40},{16,48},{24,56},{32,64},{40,72},{48,80},{56,88},{64,... | collective-permute-start | bytes 3440648 | tf_op jit(solution)/shard_map/ppermute | solution.py:357
  7.9 28.3 %collective-permute-start = (bf16[560,1024]{1,0:T(8,128)(2,1)}, bf16[560,1024]{1,0:T(8,128)(2,1)}, u32[]{:S(2)}, u32[]{:S(2)}) collective-permute-start(bf16[560,1024]{1,0:T(8,128)(2,1)} %payload.1.far_ref), channel_id=1, source_target_pairs={{0,8},{8,16},{16,24},{24,0},{32,40},{40,48},{48,56},{56,32},{64,72... | collective-permute-start | bytes 3440648 | tf_op jit(solution)/shard_map/ppermute | solution.py:357
  8.8 16.6 %all-to-all-start = ((bf16[8,64,512]{2,1,0:T(8,128)(2,1)}), bf16[8,64,512]{2,1,0:T(8,128)(2,1)S(1)}, u32[]{:S(2)}, u32[]{:S(2)}) async-start(bf16[8,64,512]{2,1,0:T(8,128)(2,1)} %broadcast_in_dim.8), calls=%async_computation | async-start | bytes 1048576 | tf_op jit(solution)/shard_map/all_to_all | solution.py:403
  37.1 27.3 %collective-permute-start.3 = (bf16[560,1024]{1,0:T(8,128)(2,1)}, bf16[560,1024]{1,0:T(8,128)(2,1)S(1)}, u32[]{:S(2)}, u32[]{:S(2)}) collective-permute-start(bf16[560,1024]{1,0:T(8,128)(2,1)} %get-tuple-element.42.refs_1_), channel_id=1, source_target_pairs={{0,32},{8,40},{16,48},{24,56},{32,64},{40,72},{48,80},{56,88},{64,... | collective-permute-start | bytes 3440648 | tf_op jit(solution)/shard_map/ppermute | solution.py:357
  37.1 27.3 %collective-permute-start.4 = (bf16[560,1024]{1,0:T(8,128)(2,1)}, bf16[560,1024]{1,0:T(8,128)(2,1)}, u32[]{:S(2)}, u32[]{:S(2)}) collective-permute-start(bf16[560,1024]{1,0:T(8,128)(2,1)} %get-tuple-element.43.refs_2_), channel_id=1, source_target_pairs={{0,24},{8,0},{16,8},{24,16},{32,56},{40,32},{48,40},{56,48},{64,88... | collective-permute-start | bytes 3440648 | tf_op jit(solution)/shard_map/ppermute | solution.py:357
  38.0 28.8 %collective-permute-start.6 = (bf16[560,1024]{1,0:T(8,128)(2,1)}, bf16[560,1024]{1,0:T(8,128)(2,1)S(1)}, u32[]{:S(2)}, u32[]{:S(2)}) collective-permute-start(bf16[560,1024]{1,0:T(8,128)(2,1)} %get-tuple-element.44.refs_0_), channel_id=1, source_target_pairs={{0,8},{24,0},{32,40},{56,32},{64,72},{88,64},{96,104},{120,96},{1,... | collective-permute-start | bytes 3440648 | tf_op jit(solution)/shard_map/ppermute | solution.py:357
  41.1 26.2 %collective-permute-start.5 = (bf16[560,1024]{1,0:T(8,128)(2,1)}, bf16[560,1024]{1,0:T(8,128)(2,1)S(1)}, u32[]{:S(2)}, u32[]{:S(2)}) collective-permute-start(bf16[560,1024]{1,0:T(8,128)(2,1)} %get-tuple-element.44.refs_0_), channel_id=1, source_target_pairs={{0,96},{8,104},{16,112},{24,120},{32,0},{40,8},{48,16},{56,24},{64... | collective-permute-start | bytes 3440648 | tf_op jit(solution)/shard_map/ppermute | solution.py:357
  68.3 25.9 %collective-permute-start.7 = (bf16[560,1024]{1,0:T(8,128)(2,1)}, bf16[560,1024]{1,0:T(8,128)(2,1)S(1)}, u32[]{:S(2)}, u32[]{:S(2)}) collective-permute-start(bf16[560,1024]{1,0:T(8,128)(2,1)} %get-tuple-element.52.refs_2_), channel_id=1, source_target_pairs={{0,8},{8,16},{16,24},{24,0},{32,40},{40,48},{48,56},{56,32},{64,72... | collective-permute-start | bytes 3440648 | tf_op jit(solution)/shard_map/ppermute | solution.py:357
  68.3 26.6 %collective-permute-start.8 = (bf16[560,1024]{1,0:T(8,128)(2,1)}, bf16[560,1024]{1,0:T(8,128)(2,1)S(1)}, u32[]{:S(2)}, u32[]{:S(2)}) collective-permute-start(bf16[560,1024]{1,0:T(8,128)(2,1)} %get-tuple-element.53.refs_1_), channel_id=1, source_target_pairs={{32,0},{40,8},{48,16},{56,24},{64,32},{72,40},{80,48},{88,56},{33,... | collective-permute-start | bytes 3440648 | tf_op jit(solution)/shard_map/ppermute | solution.py:357
  71.0 13.1 %collective-permute-start.9 = (bf16[80,512]{1,0:T(8,128)(2,1)}, bf16[80,512]{1,0:T(8,128)(2,1)S(1)}, u32[]{:S(2)}, u32[]{:S(2)}) collective-permute-start(bf16[80,512]{1,0:T(8,128)(2,1)} %get-tuple-element.60), channel_id=1, source_target_pairs={{8,0},{16,8},{24,16},{0,24},{40,32},{48,40},{56,48},{32,56},{72,64... | collective-permute-start | bytes 245768 | tf_op jit(solution)/shard_map/ppermute | solution.py:400
  95.9 21.2 %collective-permute-start.10 = (bf16[80,512]{1,0:T(8,128)(2,1)}, bf16[80,512]{1,0:T(8,128)(2,1)S(1)}, u32[]{:S(2)}, u32[]{:S(2)}) collective-permute-start(bf16[80,512]{1,0:T(8,128)(2,1)} %get-tuple-element.68), channel_id=1, source_target_pairs={{32,0},{40,8},{48,16},{56,24},{64,32},{72,40},{80,48},{88,56},{96,... | collective-permute-start | bytes 245768 | tf_op jit(solution)/shard_map/ppermute | solution.py:400
  98.9 18.2 %collective-permute-start.11 = (bf16[80,512]{1,0:T(8,128)(2,1)}, bf16[80,512]{1,0:T(8,128)(2,1)S(1)}, u32[]{:S(2)}, u32[]{:S(2)}) collective-permute-start(bf16[80,512]{1,0:T(8,128)(2,1)} %get-tuple-element.69), channel_id=1, source_target_pairs={{120,0},{96,8},{104,16},{112,24},{24,32},{0,40},{8,48},{16,56},{56... | collective-permute-start | bytes 245768 | tf_op jit(solution)/shard_map/ppermute | solution.py:400
  98.9 18.2 %collective-permute-start.12 = (bf16[80,512]{1,0:T(8,128)(2,1)}, bf16[80,512]{1,0:T(8,128)(2,1)S(1)}, u32[]{:S(2)}, u32[]{:S(2)}) collective-permute-start(bf16[80,512]{1,0:T(8,128)(2,1)} %get-tuple-element.70), channel_id=1, source_target_pairs={{104,0},{112,8},{120,16},{96,24},{8,32},{16,40},{24,48},{0,56},{40... | collective-permute-start | bytes 245768 | tf_op jit(solution)/shard_map/ppermute | solution.py:400
  101.7 15.4 %collective-permute-start.13 = (bf16[80,512]{1,0:T(8,128)(2,1)}, bf16[80,512]{1,0:T(8,128)(2,1)S(1)}, u32[]{:S(2)}, u32[]{:S(2)}) collective-permute-start(bf16[80,512]{1,0:T(8,128)(2,1)} %get-tuple-element.71), channel_id=1, source_target_pairs={{112,0},{120,8},{96,16},{104,24},{16,32},{24,40},{0,48},{8,56},{48... | collective-permute-start | bytes 245768 | tf_op jit(solution)/shard_map/ppermute | solution.py:400
  102.9 14.3 %collective-permute-start.14 = (bf16[80,512]{1,0:T(8,128)(2,1)}, bf16[80,512]{1,0:T(8,128)(2,1)S(1)}, u32[]{:S(2)}, u32[]{:S(2)}) collective-permute-start(bf16[80,512]{1,0:T(8,128)(2,1)} %get-tuple-element.72), channel_id=1, source_target_pairs={{0,64},{8,72},{16,80},{24,88},{32,96},{40,104},{48,112},{56,120},{... | collective-permute-start | bytes 245768 | tf_op jit(solution)/shard_map/ppermute | solution.py:400
  119.3 14.7 %collective-permute-start.19 = (bf16[80,512]{1,0:T(8,128)(2,1)S(1)}, bf16[80,512]{1,0:T(8,128)(2,1)S(1)}, u32[]{:S(2)}, u32[]{:S(2)}) collective-permute-start(bf16[80,512]{1,0:T(8,128)(2,1)S(1)} %copy-done.23), channel_id=1, source_target_pairs={{72,0},{80,8},{88,16},{64,24},{104,32},{112,40},{120,48},{96,56},{... | collective-permute-start | bytes 245768 | tf_op jit(solution)/shard_map/ppermute | solution.py:400
  121.3 16.0 %collective-permute-start.17 = (f32[72,512]{1,0:T(8,128)S(1)}, f32[72,512]{1,0:T(8,128)S(1)}, u32[]{:S(2)}, u32[]{:S(2)}) collective-permute-start(f32[72,512]{1,0:T(8,128)S(1)} %get-tuple-element.77), channel_id=1, source_target_pairs={{0,4},{1,5},{2,6},{3,7},{4,0},{5,1},{6,2},{7,3},{8,12},{9,13},{10,... | collective-permute-start | bytes 442376 | tf_op jit(solution)/shard_map/ppermute | solution.py:360
  125.3 12.1 %collective-permute-start.18 = (f32[72,512]{1,0:T(8,128)S(1)}, f32[72,512]{1,0:T(8,128)S(1)}, u32[]{:S(2)}, u32[]{:S(2)}) collective-permute-start(f32[72,512]{1,0:T(8,128)S(1)} %get-tuple-element.78), channel_id=1, source_target_pairs={{0,2},{1,3},{2,4},{3,5},{4,6},{5,7},{6,0},{7,1},{8,10},{9,11},{10,... | collective-permute-start | bytes 442376 | tf_op jit(solution)/shard_map/ppermute | solution.py:360
  126.3 11.1 %collective-permute-start.16 = (f32[72,512]{1,0:T(8,128)S(1)}, f32[72,512]{1,0:T(8,128)S(1)}, u32[]{:S(2)}, u32[]{:S(2)}) collective-permute-start(f32[72,512]{1,0:T(8,128)S(1)} %get-tuple-element.79), channel_id=1, source_target_pairs={{0,6},{1,7},{2,0},{3,1},{4,2},{5,3},{6,4},{7,5},{8,14},{9,15},{10,... | collective-permute-start | bytes 442376 | tf_op jit(solution)/shard_map/ppermute | solution.py:360
  128.5 7.9 %collective-permute-start.20 = (bf16[80,512]{1,0:T(8,128)(2,1)S(1)}, bf16[80,512]{1,0:T(8,128)(2,1)S(1)}, u32[]{:S(2)}, u32[]{:S(2)}) collective-permute-start(bf16[80,512]{1,0:T(8,128)(2,1)S(1)} %copy-done.24), channel_id=1, source_target_pairs={{0,16},{8,24},{32,48},{40,56},{64,80},{72,88},{96,112},{104,120},{... | collective-permute-start | bytes 245768 | tf_op jit(solution)/shard_map/ppermute | solution.py:400
  139.2 3.9 %collective-permute-start.25 = (f32[64,64]{1,0:T(8,128)S(1)}, f32[64,64]{1,0:T(8,128)S(1)}, u32[]{:S(2)}, u32[]{:S(2)}) collective-permute-start(f32[64,64]{1,0:T(8,128)S(1)} %add.404), channel_id=1, source_target_pairs={{0,6},{1,7},{2,0},{3,1},{4,2},{5,3},{6,4},{7,5},{8,14},{9,15},{10,... | collective-permute-start | bytes 49160 | tf_op jit(solution)/shard_map/ppermute | solution.py:360
  139.4 5.4 %collective-permute-start.24 = (f32[64,64]{1,0:T(8,128)S(1)}, f32[64,64]{1,0:T(8,128)S(1)}, u32[]{:S(2)}, u32[]{:S(2)}) collective-permute-start(f32[64,64]{1,0:T(8,128)S(1)} %add.404), channel_id=1, source_target_pairs={{0,4},{1,5},{2,6},{3,7},{4,0},{5,1},{6,2},{7,3},{8,12},{9,13},{10,... | collective-permute-start | bytes 49160 | tf_op jit(solution)/shard_map/ppermute | solution.py:360
  141.3 5.1 %collective-permute-start.23 = (f32[64,64]{1,0:T(8,128)S(1)}, f32[64,64]{1,0:T(8,128)S(1)}, u32[]{:S(2)}, u32[]{:S(2)}) collective-permute-start(f32[64,64]{1,0:T(8,128)S(1)} %add.404), channel_id=1, source_target_pairs={{0,2},{1,3},{2,4},{3,5},{4,6},{5,7},{6,0},{7,1},{8,10},{9,11},{10,... | collective-permute-start | bytes 49160 | tf_op jit(solution)/shard_map/ppermute | solution.py:360
  (30 other events, 216.6 us)

commit v13 on v12

--- a/solution.py
+++ b/solution.py
@@ -408,10 +408,10 @@
     far["e"] = move(far["c"], 0, -1)
     far["d"] = move(far["a"], -1, 0)
     far["g"] = move(far["a"], 0, 1, left_half)
-    group1, group2, group3 = ("a", "b", "c"), ("d", "e", "h"), ("f", "g", "k")
+    group1, group2, group3 = ("a", "b"), ("c", "d", "e", "h"), ("f", "g", "k")
     sums, parts, token = work(group1, sums)
 
-    far["h"], far["e"], *parts = tie([far["h"], far["e"], *parts], token, far["d"], far["g"])
+    far["h"], far["e"], *parts = tie([far["h"], far["e"], *parts], token, far["g"])
     far["f"] = move(far["h"], 0, 1)
     far["k"] = move(far["e"], -1, 0, top_half)
     returned = give_back(("a",), parts[0:1])
@@ -419,7 +419,7 @@
     sums, parts, token = work(group2, sums)
 
     far["f"], far["k"], *parts = tie([far["f"], far["k"], *later, *parts], *returned)
-    returned += give_back(("b", "c", *group2), parts)
+    returned += give_back(("b", *group2), parts)
     sums, parts, token = work(group3, sums)
 
     sums, *parts = tie([sums, *parts], *returned[1:])

time: 182 us -> 185 us (1.016)
  waiting for transfers between devices: 43.6 us -> 41 us
  starting transfers between devices: 50.8 us -> 52.9 us
    ppermute x9, starting transfers between devices: 22.2 us -> 26.7 us  [give_back(): returned.append(lax.ppermute(part, 'row', back))]
    ppermute x6, starting transfers between devices: 9.27 us -> 6.76 us  [turn(): lax.ppermute(array, 'col', [(i, (i + by * CORES) % COLS) for i in range(C...]
  transfers between devices with their start and end apart: 27 -> 27, of which waited for: 15 -> 14; matrix products, arithmetic and copies ran while one was open for 3% -> 3% of each run, Pallas kernels for 21% -> 21%
where the time goes in v13:
time: 185 us; the launch traced here: 184 us
  starting transfers between devices  52.9 us (29%)
  Pallas kernels  46.6 us (25%)
  waiting for transfers between devices  41 us (22%)
  blocking collectives  28.8 us (16%)
  local copies, waits for them, and re-layouts  10.4 us (6%)
  other arithmetic  3.12 us (2%)
    ppermute x9, waiting for transfers between devices, move(): return lax.ppermute(array, 'row', shift(dy, dx, keep))  32.3 us
    pallas_call x3, Pallas kernels, cells(): pl.pallas_call(functools.partial(cells_kernel, count), out_shape=[SUMS] +...  29.6 us
    all_to_all x1, blocking collectives, per_device(): gram = jnp.sum(lax.all_to_all(everyone, 'row', 0, 0), axis=0)  28.8 us
    ppermute x9, starting transfers between devices, give_back(): returned.append(lax.ppermute(part, 'row', back))  26.7 us
    ppermute x9, starting transfers between devices, move(): return lax.ppermute(array, 'row', shift(dy, dx, keep))  13.9 us
    pallas_call x1, Pallas kernels, own_cells(): pl.pallas_call(own_kernel, out_shape=[SUMS, NORM, ROW, TOKEN], grid_spec=...  9.4 us
    ppermute x6, starting transfers between devices, turn(): lax.ppermute(array, 'col', [(i, (i + by * CORES) % COLS) for i in range(C...  6.76 us
    all_to_all x1, starting transfers between devices, per_device(): lax.all_to_all(jnp.broadcast_to(vectors, (COLS, EIGS, BLOCK)), 'col', 0, 0)  5.31 us
  transfers between devices with their start and end apart: 27, of which 14 were waited for; matrix products, arithmetic and copies ran while one was open for 3% of the time, Pallas kernels for 21%

profile of v13, /device:TPU:0, one launch (start us, length us, event | category | flops | bytes accessed | tf_op | source)
XLA Modules:
  0.0 183.7 jit_solution(10423498498933901188)
XLA Ops:
  0.0 2.6 %payload.1.far_ref = bf16[560,1024]{1,0:T(8,128)(2,1)} custom-call(s32[1]{0:T(128)} %bitcast.13.index_ref, bf16[8,512,1024]{2,1,0:T(8,128)(2,1)} %bitcast.36, bf16[64,512]{1,0:T(8,128)(2,1)} %v_ref.1), custom_call_target="tpu_custom_call" | custom-call | tf_op jit(solution)/shard_map/payload/pallas_call | solution.py:78
  2.6 5.3 %collective-permute-start.2 = (bf16[560,1024]{1,0:T(8,128)(2,1)}, bf16[560,1024]{1,0:T(8,128)(2,1)S(1)}, u32[]{:S(2)}, u32[]{:S(2)}) collective-permute-start(bf16[560,1024]{1,0:T(8,128)(2,1)} %payload.1.far_ref), channel_id=1, source_target_pairs={{0,120},{8,96},{16,104},{24,112},{32,24},{40,0},{48,8},{56,16},{64... | collective-permute-start | bytes 3440648 | tf_op jit(solution)/shard_map/ppermute | solution.py:357
  8.8 5.3 %all-to-all-start = ((bf16[8,64,512]{2,1,0:T(8,128)(2,1)}), bf16[8,64,512]{2,1,0:T(8,128)(2,1)S(1)}, u32[]{:S(2)}, u32[]{:S(2)}) async-start(bf16[8,64,512]{2,1,0:T(8,128)(2,1)} %broadcast_in_dim.8), calls=%async_computation | async-start | bytes 1048576 | tf_op jit(solution)/shard_map/all_to_all | solution.py:403
  15.9 9.4 %cells_own.1 = (f32[8,72,512]{2,1,0:T(8,128)}, f32[8,512,128]{2,1,0:T(8,128)}, f32[8,8,512]{2,1,0:T(8,128)}, f32[8,128]{1,0:T(8,128)}) custom-call(s32[8]{0:T(128)} %slice_reduce_fusion.flags_ref, bf16[8,512,1024]{2,1,0:T(8,128)(2,1)} %bitcast.37, bf16[560,1024]{1,0:T(8,128)(2,1)} %payload.1.far_ref), custom_call_target="tpu_custom_call" | custom-call | flops 2147483648 | bytes 13631488 | tf_op jit(solution)/shard_map/cells_own/pallas_call | solution.py:232
  25.4 7.4 %collective-permute-done.2.refs_2_ = bf16[560,1024]{1,0:T(8,128)(2,1)S(1)} collective-permute-done((bf16[560,1024]{1,0:T(8,128)(2,1)}, bf16[560,1024]{1,0:T(8,128)(2,1)S(1)}, u32[]{:S(2)}, u32[]{:S(2)}) %collective-permute-start.2) | collective-permute-done | bytes 1146912 | tf_op jit(solution)/shard_map/ppermute | solution.py:357
  32.8 3.3 %collective-permute-done.1.refs_1_ = bf16[560,1024]{1,0:T(8,128)(2,1)S(1)} collective-permute-done((bf16[560,1024]{1,0:T(8,128)(2,1)}, bf16[560,1024]{1,0:T(8,128)(2,1)S(1)}, u32[]{:S(2)}, u32[]{:S(2)}) %collective-permute-start.1) | collective-permute-done | bytes 1146912 | tf_op jit(solution)/shard_map/ppermute | solution.py:357
  37.9 3.1 %collective-permute-start.5 = (bf16[560,1024]{1,0:T(8,128)(2,1)}, bf16[560,1024]{1,0:T(8,128)(2,1)S(1)}, u32[]{:S(2)}, u32[]{:S(2)}) collective-permute-start(bf16[560,1024]{1,0:T(8,128)(2,1)} %get-tuple-element.43.refs_0_), channel_id=1, source_target_pairs={{0,8},{24,0},{32,40},{56,32},{64,72},{88,64},{96,104},{120,96},{1,... | collective-permute-start | bytes 3440648 | tf_op jit(solution)/shard_map/ppermute | solution.py:357
  41.0 3.3 %collective-permute-start.8 = (bf16[560,1024]{1,0:T(8,128)(2,1)}, bf16[560,1024]{1,0:T(8,128)(2,1)}, u32[]{:S(2)}, u32[]{:S(2)}) collective-permute-start(bf16[560,1024]{1,0:T(8,128)(2,1)} %get-tuple-element.43.refs_0_), channel_id=1, source_target_pairs={{0,96},{8,104},{16,112},{24,120},{32,0},{40,8},{48,16},{56,24},{64... | collective-permute-start | bytes 3440648 | tf_op jit(solution)/shard_map/ppermute | solution.py:357
  45.1 10.3 %cells.3 = (f32[8,72,512]{2,1,0:T(8,128)}, bf16[80,512]{1,0:T(8,128)(2,1)}, bf16[80,512]{1,0:T(8,128)(2,1)}, f32[8,128]{1,0:T(8,128)}) custom-call(s32[16]{0:T(128)} %reshape.212.flags_ref, bf16[8,512,1024]{2,1,0:T(8,128)(2,1)} %bitcast.38, bf16[8,64,512]{2,1,0:T(8,128)(2,1)} %copy-done.1, ...), custom_call_target="tpu_custom_call", output_to_operand_aliasing={{0}: (7, {})} | custom-call | flops 4294967296 | bytes 14680064 | tf_op jit(solution)/shard_map/cells/pallas_call | solution.py:271
  55.4 9.0 %collective-permute-done.3.refs_0_ = bf16[560,1024]{1,0:T(8,128)(2,1)S(1)} collective-permute-done((bf16[560,1024]{1,0:T(8,128)(2,1)}, bf16[560,1024]{1,0:T(8,128)(2,1)S(1)}, u32[]{:S(2)}, u32[]{:S(2)}) %collective-permute-start.3) | collective-permute-done | bytes 1146912 | tf_op jit(solution)/shard_map/ppermute | solution.py:357
  64.4 2.3 %collective-permute-done.5.refs_5_.refs_1_ = bf16[560,1024]{1,0:T(8,128)(2,1)S(1)} collective-permute-done((bf16[560,1024]{1,0:T(8,128)(2,1)}, bf16[560,1024]{1,0:T(8,128)(2,1)S(1)}, u32[]{:S(2)}, u32[]{:S(2)}) %collective-permute-start.5) | collective-permute-done | bytes 1146912 | tf_op jit(solution)/shard_map/ppermute | solution.py:357
  70.8 3.1 %collective-permute-start.9 = (bf16[80,512]{1,0:T(8,128)(2,1)}, bf16[80,512]{1,0:T(8,128)(2,1)S(1)}, u32[]{:S(2)}, u32[]{:S(2)}) collective-permute-start(bf16[80,512]{1,0:T(8,128)(2,1)} %get-tuple-element.58), channel_id=1, source_target_pairs={{8,0},{16,8},{24,16},{0,24},{40,32},{48,40},{56,48},{32,56},{72,64... | collective-permute-start | bytes 245768 | tf_op jit(solution)/shard_map/ppermute | solution.py:400
  73.9 10.3 %cells.4 = (f32[8,72,512]{2,1,0:T(8,128)}, bf16[80,512]{1,0:T(8,128)(2,1)}, bf16[80,512]{1,0:T(8,128)(2,1)}, bf16[80,512]{1,0:T(8,128)(2,1)}, bf16[80,512]{1,0:T(8,128)(2,1)}, /*index=5*/f32[8,128]{1,0:T(8,128)}) custom-call(s32[32]{0:T(128)} %reshape.213.flags_ref, bf16[8,512,1024]{2,1,0:T(8,128)(2,1)} %bitcast.39, ...), custom_call_target="tpu_custom_call", output_to_operand_aliasing={{0}: (9, {})} | custom-call | flops 8589934592 | bytes 16777216 | tf_op jit(solution)/shard_map/cells/pallas_call | solution.py:271
  84.3 9.5 %collective-permute-done.6.refs_0_ = bf16[560,1024]{1,0:T(8,128)(2,1)S(1)} collective-permute-done((bf16[560,1024]{1,0:T(8,128)(2,1)}, bf16[560,1024]{1,0:T(8,128)(2,1)S(1)}, u32[]{:S(2)}, u32[]{:S(2)}) %collective-permute-start.6) | collective-permute-done | bytes 1146912 | tf_op jit(solution)/shard_map/ppermute | solution.py:357
  95.6 2.4 %collective-permute-start.10 = (bf16[80,512]{1,0:T(8,128)(2,1)}, bf16[80,512]{1,0:T(8,128)(2,1)S(1)}, u32[]{:S(2)}, u32[]{:S(2)}) collective-permute-start(bf16[80,512]{1,0:T(8,128)(2,1)} %get-tuple-element.66), channel_id=1, source_target_pairs={{32,0},{40,8},{48,16},{56,24},{64,32},{72,40},{80,48},{88,56},{96,... | collective-permute-start | bytes 245768 | tf_op jit(solution)/shard_map/ppermute | solution.py:400
  98.9 9.2 %collective-permute-start.12 = (bf16[80,512]{1,0:T(8,128)(2,1)}, bf16[80,512]{1,0:T(8,128)(2,1)S(1)}, u32[]{:S(2)}, u32[]{:S(2)}) collective-permute-start(bf16[80,512]{1,0:T(8,128)(2,1)} %get-tuple-element.68), channel_id=1, source_target_pairs={{104,0},{112,8},{120,16},{96,24},{8,32},{16,40},{24,48},{0,56},{40... | collective-permute-start | bytes 245768 | tf_op jit(solution)/shard_map/ppermute | solution.py:400
  108.7 3.1 %collective-permute-start.14 = (bf16[80,512]{1,0:T(8,128)(2,1)}, bf16[80,512]{1,0:T(8,128)(2,1)S(1)}, u32[]{:S(2)}, u32[]{:S(2)}) collective-permute-start(bf16[80,512]{1,0:T(8,128)(2,1)} %get-tuple-element.70), channel_id=1, source_target_pairs={{0,64},{8,72},{16,80},{24,88},{32,96},{40,104},{48,112},{56,120},{... | collective-permute-start | bytes 245768 | tf_op jit(solution)/shard_map/ppermute | solution.py:400
  111.8 9.0 %cells.5 = (f32[8,72,512]{2,1,0:T(8,128)}, bf16[80,512]{1,0:T(8,128)(2,1)}, bf16[80,512]{1,0:T(8,128)(2,1)}, bf16[80,512]{1,0:T(8,128)(2,1)}, f32[8,128]{1,0:T(8,128)}) custom-call(s32[24]{0:T(128)} %reshape.210.flags_ref, bf16[8,512,1024]{2,1,0:T(8,128)(2,1)} %bitcast.40, bf16[8,64,512]{2,1,0:T(8,128)(2,1)} %copy-done.1, ...), custom_call_target="tpu_custom_call", output_to_operand_aliasing={{0}: (8, {})} | custom-call | flops 6442450944 | bytes 15728640 | tf_op jit(solution)/shard_map/cells/pallas_call | solution.py:271
  123.0 1.8 collective-permute-done.15
  126.6 2.4 %collective-permute-start.16 = (f32[72,512]{1,0:T(8,128)S(1)}, f32[72,512]{1,0:T(8,128)S(1)}, u32[]{:S(2)}, u32[]{:S(2)}) collective-permute-start(f32[72,512]{1,0:T(8,128)S(1)} %get-tuple-element.77), channel_id=1, source_target_pairs={{0,6},{1,7},{2,0},{3,1},{4,2},{5,3},{6,4},{7,5},{8,14},{9,15},{10,... | collective-permute-start | bytes 442376 | tf_op jit(solution)/shard_map/ppermute | solution.py:360
  128.9 6.0 %collective-permute-start.20 = (bf16[80,512]{1,0:T(8,128)(2,1)S(1)}, bf16[80,512]{1,0:T(8,128)(2,1)S(1)}, u32[]{:S(2)}, u32[]{:S(2)}) collective-permute-start(bf16[80,512]{1,0:T(8,128)(2,1)S(1)} %copy-done.24), channel_id=1, source_target_pairs={{0,16},{8,24},{32,48},{40,56},{64,80},{72,88},{96,112},{104,120},{... | collective-permute-start | bytes 245768 | tf_op jit(solution)/shard_map/ppermute | solution.py:400
  144.1 1.9 %collective-permute-done.24 = f32[64,64]{1,0:T(8,128)S(1)} collective-permute-done((f32[64,64]{1,0:T(8,128)S(1)}, f32[64,64]{1,0:T(8,128)S(1)}, u32[]{:S(2)}, u32[]{:S(2)}) %collective-permute-start.24) | collective-permute-done | bytes 16416 | tf_op jit(solution)/shard_map/ppermute | solution.py:360
  147.3 28.8 %all_to_all.10 = f32[16,1,4096]{2,1,0:T(1,128)S(1)} all-to-all(f32[16,1,4096]{2,1,0:T(1,128)S(1)} %reshape.218), channel_id=1, replica_groups=mesh['row'=16,'col'=8] {'row'}, dimensions={0} | all-to-all | bytes 524288 | tf_op jit(solution)/shard_map/all_to_all | solution.py:445
  178.8 5.0 %solve.1 = f32[64,512]{1,0:T(8,128)} custom-call(f32[64,64]{1,0:T(8,128)} %reduce_sum.9.gram_ref, f32[64,512]{1,0:T(8,128)} %copy-done.2), custom_call_target="tpu_custom_call" | custom-call | tf_op jit(solution)/shard_map/solve/pallas_call | solution.py:341
  (149 shorter events, 29.3 us)
Async XLA Ops:
  2.6 30.1 %collective-permute-start.2 = (bf16[560,1024]{1,0:T(8,128)(2,1)}, bf16[560,1024]{1,0:T(8,128)(2,1)S(1)}, u32[]{:S(2)}, u32[]{:S(2)}) collective-permute-start(bf16[560,1024]{1,0:T(8,128)(2,1)} %payload.1.far_ref), channel_id=1, source_target_pairs={{0,120},{8,96},{16,104},{24,112},{32,24},{40,0},{48,8},{56,16},{64... | collective-permute-start | bytes 3440648 | tf_op jit(solution)/shard_map/ppermute | solution.py:357
  7.9 28.1 %collective-permute-start.1 = (bf16[560,1024]{1,0:T(8,128)(2,1)}, bf16[560,1024]{1,0:T(8,128)(2,1)S(1)}, u32[]{:S(2)}, u32[]{:S(2)}) collective-permute-start(bf16[560,1024]{1,0:T(8,128)(2,1)} %payload.1.far_ref), channel_id=1, source_target_pairs={{0,32},{8,40},{16,48},{24,56},{32,64},{40,72},{48,80},{56,88},{64,... | collective-permute-start | bytes 3440648 | tf_op jit(solution)/shard_map/ppermute | solution.py:357
  7.9 28.3 %collective-permute-start = (bf16[560,1024]{1,0:T(8,128)(2,1)}, bf16[560,1024]{1,0:T(8,128)(2,1)}, u32[]{:S(2)}, u32[]{:S(2)}) collective-permute-start(bf16[560,1024]{1,0:T(8,128)(2,1)} %payload.1.far_ref), channel_id=1, source_target_pairs={{0,8},{8,16},{16,24},{24,0},{32,40},{40,48},{48,56},{56,32},{64,72... | collective-permute-start | bytes 3440648 | tf_op jit(solution)/shard_map/ppermute | solution.py:357
  8.8 16.6 %all-to-all-start = ((bf16[8,64,512]{2,1,0:T(8,128)(2,1)}), bf16[8,64,512]{2,1,0:T(8,128)(2,1)S(1)}, u32[]{:S(2)}, u32[]{:S(2)}) async-start(bf16[8,64,512]{2,1,0:T(8,128)(2,1)} %broadcast_in_dim.8), calls=%async_computation | async-start | bytes 1048576 | tf_op jit(solution)/shard_map/all_to_all | solution.py:403
  37.1 27.3 %collective-permute-start.3 = (bf16[560,1024]{1,0:T(8,128)(2,1)}, bf16[560,1024]{1,0:T(8,128)(2,1)S(1)}, u32[]{:S(2)}, u32[]{:S(2)}) collective-permute-start(bf16[560,1024]{1,0:T(8,128)(2,1)} %get-tuple-element.41.refs_1_), channel_id=1, source_target_pairs={{0,32},{8,40},{16,48},{24,56},{32,64},{40,72},{48,80},{56,88},{64,... | collective-permute-start | bytes 3440648 | tf_op jit(solution)/shard_map/ppermute | solution.py:357
  37.1 27.3 %collective-permute-start.4 = (bf16[560,1024]{1,0:T(8,128)(2,1)}, bf16[560,1024]{1,0:T(8,128)(2,1)S(1)}, u32[]{:S(2)}, u32[]{:S(2)}) collective-permute-start(bf16[560,1024]{1,0:T(8,128)(2,1)} %get-tuple-element.42.refs_0_), channel_id=1, source_target_pairs={{0,24},{8,0},{16,8},{24,16},{32,56},{40,32},{48,40},{56,48},{64,88... | collective-permute-start | bytes 3440648 | tf_op jit(solution)/shard_map/ppermute | solution.py:357
  37.9 28.8 %collective-permute-start.5 = (bf16[560,1024]{1,0:T(8,128)(2,1)}, bf16[560,1024]{1,0:T(8,128)(2,1)S(1)}, u32[]{:S(2)}, u32[]{:S(2)}) collective-permute-start(bf16[560,1024]{1,0:T(8,128)(2,1)} %get-tuple-element.43.refs_0_), channel_id=1, source_target_pairs={{0,8},{24,0},{32,40},{56,32},{64,72},{88,64},{96,104},{120,96},{1,... | collective-permute-start | bytes 3440648 | tf_op jit(solution)/shard_map/ppermute | solution.py:357
  41.0 32.9 %collective-permute-start.8 = (bf16[560,1024]{1,0:T(8,128)(2,1)}, bf16[560,1024]{1,0:T(8,128)(2,1)}, u32[]{:S(2)}, u32[]{:S(2)}) collective-permute-start(bf16[560,1024]{1,0:T(8,128)(2,1)} %get-tuple-element.43.refs_0_), channel_id=1, source_target_pairs={{0,96},{8,104},{16,112},{24,120},{32,0},{40,8},{48,16},{56,24},{64... | collective-permute-start | bytes 3440648 | tf_op jit(solution)/shard_map/ppermute | solution.py:357
  67.8 26.0 %collective-permute-start.6 = (bf16[560,1024]{1,0:T(8,128)(2,1)}, bf16[560,1024]{1,0:T(8,128)(2,1)S(1)}, u32[]{:S(2)}, u32[]{:S(2)}) collective-permute-start(bf16[560,1024]{1,0:T(8,128)(2,1)} %get-tuple-element.50.refs_3_), channel_id=1, source_target_pairs={{0,8},{8,16},{16,24},{24,0},{32,40},{40,48},{48,56},{56,32},{64,72... | collective-permute-start | bytes 3440648 | tf_op jit(solution)/shard_map/ppermute | solution.py:357
  67.9 26.6 %collective-permute-start.7 = (bf16[560,1024]{1,0:T(8,128)(2,1)}, bf16[560,1024]{1,0:T(8,128)(2,1)S(1)}, u32[]{:S(2)}, u32[]{:S(2)}) collective-permute-start(bf16[560,1024]{1,0:T(8,128)(2,1)} %get-tuple-element.51.refs_2_), channel_id=1, source_target_pairs={{32,0},{40,8},{48,16},{56,24},{64,32},{72,40},{80,48},{88,56},{33,... | collective-permute-start | bytes 3440648 | tf_op jit(solution)/shard_map/ppermute | solution.py:357
  70.8 13.5 %collective-permute-start.9 = (bf16[80,512]{1,0:T(8,128)(2,1)}, bf16[80,512]{1,0:T(8,128)(2,1)S(1)}, u32[]{:S(2)}, u32[]{:S(2)}) collective-permute-start(bf16[80,512]{1,0:T(8,128)(2,1)} %get-tuple-element.58), channel_id=1, source_target_pairs={{8,0},{16,8},{24,16},{0,24},{40,32},{48,40},{56,48},{32,56},{72,64... | collective-permute-start | bytes 245768 | tf_op jit(solution)/shard_map/ppermute | solution.py:400
  95.6 25.2 %collective-permute-start.10 = (bf16[80,512]{1,0:T(8,128)(2,1)}, bf16[80,512]{1,0:T(8,128)(2,1)S(1)}, u32[]{:S(2)}, u32[]{:S(2)}) collective-permute-start(bf16[80,512]{1,0:T(8,128)(2,1)} %get-tuple-element.66), channel_id=1, source_target_pairs={{32,0},{40,8},{48,16},{56,24},{64,32},{72,40},{80,48},{88,56},{96,... | collective-permute-start | bytes 245768 | tf_op jit(solution)/shard_map/ppermute | solution.py:400
  98.0 22.8 %collective-permute-start.11 = (bf16[80,512]{1,0:T(8,128)(2,1)}, bf16[80,512]{1,0:T(8,128)(2,1)S(1)}, u32[]{:S(2)}, u32[]{:S(2)}) collective-permute-start(bf16[80,512]{1,0:T(8,128)(2,1)} %get-tuple-element.67), channel_id=1, source_target_pairs={{120,0},{96,8},{104,16},{112,24},{24,32},{0,40},{8,48},{16,56},{56... | collective-permute-start | bytes 245768 | tf_op jit(solution)/shard_map/ppermute | solution.py:400
  98.9 21.9 %collective-permute-start.12 = (bf16[80,512]{1,0:T(8,128)(2,1)}, bf16[80,512]{1,0:T(8,128)(2,1)S(1)}, u32[]{:S(2)}, u32[]{:S(2)}) collective-permute-start(bf16[80,512]{1,0:T(8,128)(2,1)} %get-tuple-element.68), channel_id=1, source_target_pairs={{104,0},{112,8},{120,16},{96,24},{8,32},{16,40},{24,48},{0,56},{40... | collective-permute-start | bytes 245768 | tf_op jit(solution)/shard_map/ppermute | solution.py:400
  108.1 12.7 %collective-permute-start.13 = (bf16[80,512]{1,0:T(8,128)(2,1)}, bf16[80,512]{1,0:T(8,128)(2,1)S(1)}, u32[]{:S(2)}, u32[]{:S(2)}) collective-permute-start(bf16[80,512]{1,0:T(8,128)(2,1)} %get-tuple-element.69), channel_id=1, source_target_pairs={{112,0},{120,8},{96,16},{104,24},{16,32},{24,40},{0,48},{8,56},{48... | collective-permute-start | bytes 245768 | tf_op jit(solution)/shard_map/ppermute | solution.py:400
  108.7 12.2 %collective-permute-start.14 = (bf16[80,512]{1,0:T(8,128)(2,1)}, bf16[80,512]{1,0:T(8,128)(2,1)S(1)}, u32[]{:S(2)}, u32[]{:S(2)}) collective-permute-start(bf16[80,512]{1,0:T(8,128)(2,1)} %get-tuple-element.70), channel_id=1, source_target_pairs={{0,64},{8,72},{16,80},{24,88},{32,96},{40,104},{48,112},{56,120},{... | collective-permute-start | bytes 245768 | tf_op jit(solution)/shard_map/ppermute | solution.py:400
  123.0 12.0 %collective-permute-start.19 = (bf16[80,512]{1,0:T(8,128)(2,1)S(1)}, bf16[80,512]{1,0:T(8,128)(2,1)S(1)}, u32[]{:S(2)}, u32[]{:S(2)}) collective-permute-start(bf16[80,512]{1,0:T(8,128)(2,1)S(1)} %copy-done.23), channel_id=1, source_target_pairs={{72,0},{80,8},{88,16},{64,24},{104,32},{112,40},{120,48},{96,56},{... | collective-permute-start | bytes 245768 | tf_op jit(solution)/shard_map/ppermute | solution.py:400
  125.0 13.3 %collective-permute-start.17 = (f32[72,512]{1,0:T(8,128)S(1)}, f32[72,512]{1,0:T(8,128)S(1)}, u32[]{:S(2)}, u32[]{:S(2)}) collective-permute-start(f32[72,512]{1,0:T(8,128)S(1)} %get-tuple-element.75), channel_id=1, source_target_pairs={{0,4},{1,5},{2,6},{3,7},{4,0},{5,1},{6,2},{7,3},{8,12},{9,13},{10,... | collective-permute-start | bytes 442376 | tf_op jit(solution)/shard_map/ppermute | solution.py:360
  125.7 12.6 %collective-permute-start.18 = (f32[72,512]{1,0:T(8,128)S(1)}, f32[72,512]{1,0:T(8,128)S(1)}, u32[]{:S(2)}, u32[]{:S(2)}) collective-permute-start(f32[72,512]{1,0:T(8,128)S(1)} %get-tuple-element.76), channel_id=1, source_target_pairs={{0,2},{1,3},{2,4},{3,5},{4,6},{5,7},{6,0},{7,1},{8,10},{9,11},{10,... | collective-permute-start | bytes 442376 | tf_op jit(solution)/shard_map/ppermute | solution.py:360
  126.6 11.8 %collective-permute-start.16 = (f32[72,512]{1,0:T(8,128)S(1)}, f32[72,512]{1,0:T(8,128)S(1)}, u32[]{:S(2)}, u32[]{:S(2)}) collective-permute-start(f32[72,512]{1,0:T(8,128)S(1)} %get-tuple-element.77), channel_id=1, source_target_pairs={{0,6},{1,7},{2,0},{3,1},{4,2},{5,3},{6,4},{7,5},{8,14},{9,15},{10,... | collective-permute-start | bytes 442376 | tf_op jit(solution)/shard_map/ppermute | solution.py:360
  128.9 8.5 %collective-permute-start.20 = (bf16[80,512]{1,0:T(8,128)(2,1)S(1)}, bf16[80,512]{1,0:T(8,128)(2,1)S(1)}, u32[]{:S(2)}, u32[]{:S(2)}) collective-permute-start(bf16[80,512]{1,0:T(8,128)(2,1)S(1)} %copy-done.24), channel_id=1, source_target_pairs={{0,16},{8,24},{32,48},{40,56},{64,80},{72,88},{96,112},{104,120},{... | collective-permute-start | bytes 245768 | tf_op jit(solution)/shard_map/ppermute | solution.py:400
  140.1 4.0 %collective-permute-start.25 = (f32[64,64]{1,0:T(8,128)S(1)}, f32[64,64]{1,0:T(8,128)S(1)}, u32[]{:S(2)}, u32[]{:S(2)}) collective-permute-start(f32[64,64]{1,0:T(8,128)S(1)} %add.404), channel_id=1, source_target_pairs={{0,6},{1,7},{2,0},{3,1},{4,2},{5,3},{6,4},{7,5},{8,14},{9,15},{10,... | collective-permute-start | bytes 49160 | tf_op jit(solution)/shard_map/ppermute | solution.py:360
  140.5 5.5 %collective-permute-start.24 = (f32[64,64]{1,0:T(8,128)S(1)}, f32[64,64]{1,0:T(8,128)S(1)}, u32[]{:S(2)}, u32[]{:S(2)}) collective-permute-start(f32[64,64]{1,0:T(8,128)S(1)} %add.404), channel_id=1, source_target_pairs={{0,4},{1,5},{2,6},{3,7},{4,0},{5,1},{6,2},{7,3},{8,12},{9,13},{10,... | collective-permute-start | bytes 49160 | tf_op jit(solution)/shard_map/ppermute | solution.py:360
  141.8 5.1 %collective-permute-start.23 = (f32[64,64]{1,0:T(8,128)S(1)}, f32[64,64]{1,0:T(8,128)S(1)}, u32[]{:S(2)}, u32[]{:S(2)}) collective-permute-start(f32[64,64]{1,0:T(8,128)S(1)} %add.404), channel_id=1, source_target_pairs={{0,2},{1,3},{2,4},{3,5},{4,6},{5,7},{6,0},{7,1},{8,10},{9,11},{10,... | collective-permute-start | bytes 49160 | tf_op jit(solution)/shard_map/ppermute | solution.py:360
  (30 other events, 195.6 us)

commit v14 on v12

--- a/solution.py
+++ b/solution.py
@@ -418,8 +418,10 @@
     later = parts[1:]
     sums, parts, token = work(group2, sums)
 
-    far["f"], far["k"], *parts = tie([far["f"], far["k"], *later, *parts], *returned)
-    returned += give_back(("b", "c", *group2), parts)
+    ready = tie([*later, parts[0]], *returned, token)
+    returned += give_back(("b", "c", "d"), ready)
+    far["f"], far["k"], *parts = tie([far["f"], far["k"], *parts[1:]], ready[0])
+    returned += give_back(("e", "h"), parts)
     sums, parts, token = work(group3, sums)
 
     sums, *parts = tie([sums, *parts], *returned[1:])

time: 182 us -> 181 us (level)
  waiting for transfers between devices: 43.6 us -> 30.7 us
  starting transfers between devices: 50.8 us -> 60.6 us
    ppermute x9, waiting for transfers between devices: 33.7 us -> 22.9 us  [move(): return lax.ppermute(array, 'row', shift(dy, dx, keep))]
    ppermute x9, starting transfers between devices: 22.2 us -> 30.8 us  [give_back(): returned.append(lax.ppermute(part, 'row', back))]
  transfers between devices with their start and end apart: 27 -> 27, of which waited for: 15 -> 12; matrix products, arithmetic and copies ran while one was open for 3% -> 3% of each run, Pallas kernels for 21% -> 21%
where the time goes in v14:
time: 181 us
  starting transfers between devices  60.6 us (33%)
  Pallas kernels  45.8 us (25%)
  waiting for transfers between devices  30.7 us (17%)
  blocking collectives  28.3 us (16%)
  local copies, waits for them, and re-layouts  11.3 us (6%)
  other arithmetic  3.1 us (2%)
    ppermute x9, starting transfers between devices, give_back(): returned.append(lax.ppermute(part, 'row', back))  30.8 us
    pallas_call x3, Pallas kernels, cells(): pl.pallas_call(functools.partial(cells_kernel, count), out_shape=[SUMS] +...  28.9 us
    all_to_all x1, blocking collectives, per_device(): gram = jnp.sum(lax.all_to_all(everyone, 'row', 0, 0), axis=0)  28.3 us
    ppermute x9, waiting for transfers between devices, move(): return lax.ppermute(array, 'row', shift(dy, dx, keep))  22.9 us
    ppermute x9, starting transfers between devices, move(): return lax.ppermute(array, 'row', shift(dy, dx, keep))  13.8 us
    ppermute x6, starting transfers between devices, turn(): lax.ppermute(array, 'col', [(i, (i + by * CORES) % COLS) for i in range(C...  10.5 us
    pallas_call x1, Pallas kernels, own_cells(): pl.pallas_call(own_kernel, out_shape=[SUMS, NORM, ROW, TOKEN], grid_spec=...  9.4 us
    unnamed x57, local copies, waits for them, and re-layouts  5.4 us
  transfers between devices with their start and end apart: 27, of which 12 were waited for; matrix products, arithmetic and copies ran while one was open for 3% of the time, Pallas kernels for 21%

profile of v14, /device:TPU:0, one launch (start us, length us, event | category | flops | bytes accessed | tf_op | source)
XLA Modules:
  0.0 180.9 jit_solution(16557041792196627273)
XLA Ops:
  0.0 2.6 %payload.1.far_ref = bf16[560,1024]{1,0:T(8,128)(2,1)} custom-call(s32[1]{0:T(128)} %bitcast.13.index_ref, bf16[8,512,1024]{2,1,0:T(8,128)(2,1)} %bitcast.36, bf16[64,512]{1,0:T(8,128)(2,1)} %v_ref.1), custom_call_target="tpu_custom_call" | custom-call | tf_op jit(solution)/shard_map/payload/pallas_call | solution.py:78
  2.6 5.3 %collective-permute-start.2 = (bf16[560,1024]{1,0:T(8,128)(2,1)}, bf16[560,1024]{1,0:T(8,128)(2,1)S(1)}, u32[]{:S(2)}, u32[]{:S(2)}) collective-permute-start(bf16[560,1024]{1,0:T(8,128)(2,1)} %payload.1.far_ref), channel_id=1, source_target_pairs={{0,120},{8,96},{16,104},{24,112},{32,24},{40,0},{48,8},{56,16},{64... | collective-permute-start | bytes 3440648 | tf_op jit(solution)/shard_map/ppermute | solution.py:357
  8.8 5.3 %all-to-all-start = ((bf16[8,64,512]{2,1,0:T(8,128)(2,1)}), bf16[8,64,512]{2,1,0:T(8,128)(2,1)S(1)}, u32[]{:S(2)}, u32[]{:S(2)}) async-start(bf16[8,64,512]{2,1,0:T(8,128)(2,1)} %broadcast_in_dim.8), calls=%async_computation | async-start | bytes 1048576 | tf_op jit(solution)/shard_map/all_to_all | solution.py:403
  16.0 9.4 %cells_own.1 = (f32[8,72,512]{2,1,0:T(8,128)}, f32[8,512,128]{2,1,0:T(8,128)}, f32[8,8,512]{2,1,0:T(8,128)}, f32[8,128]{1,0:T(8,128)}) custom-call(s32[8]{0:T(128)} %slice_reduce_fusion.flags_ref, bf16[8,512,1024]{2,1,0:T(8,128)(2,1)} %bitcast.37, bf16[560,1024]{1,0:T(8,128)(2,1)} %payload.1.far_ref), custom_call_target="tpu_custom_call" | custom-call | flops 2147483648 | bytes 13631488 | tf_op jit(solution)/shard_map/cells_own/pallas_call | solution.py:232
  25.4 7.3 %collective-permute-done.2.refs_2_ = bf16[560,1024]{1,0:T(8,128)(2,1)S(1)} collective-permute-done((bf16[560,1024]{1,0:T(8,128)(2,1)}, bf16[560,1024]{1,0:T(8,128)(2,1)S(1)}, u32[]{:S(2)}, u32[]{:S(2)}) %collective-permute-start.2) | collective-permute-done | bytes 1146912 | tf_op jit(solution)/shard_map/ppermute | solution.py:357
  32.7 3.3 %collective-permute-done.1.refs_1_ = bf16[560,1024]{1,0:T(8,128)(2,1)S(1)} collective-permute-done((bf16[560,1024]{1,0:T(8,128)(2,1)}, bf16[560,1024]{1,0:T(8,128)(2,1)S(1)}, u32[]{:S(2)}, u32[]{:S(2)}) %collective-permute-start.1) | collective-permute-done | bytes 1146912 | tf_op jit(solution)/shard_map/ppermute | solution.py:357
  38.0 3.1 %collective-permute-start.6 = (bf16[560,1024]{1,0:T(8,128)(2,1)}, bf16[560,1024]{1,0:T(8,128)(2,1)S(1)}, u32[]{:S(2)}, u32[]{:S(2)}) collective-permute-start(bf16[560,1024]{1,0:T(8,128)(2,1)} %get-tuple-element.45.refs_0_), channel_id=1, source_target_pairs={{0,8},{24,0},{32,40},{56,32},{64,72},{88,64},{96,104},{120,96},{1,... | collective-permute-start | bytes 3440648 | tf_op jit(solution)/shard_map/ppermute | solution.py:357
  41.1 3.3 %collective-permute-start.5 = (bf16[560,1024]{1,0:T(8,128)(2,1)}, bf16[560,1024]{1,0:T(8,128)(2,1)S(1)}, u32[]{:S(2)}, u32[]{:S(2)}) collective-permute-start(bf16[560,1024]{1,0:T(8,128)(2,1)} %get-tuple-element.45.refs_0_), channel_id=1, source_target_pairs={{0,96},{8,104},{16,112},{24,120},{32,0},{40,8},{48,16},{56,24},{64... | collective-permute-start | bytes 3440648 | tf_op jit(solution)/shard_map/ppermute | solution.py:357
  45.2 10.0 %cells.3 = (f32[8,72,512]{2,1,0:T(8,128)}, bf16[80,512]{1,0:T(8,128)(2,1)}, bf16[80,512]{1,0:T(8,128)(2,1)}, bf16[80,512]{1,0:T(8,128)(2,1)}, f32[8,128]{1,0:T(8,128)}) custom-call(s32[24]{0:T(128)} %reshape.212.flags_ref, bf16[8,512,1024]{2,1,0:T(8,128)(2,1)} %bitcast.38, bf16[8,64,512]{2,1,0:T(8,128)(2,1)} %copy-done.1, ...), custom_call_target="tpu_custom_call", output_to_operand_aliasing={{0}: (8, {})} | custom-call | flops 6442450944 | bytes 15728640 | tf_op jit(solution)/shard_map/cells/pallas_call | solution.py:271
  55.2 9.3 %collective-permute-done.3.refs_0_ = bf16[560,1024]{1,0:T(8,128)(2,1)S(1)} collective-permute-done((bf16[560,1024]{1,0:T(8,128)(2,1)}, bf16[560,1024]{1,0:T(8,128)(2,1)S(1)}, u32[]{:S(2)}, u32[]{:S(2)}) %collective-permute-start.3) | collective-permute-done | bytes 1146912 | tf_op jit(solution)/shard_map/ppermute | solution.py:357
  64.5 2.3 %collective-permute-done.6.refs_7_.refs_1_ = bf16[560,1024]{1,0:T(8,128)(2,1)S(1)} collective-permute-done((bf16[560,1024]{1,0:T(8,128)(2,1)}, bf16[560,1024]{1,0:T(8,128)(2,1)S(1)}, u32[]{:S(2)}, u32[]{:S(2)}) %collective-permute-start.6) | collective-permute-done | bytes 1146912 | tf_op jit(solution)/shard_map/ppermute | solution.py:357
  71.1 3.2 %collective-permute-start.9 = (bf16[80,512]{1,0:T(8,128)(2,1)}, bf16[80,512]{1,0:T(8,128)(2,1)S(1)}, u32[]{:S(2)}, u32[]{:S(2)}) collective-permute-start(bf16[80,512]{1,0:T(8,128)(2,1)} %get-tuple-element.61), channel_id=1, source_target_pairs={{8,0},{16,8},{24,16},{0,24},{40,32},{48,40},{56,48},{32,56},{72,64... | collective-permute-start | bytes 245768 | tf_op jit(solution)/shard_map/ppermute | solution.py:400
  74.3 9.9 %cells.4 = (f32[8,72,512]{2,1,0:T(8,128)}, bf16[80,512]{1,0:T(8,128)(2,1)}, bf16[80,512]{1,0:T(8,128)(2,1)}, bf16[80,512]{1,0:T(8,128)(2,1)}, f32[8,128]{1,0:T(8,128)}) custom-call(s32[24]{0:T(128)} %reshape.213.flags_ref, bf16[8,512,1024]{2,1,0:T(8,128)(2,1)} %bitcast.39, bf16[8,64,512]{2,1,0:T(8,128)(2,1)} %copy-done.1, ...), custom_call_target="tpu_custom_call", output_to_operand_aliasing={{0}: (8, {})} | custom-call | flops 6442450944 | bytes 15728640 | tf_op jit(solution)/shard_map/cells/pallas_call | solution.py:271
  84.8 10.3 %collective-permute-start.11 = (bf16[80,512]{1,0:T(8,128)(2,1)}, bf16[80,512]{1,0:T(8,128)(2,1)S(1)}, u32[]{:S(2)}, u32[]{:S(2)}) collective-permute-start(bf16[80,512]{1,0:T(8,128)(2,1)} %get-tuple-element.71), channel_id=1, source_target_pairs={{120,0},{96,8},{104,16},{112,24},{24,32},{0,40},{8,48},{16,56},{56... | collective-permute-start | bytes 245768 | tf_op jit(solution)/shard_map/ppermute | solution.py:400
  95.1 4.0 %collective-permute-start.12 = (bf16[80,512]{1,0:T(8,128)(2,1)}, bf16[80,512]{1,0:T(8,128)(2,1)S(1)}, u32[]{:S(2)}, u32[]{:S(2)}) collective-permute-start(bf16[80,512]{1,0:T(8,128)(2,1)} %get-tuple-element.72), channel_id=1, source_target_pairs={{104,0},{112,8},{120,16},{96,24},{8,32},{16,40},{24,48},{0,56},{40... | collective-permute-start | bytes 245768 | tf_op jit(solution)/shard_map/ppermute | solution.py:400
  100.5 2.2 %collective-permute-start.13 = (bf16[80,512]{1,0:T(8,128)(2,1)}, bf16[80,512]{1,0:T(8,128)(2,1)S(1)}, u32[]{:S(2)}, u32[]{:S(2)}) collective-permute-start(bf16[80,512]{1,0:T(8,128)(2,1)} %get-tuple-element.73), channel_id=1, source_target_pairs={{112,0},{120,8},{96,16},{104,24},{16,32},{24,40},{0,48},{8,56},{48... | collective-permute-start | bytes 245768 | tf_op jit(solution)/shard_map/ppermute | solution.py:400
  104.0 9.0 %cells.5 = (f32[8,72,512]{2,1,0:T(8,128)}, bf16[80,512]{1,0:T(8,128)(2,1)}, bf16[80,512]{1,0:T(8,128)(2,1)}, bf16[80,512]{1,0:T(8,128)(2,1)}, f32[8,128]{1,0:T(8,128)}) custom-call(s32[24]{0:T(128)} %reshape.210.flags_ref, bf16[8,512,1024]{2,1,0:T(8,128)(2,1)} %bitcast.40, bf16[8,64,512]{2,1,0:T(8,128)(2,1)} %copy-done.1, ...), custom_call_target="tpu_custom_call", output_to_operand_aliasing={{0}: (8, {})} | custom-call | flops 6442450944 | bytes 15728640 | tf_op jit(solution)/shard_map/cells/pallas_call | solution.py:271
  115.2 1.6 collective-permute-start.19
  117.3 4.9 %collective-permute-start.17 = (f32[72,512]{1,0:T(8,128)S(1)}, f32[72,512]{1,0:T(8,128)S(1)}, u32[]{:S(2)}, u32[]{:S(2)}) collective-permute-start(f32[72,512]{1,0:T(8,128)S(1)} %get-tuple-element.79), channel_id=1, source_target_pairs={{0,4},{1,5},{2,6},{3,7},{4,0},{5,1},{6,2},{7,3},{8,12},{9,13},{10,... | collective-permute-start | bytes 442376 | tf_op jit(solution)/shard_map/ppermute | solution.py:360
  122.3 3.0 %collective-permute-start.16 = (f32[72,512]{1,0:T(8,128)S(1)}, f32[72,512]{1,0:T(8,128)S(1)}, u32[]{:S(2)}, u32[]{:S(2)}) collective-permute-start(f32[72,512]{1,0:T(8,128)S(1)} %get-tuple-element.81), channel_id=1, source_target_pairs={{0,6},{1,7},{2,0},{3,1},{4,2},{5,3},{6,4},{7,5},{8,14},{9,15},{10,... | collective-permute-start | bytes 442376 | tf_op jit(solution)/shard_map/ppermute | solution.py:360
  125.4 6.9 %collective-permute-start.20 = (bf16[80,512]{1,0:T(8,128)(2,1)S(1)}, bf16[80,512]{1,0:T(8,128)(2,1)S(1)}, u32[]{:S(2)}, u32[]{:S(2)}) collective-permute-start(bf16[80,512]{1,0:T(8,128)(2,1)S(1)} %copy-done.24), channel_id=1, source_target_pairs={{0,16},{8,24},{32,48},{40,56},{64,80},{72,88},{96,112},{104,120},{... | collective-permute-start | bytes 245768 | tf_op jit(solution)/shard_map/ppermute | solution.py:400
  141.4 3.1 %collective-permute-done.24 = f32[64,64]{1,0:T(8,128)S(1)} collective-permute-done((f32[64,64]{1,0:T(8,128)S(1)}, f32[64,64]{1,0:T(8,128)S(1)}, u32[]{:S(2)}, u32[]{:S(2)}) %collective-permute-start.24) | collective-permute-done | bytes 16416 | tf_op jit(solution)/shard_map/ppermute | solution.py:360
  144.9 28.3 %all_to_all.10 = f32[16,1,4096]{2,1,0:T(1,128)S(1)} all-to-all(f32[16,1,4096]{2,1,0:T(1,128)S(1)} %reshape.218), channel_id=1, replica_groups=mesh['row'=16,'col'=8] {'row'}, dimensions={0} | all-to-all | bytes 524288 | tf_op jit(solution)/shard_map/all_to_all | solution.py:447
  175.9 5.0 %solve.1 = f32[64,512]{1,0:T(8,128)} custom-call(f32[64,64]{1,0:T(8,128)} %reduce_sum.9.gram_ref, f32[64,512]{1,0:T(8,128)} %copy-done.2), custom_call_target="tpu_custom_call" | custom-call | tf_op jit(solution)/shard_map/solve/pallas_call | solution.py:341
  (148 shorter events, 27.4 us)
Async XLA Ops:
  2.6 30.1 %collective-permute-start.2 = (bf16[560,1024]{1,0:T(8,128)(2,1)}, bf16[560,1024]{1,0:T(8,128)(2,1)S(1)}, u32[]{:S(2)}, u32[]{:S(2)}) collective-permute-start(bf16[560,1024]{1,0:T(8,128)(2,1)} %payload.1.far_ref), channel_id=1, source_target_pairs={{0,120},{8,96},{16,104},{24,112},{32,24},{40,0},{48,8},{56,16},{64... | collective-permute-start | bytes 3440648 | tf_op jit(solution)/shard_map/ppermute | solution.py:357
  7.9 28.1 %collective-permute-start.1 = (bf16[560,1024]{1,0:T(8,128)(2,1)}, bf16[560,1024]{1,0:T(8,128)(2,1)S(1)}, u32[]{:S(2)}, u32[]{:S(2)}) collective-permute-start(bf16[560,1024]{1,0:T(8,128)(2,1)} %payload.1.far_ref), channel_id=1, source_target_pairs={{0,32},{8,40},{16,48},{24,56},{32,64},{40,72},{48,80},{56,88},{64,... | collective-permute-start | bytes 3440648 | tf_op jit(solution)/shard_map/ppermute | solution.py:357
  7.9 28.3 %collective-permute-start = (bf16[560,1024]{1,0:T(8,128)(2,1)}, bf16[560,1024]{1,0:T(8,128)(2,1)}, u32[]{:S(2)}, u32[]{:S(2)}) collective-permute-start(bf16[560,1024]{1,0:T(8,128)(2,1)} %payload.1.far_ref), channel_id=1, source_target_pairs={{0,8},{8,16},{16,24},{24,0},{32,40},{40,48},{48,56},{56,32},{64,72... | collective-permute-start | bytes 3440648 | tf_op jit(solution)/shard_map/ppermute | solution.py:357
  8.8 16.6 %all-to-all-start = ((bf16[8,64,512]{2,1,0:T(8,128)(2,1)}), bf16[8,64,512]{2,1,0:T(8,128)(2,1)S(1)}, u32[]{:S(2)}, u32[]{:S(2)}) async-start(bf16[8,64,512]{2,1,0:T(8,128)(2,1)} %broadcast_in_dim.8), calls=%async_computation | async-start | bytes 1048576 | tf_op jit(solution)/shard_map/all_to_all | solution.py:403
  37.1 27.3 %collective-permute-start.3 = (bf16[560,1024]{1,0:T(8,128)(2,1)}, bf16[560,1024]{1,0:T(8,128)(2,1)S(1)}, u32[]{:S(2)}, u32[]{:S(2)}) collective-permute-start(bf16[560,1024]{1,0:T(8,128)(2,1)} %get-tuple-element.43.refs_1_), channel_id=1, source_target_pairs={{0,32},{8,40},{16,48},{24,56},{32,64},{40,72},{48,80},{56,88},{64,... | collective-permute-start | bytes 3440648 | tf_op jit(solution)/shard_map/ppermute | solution.py:357
  37.1 27.3 %collective-permute-start.4 = (bf16[560,1024]{1,0:T(8,128)(2,1)}, bf16[560,1024]{1,0:T(8,128)(2,1)}, u32[]{:S(2)}, u32[]{:S(2)}) collective-permute-start(bf16[560,1024]{1,0:T(8,128)(2,1)} %get-tuple-element.44.refs_2_), channel_id=1, source_target_pairs={{0,24},{8,0},{16,8},{24,16},{32,56},{40,32},{48,40},{56,48},{64,88... | collective-permute-start | bytes 3440648 | tf_op jit(solution)/shard_map/ppermute | solution.py:357
  38.0 28.8 %collective-permute-start.6 = (bf16[560,1024]{1,0:T(8,128)(2,1)}, bf16[560,1024]{1,0:T(8,128)(2,1)S(1)}, u32[]{:S(2)}, u32[]{:S(2)}) collective-permute-start(bf16[560,1024]{1,0:T(8,128)(2,1)} %get-tuple-element.45.refs_0_), channel_id=1, source_target_pairs={{0,8},{24,0},{32,40},{56,32},{64,72},{88,64},{96,104},{120,96},{1,... | collective-permute-start | bytes 3440648 | tf_op jit(solution)/shard_map/ppermute | solution.py:357
  41.1 26.2 %collective-permute-start.5 = (bf16[560,1024]{1,0:T(8,128)(2,1)}, bf16[560,1024]{1,0:T(8,128)(2,1)S(1)}, u32[]{:S(2)}, u32[]{:S(2)}) collective-permute-start(bf16[560,1024]{1,0:T(8,128)(2,1)} %get-tuple-element.45.refs_0_), channel_id=1, source_target_pairs={{0,96},{8,104},{16,112},{24,120},{32,0},{40,8},{48,16},{56,24},{64... | collective-permute-start | bytes 3440648 | tf_op jit(solution)/shard_map/ppermute | solution.py:357
  68.3 30.8 %collective-permute-start.7 = (bf16[560,1024]{1,0:T(8,128)(2,1)}, bf16[560,1024]{1,0:T(8,128)(2,1)S(1)}, u32[]{:S(2)}, u32[]{:S(2)}) collective-permute-start(bf16[560,1024]{1,0:T(8,128)(2,1)} %get-tuple-element.53.refs_2_), channel_id=1, source_target_pairs={{0,8},{8,16},{16,24},{24,0},{32,40},{40,48},{48,56},{56,32},{64,72... | collective-permute-start | bytes 3440648 | tf_op jit(solution)/shard_map/ppermute | solution.py:357
  68.3 30.8 %collective-permute-start.8 = (bf16[560,1024]{1,0:T(8,128)(2,1)}, bf16[560,1024]{1,0:T(8,128)(2,1)S(1)}, u32[]{:S(2)}, u32[]{:S(2)}) collective-permute-start(bf16[560,1024]{1,0:T(8,128)(2,1)} %get-tuple-element.54.refs_1_), channel_id=1, source_target_pairs={{32,0},{40,8},{48,16},{56,24},{64,32},{72,40},{80,48},{88,56},{33,... | collective-permute-start | bytes 3440648 | tf_op jit(solution)/shard_map/ppermute | solution.py:357
  71.1 13.1 %collective-permute-start.9 = (bf16[80,512]{1,0:T(8,128)(2,1)}, bf16[80,512]{1,0:T(8,128)(2,1)S(1)}, u32[]{:S(2)}, u32[]{:S(2)}) collective-permute-start(bf16[80,512]{1,0:T(8,128)(2,1)} %get-tuple-element.61), channel_id=1, source_target_pairs={{8,0},{16,8},{24,16},{0,24},{40,32},{48,40},{56,48},{32,56},{72,64... | collective-permute-start | bytes 245768 | tf_op jit(solution)/shard_map/ppermute | solution.py:400
  84.8 28.2 %collective-permute-start.11 = (bf16[80,512]{1,0:T(8,128)(2,1)}, bf16[80,512]{1,0:T(8,128)(2,1)S(1)}, u32[]{:S(2)}, u32[]{:S(2)}) collective-permute-start(bf16[80,512]{1,0:T(8,128)(2,1)} %get-tuple-element.71), channel_id=1, source_target_pairs={{120,0},{96,8},{104,16},{112,24},{24,32},{0,40},{8,48},{16,56},{56... | collective-permute-start | bytes 245768 | tf_op jit(solution)/shard_map/ppermute | solution.py:400
  95.1 17.9 %collective-permute-start.12 = (bf16[80,512]{1,0:T(8,128)(2,1)}, bf16[80,512]{1,0:T(8,128)(2,1)S(1)}, u32[]{:S(2)}, u32[]{:S(2)}) collective-permute-start(bf16[80,512]{1,0:T(8,128)(2,1)} %get-tuple-element.72), channel_id=1, source_target_pairs={{104,0},{112,8},{120,16},{96,24},{8,32},{16,40},{24,48},{0,56},{40... | collective-permute-start | bytes 245768 | tf_op jit(solution)/shard_map/ppermute | solution.py:400
  99.1 13.9 %collective-permute-start.10 = (bf16[80,512]{1,0:T(8,128)(2,1)}, bf16[80,512]{1,0:T(8,128)(2,1)S(1)}, u32[]{:S(2)}, u32[]{:S(2)}) collective-permute-start(bf16[80,512]{1,0:T(8,128)(2,1)} %get-tuple-element.63.refs_4_), channel_id=1, source_target_pairs={{32,0},{40,8},{48,16},{56,24},{64,32},{72,40},{80,48},{88,56},{96,... | collective-permute-start | bytes 245768 | tf_op jit(solution)/shard_map/ppermute | solution.py:400
  100.5 12.5 %collective-permute-start.13 = (bf16[80,512]{1,0:T(8,128)(2,1)}, bf16[80,512]{1,0:T(8,128)(2,1)S(1)}, u32[]{:S(2)}, u32[]{:S(2)}) collective-permute-start(bf16[80,512]{1,0:T(8,128)(2,1)} %get-tuple-element.73), channel_id=1, source_target_pairs={{112,0},{120,8},{96,16},{104,24},{16,32},{24,40},{0,48},{8,56},{48... | collective-permute-start | bytes 245768 | tf_op jit(solution)/shard_map/ppermute | solution.py:400
  102.7 10.3 %collective-permute-start.14 = (bf16[80,512]{1,0:T(8,128)(2,1)}, bf16[80,512]{1,0:T(8,128)(2,1)S(1)}, u32[]{:S(2)}, u32[]{:S(2)}) collective-permute-start(bf16[80,512]{1,0:T(8,128)(2,1)} %get-tuple-element.74), channel_id=1, source_target_pairs={{0,64},{8,72},{16,80},{24,88},{32,96},{40,104},{48,112},{56,120},{... | collective-permute-start | bytes 245768 | tf_op jit(solution)/shard_map/ppermute | solution.py:400
  115.2 17.1 %collective-permute-start.19 = (bf16[80,512]{1,0:T(8,128)(2,1)S(1)}, bf16[80,512]{1,0:T(8,128)(2,1)S(1)}, u32[]{:S(2)}, u32[]{:S(2)}) collective-permute-start(bf16[80,512]{1,0:T(8,128)(2,1)S(1)} %copy-done.23), channel_id=1, source_target_pairs={{72,0},{80,8},{88,16},{64,24},{104,32},{112,40},{120,48},{96,56},{... | collective-permute-start | bytes 245768 | tf_op jit(solution)/shard_map/ppermute | solution.py:400
  117.3 18.4 %collective-permute-start.17 = (f32[72,512]{1,0:T(8,128)S(1)}, f32[72,512]{1,0:T(8,128)S(1)}, u32[]{:S(2)}, u32[]{:S(2)}) collective-permute-start(f32[72,512]{1,0:T(8,128)S(1)} %get-tuple-element.79), channel_id=1, source_target_pairs={{0,4},{1,5},{2,6},{3,7},{4,0},{5,1},{6,2},{7,3},{8,12},{9,13},{10,... | collective-permute-start | bytes 442376 | tf_op jit(solution)/shard_map/ppermute | solution.py:360
  122.1 13.6 %collective-permute-start.18 = (f32[72,512]{1,0:T(8,128)S(1)}, f32[72,512]{1,0:T(8,128)S(1)}, u32[]{:S(2)}, u32[]{:S(2)}) collective-permute-start(f32[72,512]{1,0:T(8,128)S(1)} %get-tuple-element.80), channel_id=1, source_target_pairs={{0,2},{1,3},{2,4},{3,5},{4,6},{5,7},{6,0},{7,1},{8,10},{9,11},{10,... | collective-permute-start | bytes 442376 | tf_op jit(solution)/shard_map/ppermute | solution.py:360
  122.3 13.4 %collective-permute-start.16 = (f32[72,512]{1,0:T(8,128)S(1)}, f32[72,512]{1,0:T(8,128)S(1)}, u32[]{:S(2)}, u32[]{:S(2)}) collective-permute-start(f32[72,512]{1,0:T(8,128)S(1)} %get-tuple-element.81), channel_id=1, source_target_pairs={{0,6},{1,7},{2,0},{3,1},{4,2},{5,3},{6,4},{7,5},{8,14},{9,15},{10,... | collective-permute-start | bytes 442376 | tf_op jit(solution)/shard_map/ppermute | solution.py:360
  125.4 9.4 %collective-permute-start.20 = (bf16[80,512]{1,0:T(8,128)(2,1)S(1)}, bf16[80,512]{1,0:T(8,128)(2,1)S(1)}, u32[]{:S(2)}, u32[]{:S(2)}) collective-permute-start(bf16[80,512]{1,0:T(8,128)(2,1)S(1)} %copy-done.24), channel_id=1, source_target_pairs={{0,16},{8,24},{32,48},{40,56},{64,80},{72,88},{96,112},{104,120},{... | collective-permute-start | bytes 245768 | tf_op jit(solution)/shard_map/ppermute | solution.py:400
  137.5 3.9 %collective-permute-start.25 = (f32[64,64]{1,0:T(8,128)S(1)}, f32[64,64]{1,0:T(8,128)S(1)}, u32[]{:S(2)}, u32[]{:S(2)}) collective-permute-start(f32[64,64]{1,0:T(8,128)S(1)} %add.404), channel_id=1, source_target_pairs={{0,6},{1,7},{2,0},{3,1},{4,2},{5,3},{6,4},{7,5},{8,14},{9,15},{10,... | collective-permute-start | bytes 49160 | tf_op jit(solution)/shard_map/ppermute | solution.py:360
  138.9 5.6 %collective-permute-start.24 = (f32[64,64]{1,0:T(8,128)S(1)}, f32[64,64]{1,0:T(8,128)S(1)}, u32[]{:S(2)}, u32[]{:S(2)}) collective-permute-start(f32[64,64]{1,0:T(8,128)S(1)} %add.404), channel_id=1, source_target_pairs={{0,4},{1,5},{2,6},{3,7},{4,0},{5,1},{6,2},{7,3},{8,12},{9,13},{10,... | collective-permute-start | bytes 49160 | tf_op jit(solution)/shard_map/ppermute | solution.py:360
  138.9 5.6 %collective-permute-start.23 = (f32[64,64]{1,0:T(8,128)S(1)}, f32[64,64]{1,0:T(8,128)S(1)}, u32[]{:S(2)}, u32[]{:S(2)}) collective-permute-start(f32[64,64]{1,0:T(8,128)S(1)} %add.404), channel_id=1, source_target_pairs={{0,2},{1,3},{2,4},{3,5},{4,6},{5,7},{6,0},{7,1},{8,10},{9,11},{10,... | collective-permute-start | bytes 49160 | tf_op jit(solution)/shard_map/ppermute | solution.py:360
  (30 other events, 225.5 us)

commit v15 on v12

--- a/solution.py
+++ b/solution.py
@@ -425,13 +425,10 @@
     sums, *parts = tie([sums, *parts], *returned[1:])
     returned += give_back(group3, parts)
 
-    layer, core = here_col // CORES, here_col % CORES
-    halves = sums.reshape(SIDE, CORES, ACC, BLOCK)
-    mine = lax.dynamic_index_in_dim(halves, core, 1, keepdims=False)
-    kept = mine + swap(lax.dynamic_index_in_dim(halves, 1 - core, 1, keepdims=False))
-    layers = [lax.dynamic_index_in_dim(kept, (layer - k) % SIDE, 0, keepdims=False) for k in range(SIDE)]
-    summed = layers[0] + (turn(layers[1], 3) + turn(layers[2], 2) + turn(layers[3], 1))
-    totals, degrees = summed[0:EIGS], summed[EIGS : EIGS + 1]
+    high = lax.reduce_precision(sums, 8, 7)
+    sent = jnp.concatenate([high, sums[:, EIGS:ACC] - high[:, EIGS:ACC]], axis=1).astype(jnp.bfloat16)
+    summed = jnp.sum(lax.all_to_all(sent, "col", 0, 0).astype(jnp.float32), axis=0)
+    totals, degrees = summed[0:EIGS], summed[EIGS : EIGS + 1] + summed[ACC : ACC + 1]
     for part in returned:
         part = part.astype(jnp.float32)
         totals, degrees = totals + part[0:EIGS], degrees + (part[EIGS : EIGS + 1] + part[ACC : ACC + 1])

time: 182 us -> 184 us (1.011)
  other arithmetic: 3.11 us -> 6.32 us
    ppermute x6 -> x3, starting transfers between devices: 9.27 us -> 3.61 us  [turn(): lax.ppermute(array, 'col', [(i, (i + by * CORES) % COLS) for i in range(C...]
    all_to_all x0 -> x1, starting transfers between devices: none -> 5.46 us  [per_device(): lax.all_to_all(sent, 'col', 0, 0).astype(jnp.float32)]
    another operation x0 -> x2, other arithmetic: none -> 2.4 us
    ppermute x6 -> x3, waiting for transfers between devices: 5.13 us -> 4.27 us  [turn(): lax.ppermute(array, 'col', [(i, (i + by * CORES) % COLS) for i in range(C...]
    unnamed x57 -> x53, local copies, waits for them, and re-layouts: 4.4 us -> 4.37 us
  transfers between devices with their start and end apart: 27 -> 24, of which waited for: 15 -> 14; matrix products, arithmetic and copies ran while one was open for 3% -> 3% of each run, Pallas kernels for 21% -> 21%
where the time goes in v15:
time: 184 us; the launch traced here: 183 us
  starting transfers between devices  52 us (28%)
  Pallas kernels  45.4 us (25%)
  waiting for transfers between devices  42.8 us (23%)
  blocking collectives  26.6 us (14%)
  local copies, waits for them, and re-layouts  8.89 us (5%)
  other arithmetic  6.32 us (3%)
    ppermute x9, waiting for transfers between devices, move(): return lax.ppermute(array, 'row', shift(dy, dx, keep))  34.2 us
    pallas_call x3, Pallas kernels, cells(): pl.pallas_call(functools.partial(cells_kernel, count), out_shape=[SUMS] +...  28.4 us
    all_to_all x1, blocking collectives, per_device(): gram = jnp.sum(lax.all_to_all(everyone, 'row', 0, 0), axis=0)  26.6 us
    ppermute x9, starting transfers between devices, give_back(): returned.append(lax.ppermute(part, 'row', back))  23.7 us
    ppermute x9, starting transfers between devices, move(): return lax.ppermute(array, 'row', shift(dy, dx, keep))  13.8 us
    pallas_call x1, Pallas kernels, own_cells(): pl.pallas_call(own_kernel, out_shape=[SUMS, NORM, ROW, TOKEN], grid_spec=...  9.38 us
    all_to_all x1, starting transfers between devices, per_device(): lax.all_to_all(sent, 'col', 0, 0).astype(jnp.float32)  5.46 us
    all_to_all x1, starting transfers between devices, per_device(): lax.all_to_all(jnp.broadcast_to(vectors, (COLS, EIGS, BLOCK)), 'col', 0, 0)  5.31 us
  transfers between devices with their start and end apart: 24, of which 14 were waited for; matrix products, arithmetic and copies ran while one was open for 3% of the time, Pallas kernels for 21%

profile of v15, /device:TPU:0, one launch (start us, length us, event | category | flops | bytes accessed | tf_op | source)
XLA Modules:
  0.0 182.7 jit_solution(9493446729277254307)
XLA Ops:
  0.0 2.6 %payload.1.far_ref = bf16[560,1024]{1,0:T(8,128)(2,1)} custom-call(s32[1]{0:T(128)} %bitcast.13.index_ref, bf16[8,512,1024]{2,1,0:T(8,128)(2,1)} %bitcast.23, bf16[64,512]{1,0:T(8,128)(2,1)} %v_ref.1), custom_call_target="tpu_custom_call" | custom-call | tf_op jit(solution)/shard_map/payload/pallas_call | solution.py:78
  2.6 5.3 %collective-permute-start.2 = (bf16[560,1024]{1,0:T(8,128)(2,1)}, bf16[560,1024]{1,0:T(8,128)(2,1)S(1)}, u32[]{:S(2)}, u32[]{:S(2)}) collective-permute-start(bf16[560,1024]{1,0:T(8,128)(2,1)} %payload.1.far_ref), channel_id=1, source_target_pairs={{0,120},{8,96},{16,104},{24,112},{32,24},{40,0},{48,8},{56,16},{64... | collective-permute-start | bytes 3440648 | tf_op jit(solution)/shard_map/ppermute | solution.py:357
  8.8 5.3 %all-to-all-start = ((bf16[8,64,512]{2,1,0:T(8,128)(2,1)}), bf16[8,64,512]{2,1,0:T(8,128)(2,1)S(1)}, u32[]{:S(2)}, u32[]{:S(2)}) async-start(bf16[8,64,512]{2,1,0:T(8,128)(2,1)} %broadcast_in_dim.8), calls=%async_computation | async-start | bytes 1048576 | tf_op jit(solution)/shard_map/all_to_all | solution.py:403
  15.9 9.4 %cells_own.1 = (f32[8,72,512]{2,1,0:T(8,128)}, f32[8,512,128]{2,1,0:T(8,128)}, f32[8,8,512]{2,1,0:T(8,128)}, f32[8,128]{1,0:T(8,128)}) custom-call(s32[8]{0:T(128)} %slice_reduce_fusion.flags_ref, bf16[8,512,1024]{2,1,0:T(8,128)(2,1)} %bitcast.24, bf16[560,1024]{1,0:T(8,128)(2,1)} %payload.1.far_ref), custom_call_target="tpu_custom_call" | custom-call | flops 2147483648 | bytes 13631488 | tf_op jit(solution)/shard_map/cells_own/pallas_call | solution.py:232
  25.3 7.4 %collective-permute-done.2.refs_2_ = bf16[560,1024]{1,0:T(8,128)(2,1)S(1)} collective-permute-done((bf16[560,1024]{1,0:T(8,128)(2,1)}, bf16[560,1024]{1,0:T(8,128)(2,1)S(1)}, u32[]{:S(2)}, u32[]{:S(2)}) %collective-permute-start.2) | collective-permute-done | bytes 1146912 | tf_op jit(solution)/shard_map/ppermute | solution.py:357
  32.8 3.3 %collective-permute-done.1.refs_1_ = bf16[560,1024]{1,0:T(8,128)(2,1)S(1)} collective-permute-done((bf16[560,1024]{1,0:T(8,128)(2,1)}, bf16[560,1024]{1,0:T(8,128)(2,1)S(1)}, u32[]{:S(2)}, u32[]{:S(2)}) %collective-permute-start.1) | collective-permute-done | bytes 1146912 | tf_op jit(solution)/shard_map/ppermute | solution.py:357
  38.0 3.1 %collective-permute-start.6 = (bf16[560,1024]{1,0:T(8,128)(2,1)}, bf16[560,1024]{1,0:T(8,128)(2,1)S(1)}, u32[]{:S(2)}, u32[]{:S(2)}) collective-permute-start(bf16[560,1024]{1,0:T(8,128)(2,1)} %get-tuple-element.44.refs_0_), channel_id=1, source_target_pairs={{0,8},{24,0},{32,40},{56,32},{64,72},{88,64},{96,104},{120,96},{1,... | collective-permute-start | bytes 3440648 | tf_op jit(solution)/shard_map/ppermute | solution.py:357
  41.1 3.3 %collective-permute-start.5 = (bf16[560,1024]{1,0:T(8,128)(2,1)}, bf16[560,1024]{1,0:T(8,128)(2,1)S(1)}, u32[]{:S(2)}, u32[]{:S(2)}) collective-permute-start(bf16[560,1024]{1,0:T(8,128)(2,1)} %get-tuple-element.44.refs_0_), channel_id=1, source_target_pairs={{0,96},{8,104},{16,112},{24,120},{32,0},{40,8},{48,16},{56,24},{64... | collective-permute-start | bytes 3440648 | tf_op jit(solution)/shard_map/ppermute | solution.py:357
  45.2 9.6 %cells.3 = (f32[8,72,512]{2,1,0:T(8,128)}, bf16[80,512]{1,0:T(8,128)(2,1)}, bf16[80,512]{1,0:T(8,128)(2,1)}, bf16[80,512]{1,0:T(8,128)(2,1)}, f32[8,128]{1,0:T(8,128)}) custom-call(s32[24]{0:T(128)} %reshape.209.flags_ref, bf16[8,512,1024]{2,1,0:T(8,128)(2,1)} %bitcast.25, bf16[8,64,512]{2,1,0:T(8,128)(2,1)} %copy-done, ...), custom_call_target="tpu_custom_call", output_to_operand_aliasing={{0}: (8, {})} | custom-call | flops 6442450944 | bytes 15728640 | tf_op jit(solution)/shard_map/cells/pallas_call | solution.py:271
  54.8 9.8 %collective-permute-done.3.refs_0_ = bf16[560,1024]{1,0:T(8,128)(2,1)} collective-permute-done((bf16[560,1024]{1,0:T(8,128)(2,1)}, bf16[560,1024]{1,0:T(8,128)(2,1)}, u32[]{:S(2)}, u32[]{:S(2)}) %collective-permute-start.3) | collective-permute-done | bytes 1146912 | tf_op jit(solution)/shard_map/ppermute | solution.py:357
  64.6 2.2 %collective-permute-done.6.refs_7_.refs_1_ = bf16[560,1024]{1,0:T(8,128)(2,1)S(1)} collective-permute-done((bf16[560,1024]{1,0:T(8,128)(2,1)}, bf16[560,1024]{1,0:T(8,128)(2,1)S(1)}, u32[]{:S(2)}, u32[]{:S(2)}) %collective-permute-start.6) | collective-permute-done | bytes 1146912 | tf_op jit(solution)/shard_map/ppermute | solution.py:357
  71.0 3.2 %collective-permute-start.9 = (bf16[80,512]{1,0:T(8,128)(2,1)}, bf16[80,512]{1,0:T(8,128)(2,1)S(1)}, u32[]{:S(2)}, u32[]{:S(2)}) collective-permute-start(bf16[80,512]{1,0:T(8,128)(2,1)} %get-tuple-element.60), channel_id=1, source_target_pairs={{8,0},{16,8},{24,16},{0,24},{40,32},{48,40},{56,48},{32,56},{72,64... | collective-permute-start | bytes 245768 | tf_op jit(solution)/shard_map/ppermute | solution.py:400
  74.2 9.9 %cells.4 = (f32[8,72,512]{2,1,0:T(8,128)}, bf16[80,512]{1,0:T(8,128)(2,1)}, bf16[80,512]{1,0:T(8,128)(2,1)}, bf16[80,512]{1,0:T(8,128)(2,1)}, f32[8,128]{1,0:T(8,128)}) custom-call(s32[24]{0:T(128)} %reshape.210.flags_ref, bf16[8,512,1024]{2,1,0:T(8,128)(2,1)} %bitcast.26, bf16[8,64,512]{2,1,0:T(8,128)(2,1)} %copy-done, ...), custom_call_target="tpu_custom_call", output_to_operand_aliasing={{0}: (8, {})} | custom-call | flops 6442450944 | bytes 15728640 | tf_op jit(solution)/shard_map/cells/pallas_call | solution.py:271
  84.1 10.2 %collective-permute-done.7.refs_0_ = bf16[560,1024]{1,0:T(8,128)(2,1)S(1)} collective-permute-done((bf16[560,1024]{1,0:T(8,128)(2,1)}, bf16[560,1024]{1,0:T(8,128)(2,1)S(1)}, u32[]{:S(2)}, u32[]{:S(2)}) %collective-permute-start.7) | collective-permute-done | bytes 1146912 | tf_op jit(solution)/shard_map/ppermute | solution.py:357
  96.0 2.9 %collective-permute-start.10 = (bf16[80,512]{1,0:T(8,128)(2,1)}, bf16[80,512]{1,0:T(8,128)(2,1)S(1)}, u32[]{:S(2)}, u32[]{:S(2)}) collective-permute-start(bf16[80,512]{1,0:T(8,128)(2,1)} %get-tuple-element.68), channel_id=1, source_target_pairs={{32,0},{40,8},{48,16},{56,24},{64,32},{72,40},{80,48},{88,56},{96,... | collective-permute-start | bytes 245768 | tf_op jit(solution)/shard_map/ppermute | solution.py:400
  98.9 2.8 %collective-permute-start.12 = (bf16[80,512]{1,0:T(8,128)(2,1)}, bf16[80,512]{1,0:T(8,128)(2,1)S(1)}, u32[]{:S(2)}, u32[]{:S(2)}) collective-permute-start(bf16[80,512]{1,0:T(8,128)(2,1)} %get-tuple-element.70), channel_id=1, source_target_pairs={{104,0},{112,8},{120,16},{96,24},{8,32},{16,40},{24,48},{0,56},{40... | collective-permute-start | bytes 245768 | tf_op jit(solution)/shard_map/ppermute | solution.py:400
  103.0 5.2 %collective-permute-start.14 = (bf16[80,512]{1,0:T(8,128)(2,1)}, bf16[80,512]{1,0:T(8,128)(2,1)S(1)}, u32[]{:S(2)}, u32[]{:S(2)}) collective-permute-start(bf16[80,512]{1,0:T(8,128)(2,1)} %get-tuple-element.72), channel_id=1, source_target_pairs={{0,64},{8,72},{16,80},{24,88},{32,96},{40,104},{48,112},{56,120},{... | collective-permute-start | bytes 245768 | tf_op jit(solution)/shard_map/ppermute | solution.py:400
  108.2 8.9 %cells.5 = (f32[8,72,512]{2,1,0:T(8,128)}, bf16[80,512]{1,0:T(8,128)(2,1)}, bf16[80,512]{1,0:T(8,128)(2,1)}, bf16[80,512]{1,0:T(8,128)(2,1)}, f32[8,128]{1,0:T(8,128)}) custom-call(s32[24]{0:T(128)} %reshape.207.flags_ref, bf16[8,512,1024]{2,1,0:T(8,128)(2,1)} %bitcast.27, bf16[8,64,512]{2,1,0:T(8,128)(2,1)} %copy-done, ...), custom_call_target="tpu_custom_call", output_to_operand_aliasing={{0}: (8, {})} | custom-call | flops 6442450944 | bytes 15728640 | tf_op jit(solution)/shard_map/cells/pallas_call | solution.py:271
  121.2 5.5 %all-to-all-start.1 = ((bf16[8,80,512]{2,1,0:T(8,128)(2,1)}), bf16[8,80,512]{2,1,0:T(8,128)(2,1)S(1)}, u32[]{:S(2)}, u32[]{:S(2)}) async-start(bf16[8,80,512]{2,1,0:T(8,128)(2,1)} %pad_maximum_fusion), calls=%async_computation.1 | async-start | bytes 1310720 | tf_op jit(solution)/shard_map/all_to_all | solution.py:430
  126.8 6.2 %collective-permute-start.16 = (bf16[80,512]{1,0:T(8,128)(2,1)S(1)}, bf16[80,512]{1,0:T(8,128)(2,1)S(1)}, u32[]{:S(2)}, u32[]{:S(2)}) collective-permute-start(bf16[80,512]{1,0:T(8,128)(2,1)S(1)} %copy-done.22), channel_id=1, source_target_pairs={{0,16},{8,24},{32,48},{40,56},{64,80},{72,88},{96,112},{104,120},{... | collective-permute-start | bytes 245768 | tf_op jit(solution)/shard_map/ppermute | solution.py:400
  133.0 2.1 %collective-permute-start.17 = (bf16[80,512]{1,0:T(8,128)(2,1)S(1)}, bf16[80,512]{1,0:T(8,128)(2,1)S(1)}, u32[]{:S(2)}, u32[]{:S(2)}) collective-permute-start(bf16[80,512]{1,0:T(8,128)(2,1)S(1)} %copy-done.23), channel_id=1, source_target_pairs={{16,64},{24,72},{0,80},{8,88},{48,96},{56,104},{32,112},{40,120},{... | collective-permute-start | bytes 245768 | tf_op jit(solution)/shard_map/ppermute | solution.py:400
  144.1 3.4 %collective-permute-done.20 = f32[64,64]{1,0:T(8,128)S(1)} collective-permute-done((f32[64,64]{1,0:T(8,128)S(1)}, f32[64,64]{1,0:T(8,128)S(1)}, u32[]{:S(2)}, u32[]{:S(2)}) %collective-permute-start.20) | collective-permute-done | bytes 16416 | tf_op jit(solution)/shard_map/ppermute | solution.py:360
  148.5 26.6 %all_to_all.15 = f32[16,1,4096]{2,1,0:T(1,128)S(1)} all-to-all(f32[16,1,4096]{2,1,0:T(1,128)S(1)} %reshape.214), channel_id=1, replica_groups=mesh['row'=16,'col'=8] {'row'}, dimensions={0} | all-to-all | bytes 524288 | tf_op jit(solution)/shard_map/all_to_all | solution.py:442
  177.8 5.0 %solve.1 = f32[64,512]{1,0:T(8,128)} custom-call(f32[64,64]{1,0:T(8,128)} %reduce_sum.19.gram_ref, f32[64,512]{1,0:T(8,128)} %copy-done.1), custom_call_target="tpu_custom_call" | custom-call | tf_op jit(solution)/shard_map/solve/pallas_call | solution.py:341
  (137 shorter events, 29.0 us)
Async XLA Ops:
  2.6 30.1 %collective-permute-start.2 = (bf16[560,1024]{1,0:T(8,128)(2,1)}, bf16[560,1024]{1,0:T(8,128)(2,1)S(1)}, u32[]{:S(2)}, u32[]{:S(2)}) collective-permute-start(bf16[560,1024]{1,0:T(8,128)(2,1)} %payload.1.far_ref), channel_id=1, source_target_pairs={{0,120},{8,96},{16,104},{24,112},{32,24},{40,0},{48,8},{56,16},{64... | collective-permute-start | bytes 3440648 | tf_op jit(solution)/shard_map/ppermute | solution.py:357
  7.9 28.1 %collective-permute-start.1 = (bf16[560,1024]{1,0:T(8,128)(2,1)}, bf16[560,1024]{1,0:T(8,128)(2,1)S(1)}, u32[]{:S(2)}, u32[]{:S(2)}) collective-permute-start(bf16[560,1024]{1,0:T(8,128)(2,1)} %payload.1.far_ref), channel_id=1, source_target_pairs={{0,32},{8,40},{16,48},{24,56},{32,64},{40,72},{48,80},{56,88},{64,... | collective-permute-start | bytes 3440648 | tf_op jit(solution)/shard_map/ppermute | solution.py:357
  7.9 28.3 %collective-permute-start = (bf16[560,1024]{1,0:T(8,128)(2,1)}, bf16[560,1024]{1,0:T(8,128)(2,1)}, u32[]{:S(2)}, u32[]{:S(2)}) collective-permute-start(bf16[560,1024]{1,0:T(8,128)(2,1)} %payload.1.far_ref), channel_id=1, source_target_pairs={{0,8},{8,16},{16,24},{24,0},{32,40},{40,48},{48,56},{56,32},{64,72... | collective-permute-start | bytes 3440648 | tf_op jit(solution)/shard_map/ppermute | solution.py:357
  8.8 16.5 %all-to-all-start = ((bf16[8,64,512]{2,1,0:T(8,128)(2,1)}), bf16[8,64,512]{2,1,0:T(8,128)(2,1)S(1)}, u32[]{:S(2)}, u32[]{:S(2)}) async-start(bf16[8,64,512]{2,1,0:T(8,128)(2,1)} %broadcast_in_dim.8), calls=%async_computation | async-start | bytes 1048576 | tf_op jit(solution)/shard_map/all_to_all | solution.py:403
  37.2 27.4 %collective-permute-start.3 = (bf16[560,1024]{1,0:T(8,128)(2,1)}, bf16[560,1024]{1,0:T(8,128)(2,1)}, u32[]{:S(2)}, u32[]{:S(2)}) collective-permute-start(bf16[560,1024]{1,0:T(8,128)(2,1)} %get-tuple-element.42.refs_1_), channel_id=1, source_target_pairs={{0,32},{8,40},{16,48},{24,56},{32,64},{40,72},{48,80},{56,88},{64,... | collective-permute-start | bytes 3440648 | tf_op jit(solution)/shard_map/ppermute | solution.py:357
  37.2 27.4 %collective-permute-start.4 = (bf16[560,1024]{1,0:T(8,128)(2,1)}, bf16[560,1024]{1,0:T(8,128)(2,1)}, u32[]{:S(2)}, u32[]{:S(2)}) collective-permute-start(bf16[560,1024]{1,0:T(8,128)(2,1)} %get-tuple-element.43.refs_2_), channel_id=1, source_target_pairs={{0,24},{8,0},{16,8},{24,16},{32,56},{40,32},{48,40},{56,48},{64,88... | collective-permute-start | bytes 3440648 | tf_op jit(solution)/shard_map/ppermute | solution.py:357
  38.0 28.8 %collective-permute-start.6 = (bf16[560,1024]{1,0:T(8,128)(2,1)}, bf16[560,1024]{1,0:T(8,128)(2,1)S(1)}, u32[]{:S(2)}, u32[]{:S(2)}) collective-permute-start(bf16[560,1024]{1,0:T(8,128)(2,1)} %get-tuple-element.44.refs_0_), channel_id=1, source_target_pairs={{0,8},{24,0},{32,40},{56,32},{64,72},{88,64},{96,104},{120,96},{1,... | collective-permute-start | bytes 3440648 | tf_op jit(solution)/shard_map/ppermute | solution.py:357
  41.1 26.2 %collective-permute-start.5 = (bf16[560,1024]{1,0:T(8,128)(2,1)}, bf16[560,1024]{1,0:T(8,128)(2,1)S(1)}, u32[]{:S(2)}, u32[]{:S(2)}) collective-permute-start(bf16[560,1024]{1,0:T(8,128)(2,1)} %get-tuple-element.44.refs_0_), channel_id=1, source_target_pairs={{0,96},{8,104},{16,112},{24,120},{32,0},{40,8},{48,16},{56,24},{64... | collective-permute-start | bytes 3440648 | tf_op jit(solution)/shard_map/ppermute | solution.py:357
  68.3 26.0 %collective-permute-start.7 = (bf16[560,1024]{1,0:T(8,128)(2,1)}, bf16[560,1024]{1,0:T(8,128)(2,1)S(1)}, u32[]{:S(2)}, u32[]{:S(2)}) collective-permute-start(bf16[560,1024]{1,0:T(8,128)(2,1)} %get-tuple-element.52.refs_2_), channel_id=1, source_target_pairs={{0,8},{8,16},{16,24},{24,0},{32,40},{40,48},{48,56},{56,32},{64,72... | collective-permute-start | bytes 3440648 | tf_op jit(solution)/shard_map/ppermute | solution.py:357
  68.3 26.7 %collective-permute-start.8 = (bf16[560,1024]{1,0:T(8,128)(2,1)}, bf16[560,1024]{1,0:T(8,128)(2,1)S(1)}, u32[]{:S(2)}, u32[]{:S(2)}) collective-permute-start(bf16[560,1024]{1,0:T(8,128)(2,1)} %get-tuple-element.53.refs_1_), channel_id=1, source_target_pairs={{32,0},{40,8},{48,16},{56,24},{64,32},{72,40},{80,48},{88,56},{33,... | collective-permute-start | bytes 3440648 | tf_op jit(solution)/shard_map/ppermute | solution.py:357
  71.0 13.1 %collective-permute-start.9 = (bf16[80,512]{1,0:T(8,128)(2,1)}, bf16[80,512]{1,0:T(8,128)(2,1)S(1)}, u32[]{:S(2)}, u32[]{:S(2)}) collective-permute-start(bf16[80,512]{1,0:T(8,128)(2,1)} %get-tuple-element.60), channel_id=1, source_target_pairs={{8,0},{16,8},{24,16},{0,24},{40,32},{48,40},{56,48},{32,56},{72,64... | collective-permute-start | bytes 245768 | tf_op jit(solution)/shard_map/ppermute | solution.py:400
  96.0 21.1 %collective-permute-start.10 = (bf16[80,512]{1,0:T(8,128)(2,1)}, bf16[80,512]{1,0:T(8,128)(2,1)S(1)}, u32[]{:S(2)}, u32[]{:S(2)}) collective-permute-start(bf16[80,512]{1,0:T(8,128)(2,1)} %get-tuple-element.68), channel_id=1, source_target_pairs={{32,0},{40,8},{48,16},{56,24},{64,32},{72,40},{80,48},{88,56},{96,... | collective-permute-start | bytes 245768 | tf_op jit(solution)/shard_map/ppermute | solution.py:400
  98.9 18.2 %collective-permute-start.11 = (bf16[80,512]{1,0:T(8,128)(2,1)}, bf16[80,512]{1,0:T(8,128)(2,1)S(1)}, u32[]{:S(2)}, u32[]{:S(2)}) collective-permute-start(bf16[80,512]{1,0:T(8,128)(2,1)} %get-tuple-element.69), channel_id=1, source_target_pairs={{120,0},{96,8},{104,16},{112,24},{24,32},{0,40},{8,48},{16,56},{56... | collective-permute-start | bytes 245768 | tf_op jit(solution)/shard_map/ppermute | solution.py:400
  98.9 18.2 %collective-permute-start.12 = (bf16[80,512]{1,0:T(8,128)(2,1)}, bf16[80,512]{1,0:T(8,128)(2,1)S(1)}, u32[]{:S(2)}, u32[]{:S(2)}) collective-permute-start(bf16[80,512]{1,0:T(8,128)(2,1)} %get-tuple-element.70), channel_id=1, source_target_pairs={{104,0},{112,8},{120,16},{96,24},{8,32},{16,40},{24,48},{0,56},{40... | collective-permute-start | bytes 245768 | tf_op jit(solution)/shard_map/ppermute | solution.py:400
  101.8 15.4 %collective-permute-start.13 = (bf16[80,512]{1,0:T(8,128)(2,1)}, bf16[80,512]{1,0:T(8,128)(2,1)S(1)}, u32[]{:S(2)}, u32[]{:S(2)}) collective-permute-start(bf16[80,512]{1,0:T(8,128)(2,1)} %get-tuple-element.71), channel_id=1, source_target_pairs={{112,0},{120,8},{96,16},{104,24},{16,32},{24,40},{0,48},{8,56},{48... | collective-permute-start | bytes 245768 | tf_op jit(solution)/shard_map/ppermute | solution.py:400
  103.0 14.2 %collective-permute-start.14 = (bf16[80,512]{1,0:T(8,128)(2,1)}, bf16[80,512]{1,0:T(8,128)(2,1)S(1)}, u32[]{:S(2)}, u32[]{:S(2)}) collective-permute-start(bf16[80,512]{1,0:T(8,128)(2,1)} %get-tuple-element.72), channel_id=1, source_target_pairs={{0,64},{8,72},{16,80},{24,88},{32,96},{40,104},{48,112},{56,120},{... | collective-permute-start | bytes 245768 | tf_op jit(solution)/shard_map/ppermute | solution.py:400
  121.2 17.2 %all-to-all-start.1 = ((bf16[8,80,512]{2,1,0:T(8,128)(2,1)}), bf16[8,80,512]{2,1,0:T(8,128)(2,1)S(1)}, u32[]{:S(2)}, u32[]{:S(2)}) async-start(bf16[8,80,512]{2,1,0:T(8,128)(2,1)} %pad_maximum_fusion), calls=%async_computation.1 | async-start | bytes 1310720 | tf_op jit(solution)/shard_map/all_to_all | solution.py:430
  126.7 8.6 %collective-permute-start.15 = (bf16[80,512]{1,0:T(8,128)(2,1)S(1)}, bf16[80,512]{1,0:T(8,128)(2,1)S(1)}, u32[]{:S(2)}, u32[]{:S(2)}) collective-permute-start(bf16[80,512]{1,0:T(8,128)(2,1)S(1)} %copy-done.21), channel_id=1, source_target_pairs={{72,0},{80,8},{88,16},{64,24},{104,32},{112,40},{120,48},{96,56},{... | collective-permute-start | bytes 245768 | tf_op jit(solution)/shard_map/ppermute | solution.py:400
  126.8 8.5 %collective-permute-start.16 = (bf16[80,512]{1,0:T(8,128)(2,1)S(1)}, bf16[80,512]{1,0:T(8,128)(2,1)S(1)}, u32[]{:S(2)}, u32[]{:S(2)}) collective-permute-start(bf16[80,512]{1,0:T(8,128)(2,1)S(1)} %copy-done.22), channel_id=1, source_target_pairs={{0,16},{8,24},{32,48},{40,56},{64,80},{72,88},{96,112},{104,120},{... | collective-permute-start | bytes 245768 | tf_op jit(solution)/shard_map/ppermute | solution.py:400
  133.0 4.2 %collective-permute-start.17 = (bf16[80,512]{1,0:T(8,128)(2,1)S(1)}, bf16[80,512]{1,0:T(8,128)(2,1)S(1)}, u32[]{:S(2)}, u32[]{:S(2)}) collective-permute-start(bf16[80,512]{1,0:T(8,128)(2,1)S(1)} %copy-done.23), channel_id=1, source_target_pairs={{16,64},{24,72},{0,80},{8,88},{48,96},{56,104},{32,112},{40,120},{... | collective-permute-start | bytes 245768 | tf_op jit(solution)/shard_map/ppermute | solution.py:400
  138.9 1.3 collective-permute-start.18
  140.2 3.9 %collective-permute-start.21 = (f32[64,64]{1,0:T(8,128)S(1)}, f32[64,64]{1,0:T(8,128)S(1)}, u32[]{:S(2)}, u32[]{:S(2)}) collective-permute-start(f32[64,64]{1,0:T(8,128)S(1)} %add.341), channel_id=1, source_target_pairs={{0,6},{1,7},{2,0},{3,1},{4,2},{5,3},{6,4},{7,5},{8,14},{9,15},{10,... | collective-permute-start | bytes 49160 | tf_op jit(solution)/shard_map/ppermute | solution.py:360
  142.1 5.4 %collective-permute-start.20 = (f32[64,64]{1,0:T(8,128)S(1)}, f32[64,64]{1,0:T(8,128)S(1)}, u32[]{:S(2)}, u32[]{:S(2)}) collective-permute-start(f32[64,64]{1,0:T(8,128)S(1)} %add.341), channel_id=1, source_target_pairs={{0,4},{1,5},{2,6},{3,7},{4,0},{5,1},{6,2},{7,3},{8,12},{9,13},{10,... | collective-permute-start | bytes 49160 | tf_op jit(solution)/shard_map/ppermute | solution.py:360
  143.0 5.1 %collective-permute-start.19 = (f32[64,64]{1,0:T(8,128)S(1)}, f32[64,64]{1,0:T(8,128)S(1)}, u32[]{:S(2)}, u32[]{:S(2)}) collective-permute-start(f32[64,64]{1,0:T(8,128)S(1)} %add.341), channel_id=1, source_target_pairs={{0,2},{1,3},{2,4},{3,5},{4,6},{5,7},{6,0},{7,1},{8,10},{9,11},{10,... | collective-permute-start | bytes 49160 | tf_op jit(solution)/shard_map/ppermute | solution.py:360
  (25 other events, 200.9 us)

commit v16 on v12

--- a/solution.py
+++ b/solution.py
@@ -411,7 +411,7 @@
     group1, group2, group3 = ("a", "b", "c"), ("d", "e", "h"), ("f", "g", "k")
     sums, parts, token = work(group1, sums)
 
-    far["h"], far["e"], *parts = tie([far["h"], far["e"], *parts], token, far["d"], far["g"])
+    far["h"], far["e"], *parts = tie([far["h"], far["e"], *parts], token, far["g"])
     far["f"] = move(far["h"], 0, 1)
     far["k"] = move(far["e"], -1, 0, top_half)
     returned = give_back(("a",), parts[0:1])

time: 182 us -> 181 us (level)
  blocking collectives: 27.3 us -> 23.6 us
  starting transfers between devices: 50.8 us -> 53.1 us
    all_to_all x1, blocking collectives: 27.3 us -> 23.6 us  [per_device(): gram = jnp.sum(lax.all_to_all(everyone, 'row', 0, 0), axis=0)]
  transfers between devices with their start and end apart: 27 -> 27, of which waited for: 15 -> 14; matrix products, arithmetic and copies ran while one was open for 3% -> 3% of each run, Pallas kernels for 21% -> 22%
where the time goes in v16:
time: 181 us; the launch traced here: 180 us
  starting transfers between devices  53.1 us (29%)
  Pallas kernels  46.6 us (26%)
  waiting for transfers between devices  42.4 us (23%)
  blocking collectives  23.6 us (13%)
  local copies, waits for them, and re-layouts  10.2 us (6%)
  other arithmetic  3.11 us (2%)
    ppermute x9, waiting for transfers between devices, move(): return lax.ppermute(array, 'row', shift(dy, dx, keep))  32.7 us
    pallas_call x3, Pallas kernels, cells(): pl.pallas_call(functools.partial(cells_kernel, count), out_shape=[SUMS] +...  29.6 us
    ppermute x9, starting transfers between devices, give_back(): returned.append(lax.ppermute(part, 'row', back))  23.9 us
    all_to_all x1, blocking collectives, per_device(): gram = jnp.sum(lax.all_to_all(everyone, 'row', 0, 0), axis=0)  23.6 us
    ppermute x9, starting transfers between devices, move(): return lax.ppermute(array, 'row', shift(dy, dx, keep))  13.8 us
    ppermute x6, starting transfers between devices, turn(): lax.ppermute(array, 'col', [(i, (i + by * CORES) % COLS) for i in range(C...  9.93 us
    pallas_call x1, Pallas kernels, own_cells(): pl.pallas_call(own_kernel, out_shape=[SUMS, NORM, ROW, TOKEN], grid_spec=...  9.4 us
    all_to_all x1, starting transfers between devices, per_device(): lax.all_to_all(jnp.broadcast_to(vectors, (COLS, EIGS, BLOCK)), 'col', 0, 0)  5.31 us
  transfers between devices with their start and end apart: 27, of which 14 were waited for; matrix products, arithmetic and copies ran while one was open for 3% of the time, Pallas kernels for 22%

profile of v16, /device:TPU:0, one launch (start us, length us, event | category | flops | bytes accessed | tf_op | source)
XLA Modules:
  0.0 179.9 jit_solution(348385387895044391)
XLA Ops:
  0.0 2.6 %payload.1.far_ref = bf16[560,1024]{1,0:T(8,128)(2,1)} custom-call(s32[1]{0:T(128)} %bitcast.13.index_ref, bf16[8,512,1024]{2,1,0:T(8,128)(2,1)} %bitcast.36, bf16[64,512]{1,0:T(8,128)(2,1)} %v_ref.1), custom_call_target="tpu_custom_call" | custom-call | tf_op jit(solution)/shard_map/payload/pallas_call | solution.py:78
  2.6 5.3 %collective-permute-start.2 = (bf16[560,1024]{1,0:T(8,128)(2,1)}, bf16[560,1024]{1,0:T(8,128)(2,1)S(1)}, u32[]{:S(2)}, u32[]{:S(2)}) collective-permute-start(bf16[560,1024]{1,0:T(8,128)(2,1)} %payload.1.far_ref), channel_id=1, source_target_pairs={{0,120},{8,96},{16,104},{24,112},{32,24},{40,0},{48,8},{56,16},{64... | collective-permute-start | bytes 3440648 | tf_op jit(solution)/shard_map/ppermute | solution.py:357
  8.8 5.3 %all-to-all-start = ((bf16[8,64,512]{2,1,0:T(8,128)(2,1)}), bf16[8,64,512]{2,1,0:T(8,128)(2,1)S(1)}, u32[]{:S(2)}, u32[]{:S(2)}) async-start(bf16[8,64,512]{2,1,0:T(8,128)(2,1)} %broadcast_in_dim.8), calls=%async_computation | async-start | bytes 1048576 | tf_op jit(solution)/shard_map/all_to_all | solution.py:403
  15.9 9.4 %cells_own.1 = (f32[8,72,512]{2,1,0:T(8,128)}, f32[8,512,128]{2,1,0:T(8,128)}, f32[8,8,512]{2,1,0:T(8,128)}, f32[8,128]{1,0:T(8,128)}) custom-call(s32[8]{0:T(128)} %slice_reduce_fusion.flags_ref, bf16[8,512,1024]{2,1,0:T(8,128)(2,1)} %bitcast.37, bf16[560,1024]{1,0:T(8,128)(2,1)} %payload.1.far_ref), custom_call_target="tpu_custom_call" | custom-call | flops 2147483648 | bytes 13631488 | tf_op jit(solution)/shard_map/cells_own/pallas_call | solution.py:232
  25.3 7.4 %collective-permute-done.2.refs_2_ = bf16[560,1024]{1,0:T(8,128)(2,1)S(1)} collective-permute-done((bf16[560,1024]{1,0:T(8,128)(2,1)}, bf16[560,1024]{1,0:T(8,128)(2,1)S(1)}, u32[]{:S(2)}, u32[]{:S(2)}) %collective-permute-start.2) | collective-permute-done | bytes 1146912 | tf_op jit(solution)/shard_map/ppermute | solution.py:357
  32.8 3.3 %collective-permute-done.1.refs_1_ = bf16[560,1024]{1,0:T(8,128)(2,1)S(1)} collective-permute-done((bf16[560,1024]{1,0:T(8,128)(2,1)}, bf16[560,1024]{1,0:T(8,128)(2,1)S(1)}, u32[]{:S(2)}, u32[]{:S(2)}) %collective-permute-start.1) | collective-permute-done | bytes 1146912 | tf_op jit(solution)/shard_map/ppermute | solution.py:357
  38.0 3.1 %collective-permute-start.5 = (bf16[560,1024]{1,0:T(8,128)(2,1)}, bf16[560,1024]{1,0:T(8,128)(2,1)S(1)}, u32[]{:S(2)}, u32[]{:S(2)}) collective-permute-start(bf16[560,1024]{1,0:T(8,128)(2,1)} %get-tuple-element.44.refs_0_), channel_id=1, source_target_pairs={{0,8},{24,0},{32,40},{56,32},{64,72},{88,64},{96,104},{120,96},{1,... | collective-permute-start | bytes 3440648 | tf_op jit(solution)/shard_map/ppermute | solution.py:357
  41.9 3.2 %collective-permute-start.8 = (bf16[560,1024]{1,0:T(8,128)(2,1)}, bf16[560,1024]{1,0:T(8,128)(2,1)}, u32[]{:S(2)}, u32[]{:S(2)}) collective-permute-start(bf16[560,1024]{1,0:T(8,128)(2,1)} %get-tuple-element.44.refs_0_), channel_id=1, source_target_pairs={{0,96},{8,104},{16,112},{24,120},{32,0},{40,8},{48,16},{56,24},{64... | collective-permute-start | bytes 3440648 | tf_op jit(solution)/shard_map/ppermute | solution.py:357
  45.1 10.7 %cells.3 = (f32[8,72,512]{2,1,0:T(8,128)}, bf16[80,512]{1,0:T(8,128)(2,1)}, bf16[80,512]{1,0:T(8,128)(2,1)}, bf16[80,512]{1,0:T(8,128)(2,1)}, f32[8,128]{1,0:T(8,128)}) custom-call(s32[24]{0:T(128)} %reshape.212.flags_ref, bf16[8,512,1024]{2,1,0:T(8,128)(2,1)} %bitcast.38, bf16[8,64,512]{2,1,0:T(8,128)(2,1)} %copy-done.1, ...), custom_call_target="tpu_custom_call", output_to_operand_aliasing={{0}: (8, {})} | custom-call | flops 6442450944 | bytes 15728640 | tf_op jit(solution)/shard_map/cells/pallas_call | solution.py:271
  55.7 8.7 %collective-permute-done.3.refs_0_ = bf16[560,1024]{1,0:T(8,128)(2,1)S(1)} collective-permute-done((bf16[560,1024]{1,0:T(8,128)(2,1)}, bf16[560,1024]{1,0:T(8,128)(2,1)S(1)}, u32[]{:S(2)}, u32[]{:S(2)}) %collective-permute-start.3) | collective-permute-done | bytes 1146912 | tf_op jit(solution)/shard_map/ppermute | solution.py:357
  64.5 2.3 %collective-permute-done.5.refs_6_.refs_1_ = bf16[560,1024]{1,0:T(8,128)(2,1)S(1)} collective-permute-done((bf16[560,1024]{1,0:T(8,128)(2,1)}, bf16[560,1024]{1,0:T(8,128)(2,1)S(1)}, u32[]{:S(2)}, u32[]{:S(2)}) %collective-permute-start.5) | collective-permute-done | bytes 1146912 | tf_op jit(solution)/shard_map/ppermute | solution.py:357
  70.6 3.1 %collective-permute-start.9 = (bf16[80,512]{1,0:T(8,128)(2,1)}, bf16[80,512]{1,0:T(8,128)(2,1)S(1)}, u32[]{:S(2)}, u32[]{:S(2)}) collective-permute-start(bf16[80,512]{1,0:T(8,128)(2,1)} %get-tuple-element.60), channel_id=1, source_target_pairs={{8,0},{16,8},{24,16},{0,24},{40,32},{48,40},{56,48},{32,56},{72,64... | collective-permute-start | bytes 245768 | tf_op jit(solution)/shard_map/ppermute | solution.py:400
  73.8 9.9 %cells.4 = (f32[8,72,512]{2,1,0:T(8,128)}, bf16[80,512]{1,0:T(8,128)(2,1)}, bf16[80,512]{1,0:T(8,128)(2,1)}, bf16[80,512]{1,0:T(8,128)(2,1)}, f32[8,128]{1,0:T(8,128)}) custom-call(s32[24]{0:T(128)} %reshape.213.flags_ref, bf16[8,512,1024]{2,1,0:T(8,128)(2,1)} %bitcast.39, bf16[8,64,512]{2,1,0:T(8,128)(2,1)} %copy-done.1, ...), custom_call_target="tpu_custom_call", output_to_operand_aliasing={{0}: (8, {})} | custom-call | flops 6442450944 | bytes 15728640 | tf_op jit(solution)/shard_map/cells/pallas_call | solution.py:271
  83.7 10.1 %collective-permute-done.6.refs_0_ = bf16[560,1024]{1,0:T(8,128)(2,1)S(1)} collective-permute-done((bf16[560,1024]{1,0:T(8,128)(2,1)}, bf16[560,1024]{1,0:T(8,128)(2,1)S(1)}, u32[]{:S(2)}, u32[]{:S(2)}) %collective-permute-start.6) | collective-permute-done | bytes 1146912 | tf_op jit(solution)/shard_map/ppermute | solution.py:357
  95.7 4.9 %collective-permute-start.10 = (bf16[80,512]{1,0:T(8,128)(2,1)}, bf16[80,512]{1,0:T(8,128)(2,1)S(1)}, u32[]{:S(2)}, u32[]{:S(2)}) collective-permute-start(bf16[80,512]{1,0:T(8,128)(2,1)} %get-tuple-element.68), channel_id=1, source_target_pairs={{32,0},{40,8},{48,16},{56,24},{64,32},{72,40},{80,48},{88,56},{96,... | collective-permute-start | bytes 245768 | tf_op jit(solution)/shard_map/ppermute | solution.py:400
  100.6 2.4 %collective-permute-start.12 = (bf16[80,512]{1,0:T(8,128)(2,1)}, bf16[80,512]{1,0:T(8,128)(2,1)S(1)}, u32[]{:S(2)}, u32[]{:S(2)}) collective-permute-start(bf16[80,512]{1,0:T(8,128)(2,1)} %get-tuple-element.70), channel_id=1, source_target_pairs={{104,0},{112,8},{120,16},{96,24},{8,32},{16,40},{24,48},{0,56},{40... | collective-permute-start | bytes 245768 | tf_op jit(solution)/shard_map/ppermute | solution.py:400
  102.9 6.3 %collective-permute-start.14 = (bf16[80,512]{1,0:T(8,128)(2,1)}, bf16[80,512]{1,0:T(8,128)(2,1)S(1)}, u32[]{:S(2)}, u32[]{:S(2)}) collective-permute-start(bf16[80,512]{1,0:T(8,128)(2,1)} %get-tuple-element.72), channel_id=1, source_target_pairs={{0,64},{8,72},{16,80},{24,88},{32,96},{40,104},{48,112},{56,120},{... | collective-permute-start | bytes 245768 | tf_op jit(solution)/shard_map/ppermute | solution.py:400
  109.3 9.0 %cells.5 = (f32[8,72,512]{2,1,0:T(8,128)}, bf16[80,512]{1,0:T(8,128)(2,1)}, bf16[80,512]{1,0:T(8,128)(2,1)}, bf16[80,512]{1,0:T(8,128)(2,1)}, f32[8,128]{1,0:T(8,128)}) custom-call(s32[24]{0:T(128)} %reshape.210.flags_ref, bf16[8,512,1024]{2,1,0:T(8,128)(2,1)} %bitcast.40, bf16[8,64,512]{2,1,0:T(8,128)(2,1)} %copy-done.1, ...), custom_call_target="tpu_custom_call", output_to_operand_aliasing={{0}: (8, {})} | custom-call | flops 6442450944 | bytes 15728640 | tf_op jit(solution)/shard_map/cells/pallas_call | solution.py:271
  122.5 3.1 %collective-permute-start.17 = (f32[72,512]{1,0:T(8,128)S(1)}, f32[72,512]{1,0:T(8,128)S(1)}, u32[]{:S(2)}, u32[]{:S(2)}) collective-permute-start(f32[72,512]{1,0:T(8,128)S(1)} %get-tuple-element.77), channel_id=1, source_target_pairs={{0,4},{1,5},{2,6},{3,7},{4,0},{5,1},{6,2},{7,3},{8,12},{9,13},{10,... | collective-permute-start | bytes 442376 | tf_op jit(solution)/shard_map/ppermute | solution.py:360
  128.9 4.9 %collective-permute-start.20 = (bf16[80,512]{1,0:T(8,128)(2,1)S(1)}, bf16[80,512]{1,0:T(8,128)(2,1)S(1)}, u32[]{:S(2)}, u32[]{:S(2)}) collective-permute-start(bf16[80,512]{1,0:T(8,128)(2,1)S(1)} %copy-done.24), channel_id=1, source_target_pairs={{0,16},{8,24},{32,48},{40,56},{64,80},{72,88},{96,112},{104,120},{... | collective-permute-start | bytes 245768 | tf_op jit(solution)/shard_map/ppermute | solution.py:400
  140.5 2.6 %collective-permute-start.24 = (f32[64,64]{1,0:T(8,128)S(1)}, f32[64,64]{1,0:T(8,128)S(1)}, u32[]{:S(2)}, u32[]{:S(2)}) collective-permute-start(f32[64,64]{1,0:T(8,128)S(1)} %add.404), channel_id=1, source_target_pairs={{0,4},{1,5},{2,6},{3,7},{4,0},{5,1},{6,2},{7,3},{8,12},{9,13},{10,... | collective-permute-start | bytes 49160 | tf_op jit(solution)/shard_map/ppermute | solution.py:360
  145.9 2.3 %collective-permute-done.23 = f32[64,64]{1,0:T(8,128)S(1)} collective-permute-done((f32[64,64]{1,0:T(8,128)S(1)}, f32[64,64]{1,0:T(8,128)S(1)}, u32[]{:S(2)}, u32[]{:S(2)}) %collective-permute-start.23) | collective-permute-done | bytes 16416 | tf_op jit(solution)/shard_map/ppermute | solution.py:360
  148.6 23.6 %all_to_all.10 = f32[16,1,4096]{2,1,0:T(1,128)S(1)} all-to-all(f32[16,1,4096]{2,1,0:T(1,128)S(1)} %reshape.218), channel_id=1, replica_groups=mesh['row'=16,'col'=8] {'row'}, dimensions={0} | all-to-all | bytes 524288 | tf_op jit(solution)/shard_map/all_to_all | solution.py:445
  174.9 5.0 %solve.1 = f32[64,512]{1,0:T(8,128)} custom-call(f32[64,64]{1,0:T(8,128)} %reduce_sum.9.gram_ref, f32[64,512]{1,0:T(8,128)} %copy-done.2), custom_call_target="tpu_custom_call" | custom-call | tf_op jit(solution)/shard_map/solve/pallas_call | solution.py:341
  (147 shorter events, 30.4 us)
Async XLA Ops:
  2.6 30.1 %collective-permute-start.2 = (bf16[560,1024]{1,0:T(8,128)(2,1)}, bf16[560,1024]{1,0:T(8,128)(2,1)S(1)}, u32[]{:S(2)}, u32[]{:S(2)}) collective-permute-start(bf16[560,1024]{1,0:T(8,128)(2,1)} %payload.1.far_ref), channel_id=1, source_target_pairs={{0,120},{8,96},{16,104},{24,112},{32,24},{40,0},{48,8},{56,16},{64... | collective-permute-start | bytes 3440648 | tf_op jit(solution)/shard_map/ppermute | solution.py:357
  7.9 28.1 %collective-permute-start.1 = (bf16[560,1024]{1,0:T(8,128)(2,1)}, bf16[560,1024]{1,0:T(8,128)(2,1)S(1)}, u32[]{:S(2)}, u32[]{:S(2)}) collective-permute-start(bf16[560,1024]{1,0:T(8,128)(2,1)} %payload.1.far_ref), channel_id=1, source_target_pairs={{0,32},{8,40},{16,48},{24,56},{32,64},{40,72},{48,80},{56,88},{64,... | collective-permute-start | bytes 3440648 | tf_op jit(solution)/shard_map/ppermute | solution.py:357
  7.9 28.3 %collective-permute-start = (bf16[560,1024]{1,0:T(8,128)(2,1)}, bf16[560,1024]{1,0:T(8,128)(2,1)}, u32[]{:S(2)}, u32[]{:S(2)}) collective-permute-start(bf16[560,1024]{1,0:T(8,128)(2,1)} %payload.1.far_ref), channel_id=1, source_target_pairs={{0,8},{8,16},{16,24},{24,0},{32,40},{40,48},{48,56},{56,32},{64,72... | collective-permute-start | bytes 3440648 | tf_op jit(solution)/shard_map/ppermute | solution.py:357
  8.8 16.5 %all-to-all-start = ((bf16[8,64,512]{2,1,0:T(8,128)(2,1)}), bf16[8,64,512]{2,1,0:T(8,128)(2,1)S(1)}, u32[]{:S(2)}, u32[]{:S(2)}) async-start(bf16[8,64,512]{2,1,0:T(8,128)(2,1)} %broadcast_in_dim.8), calls=%async_computation | async-start | bytes 1048576 | tf_op jit(solution)/shard_map/all_to_all | solution.py:403
  37.2 27.3 %collective-permute-start.3 = (bf16[560,1024]{1,0:T(8,128)(2,1)}, bf16[560,1024]{1,0:T(8,128)(2,1)S(1)}, u32[]{:S(2)}, u32[]{:S(2)}) collective-permute-start(bf16[560,1024]{1,0:T(8,128)(2,1)} %get-tuple-element.42.refs_1_), channel_id=1, source_target_pairs={{0,32},{8,40},{16,48},{24,56},{32,64},{40,72},{48,80},{56,88},{64,... | collective-permute-start | bytes 3440648 | tf_op jit(solution)/shard_map/ppermute | solution.py:357
  37.2 27.3 %collective-permute-start.4 = (bf16[560,1024]{1,0:T(8,128)(2,1)}, bf16[560,1024]{1,0:T(8,128)(2,1)S(1)}, u32[]{:S(2)}, u32[]{:S(2)}) collective-permute-start(bf16[560,1024]{1,0:T(8,128)(2,1)} %get-tuple-element.43.refs_2_), channel_id=1, source_target_pairs={{0,24},{8,0},{16,8},{24,16},{32,56},{40,32},{48,40},{56,48},{64,88... | collective-permute-start | bytes 3440648 | tf_op jit(solution)/shard_map/ppermute | solution.py:357
  38.0 28.8 %collective-permute-start.5 = (bf16[560,1024]{1,0:T(8,128)(2,1)}, bf16[560,1024]{1,0:T(8,128)(2,1)S(1)}, u32[]{:S(2)}, u32[]{:S(2)}) collective-permute-start(bf16[560,1024]{1,0:T(8,128)(2,1)} %get-tuple-element.44.refs_0_), channel_id=1, source_target_pairs={{0,8},{24,0},{32,40},{56,32},{64,72},{88,64},{96,104},{120,96},{1,... | collective-permute-start | bytes 3440648 | tf_op jit(solution)/shard_map/ppermute | solution.py:357
  41.9 31.9 %collective-permute-start.8 = (bf16[560,1024]{1,0:T(8,128)(2,1)}, bf16[560,1024]{1,0:T(8,128)(2,1)}, u32[]{:S(2)}, u32[]{:S(2)}) collective-permute-start(bf16[560,1024]{1,0:T(8,128)(2,1)} %get-tuple-element.44.refs_0_), channel_id=1, source_target_pairs={{0,96},{8,104},{16,112},{24,120},{32,0},{40,8},{48,16},{56,24},{64... | collective-permute-start | bytes 3440648 | tf_op jit(solution)/shard_map/ppermute | solution.py:357
  67.8 26.0 %collective-permute-start.6 = (bf16[560,1024]{1,0:T(8,128)(2,1)}, bf16[560,1024]{1,0:T(8,128)(2,1)S(1)}, u32[]{:S(2)}, u32[]{:S(2)}) collective-permute-start(bf16[560,1024]{1,0:T(8,128)(2,1)} %get-tuple-element.52.refs_2_), channel_id=1, source_target_pairs={{0,8},{8,16},{16,24},{24,0},{32,40},{40,48},{48,56},{56,32},{64,72... | collective-permute-start | bytes 3440648 | tf_op jit(solution)/shard_map/ppermute | solution.py:357
  67.9 26.6 %collective-permute-start.7 = (bf16[560,1024]{1,0:T(8,128)(2,1)}, bf16[560,1024]{1,0:T(8,128)(2,1)S(1)}, u32[]{:S(2)}, u32[]{:S(2)}) collective-permute-start(bf16[560,1024]{1,0:T(8,128)(2,1)} %get-tuple-element.53.refs_1_), channel_id=1, source_target_pairs={{32,0},{40,8},{48,16},{56,24},{64,32},{72,40},{80,48},{88,56},{33,... | collective-permute-start | bytes 3440648 | tf_op jit(solution)/shard_map/ppermute | solution.py:357
  70.6 13.1 %collective-permute-start.9 = (bf16[80,512]{1,0:T(8,128)(2,1)}, bf16[80,512]{1,0:T(8,128)(2,1)S(1)}, u32[]{:S(2)}, u32[]{:S(2)}) collective-permute-start(bf16[80,512]{1,0:T(8,128)(2,1)} %get-tuple-element.60), channel_id=1, source_target_pairs={{8,0},{16,8},{24,16},{0,24},{40,32},{48,40},{56,48},{32,56},{72,64... | collective-permute-start | bytes 245768 | tf_op jit(solution)/shard_map/ppermute | solution.py:400
  95.7 22.6 %collective-permute-start.10 = (bf16[80,512]{1,0:T(8,128)(2,1)}, bf16[80,512]{1,0:T(8,128)(2,1)S(1)}, u32[]{:S(2)}, u32[]{:S(2)}) collective-permute-start(bf16[80,512]{1,0:T(8,128)(2,1)} %get-tuple-element.68), channel_id=1, source_target_pairs={{32,0},{40,8},{48,16},{56,24},{64,32},{72,40},{80,48},{88,56},{96,... | collective-permute-start | bytes 245768 | tf_op jit(solution)/shard_map/ppermute | solution.py:400
  100.6 17.8 %collective-permute-start.11 = (bf16[80,512]{1,0:T(8,128)(2,1)}, bf16[80,512]{1,0:T(8,128)(2,1)S(1)}, u32[]{:S(2)}, u32[]{:S(2)}) collective-permute-start(bf16[80,512]{1,0:T(8,128)(2,1)} %get-tuple-element.69), channel_id=1, source_target_pairs={{120,0},{96,8},{104,16},{112,24},{24,32},{0,40},{8,48},{16,56},{56... | collective-permute-start | bytes 245768 | tf_op jit(solution)/shard_map/ppermute | solution.py:400
  100.6 17.8 %collective-permute-start.12 = (bf16[80,512]{1,0:T(8,128)(2,1)}, bf16[80,512]{1,0:T(8,128)(2,1)S(1)}, u32[]{:S(2)}, u32[]{:S(2)}) collective-permute-start(bf16[80,512]{1,0:T(8,128)(2,1)} %get-tuple-element.70), channel_id=1, source_target_pairs={{104,0},{112,8},{120,16},{96,24},{8,32},{16,40},{24,48},{0,56},{40... | collective-permute-start | bytes 245768 | tf_op jit(solution)/shard_map/ppermute | solution.py:400
  102.9 15.4 %collective-permute-start.13 = (bf16[80,512]{1,0:T(8,128)(2,1)}, bf16[80,512]{1,0:T(8,128)(2,1)S(1)}, u32[]{:S(2)}, u32[]{:S(2)}) collective-permute-start(bf16[80,512]{1,0:T(8,128)(2,1)} %get-tuple-element.71), channel_id=1, source_target_pairs={{112,0},{120,8},{96,16},{104,24},{16,32},{24,40},{0,48},{8,56},{48... | collective-permute-start | bytes 245768 | tf_op jit(solution)/shard_map/ppermute | solution.py:400
  102.9 15.4 %collective-permute-start.14 = (bf16[80,512]{1,0:T(8,128)(2,1)}, bf16[80,512]{1,0:T(8,128)(2,1)S(1)}, u32[]{:S(2)}, u32[]{:S(2)}) collective-permute-start(bf16[80,512]{1,0:T(8,128)(2,1)} %get-tuple-element.72), channel_id=1, source_target_pairs={{0,64},{8,72},{16,80},{24,88},{32,96},{40,104},{48,112},{56,120},{... | collective-permute-start | bytes 245768 | tf_op jit(solution)/shard_map/ppermute | solution.py:400
  120.5 13.4 %collective-permute-start.19 = (bf16[80,512]{1,0:T(8,128)(2,1)S(1)}, bf16[80,512]{1,0:T(8,128)(2,1)S(1)}, u32[]{:S(2)}, u32[]{:S(2)}) collective-permute-start(bf16[80,512]{1,0:T(8,128)(2,1)S(1)} %copy-done.23), channel_id=1, source_target_pairs={{72,0},{80,8},{88,16},{64,24},{104,32},{112,40},{120,48},{96,56},{... | collective-permute-start | bytes 245768 | tf_op jit(solution)/shard_map/ppermute | solution.py:400
  122.5 15.2 %collective-permute-start.17 = (f32[72,512]{1,0:T(8,128)S(1)}, f32[72,512]{1,0:T(8,128)S(1)}, u32[]{:S(2)}, u32[]{:S(2)}) collective-permute-start(f32[72,512]{1,0:T(8,128)S(1)} %get-tuple-element.77), channel_id=1, source_target_pairs={{0,4},{1,5},{2,6},{3,7},{4,0},{5,1},{6,2},{7,3},{8,12},{9,13},{10,... | collective-permute-start | bytes 442376 | tf_op jit(solution)/shard_map/ppermute | solution.py:360
  125.7 12.1 %collective-permute-start.18 = (f32[72,512]{1,0:T(8,128)S(1)}, f32[72,512]{1,0:T(8,128)S(1)}, u32[]{:S(2)}, u32[]{:S(2)}) collective-permute-start(f32[72,512]{1,0:T(8,128)S(1)} %get-tuple-element.78), channel_id=1, source_target_pairs={{0,2},{1,3},{2,4},{3,5},{4,6},{5,7},{6,0},{7,1},{8,10},{9,11},{10,... | collective-permute-start | bytes 442376 | tf_op jit(solution)/shard_map/ppermute | solution.py:360
  127.3 10.5 %collective-permute-start.16 = (f32[72,512]{1,0:T(8,128)S(1)}, f32[72,512]{1,0:T(8,128)S(1)}, u32[]{:S(2)}, u32[]{:S(2)}) collective-permute-start(f32[72,512]{1,0:T(8,128)S(1)} %get-tuple-element.79), channel_id=1, source_target_pairs={{0,6},{1,7},{2,0},{3,1},{4,2},{5,3},{6,4},{7,5},{8,14},{9,15},{10,... | collective-permute-start | bytes 442376 | tf_op jit(solution)/shard_map/ppermute | solution.py:360
  128.9 7.6 %collective-permute-start.20 = (bf16[80,512]{1,0:T(8,128)(2,1)S(1)}, bf16[80,512]{1,0:T(8,128)(2,1)S(1)}, u32[]{:S(2)}, u32[]{:S(2)}) collective-permute-start(bf16[80,512]{1,0:T(8,128)(2,1)S(1)} %copy-done.24), channel_id=1, source_target_pairs={{0,16},{8,24},{32,48},{40,56},{64,80},{72,88},{96,112},{104,120},{... | collective-permute-start | bytes 245768 | tf_op jit(solution)/shard_map/ppermute | solution.py:400
  139.6 4.2 %collective-permute-start.25 = (f32[64,64]{1,0:T(8,128)S(1)}, f32[64,64]{1,0:T(8,128)S(1)}, u32[]{:S(2)}, u32[]{:S(2)}) collective-permute-start(f32[64,64]{1,0:T(8,128)S(1)} %add.404), channel_id=1, source_target_pairs={{0,6},{1,7},{2,0},{3,1},{4,2},{5,3},{6,4},{7,5},{8,14},{9,15},{10,... | collective-permute-start | bytes 49160 | tf_op jit(solution)/shard_map/ppermute | solution.py:360
  140.5 5.4 %collective-permute-start.24 = (f32[64,64]{1,0:T(8,128)S(1)}, f32[64,64]{1,0:T(8,128)S(1)}, u32[]{:S(2)}, u32[]{:S(2)}) collective-permute-start(f32[64,64]{1,0:T(8,128)S(1)} %add.404), channel_id=1, source_target_pairs={{0,4},{1,5},{2,6},{3,7},{4,0},{5,1},{6,2},{7,3},{8,12},{9,13},{10,... | collective-permute-start | bytes 49160 | tf_op jit(solution)/shard_map/ppermute | solution.py:360
  143.1 5.1 %collective-permute-start.23 = (f32[64,64]{1,0:T(8,128)S(1)}, f32[64,64]{1,0:T(8,128)S(1)}, u32[]{:S(2)}, u32[]{:S(2)}) collective-permute-start(f32[64,64]{1,0:T(8,128)S(1)} %add.404), channel_id=1, source_target_pairs={{0,2},{1,3},{2,4},{3,5},{4,6},{5,7},{6,0},{7,1},{8,10},{9,11},{10,... | collective-permute-start | bytes 49160 | tf_op jit(solution)/shard_map/ppermute | solution.py:360
  (30 other events, 209.0 us)

commit v17 on v14

--- a/solution.py
+++ b/solution.py
@@ -411,7 +411,7 @@
     group1, group2, group3 = ("a", "b", "c"), ("d", "e", "h"), ("f", "g", "k")
     sums, parts, token = work(group1, sums)
 
-    far["h"], far["e"], *parts = tie([far["h"], far["e"], *parts], token, far["d"], far["g"])
+    far["h"], far["e"], *parts = tie([far["h"], far["e"], *parts], token, far["g"])
     far["f"] = move(far["h"], 0, 1)
     far["k"] = move(far["e"], -1, 0, top_half)
     returned = give_back(("a",), parts[0:1])

time: 181 us -> 181 us (level)
  starting transfers between devices: 60.6 us -> 57.9 us
  Pallas kernels: 45.8 us -> 48.1 us
    ppermute x6, starting transfers between devices: 10.5 us -> 6.78 us  [turn(): lax.ppermute(array, 'col', [(i, (i + by * CORES) % COLS) for i in range(C...]
    ppermute x9, waiting for transfers between devices: 22.9 us -> 20.4 us  [move(): return lax.ppermute(array, 'row', shift(dy, dx, keep))]
    pallas_call x3, Pallas kernels: 28.9 us -> 31.1 us  [cells(): pl.pallas_call(functools.partial(cells_kernel, count), out_shape=[SUMS] +...]
  transfers between devices with their start and end apart: 27 -> 27, of which waited for: 12 -> 12; matrix products, arithmetic and copies ran while one was open for 3% -> 3% of each run, Pallas kernels for 21% -> 23%
where the time goes in v17:
time: 181 us; the launch traced here: 179 us
  starting transfers between devices  57.9 us (32%)
  Pallas kernels  48.1 us (27%)
  waiting for transfers between devices  30.3 us (17%)
  blocking collectives  27.8 us (15%)
  local copies, waits for them, and re-layouts  11.1 us (6%)
  other arithmetic  3.1 us (2%)
    ppermute x9, starting transfers between devices, give_back(): returned.append(lax.ppermute(part, 'row', back))  31.9 us
    pallas_call x3, Pallas kernels, cells(): pl.pallas_call(functools.partial(cells_kernel, count), out_shape=[SUMS] +...  31.1 us
    all_to_all x1, blocking collectives, per_device(): gram = jnp.sum(lax.all_to_all(everyone, 'row', 0, 0), axis=0)  27.8 us
    ppermute x9, waiting for transfers between devices, move(): return lax.ppermute(array, 'row', shift(dy, dx, keep))  20.4 us
    ppermute x9, starting transfers between devices, move(): return lax.ppermute(array, 'row', shift(dy, dx, keep))  13.8 us
    pallas_call x1, Pallas kernels, own_cells(): pl.pallas_call(own_kernel, out_shape=[SUMS, NORM, ROW, TOKEN], grid_spec=...  9.42 us
    ppermute x6, starting transfers between devices, turn(): lax.ppermute(array, 'col', [(i, (i + by * CORES) % COLS) for i in range(C...  6.78 us
    all_to_all x1, starting transfers between devices, per_device(): lax.all_to_all(jnp.broadcast_to(vectors, (COLS, EIGS, BLOCK)), 'col', 0, 0)  5.31 us
  transfers between devices with their start and end apart: 27, of which 12 were waited for; matrix products, arithmetic and copies ran while one was open for 3% of the time, Pallas kernels for 23%

profile of v17, /device:TPU:0, one launch (start us, length us, event | category | flops | bytes accessed | tf_op | source)
XLA Modules:
  0.0 179.4 jit_solution(15957014952092594520)
XLA Ops:
  0.0 2.6 %payload.1.far_ref = bf16[560,1024]{1,0:T(8,128)(2,1)} custom-call(s32[1]{0:T(128)} %bitcast.13.index_ref, bf16[8,512,1024]{2,1,0:T(8,128)(2,1)} %bitcast.36, bf16[64,512]{1,0:T(8,128)(2,1)} %v_ref.1), custom_call_target="tpu_custom_call" | custom-call | tf_op jit(solution)/shard_map/payload/pallas_call | solution.py:78
  2.6 5.3 %collective-permute-start.2 = (bf16[560,1024]{1,0:T(8,128)(2,1)}, bf16[560,1024]{1,0:T(8,128)(2,1)S(1)}, u32[]{:S(2)}, u32[]{:S(2)}) collective-permute-start(bf16[560,1024]{1,0:T(8,128)(2,1)} %payload.1.far_ref), channel_id=1, source_target_pairs={{0,120},{8,96},{16,104},{24,112},{32,24},{40,0},{48,8},{56,16},{64... | collective-permute-start | bytes 3440648 | tf_op jit(solution)/shard_map/ppermute | solution.py:357
  8.8 5.3 %all-to-all-start = ((bf16[8,64,512]{2,1,0:T(8,128)(2,1)}), bf16[8,64,512]{2,1,0:T(8,128)(2,1)S(1)}, u32[]{:S(2)}, u32[]{:S(2)}) async-start(bf16[8,64,512]{2,1,0:T(8,128)(2,1)} %broadcast_in_dim.8), calls=%async_computation | async-start | bytes 1048576 | tf_op jit(solution)/shard_map/all_to_all | solution.py:403
  15.9 9.4 %cells_own.1 = (f32[8,72,512]{2,1,0:T(8,128)}, f32[8,512,128]{2,1,0:T(8,128)}, f32[8,8,512]{2,1,0:T(8,128)}, f32[8,128]{1,0:T(8,128)}) custom-call(s32[8]{0:T(128)} %slice_reduce_fusion.flags_ref, bf16[8,512,1024]{2,1,0:T(8,128)(2,1)} %bitcast.37, bf16[560,1024]{1,0:T(8,128)(2,1)} %payload.1.far_ref), custom_call_target="tpu_custom_call" | custom-call | flops 2147483648 | bytes 13631488 | tf_op jit(solution)/shard_map/cells_own/pallas_call | solution.py:232
  25.3 7.4 %collective-permute-done.2.refs_2_ = bf16[560,1024]{1,0:T(8,128)(2,1)S(1)} collective-permute-done((bf16[560,1024]{1,0:T(8,128)(2,1)}, bf16[560,1024]{1,0:T(8,128)(2,1)S(1)}, u32[]{:S(2)}, u32[]{:S(2)}) %collective-permute-start.2) | collective-permute-done | bytes 1146912 | tf_op jit(solution)/shard_map/ppermute | solution.py:357
  32.8 3.3 %collective-permute-done.1.refs_1_ = bf16[560,1024]{1,0:T(8,128)(2,1)S(1)} collective-permute-done((bf16[560,1024]{1,0:T(8,128)(2,1)}, bf16[560,1024]{1,0:T(8,128)(2,1)S(1)}, u32[]{:S(2)}, u32[]{:S(2)}) %collective-permute-start.1) | collective-permute-done | bytes 1146912 | tf_op jit(solution)/shard_map/ppermute | solution.py:357
  37.9 3.1 %collective-permute-start.5 = (bf16[560,1024]{1,0:T(8,128)(2,1)}, bf16[560,1024]{1,0:T(8,128)(2,1)S(1)}, u32[]{:S(2)}, u32[]{:S(2)}) collective-permute-start(bf16[560,1024]{1,0:T(8,128)(2,1)} %get-tuple-element.45.refs_0_), channel_id=1, source_target_pairs={{0,8},{24,0},{32,40},{56,32},{64,72},{88,64},{96,104},{120,96},{1,... | collective-permute-start | bytes 3440648 | tf_op jit(solution)/shard_map/ppermute | solution.py:357
  41.8 3.2 %collective-permute-start.8 = (bf16[560,1024]{1,0:T(8,128)(2,1)}, bf16[560,1024]{1,0:T(8,128)(2,1)}, u32[]{:S(2)}, u32[]{:S(2)}) collective-permute-start(bf16[560,1024]{1,0:T(8,128)(2,1)} %get-tuple-element.45.refs_0_), channel_id=1, source_target_pairs={{0,96},{8,104},{16,112},{24,120},{32,0},{40,8},{48,16},{56,24},{64... | collective-permute-start | bytes 3440648 | tf_op jit(solution)/shard_map/ppermute | solution.py:357
  45.0 12.1 %cells.3 = (f32[8,72,512]{2,1,0:T(8,128)}, bf16[80,512]{1,0:T(8,128)(2,1)}, bf16[80,512]{1,0:T(8,128)(2,1)}, bf16[80,512]{1,0:T(8,128)(2,1)}, f32[8,128]{1,0:T(8,128)}) custom-call(s32[24]{0:T(128)} %reshape.212.flags_ref, bf16[8,512,1024]{2,1,0:T(8,128)(2,1)} %bitcast.38, bf16[8,64,512]{2,1,0:T(8,128)(2,1)} %copy-done.1, ...), custom_call_target="tpu_custom_call", output_to_operand_aliasing={{0}: (8, {})} | custom-call | flops 6442450944 | bytes 15728640 | tf_op jit(solution)/shard_map/cells/pallas_call | solution.py:271
  57.1 7.3 %collective-permute-done.3.refs_0_ = bf16[560,1024]{1,0:T(8,128)(2,1)S(1)} collective-permute-done((bf16[560,1024]{1,0:T(8,128)(2,1)}, bf16[560,1024]{1,0:T(8,128)(2,1)S(1)}, u32[]{:S(2)}, u32[]{:S(2)}) %collective-permute-start.3) | collective-permute-done | bytes 1146912 | tf_op jit(solution)/shard_map/ppermute | solution.py:357
  64.4 2.3 %collective-permute-done.5.refs_6_.refs_1_ = bf16[560,1024]{1,0:T(8,128)(2,1)S(1)} collective-permute-done((bf16[560,1024]{1,0:T(8,128)(2,1)}, bf16[560,1024]{1,0:T(8,128)(2,1)S(1)}, u32[]{:S(2)}, u32[]{:S(2)}) %collective-permute-start.5) | collective-permute-done | bytes 1146912 | tf_op jit(solution)/shard_map/ppermute | solution.py:357
  70.6 3.1 %collective-permute-start.9 = (bf16[80,512]{1,0:T(8,128)(2,1)}, bf16[80,512]{1,0:T(8,128)(2,1)S(1)}, u32[]{:S(2)}, u32[]{:S(2)}) collective-permute-start(bf16[80,512]{1,0:T(8,128)(2,1)} %get-tuple-element.61), channel_id=1, source_target_pairs={{8,0},{16,8},{24,16},{0,24},{40,32},{48,40},{56,48},{32,56},{72,64... | collective-permute-start | bytes 245768 | tf_op jit(solution)/shard_map/ppermute | solution.py:400
  73.8 9.9 %cells.4 = (f32[8,72,512]{2,1,0:T(8,128)}, bf16[80,512]{1,0:T(8,128)(2,1)}, bf16[80,512]{1,0:T(8,128)(2,1)}, bf16[80,512]{1,0:T(8,128)(2,1)}, f32[8,128]{1,0:T(8,128)}) custom-call(s32[24]{0:T(128)} %reshape.213.flags_ref, bf16[8,512,1024]{2,1,0:T(8,128)(2,1)} %bitcast.39, bf16[8,64,512]{2,1,0:T(8,128)(2,1)} %copy-done.1, ...), custom_call_target="tpu_custom_call", output_to_operand_aliasing={{0}: (8, {})} | custom-call | flops 6442450944 | bytes 15728640 | tf_op jit(solution)/shard_map/cells/pallas_call | solution.py:271
  84.4 5.5 %collective-permute-start.11 = (bf16[80,512]{1,0:T(8,128)(2,1)}, bf16[80,512]{1,0:T(8,128)(2,1)S(1)}, u32[]{:S(2)}, u32[]{:S(2)}) collective-permute-start(bf16[80,512]{1,0:T(8,128)(2,1)} %get-tuple-element.71), channel_id=1, source_target_pairs={{120,0},{96,8},{104,16},{112,24},{24,32},{0,40},{8,48},{16,56},{56... | collective-permute-start | bytes 245768 | tf_op jit(solution)/shard_map/ppermute | solution.py:400
  89.8 8.3 %collective-permute-start.12 = (bf16[80,512]{1,0:T(8,128)(2,1)}, bf16[80,512]{1,0:T(8,128)(2,1)S(1)}, u32[]{:S(2)}, u32[]{:S(2)}) collective-permute-start(bf16[80,512]{1,0:T(8,128)(2,1)} %get-tuple-element.72), channel_id=1, source_target_pairs={{104,0},{112,8},{120,16},{96,24},{8,32},{16,40},{24,48},{0,56},{40... | collective-permute-start | bytes 245768 | tf_op jit(solution)/shard_map/ppermute | solution.py:400
  98.2 4.1 %collective-permute-start.10 = (bf16[80,512]{1,0:T(8,128)(2,1)}, bf16[80,512]{1,0:T(8,128)(2,1)S(1)}, u32[]{:S(2)}, u32[]{:S(2)}) collective-permute-start(bf16[80,512]{1,0:T(8,128)(2,1)} %get-tuple-element.63.refs_4_), channel_id=1, source_target_pairs={{32,0},{40,8},{48,16},{56,24},{64,32},{72,40},{80,48},{88,56},{96,... | collective-permute-start | bytes 245768 | tf_op jit(solution)/shard_map/ppermute | solution.py:400
  105.0 9.0 %cells.5 = (f32[8,72,512]{2,1,0:T(8,128)}, bf16[80,512]{1,0:T(8,128)(2,1)}, bf16[80,512]{1,0:T(8,128)(2,1)}, bf16[80,512]{1,0:T(8,128)(2,1)}, f32[8,128]{1,0:T(8,128)}) custom-call(s32[24]{0:T(128)} %reshape.210.flags_ref, bf16[8,512,1024]{2,1,0:T(8,128)(2,1)} %bitcast.40, bf16[8,64,512]{2,1,0:T(8,128)(2,1)} %copy-done.1, ...), custom_call_target="tpu_custom_call", output_to_operand_aliasing={{0}: (8, {})} | custom-call | flops 6442450944 | bytes 15728640 | tf_op jit(solution)/shard_map/cells/pallas_call | solution.py:271
  116.3 1.8 collective-permute-done.15
  119.7 2.8 %collective-permute-start.18 = (f32[72,512]{1,0:T(8,128)S(1)}, f32[72,512]{1,0:T(8,128)S(1)}, u32[]{:S(2)}, u32[]{:S(2)}) collective-permute-start(f32[72,512]{1,0:T(8,128)S(1)} %get-tuple-element.80), channel_id=1, source_target_pairs={{0,2},{1,3},{2,4},{3,5},{4,6},{5,7},{6,0},{7,1},{8,10},{9,11},{10,... | collective-permute-start | bytes 442376 | tf_op jit(solution)/shard_map/ppermute | solution.py:360
  122.9 8.1 %collective-permute-start.20 = (bf16[80,512]{1,0:T(8,128)(2,1)S(1)}, bf16[80,512]{1,0:T(8,128)(2,1)S(1)}, u32[]{:S(2)}, u32[]{:S(2)}) collective-permute-start(bf16[80,512]{1,0:T(8,128)(2,1)S(1)} %copy-done.24), channel_id=1, source_target_pairs={{0,16},{8,24},{32,48},{40,56},{64,80},{72,88},{96,112},{104,120},{... | collective-permute-start | bytes 245768 | tf_op jit(solution)/shard_map/ppermute | solution.py:400
  136.5 1.9 %collective-permute-start.24 = (f32[64,64]{1,0:T(8,128)S(1)}, f32[64,64]{1,0:T(8,128)S(1)}, u32[]{:S(2)}, u32[]{:S(2)}) collective-permute-start(f32[64,64]{1,0:T(8,128)S(1)} %add.404), channel_id=1, source_target_pairs={{0,4},{1,5},{2,6},{3,7},{4,0},{5,1},{6,2},{7,3},{8,12},{9,13},{10,... | collective-permute-start | bytes 49160 | tf_op jit(solution)/shard_map/ppermute | solution.py:360
  138.4 1.8 %collective-permute-done.25 = f32[64,64]{1,0:T(8,128)S(1)} collective-permute-done((f32[64,64]{1,0:T(8,128)S(1)}, f32[64,64]{1,0:T(8,128)S(1)}, u32[]{:S(2)}, u32[]{:S(2)}) %collective-permute-start.25) | collective-permute-done | bytes 16416 | tf_op jit(solution)/shard_map/ppermute | solution.py:360
  143.9 27.8 %all_to_all.10 = f32[16,1,4096]{2,1,0:T(1,128)S(1)} all-to-all(f32[16,1,4096]{2,1,0:T(1,128)S(1)} %reshape.218), channel_id=1, replica_groups=mesh['row'=16,'col'=8] {'row'}, dimensions={0} | all-to-all | bytes 524288 | tf_op jit(solution)/shard_map/all_to_all | solution.py:447
  174.4 5.0 %solve.1 = f32[64,512]{1,0:T(8,128)} custom-call(f32[64,64]{1,0:T(8,128)} %reduce_sum.9.gram_ref, f32[64,512]{1,0:T(8,128)} %copy-done.2), custom_call_target="tpu_custom_call" | custom-call | tf_op jit(solution)/shard_map/solve/pallas_call | solution.py:341
  (148 shorter events, 28.1 us)
Async XLA Ops:
  2.6 30.1 %collective-permute-start.2 = (bf16[560,1024]{1,0:T(8,128)(2,1)}, bf16[560,1024]{1,0:T(8,128)(2,1)S(1)}, u32[]{:S(2)}, u32[]{:S(2)}) collective-permute-start(bf16[560,1024]{1,0:T(8,128)(2,1)} %payload.1.far_ref), channel_id=1, source_target_pairs={{0,120},{8,96},{16,104},{24,112},{32,24},{40,0},{48,8},{56,16},{64... | collective-permute-start | bytes 3440648 | tf_op jit(solution)/shard_map/ppermute | solution.py:357
  7.9 28.1 %collective-permute-start.1 = (bf16[560,1024]{1,0:T(8,128)(2,1)}, bf16[560,1024]{1,0:T(8,128)(2,1)S(1)}, u32[]{:S(2)}, u32[]{:S(2)}) collective-permute-start(bf16[560,1024]{1,0:T(8,128)(2,1)} %payload.1.far_ref), channel_id=1, source_target_pairs={{0,32},{8,40},{16,48},{24,56},{32,64},{40,72},{48,80},{56,88},{64,... | collective-permute-start | bytes 3440648 | tf_op jit(solution)/shard_map/ppermute | solution.py:357
  7.9 28.3 %collective-permute-start = (bf16[560,1024]{1,0:T(8,128)(2,1)}, bf16[560,1024]{1,0:T(8,128)(2,1)}, u32[]{:S(2)}, u32[]{:S(2)}) collective-permute-start(bf16[560,1024]{1,0:T(8,128)(2,1)} %payload.1.far_ref), channel_id=1, source_target_pairs={{0,8},{8,16},{16,24},{24,0},{32,40},{40,48},{48,56},{56,32},{64,72... | collective-permute-start | bytes 3440648 | tf_op jit(solution)/shard_map/ppermute | solution.py:357
  8.8 16.6 %all-to-all-start = ((bf16[8,64,512]{2,1,0:T(8,128)(2,1)}), bf16[8,64,512]{2,1,0:T(8,128)(2,1)S(1)}, u32[]{:S(2)}, u32[]{:S(2)}) async-start(bf16[8,64,512]{2,1,0:T(8,128)(2,1)} %broadcast_in_dim.8), calls=%async_computation | async-start | bytes 1048576 | tf_op jit(solution)/shard_map/all_to_all | solution.py:403
  37.1 27.3 %collective-permute-start.3 = (bf16[560,1024]{1,0:T(8,128)(2,1)}, bf16[560,1024]{1,0:T(8,128)(2,1)S(1)}, u32[]{:S(2)}, u32[]{:S(2)}) collective-permute-start(bf16[560,1024]{1,0:T(8,128)(2,1)} %get-tuple-element.43.refs_1_), channel_id=1, source_target_pairs={{0,32},{8,40},{16,48},{24,56},{32,64},{40,72},{48,80},{56,88},{64,... | collective-permute-start | bytes 3440648 | tf_op jit(solution)/shard_map/ppermute | solution.py:357
  37.1 27.3 %collective-permute-start.4 = (bf16[560,1024]{1,0:T(8,128)(2,1)}, bf16[560,1024]{1,0:T(8,128)(2,1)S(1)}, u32[]{:S(2)}, u32[]{:S(2)}) collective-permute-start(bf16[560,1024]{1,0:T(8,128)(2,1)} %get-tuple-element.44.refs_2_), channel_id=1, source_target_pairs={{0,24},{8,0},{16,8},{24,16},{32,56},{40,32},{48,40},{56,48},{64,88... | collective-permute-start | bytes 3440648 | tf_op jit(solution)/shard_map/ppermute | solution.py:357
  37.9 28.8 %collective-permute-start.5 = (bf16[560,1024]{1,0:T(8,128)(2,1)}, bf16[560,1024]{1,0:T(8,128)(2,1)S(1)}, u32[]{:S(2)}, u32[]{:S(2)}) collective-permute-start(bf16[560,1024]{1,0:T(8,128)(2,1)} %get-tuple-element.45.refs_0_), channel_id=1, source_target_pairs={{0,8},{24,0},{32,40},{56,32},{64,72},{88,64},{96,104},{120,96},{1,... | collective-permute-start | bytes 3440648 | tf_op jit(solution)/shard_map/ppermute | solution.py:357
  41.8 32.0 %collective-permute-start.8 = (bf16[560,1024]{1,0:T(8,128)(2,1)}, bf16[560,1024]{1,0:T(8,128)(2,1)}, u32[]{:S(2)}, u32[]{:S(2)}) collective-permute-start(bf16[560,1024]{1,0:T(8,128)(2,1)} %get-tuple-element.45.refs_0_), channel_id=1, source_target_pairs={{0,96},{8,104},{16,112},{24,120},{32,0},{40,8},{48,16},{56,24},{64... | collective-permute-start | bytes 3440648 | tf_op jit(solution)/shard_map/ppermute | solution.py:357
  67.8 34.5 %collective-permute-start.6 = (bf16[560,1024]{1,0:T(8,128)(2,1)}, bf16[560,1024]{1,0:T(8,128)(2,1)S(1)}, u32[]{:S(2)}, u32[]{:S(2)}) collective-permute-start(bf16[560,1024]{1,0:T(8,128)(2,1)} %get-tuple-element.53.refs_2_), channel_id=1, source_target_pairs={{0,8},{8,16},{16,24},{24,0},{32,40},{40,48},{48,56},{56,32},{64,72... | collective-permute-start | bytes 3440648 | tf_op jit(solution)/shard_map/ppermute | solution.py:357
  67.9 34.4 %collective-permute-start.7 = (bf16[560,1024]{1,0:T(8,128)(2,1)}, bf16[560,1024]{1,0:T(8,128)(2,1)S(1)}, u32[]{:S(2)}, u32[]{:S(2)}) collective-permute-start(bf16[560,1024]{1,0:T(8,128)(2,1)} %get-tuple-element.54.refs_1_), channel_id=1, source_target_pairs={{32,0},{40,8},{48,16},{56,24},{64,32},{72,40},{80,48},{88,56},{33,... | collective-permute-start | bytes 3440648 | tf_op jit(solution)/shard_map/ppermute | solution.py:357
  70.6 13.1 %collective-permute-start.9 = (bf16[80,512]{1,0:T(8,128)(2,1)}, bf16[80,512]{1,0:T(8,128)(2,1)S(1)}, u32[]{:S(2)}, u32[]{:S(2)}) collective-permute-start(bf16[80,512]{1,0:T(8,128)(2,1)} %get-tuple-element.61), channel_id=1, source_target_pairs={{8,0},{16,8},{24,16},{0,24},{40,32},{48,40},{56,48},{32,56},{72,64... | collective-permute-start | bytes 245768 | tf_op jit(solution)/shard_map/ppermute | solution.py:400
  84.4 29.7 %collective-permute-start.11 = (bf16[80,512]{1,0:T(8,128)(2,1)}, bf16[80,512]{1,0:T(8,128)(2,1)S(1)}, u32[]{:S(2)}, u32[]{:S(2)}) collective-permute-start(bf16[80,512]{1,0:T(8,128)(2,1)} %get-tuple-element.71), channel_id=1, source_target_pairs={{120,0},{96,8},{104,16},{112,24},{24,32},{0,40},{8,48},{16,56},{56... | collective-permute-start | bytes 245768 | tf_op jit(solution)/shard_map/ppermute | solution.py:400
  89.8 24.2 %collective-permute-start.12 = (bf16[80,512]{1,0:T(8,128)(2,1)}, bf16[80,512]{1,0:T(8,128)(2,1)S(1)}, u32[]{:S(2)}, u32[]{:S(2)}) collective-permute-start(bf16[80,512]{1,0:T(8,128)(2,1)} %get-tuple-element.72), channel_id=1, source_target_pairs={{104,0},{112,8},{120,16},{96,24},{8,32},{16,40},{24,48},{0,56},{40... | collective-permute-start | bytes 245768 | tf_op jit(solution)/shard_map/ppermute | solution.py:400
  98.2 15.9 %collective-permute-start.10 = (bf16[80,512]{1,0:T(8,128)(2,1)}, bf16[80,512]{1,0:T(8,128)(2,1)S(1)}, u32[]{:S(2)}, u32[]{:S(2)}) collective-permute-start(bf16[80,512]{1,0:T(8,128)(2,1)} %get-tuple-element.63.refs_4_), channel_id=1, source_target_pairs={{32,0},{40,8},{48,16},{56,24},{64,32},{72,40},{80,48},{88,56},{96,... | collective-permute-start | bytes 245768 | tf_op jit(solution)/shard_map/ppermute | solution.py:400
  103.7 10.4 %collective-permute-start.13 = (bf16[80,512]{1,0:T(8,128)(2,1)}, bf16[80,512]{1,0:T(8,128)(2,1)S(1)}, u32[]{:S(2)}, u32[]{:S(2)}) collective-permute-start(bf16[80,512]{1,0:T(8,128)(2,1)} %get-tuple-element.73), channel_id=1, source_target_pairs={{112,0},{120,8},{96,16},{104,24},{16,32},{24,40},{0,48},{8,56},{48... | collective-permute-start | bytes 245768 | tf_op jit(solution)/shard_map/ppermute | solution.py:400
  103.7 10.4 %collective-permute-start.14 = (bf16[80,512]{1,0:T(8,128)(2,1)}, bf16[80,512]{1,0:T(8,128)(2,1)S(1)}, u32[]{:S(2)}, u32[]{:S(2)}) collective-permute-start(bf16[80,512]{1,0:T(8,128)(2,1)} %get-tuple-element.74), channel_id=1, source_target_pairs={{0,64},{8,72},{16,80},{24,88},{32,96},{40,104},{48,112},{56,120},{... | collective-permute-start | bytes 245768 | tf_op jit(solution)/shard_map/ppermute | solution.py:400
  116.2 14.9 %collective-permute-start.19 = (bf16[80,512]{1,0:T(8,128)(2,1)S(1)}, bf16[80,512]{1,0:T(8,128)(2,1)S(1)}, u32[]{:S(2)}, u32[]{:S(2)}) collective-permute-start(bf16[80,512]{1,0:T(8,128)(2,1)S(1)} %copy-done.23), channel_id=1, source_target_pairs={{72,0},{80,8},{88,16},{64,24},{104,32},{112,40},{120,48},{96,56},{... | collective-permute-start | bytes 245768 | tf_op jit(solution)/shard_map/ppermute | solution.py:400
  118.3 16.2 %collective-permute-start.17 = (f32[72,512]{1,0:T(8,128)S(1)}, f32[72,512]{1,0:T(8,128)S(1)}, u32[]{:S(2)}, u32[]{:S(2)}) collective-permute-start(f32[72,512]{1,0:T(8,128)S(1)} %get-tuple-element.79), channel_id=1, source_target_pairs={{0,4},{1,5},{2,6},{3,7},{4,0},{5,1},{6,2},{7,3},{8,12},{9,13},{10,... | collective-permute-start | bytes 442376 | tf_op jit(solution)/shard_map/ppermute | solution.py:360
  119.7 14.8 %collective-permute-start.18 = (f32[72,512]{1,0:T(8,128)S(1)}, f32[72,512]{1,0:T(8,128)S(1)}, u32[]{:S(2)}, u32[]{:S(2)}) collective-permute-start(f32[72,512]{1,0:T(8,128)S(1)} %get-tuple-element.80), channel_id=1, source_target_pairs={{0,2},{1,3},{2,4},{3,5},{4,6},{5,7},{6,0},{7,1},{8,10},{9,11},{10,... | collective-permute-start | bytes 442376 | tf_op jit(solution)/shard_map/ppermute | solution.py:360
  122.5 12.0 %collective-permute-start.16 = (f32[72,512]{1,0:T(8,128)S(1)}, f32[72,512]{1,0:T(8,128)S(1)}, u32[]{:S(2)}, u32[]{:S(2)}) collective-permute-start(f32[72,512]{1,0:T(8,128)S(1)} %get-tuple-element.81), channel_id=1, source_target_pairs={{0,6},{1,7},{2,0},{3,1},{4,2},{5,3},{6,4},{7,5},{8,14},{9,15},{10,... | collective-permute-start | bytes 442376 | tf_op jit(solution)/shard_map/ppermute | solution.py:360
  122.9 10.6 %collective-permute-start.20 = (bf16[80,512]{1,0:T(8,128)(2,1)S(1)}, bf16[80,512]{1,0:T(8,128)(2,1)S(1)}, u32[]{:S(2)}, u32[]{:S(2)}) collective-permute-start(bf16[80,512]{1,0:T(8,128)(2,1)S(1)} %copy-done.24), channel_id=1, source_target_pairs={{0,16},{8,24},{32,48},{40,56},{64,80},{72,88},{96,112},{104,120},{... | collective-permute-start | bytes 245768 | tf_op jit(solution)/shard_map/ppermute | solution.py:400
  136.3 3.9 %collective-permute-start.25 = (f32[64,64]{1,0:T(8,128)S(1)}, f32[64,64]{1,0:T(8,128)S(1)}, u32[]{:S(2)}, u32[]{:S(2)}) collective-permute-start(f32[64,64]{1,0:T(8,128)S(1)} %add.404), channel_id=1, source_target_pairs={{0,6},{1,7},{2,0},{3,1},{4,2},{5,3},{6,4},{7,5},{8,14},{9,15},{10,... | collective-permute-start | bytes 49160 | tf_op jit(solution)/shard_map/ppermute | solution.py:360
  136.5 5.4 %collective-permute-start.24 = (f32[64,64]{1,0:T(8,128)S(1)}, f32[64,64]{1,0:T(8,128)S(1)}, u32[]{:S(2)}, u32[]{:S(2)}) collective-permute-start(f32[64,64]{1,0:T(8,128)S(1)} %add.404), channel_id=1, source_target_pairs={{0,4},{1,5},{2,6},{3,7},{4,0},{5,1},{6,2},{7,3},{8,12},{9,13},{10,... | collective-permute-start | bytes 49160 | tf_op jit(solution)/shard_map/ppermute | solution.py:360
  138.4 5.1 %collective-permute-start.23 = (f32[64,64]{1,0:T(8,128)S(1)}, f32[64,64]{1,0:T(8,128)S(1)}, u32[]{:S(2)}, u32[]{:S(2)}) collective-permute-start(f32[64,64]{1,0:T(8,128)S(1)} %add.404), channel_id=1, source_target_pairs={{0,2},{1,3},{2,4},{3,5},{4,6},{5,7},{6,0},{7,1},{8,10},{9,11},{10,... | collective-permute-start | bytes 49160 | tf_op jit(solution)/shard_map/ppermute | solution.py:360
  (30 other events, 206.9 us)
